TPU v7x, 128 devices: a whole 4x4x4 slice. The times are simulated.
128 devices in a mesh: tm: 32 (over y, x, core), blk: 4 (over z).
Axes of the slice: x: 4, y: 4, z: 4, core: 2. Of those that a mesh axis runs over, the one named last changes fastest.
Arguments:
- dynamics: float32 [256, 256], replicated
- dynamics_mask: int32 [8, 8], replicated, may hold values from 0 to 1, as said below
- obs_op: float32 [256, 256], replicated, may hold values from -0.375 to 0.375
- obs_mask: int32 [8, 8], replicated, may hold values from 0 to 1, as said below
- process_noise: float32 [256], replicated, may hold values from 0.0005 to 0.005
- initial_expectation: float32 [256], replicated, may hold values from -6 to 6
- filter_gains: float32 [512, 256, 256], P('tm', 'blk'), may hold values from -0.009765625 to 0.009765625
- observations: float32 [512, 256], P('tm'), may hold values from -6 to 6
- smooth_gains: float32 [512, 256, 256], P('tm', 'blk')
- filt_cov: float32 [512, 256, 256], P('tm', 'blk')
Outputs:
- smoothed_means: float32 [512, 256], P('tm', 'blk')
- smoothed_cov: float32 [512, 256, 256], P('tm', 'blk')
Inputs may be any that keep to these rules, and one draw needn't show every extreme that they name: `dynamics_mask`: diagonal blocks are 1. `obs_mask`: blocks with equal row and column index are 1.
All inputs are finite; a program needn't handle non-finite values.
Results may differ from a plain program's by a relative error of at most 0.0003.
Values sent between devices are 32-bit elements; how exact they have to be, the bound alone decides.
A program may use at most 256 MiB of HBM per device.

v0:
```python
import jax
import jax.numpy as jnp
from jax import lax
from jax.sharding import PartitionSpec as P

highest = lax.Precision.HIGHEST


def from_behind(block, axis, distance):
    devices = range(lax.axis_size(axis))
    route = [(i - distance, i) for i in devices if i - distance in devices]
    return lax.ppermute(block, axis, route)


def expand_mask(mask, row_total, col_total):
    row_block = row_total // mask.shape[0]
    col_block = col_total // mask.shape[1]
    return jnp.repeat(jnp.repeat(mask.astype(jnp.float32), row_block, axis=0), col_block, axis=1)


def matmul(left, right):
    return jnp.matmul(left, right, precision=highest)


def filter_join(earlier, latter):
    return (matmul(latter[0], earlier[0]), matmul(latter[0], earlier[1]) + latter[1])


def smooth_join(earlier, latter):
    gain_late = latter[0]
    return (
        matmul(gain_late, earlier[0]),
        matmul(matmul(gain_late, earlier[1]), gain_late.T) + latter[1],
        matmul(gain_late, earlier[2]) + latter[2],
    )


def pack_filter(parts):
    return jnp.concatenate([parts[0], parts[1][None, :]], axis=0)


def unpack_filter(packed, width):
    return (packed[:width], packed[width])


def pack_smooth(parts):
    return jnp.concatenate([parts[0], parts[1], parts[2][None, :]], axis=0)


def unpack_smooth(packed, width):
    return (packed[:width], packed[width : 2 * width], packed[2 * width])


def window_work(
    trans_map,
    process_noise,
    initial_expectation,
    transition_operators,
    step_shifts,
    gain_full,
    cov_full,
    is_final,
    filter_prefix,
    smooth_prefix,
):
    width = trans_map.shape[0]
    step_count = transition_operators.shape[0]
    final_step = jnp.logical_and(is_final, jnp.arange(step_count) == step_count - 1)
    gain_full = jnp.where(final_step[:, None, None], jnp.float32(0.0), gain_full)
    ident_map = jnp.eye(width, dtype=jnp.float32)
    zero_mat = jnp.zeros((width, width), jnp.float32)
    zero_vec = jnp.zeros((width,), jnp.float32)

    def window_filter(running, step_parts):
        return (filter_join(running, step_parts), None)

    filt_window = lax.scan(
        window_filter, (ident_map, zero_vec), (transition_operators, step_shifts)
    )[0]
    filt_before = filter_prefix(filt_window)
    mean_in = matmul(filt_before[0], initial_expectation) + filt_before[1]

    def filter_walk(current, step_parts):
        current = matmul(step_parts[0], current) + step_parts[1]
        return (current, current)

    filt_means = lax.scan(filter_walk, mean_in, (transition_operators, step_shifts))[1]
    predicted = matmul(matmul(trans_map, cov_full), trans_map.T) + jnp.diag(process_noise)
    gain_trans = jnp.swapaxes(gain_full, 1, 2)
    residual_cov = cov_full - matmul(matmul(gain_full, predicted), gain_trans)
    moved_means = jnp.einsum("ij,tj->ti", trans_map, filt_means, precision=highest)
    offsets = filt_means - jnp.einsum("tij,tj->ti", gain_full, moved_means, precision=highest)

    def window_smooth(running, step_parts):
        return (smooth_join(running, step_parts), None)

    smooth_window = lax.scan(
        window_smooth,
        (ident_map, zero_mat, zero_vec),
        (gain_full, residual_cov, offsets),
        reverse=True,
    )[0]
    smooth_after = smooth_prefix(smooth_window)

    def smooth_walk(current, step_parts):
        cov_next, mean_next = current
        gain_now, resid_now, offset_now = step_parts
        cov_now = matmul(matmul(gain_now, cov_next), gain_now.T) + resid_now
        current_mean = matmul(gain_now, mean_next) + offset_now
        return ((cov_now, current_mean), (current_mean, cov_now))

    return lax.scan(
        smooth_walk,
        (smooth_after[1], smooth_after[2]),
        (gain_full, residual_cov, offsets),
        reverse=True,
    )[1]


def per_device(
    dynamics,
    dynamics_mask,
    obs_op,
    obs_mask,
    process_noise,
    initial_expectation,
    filter_gains,
    observations,
    smooth_gains,
    filt_cov,
):
    width = dynamics.shape[0]
    obs_width = obs_op.shape[0]
    row_count = filter_gains.shape[1]
    row_start = lax.axis_index("blk") * row_count
    trans_map = dynamics * expand_mask(dynamics_mask, width, width)
    obs_map = obs_op * expand_mask(obs_mask, obs_width, width)
    obs_dyn = matmul(obs_map, trans_map)
    own_rows = lax.dynamic_slice_in_dim(trans_map, row_start, row_count, 0)
    map_rows = own_rows[None] - matmul(filter_gains, obs_dyn)
    shift_rows = jnp.einsum("tro,to->tr", filter_gains, observations, precision=highest)
    ident_map = jnp.eye(width, dtype=jnp.float32)
    zero_mat = jnp.zeros((width, width), jnp.float32)
    zero_vec = jnp.zeros((width,), jnp.float32)
    transition_operators, step_shifts, gain_full, cov_full = (
        lax.all_gather(map_rows, "blk", axis=1, tiled=True),
        lax.all_gather(shift_rows, "blk", axis=1, tiled=True),
        lax.all_gather(smooth_gains, "blk", axis=1, tiled=True),
        lax.all_gather(filt_cov, "blk", axis=1, tiled=True),
    )
    tm_index = lax.axis_index("tm")
    tm_count = lax.axis_size("tm")

    def before_filter(filt_window):

        def chain_filter(turn_no, running):
            arrived = from_behind(pack_filter(filter_join(running, filt_window)), "tm", 1)
            parts = unpack_filter(arrived, width)
            first_window = tm_index == 0
            return (
                jnp.where(first_window, ident_map, parts[0]),
                jnp.where(first_window, zero_vec, parts[1]),
            )

        return lax.fori_loop(0, tm_count - 1, chain_filter, (ident_map, zero_vec))

    def after_smooth(smooth_window):

        def chain_smooth(turn_no, running):
            arrived = from_behind(pack_smooth(smooth_join(running, smooth_window)), "tm", -1)
            parts = unpack_smooth(arrived, width)
            last_window = tm_index == tm_count - 1
            return (
                jnp.where(last_window, ident_map, parts[0]),
                jnp.where(last_window, zero_mat, parts[1]),
                jnp.where(last_window, zero_vec, parts[2]),
            )

        return lax.fori_loop(0, tm_count - 1, chain_smooth, (ident_map, zero_mat, zero_vec))

    means_out, cov_out = window_work(
        trans_map,
        process_noise,
        initial_expectation,
        transition_operators,
        step_shifts,
        gain_full,
        cov_full,
        tm_index == tm_count - 1,
        before_filter,
        after_smooth,
    )
    means_rows = lax.dynamic_slice_in_dim(means_out, row_start, row_count, 1)
    cov_rows = lax.dynamic_slice_in_dim(cov_out, row_start, row_count, 1)
    return (means_rows, cov_rows)


def solution(mesh):
    return jax.shard_map(
        per_device,
        mesh=mesh,
        in_specs=(
            P(),
            P(),
            P(),
            P(),
            P(),
            P(),
            P("tm", "blk", None),
            P("tm", None),
            P("tm", "blk", None),
            P("tm", "blk", None),
        ),
        out_specs=(P("tm", "blk"), P("tm", "blk", None)),
        check_vma=False,
    )
```

profile of v0, /device:TPU:15, one launch (start us, length us, event | category | flops | bytes accessed | tf_op | source)
XLA Modules:
  0.0 1111.2 jit_solution(17786515966806534478)
XLA Ops:
  16.8 10.5 all-gather
  28.2 36.8 %all-gather.9.cloned.1.call-done = f32[16,256,256]{2,1,0:T(8,128)} async-done(((f32[16,64,256]{2,1,0:T(8,128)}), f32[16,256,256]{2,1,0:T(8,128)}) %all-gather.9.cloned.1.call-update) | async-done | bytes 4194320 | tf_op jit(solution)/shard_map/all_gather | solution.py:146
  65.0 43.3 %while.99 = (s32[]{:T(128)}, f32[256,256]{1,0:T(8,128)S(1)}, f32[256]{0:T(256)S(1)}, f32[16,256,256]{2,1,0:T(8,128)}, f32[16,256]{1,0:T(8,128)S(1)}, /*index=5*/s32[]{:T(128)}, s32[]{:T(128)}) while((s32[]{:T(128)}, f32[256,256]{1,0:T(8,128)S(1)}, f32[256]{0:T(256)S(1)}, f32[16,256,256]{2,1,0:T(8,128)}, f32[16,256]{1,0:T(8,128)S(1)}, ...), condition=%wide.region_1.2_spmd.clone, body=%wide.region_0.1_spmd.clone.sunk | while | flops 202113536 | bytes 1583195 | solution.py:77
  108.4 329.0 %while.98 = (s32[]{:T(128)}, f32[256,256]{1,0:T(8,128)S(1)}, f32[256]{0:T(256)S(1)}, pred[]{:T(512)}, f32[256,256]{1,0:T(8,128)S(1)}, /*index=5*/f32[256]{0:T(256)S(1)}, s32[]{:T(128)}) while((s32[]{:T(128)}, f32[256,256]{1,0:T(8,128)S(1)}, f32[256]{0:T(256)S(1)}, pred[]{:T(512)}, f32[256,256]{1,0:T(8,128)S(1)}, ...), condition=%wide.region_3.4_spmd.clone, body=%wide.region_2.3_spmd.clone.sunk | while | flops 202375936 | bytes 3159159 | solution.py:165
  127.7 6.5 collective-permute-start
  138.4 6.5 collective-permute-start
  149.1 6.5 collective-permute-start
  159.9 6.5 collective-permute-start
  170.6 6.5 collective-permute-start
  181.3 6.5 collective-permute-start
  192.0 6.5 collective-permute-start
  213.4 6.5 collective-permute-start
  224.1 6.5 collective-permute-start
  234.8 6.5 collective-permute-start
  245.5 6.5 collective-permute-start
  256.2 6.5 collective-permute-start
  266.9 6.5 collective-permute-start
  277.6 6.5 collective-permute-start
  288.3 6.5 collective-permute-start
  299.0 6.5 collective-permute-start
  320.4 6.5 collective-permute-start
  331.1 6.5 collective-permute-start
  341.8 6.5 collective-permute-start
  352.5 6.5 collective-permute-start
  363.2 6.5 collective-permute-start
  373.9 6.5 collective-permute-start
  384.6 6.5 collective-permute-start
  406.0 6.5 collective-permute-start
  427.4 6.5 collective-permute-start
  437.7 21.9 %while.96 = (s32[]{:T(128)}, f32[256]{0:T(256)S(1)}, f32[16,256]{1,0:T(8,128)S(1)}, f32[16,256,256]{2,1,0:T(8,128)}, f32[16,256]{1,0:T(8,128)S(1)}, /*index=5*/s32[]{:T(128)}, s32[]{:T(128)}) while((s32[]{:T(128)}, f32[256]{0:T(256)S(1)}, f32[16,256]{1,0:T(8,128)S(1)}, f32[16,256,256]{2,1,0:T(8,128)}, f32[16,256]{1,0:T(8,128)S(1)}, ...), condition=%wide.region_5.6_spmd, body=%wide.region_4.5_spmd.sunk | while | flops 786690 | bytes 271957 | solution.py:87
  487.5 88.0 %while.100 = (s32[]{:T(128)}, f32[256,256]{1,0:T(8,128)S(1)}, f32[256,256]{1,0:T(8,128)S(1)}, f32[256]{0:T(256)S(1)}, f32[16,256,256]{2,1,0:T(8,128)}, /*index=5...) while((s32[]{:T(128)}, f32[256,256]{1,0:T(8,128)S(1)}, ...), condition=%wide.region_7.8_spmd.clone, body=%wide.region_6.7_spmd.clone.sunk | while | flops 604897792 | bytes 3418252 | solution.py:97
  575.6 446.2 %while.101 = (s32[]{:T(128)}, f32[256,256]{1,0:T(8,128)S(1)}, f32[256,256]{1,0:T(8,128)S(1)}, f32[256]{0:T(256)S(1)}, pred[]{:T(512)}, /*index=5*/f32[256,256]{1...) while((s32[]{:T(128)}, f32[256,256]{1,0:T(8,128)S(1)}, ...), condition=%wide.region_9.10_spmd.clone, body=%wide.region_8.9_spmd.clone.sunk | while | flops 605422592 | bytes 7091353 | solution.py:179
  579.3 11.5 %collective-permute-done.1 = f32[513,256]{1,0:T(8,128)S(1)} collective-permute-done((f32[513,256]{1,0:T(8,128)S(1)}, f32[513,256]{1,0:T(8,128)S(1)}, u32[]{:S(2)}, u32[]{:S(2)}) %collective-permute-start.1) | collective-permute-done | bytes 525344 | tf_op jit(solution)/shard_map/while/body/eval_jaxpr/ppermute | solution.py:12
  594.4 10.8 collective-permute-done.1
  608.8 10.8 collective-permute-done.1
  623.1 10.8 collective-permute-done.1
  637.5 10.8 collective-permute-done.1
  651.9 10.8 collective-permute-done.1
  666.2 10.8 collective-permute-done.1
  680.6 10.8 collective-permute-done.1
  695.0 10.8 collective-permute-done.1
  709.3 10.8 collective-permute-done.1
  723.7 10.8 collective-permute-done.1
  738.0 10.8 collective-permute-done.1
  752.4 10.8 collective-permute-done.1
  766.8 10.8 collective-permute-done.1
  781.1 10.8 collective-permute-done.1
  795.5 10.8 collective-permute-done.1
  809.8 10.8 collective-permute-done.1
  824.2 10.8 collective-permute-done.1
  838.6 10.8 collective-permute-done.1
  852.9 10.8 collective-permute-done.1
  867.3 10.8 collective-permute-done.1
  881.6 10.8 collective-permute-done.1
  896.0 10.8 collective-permute-done.1
  910.4 10.8 collective-permute-done.1
  924.7 10.8 collective-permute-done.1
  939.1 10.8 collective-permute-done.1
  953.5 10.8 collective-permute-done.1
  967.8 10.8 collective-permute-done.1
  982.2 10.8 collective-permute-done.1
  996.5 10.8 collective-permute-done.1
  1010.9 10.8 collective-permute-done.1
  1024.2 77.5 %while.97 = (s32[]{:T(128)}, f32[256,256]{1,0:T(8,128)S(1)}, f32[256]{0:T(256)S(1)}, f32[16,256]{1,0:T(8,128)S(1)}, f32[16,256,256]{2,1,0:T(8,128)}, /*index=5*/...) while((s32[]{:T(128)}, f32[256,256]{1,0:T(8,128)S(1)}, ...), condition=%wide.region_11.12_spmd, body=%wide.region_10.11_spmd.sunk | while | flops 403505408 | bytes 2369673 | solution.py:112
  (961 shorter events, 545.2 us)
Async XLA Ops:
  7.2 57.9 %all-gather.9.cloned.1.call-start = ((), (), s32[]{:S(2)}) async-start(), calls=%async_computation.2 | async-start | bytes 5242880 | tf_op jit(solution)/shard_map/all_gather | solution.py:146
  14.2 445.6 %all-gather.5.cloned.1.call-start = ((), (), s32[]{:S(2)}) async-start(), calls=%async_computation | async-start | bytes 5242880 | tf_op jit(solution)/shard_map/all_gather | solution.py:148
  15.0 453.3 %all-gather.7.cloned.1.call-start = ((), (), s32[]{:S(2)}) async-start(), calls=%async_computation.1 | async-start | bytes 5242880 | tf_op jit(solution)/shard_map/all_gather | solution.py:149
  117.0 9.9 collective-permute-start
  127.7 9.9 collective-permute-start
  138.4 9.9 collective-permute-start
  149.1 9.9 collective-permute-start
  159.9 9.9 collective-permute-start
  170.6 9.9 collective-permute-start
  181.3 9.9 collective-permute-start
  192.0 9.9 collective-permute-start
  202.7 9.9 collective-permute-start
  213.4 9.9 collective-permute-start
  224.1 9.9 collective-permute-start
  234.8 9.9 collective-permute-start
  245.5 9.9 collective-permute-start
  256.2 9.9 collective-permute-start
  266.9 9.9 collective-permute-start
  277.6 9.9 collective-permute-start
  288.3 9.9 collective-permute-start
  299.0 9.9 collective-permute-start
  309.7 9.9 collective-permute-start
  320.4 9.9 collective-permute-start
  331.1 9.9 collective-permute-start
  341.8 9.9 collective-permute-start
  352.5 9.9 collective-permute-start
  363.2 9.9 collective-permute-start
  373.9 9.9 collective-permute-start
  384.6 9.9 collective-permute-start
  395.3 9.9 collective-permute-start
  406.0 9.9 collective-permute-start
  416.7 9.9 collective-permute-start
  427.4 9.9 collective-permute-start
  577.4 13.4 %collective-permute-start.1 = (f32[513,256]{1,0:T(8,128)S(1)}, f32[513,256]{1,0:T(8,128)S(1)}, u32[]{:S(2)}, u32[]{:S(2)}) collective-permute-start(f32[513,256]{1,0:T(8,128)S(1)} %pad_maximum_fusion.5), channel_id=1, source_target_pairs={{4,0},{8,4},{12,8},{16,12},{20,16},{24,20},{28,24},{32,28},{36,32}... | collective-permute-start | bytes 1575944 | tf_op jit(solution)/shard_map/while/body/eval_jaxpr/ppermute | solution.py:12
  592.5 12.7 %collective-permute-start.1 = (f32[513,256]{1,0:T(8,128)S(1)}, f32[513,256]{1,0:T(8,128)S(1)}, u32[]{:S(2)}, u32[]{:S(2)}) collective-permute-start(f32[513,256]{1,0:T(8,128)S(1)} %pad_maximum_fusion.5), channel_id=1, source_target_pairs={{4,0},{8,4},{12,8},{16,12},{20,16},{24,20},{28,24},{32,28},{36,32}... | collective-permute-start | bytes 1575944 | tf_op jit(solution)/shard_map/while/body/eval_jaxpr/ppermute | solution.py:12
  606.9 12.7 %collective-permute-start.1 = (f32[513,256]{1,0:T(8,128)S(1)}, f32[513,256]{1,0:T(8,128)S(1)}, u32[]{:S(2)}, u32[]{:S(2)}) collective-permute-start(f32[513,256]{1,0:T(8,128)S(1)} %pad_maximum_fusion.5), channel_id=1, source_target_pairs={{4,0},{8,4},{12,8},{16,12},{20,16},{24,20},{28,24},{32,28},{36,32}... | collective-permute-start | bytes 1575944 | tf_op jit(solution)/shard_map/while/body/eval_jaxpr/ppermute | solution.py:12
  621.2 12.7 %collective-permute-start.1 = (f32[513,256]{1,0:T(8,128)S(1)}, f32[513,256]{1,0:T(8,128)S(1)}, u32[]{:S(2)}, u32[]{:S(2)}) collective-permute-start(f32[513,256]{1,0:T(8,128)S(1)} %pad_maximum_fusion.5), channel_id=1, source_target_pairs={{4,0},{8,4},{12,8},{16,12},{20,16},{24,20},{28,24},{32,28},{36,32}... | collective-permute-start | bytes 1575944 | tf_op jit(solution)/shard_map/while/body/eval_jaxpr/ppermute | solution.py:12
  635.6 12.7 %collective-permute-start.1 = (f32[513,256]{1,0:T(8,128)S(1)}, f32[513,256]{1,0:T(8,128)S(1)}, u32[]{:S(2)}, u32[]{:S(2)}) collective-permute-start(f32[513,256]{1,0:T(8,128)S(1)} %pad_maximum_fusion.5), channel_id=1, source_target_pairs={{4,0},{8,4},{12,8},{16,12},{20,16},{24,20},{28,24},{32,28},{36,32}... | collective-permute-start | bytes 1575944 | tf_op jit(solution)/shard_map/while/body/eval_jaxpr/ppermute | solution.py:12
  649.9 12.7 %collective-permute-start.1 = (f32[513,256]{1,0:T(8,128)S(1)}, f32[513,256]{1,0:T(8,128)S(1)}, u32[]{:S(2)}, u32[]{:S(2)}) collective-permute-start(f32[513,256]{1,0:T(8,128)S(1)} %pad_maximum_fusion.5), channel_id=1, source_target_pairs={{4,0},{8,4},{12,8},{16,12},{20,16},{24,20},{28,24},{32,28},{36,32}... | collective-permute-start | bytes 1575944 | tf_op jit(solution)/shard_map/while/body/eval_jaxpr/ppermute | solution.py:12
  664.3 12.7 %collective-permute-start.1 = (f32[513,256]{1,0:T(8,128)S(1)}, f32[513,256]{1,0:T(8,128)S(1)}, u32[]{:S(2)}, u32[]{:S(2)}) collective-permute-start(f32[513,256]{1,0:T(8,128)S(1)} %pad_maximum_fusion.5), channel_id=1, source_target_pairs={{4,0},{8,4},{12,8},{16,12},{20,16},{24,20},{28,24},{32,28},{36,32}... | collective-permute-start | bytes 1575944 | tf_op jit(solution)/shard_map/while/body/eval_jaxpr/ppermute | solution.py:12
  678.7 12.7 %collective-permute-start.1 = (f32[513,256]{1,0:T(8,128)S(1)}, f32[513,256]{1,0:T(8,128)S(1)}, u32[]{:S(2)}, u32[]{:S(2)}) collective-permute-start(f32[513,256]{1,0:T(8,128)S(1)} %pad_maximum_fusion.5), channel_id=1, source_target_pairs={{4,0},{8,4},{12,8},{16,12},{20,16},{24,20},{28,24},{32,28},{36,32}... | collective-permute-start | bytes 1575944 | tf_op jit(solution)/shard_map/while/body/eval_jaxpr/ppermute | solution.py:12
  693.0 12.7 %collective-permute-start.1 = (f32[513,256]{1,0:T(8,128)S(1)}, f32[513,256]{1,0:T(8,128)S(1)}, u32[]{:S(2)}, u32[]{:S(2)}) collective-permute-start(f32[513,256]{1,0:T(8,128)S(1)} %pad_maximum_fusion.5), channel_id=1, source_target_pairs={{4,0},{8,4},{12,8},{16,12},{20,16},{24,20},{28,24},{32,28},{36,32}... | collective-permute-start | bytes 1575944 | tf_op jit(solution)/shard_map/while/body/eval_jaxpr/ppermute | solution.py:12
  707.4 12.7 %collective-permute-start.1 = (f32[513,256]{1,0:T(8,128)S(1)}, f32[513,256]{1,0:T(8,128)S(1)}, u32[]{:S(2)}, u32[]{:S(2)}) collective-permute-start(f32[513,256]{1,0:T(8,128)S(1)} %pad_maximum_fusion.5), channel_id=1, source_target_pairs={{4,0},{8,4},{12,8},{16,12},{20,16},{24,20},{28,24},{32,28},{36,32}... | collective-permute-start | bytes 1575944 | tf_op jit(solution)/shard_map/while/body/eval_jaxpr/ppermute | solution.py:12
  721.7 12.7 %collective-permute-start.1 = (f32[513,256]{1,0:T(8,128)S(1)}, f32[513,256]{1,0:T(8,128)S(1)}, u32[]{:S(2)}, u32[]{:S(2)}) collective-permute-start(f32[513,256]{1,0:T(8,128)S(1)} %pad_maximum_fusion.5), channel_id=1, source_target_pairs={{4,0},{8,4},{12,8},{16,12},{20,16},{24,20},{28,24},{32,28},{36,32}... | collective-permute-start | bytes 1575944 | tf_op jit(solution)/shard_map/while/body/eval_jaxpr/ppermute | solution.py:12
  736.1 12.7 %collective-permute-start.1 = (f32[513,256]{1,0:T(8,128)S(1)}, f32[513,256]{1,0:T(8,128)S(1)}, u32[]{:S(2)}, u32[]{:S(2)}) collective-permute-start(f32[513,256]{1,0:T(8,128)S(1)} %pad_maximum_fusion.5), channel_id=1, source_target_pairs={{4,0},{8,4},{12,8},{16,12},{20,16},{24,20},{28,24},{32,28},{36,32}... | collective-permute-start | bytes 1575944 | tf_op jit(solution)/shard_map/while/body/eval_jaxpr/ppermute | solution.py:12
  750.5 12.7 %collective-permute-start.1 = (f32[513,256]{1,0:T(8,128)S(1)}, f32[513,256]{1,0:T(8,128)S(1)}, u32[]{:S(2)}, u32[]{:S(2)}) collective-permute-start(f32[513,256]{1,0:T(8,128)S(1)} %pad_maximum_fusion.5), channel_id=1, source_target_pairs={{4,0},{8,4},{12,8},{16,12},{20,16},{24,20},{28,24},{32,28},{36,32}... | collective-permute-start | bytes 1575944 | tf_op jit(solution)/shard_map/while/body/eval_jaxpr/ppermute | solution.py:12
  764.8 12.7 %collective-permute-start.1 = (f32[513,256]{1,0:T(8,128)S(1)}, f32[513,256]{1,0:T(8,128)S(1)}, u32[]{:S(2)}, u32[]{:S(2)}) collective-permute-start(f32[513,256]{1,0:T(8,128)S(1)} %pad_maximum_fusion.5), channel_id=1, source_target_pairs={{4,0},{8,4},{12,8},{16,12},{20,16},{24,20},{28,24},{32,28},{36,32}... | collective-permute-start | bytes 1575944 | tf_op jit(solution)/shard_map/while/body/eval_jaxpr/ppermute | solution.py:12
  779.2 12.7 %collective-permute-start.1 = (f32[513,256]{1,0:T(8,128)S(1)}, f32[513,256]{1,0:T(8,128)S(1)}, u32[]{:S(2)}, u32[]{:S(2)}) collective-permute-start(f32[513,256]{1,0:T(8,128)S(1)} %pad_maximum_fusion.5), channel_id=1, source_target_pairs={{4,0},{8,4},{12,8},{16,12},{20,16},{24,20},{28,24},{32,28},{36,32}... | collective-permute-start | bytes 1575944 | tf_op jit(solution)/shard_map/while/body/eval_jaxpr/ppermute | solution.py:12
  793.5 12.7 %collective-permute-start.1 = (f32[513,256]{1,0:T(8,128)S(1)}, f32[513,256]{1,0:T(8,128)S(1)}, u32[]{:S(2)}, u32[]{:S(2)}) collective-permute-start(f32[513,256]{1,0:T(8,128)S(1)} %pad_maximum_fusion.5), channel_id=1, source_target_pairs={{4,0},{8,4},{12,8},{16,12},{20,16},{24,20},{28,24},{32,28},{36,32}... | collective-permute-start | bytes 1575944 | tf_op jit(solution)/shard_map/while/body/eval_jaxpr/ppermute | solution.py:12
  807.9 12.7 %collective-permute-start.1 = (f32[513,256]{1,0:T(8,128)S(1)}, f32[513,256]{1,0:T(8,128)S(1)}, u32[]{:S(2)}, u32[]{:S(2)}) collective-permute-start(f32[513,256]{1,0:T(8,128)S(1)} %pad_maximum_fusion.5), channel_id=1, source_target_pairs={{4,0},{8,4},{12,8},{16,12},{20,16},{24,20},{28,24},{32,28},{36,32}... | collective-permute-start | bytes 1575944 | tf_op jit(solution)/shard_map/while/body/eval_jaxpr/ppermute | solution.py:12
  822.3 12.7 %collective-permute-start.1 = (f32[513,256]{1,0:T(8,128)S(1)}, f32[513,256]{1,0:T(8,128)S(1)}, u32[]{:S(2)}, u32[]{:S(2)}) collective-permute-start(f32[513,256]{1,0:T(8,128)S(1)} %pad_maximum_fusion.5), channel_id=1, source_target_pairs={{4,0},{8,4},{12,8},{16,12},{20,16},{24,20},{28,24},{32,28},{36,32}... | collective-permute-start | bytes 1575944 | tf_op jit(solution)/shard_map/while/body/eval_jaxpr/ppermute | solution.py:12
  836.6 12.7 %collective-permute-start.1 = (f32[513,256]{1,0:T(8,128)S(1)}, f32[513,256]{1,0:T(8,128)S(1)}, u32[]{:S(2)}, u32[]{:S(2)}) collective-permute-start(f32[513,256]{1,0:T(8,128)S(1)} %pad_maximum_fusion.5), channel_id=1, source_target_pairs={{4,0},{8,4},{12,8},{16,12},{20,16},{24,20},{28,24},{32,28},{36,32}... | collective-permute-start | bytes 1575944 | tf_op jit(solution)/shard_map/while/body/eval_jaxpr/ppermute | solution.py:12
  851.0 12.7 %collective-permute-start.1 = (f32[513,256]{1,0:T(8,128)S(1)}, f32[513,256]{1,0:T(8,128)S(1)}, u32[]{:S(2)}, u32[]{:S(2)}) collective-permute-start(f32[513,256]{1,0:T(8,128)S(1)} %pad_maximum_fusion.5), channel_id=1, source_target_pairs={{4,0},{8,4},{12,8},{16,12},{20,16},{24,20},{28,24},{32,28},{36,32}... | collective-permute-start | bytes 1575944 | tf_op jit(solution)/shard_map/while/body/eval_jaxpr/ppermute | solution.py:12
  865.4 12.7 %collective-permute-start.1 = (f32[513,256]{1,0:T(8,128)S(1)}, f32[513,256]{1,0:T(8,128)S(1)}, u32[]{:S(2)}, u32[]{:S(2)}) collective-permute-start(f32[513,256]{1,0:T(8,128)S(1)} %pad_maximum_fusion.5), channel_id=1, source_target_pairs={{4,0},{8,4},{12,8},{16,12},{20,16},{24,20},{28,24},{32,28},{36,32}... | collective-permute-start | bytes 1575944 | tf_op jit(solution)/shard_map/while/body/eval_jaxpr/ppermute | solution.py:12
  879.7 12.7 %collective-permute-start.1 = (f32[513,256]{1,0:T(8,128)S(1)}, f32[513,256]{1,0:T(8,128)S(1)}, u32[]{:S(2)}, u32[]{:S(2)}) collective-permute-start(f32[513,256]{1,0:T(8,128)S(1)} %pad_maximum_fusion.5), channel_id=1, source_target_pairs={{4,0},{8,4},{12,8},{16,12},{20,16},{24,20},{28,24},{32,28},{36,32}... | collective-permute-start | bytes 1575944 | tf_op jit(solution)/shard_map/while/body/eval_jaxpr/ppermute | solution.py:12
  894.1 12.7 %collective-permute-start.1 = (f32[513,256]{1,0:T(8,128)S(1)}, f32[513,256]{1,0:T(8,128)S(1)}, u32[]{:S(2)}, u32[]{:S(2)}) collective-permute-start(f32[513,256]{1,0:T(8,128)S(1)} %pad_maximum_fusion.5), channel_id=1, source_target_pairs={{4,0},{8,4},{12,8},{16,12},{20,16},{24,20},{28,24},{32,28},{36,32}... | collective-permute-start | bytes 1575944 | tf_op jit(solution)/shard_map/while/body/eval_jaxpr/ppermute | solution.py:12
  908.4 12.7 %collective-permute-start.1 = (f32[513,256]{1,0:T(8,128)S(1)}, f32[513,256]{1,0:T(8,128)S(1)}, u32[]{:S(2)}, u32[]{:S(2)}) collective-permute-start(f32[513,256]{1,0:T(8,128)S(1)} %pad_maximum_fusion.5), channel_id=1, source_target_pairs={{4,0},{8,4},{12,8},{16,12},{20,16},{24,20},{28,24},{32,28},{36,32}... | collective-permute-start | bytes 1575944 | tf_op jit(solution)/shard_map/while/body/eval_jaxpr/ppermute | solution.py:12
  922.8 12.7 %collective-permute-start.1 = (f32[513,256]{1,0:T(8,128)S(1)}, f32[513,256]{1,0:T(8,128)S(1)}, u32[]{:S(2)}, u32[]{:S(2)}) collective-permute-start(f32[513,256]{1,0:T(8,128)S(1)} %pad_maximum_fusion.5), channel_id=1, source_target_pairs={{4,0},{8,4},{12,8},{16,12},{20,16},{24,20},{28,24},{32,28},{36,32}... | collective-permute-start | bytes 1575944 | tf_op jit(solution)/shard_map/while/body/eval_jaxpr/ppermute | solution.py:12
  937.2 12.7 %collective-permute-start.1 = (f32[513,256]{1,0:T(8,128)S(1)}, f32[513,256]{1,0:T(8,128)S(1)}, u32[]{:S(2)}, u32[]{:S(2)}) collective-permute-start(f32[513,256]{1,0:T(8,128)S(1)} %pad_maximum_fusion.5), channel_id=1, source_target_pairs={{4,0},{8,4},{12,8},{16,12},{20,16},{24,20},{28,24},{32,28},{36,32}... | collective-permute-start | bytes 1575944 | tf_op jit(solution)/shard_map/while/body/eval_jaxpr/ppermute | solution.py:12
  951.5 12.7 %collective-permute-start.1 = (f32[513,256]{1,0:T(8,128)S(1)}, f32[513,256]{1,0:T(8,128)S(1)}, u32[]{:S(2)}, u32[]{:S(2)}) collective-permute-start(f32[513,256]{1,0:T(8,128)S(1)} %pad_maximum_fusion.5), channel_id=1, source_target_pairs={{4,0},{8,4},{12,8},{16,12},{20,16},{24,20},{28,24},{32,28},{36,32}... | collective-permute-start | bytes 1575944 | tf_op jit(solution)/shard_map/while/body/eval_jaxpr/ppermute | solution.py:12
  965.9 12.7 %collective-permute-start.1 = (f32[513,256]{1,0:T(8,128)S(1)}, f32[513,256]{1,0:T(8,128)S(1)}, u32[]{:S(2)}, u32[]{:S(2)}) collective-permute-start(f32[513,256]{1,0:T(8,128)S(1)} %pad_maximum_fusion.5), channel_id=1, source_target_pairs={{4,0},{8,4},{12,8},{16,12},{20,16},{24,20},{28,24},{32,28},{36,32}... | collective-permute-start | bytes 1575944 | tf_op jit(solution)/shard_map/while/body/eval_jaxpr/ppermute | solution.py:12
  980.2 12.7 %collective-permute-start.1 = (f32[513,256]{1,0:T(8,128)S(1)}, f32[513,256]{1,0:T(8,128)S(1)}, u32[]{:S(2)}, u32[]{:S(2)}) collective-permute-start(f32[513,256]{1,0:T(8,128)S(1)} %pad_maximum_fusion.5), channel_id=1, source_target_pairs={{4,0},{8,4},{12,8},{16,12},{20,16},{24,20},{28,24},{32,28},{36,32}... | collective-permute-start | bytes 1575944 | tf_op jit(solution)/shard_map/while/body/eval_jaxpr/ppermute | solution.py:12
  994.6 12.7 %collective-permute-start.1 = (f32[513,256]{1,0:T(8,128)S(1)}, f32[513,256]{1,0:T(8,128)S(1)}, u32[]{:S(2)}, u32[]{:S(2)}) collective-permute-start(f32[513,256]{1,0:T(8,128)S(1)} %pad_maximum_fusion.5), channel_id=1, source_target_pairs={{4,0},{8,4},{12,8},{16,12},{20,16},{24,20},{28,24},{32,28},{36,32}... | collective-permute-start | bytes 1575944 | tf_op jit(solution)/shard_map/while/body/eval_jaxpr/ppermute | solution.py:12
  1009.0 12.7 %collective-permute-start.1 = (f32[513,256]{1,0:T(8,128)S(1)}, f32[513,256]{1,0:T(8,128)S(1)}, u32[]{:S(2)}, u32[]{:S(2)}) collective-permute-start(f32[513,256]{1,0:T(8,128)S(1)} %pad_maximum_fusion.5), channel_id=1, source_target_pairs={{4,0},{8,4},{12,8},{16,12},{20,16},{24,20},{28,24},{32,28},{36,32}... | collective-permute-start | bytes 1575944 | tf_op jit(solution)/shard_map/while/body/eval_jaxpr/ppermute | solution.py:12
  (12 other events, 517.0 us)
Sparse Core Ops, SparseCore 0:
  14.3 50.6 all-gather.8
  66.7 48.9 all-gather.4
  117.4 48.4 all-gather.6
where the time goes:
time: 1120 us; the launch traced here: 1110 us
  waiting for transfers between devices  478 us (43%)
  matrix products  317 us (28%)
  starting transfers between devices  258 us (23%)
  local copies, waits for them, and re-layouts  16.4 us (1%)
  between operations  14.1 us (1%)
    ppermute x62, waiting for transfers between devices, from_behind(): return lax.ppermute(block, axis, route)  439 us
    dot_general x353, matrix products, matmul(): return jnp.matmul(left, right, precision=highest)  312 us
    ppermute x62, starting transfers between devices, from_behind(): return lax.ppermute(block, axis, route)  258 us
    all_gather x1, waiting for transfers between devices, per_device(): lax.all_gather(map_rows, 'blk', axis=1, tiled=True)  36.8 us
  transfers between devices with their start and end apart: 65, of which 63 were waited for; matrix products, arithmetic and copies ran while one was open for 9% of the time, Pallas kernels for 0%

commit v1 on v0

v1 whole, which is shorter than its diff:
```python
import jax
import jax.numpy as jnp
from jax import lax
from jax.sharding import PartitionSpec as P

highest = lax.Precision.HIGHEST


def from_behind(block, axis, distance):
    devices = range(lax.axis_size(axis))
    route = [(i - distance, i) for i in devices if i - distance in devices]
    return lax.ppermute(block, axis, route)


def expand_mask(mask, row_total, col_total):
    row_block = row_total // mask.shape[0]
    col_block = col_total // mask.shape[1]
    return jnp.repeat(jnp.repeat(mask.astype(jnp.float32), row_block, axis=0), col_block, axis=1)


def matmul(left, right):
    return jnp.matmul(left, right, precision=highest)


def matvec(left, right):
    return jnp.einsum("...ij,...j->...i", left, right, precision=highest)


def transpose(mats):
    return jnp.swapaxes(mats, -1, -2)


def filter_tree(maps, shifts):
    while maps.shape[0] > 1:
        early_map, late_map = maps[0::2], maps[1::2]
        shifts = matvec(late_map, shifts[0::2]) + shifts[1::2]
        maps = matmul(late_map, early_map)
    return maps[0], shifts[0]


def smooth_tree(gains, resids, offsets):
    while gains.shape[0] > 1:
        outer, inner = gains[0::2], gains[1::2]
        resids = matmul(matmul(outer, resids[1::2]), transpose(outer)) + resids[0::2]
        offsets = matvec(outer, offsets[1::2]) + offsets[0::2]
        gains = matmul(outer, inner)
    return gains[0], resids[0], offsets[0]


def filter_scan(window_map, window_shift, initial_expectation, tm_index, tm_count):
    width = window_map.shape[0]
    first_window = tm_index == 0
    shift = jnp.where(first_window, matvec(window_map, initial_expectation) + window_shift, window_shift)
    cmap = jnp.where(first_window, jnp.float32(0.0), window_map)
    distance = 1
    while distance < tm_count:
        has_left = tm_index >= distance
        if 2 * distance >= tm_count:
            shift_left = from_behind(shift, "tm", distance)
            shift = jnp.where(has_left, matvec(cmap, shift_left) + shift, shift)
        else:
            arrived = from_behind(jnp.concatenate([cmap, shift[None]], axis=0), "tm", distance)
            map_left, shift_left = arrived[:width], arrived[width]
            shift = jnp.where(has_left, matvec(cmap, shift_left) + shift, shift)
            cmap = jnp.where(has_left, matmul(cmap, map_left), cmap)
        distance *= 2
    mean_in = from_behind(shift, "tm", 1)
    return jnp.where(first_window, initial_expectation, mean_in)


def smooth_scan(window_gain, window_resid, window_offset, tm_index, tm_count):
    width = window_gain.shape[0]
    gain, resid, offset = window_gain, window_resid, window_offset
    distance = 1
    while distance < tm_count:
        has_right = tm_index + distance < tm_count
        if 2 * distance >= tm_count:
            arrived = from_behind(jnp.concatenate([resid, offset[None]], axis=0), "tm", -distance)
            resid_right, offset_right = arrived[:width], arrived[width]
        else:
            arrived = from_behind(
                jnp.concatenate([gain, resid, offset[None]], axis=0), "tm", -distance
            )
            gain_right = arrived[:width]
            resid_right = arrived[width : 2 * width]
            offset_right = arrived[2 * width]
        new_resid = matmul(matmul(gain, resid_right), gain.T) + resid
        offset = jnp.where(has_right, matvec(gain, offset_right) + offset, offset)
        resid = jnp.where(has_right, new_resid, resid)
        if 2 * distance < tm_count:
            gain = jnp.where(has_right, matmul(gain, gain_right), gain)
        distance *= 2
    arrived = from_behind(jnp.concatenate([resid, offset[None]], axis=0), "tm", -1)
    last_window = tm_index == tm_count - 1
    arrived = jnp.where(last_window, jnp.float32(0.0), arrived)
    return arrived[:width], arrived[width]


def window_work(
    trans_map,
    process_noise,
    initial_expectation,
    transition_operators,
    step_shifts,
    gain_full,
    cov_full,
    tm_index,
    tm_count,
):
    step_count = transition_operators.shape[0]
    final_step = jnp.logical_and(tm_index == tm_count - 1, jnp.arange(step_count) == step_count - 1)
    gain_full = jnp.where(final_step[:, None, None], jnp.float32(0.0), gain_full)

    window_map, window_shift = filter_tree(transition_operators, step_shifts)
    mean_in = filter_scan(window_map, window_shift, initial_expectation, tm_index, tm_count)

    def filter_walk(current, step_parts):
        current = matmul(step_parts[0], current) + step_parts[1]
        return (current, current)

    filt_means = lax.scan(filter_walk, mean_in, (transition_operators, step_shifts))[1]
    predicted = matmul(matmul(trans_map, cov_full), trans_map.T) + jnp.diag(process_noise)
    gain_trans = jnp.swapaxes(gain_full, 1, 2)
    residual_cov = cov_full - matmul(matmul(gain_full, predicted), gain_trans)
    moved_means = jnp.einsum("ij,tj->ti", trans_map, filt_means, precision=highest)
    offsets = filt_means - jnp.einsum("tij,tj->ti", gain_full, moved_means, precision=highest)

    window_gain, window_resid, window_offset = smooth_tree(gain_full, residual_cov, offsets)
    cov_after, mean_after = smooth_scan(window_gain, window_resid, window_offset, tm_index, tm_count)

    def smooth_walk(current, step_parts):
        cov_next, mean_next = current
        gain_now, resid_now, offset_now = step_parts
        cov_now = matmul(matmul(gain_now, cov_next), gain_now.T) + resid_now
        current_mean = matmul(gain_now, mean_next) + offset_now
        return ((cov_now, current_mean), (current_mean, cov_now))

    return lax.scan(
        smooth_walk,
        (cov_after, mean_after),
        (gain_full, residual_cov, offsets),
        reverse=True,
    )[1]


def per_device(
    dynamics,
    dynamics_mask,
    obs_op,
    obs_mask,
    process_noise,
    initial_expectation,
    filter_gains,
    observations,
    smooth_gains,
    filt_cov,
):
    width = dynamics.shape[0]
    obs_width = obs_op.shape[0]
    row_count = filter_gains.shape[1]
    row_start = lax.axis_index("blk") * row_count
    trans_map = dynamics * expand_mask(dynamics_mask, width, width)
    obs_map = obs_op * expand_mask(obs_mask, obs_width, width)
    obs_dyn = matmul(obs_map, trans_map)
    own_rows = lax.dynamic_slice_in_dim(trans_map, row_start, row_count, 0)
    map_rows = own_rows[None] - matmul(filter_gains, obs_dyn)
    shift_rows = jnp.einsum("tro,to->tr", filter_gains, observations, precision=highest)
    transition_operators, step_shifts, gain_full, cov_full = (
        lax.all_gather(map_rows, "blk", axis=1, tiled=True),
        lax.all_gather(shift_rows, "blk", axis=1, tiled=True),
        lax.all_gather(smooth_gains, "blk", axis=1, tiled=True),
        lax.all_gather(filt_cov, "blk", axis=1, tiled=True),
    )
    means_out, cov_out = window_work(
        trans_map,
        process_noise,
        initial_expectation,
        transition_operators,
        step_shifts,
        gain_full,
        cov_full,
        lax.axis_index("tm"),
        lax.axis_size("tm"),
    )
    means_rows = lax.dynamic_slice_in_dim(means_out, row_start, row_count, 1)
    cov_rows = lax.dynamic_slice_in_dim(cov_out, row_start, row_count, 1)
    return (means_rows, cov_rows)


def solution(mesh):
    return jax.shard_map(
        per_device,
        mesh=mesh,
        in_specs=(
            P(),
            P(),
            P(),
            P(),
            P(),
            P(),
            P("tm", "blk", None),
            P("tm", None),
            P("tm", "blk", None),
            P("tm", "blk", None),
        ),
        out_specs=(P("tm", "blk"), P("tm", "blk", None)),
        check_vma=False,
    )
```

time: 1120 us -> 464 us (0.41)
  waiting for transfers between devices: 478 us -> 200 us
  starting transfers between devices: 258 us -> 42.6 us
  matrix products: 317 us -> 169 us
    ppermute x62 -> x12, waiting for transfers between devices: 439 us -> 82.8 us  [from_behind(): return lax.ppermute(block, axis, route)]
    ppermute x62 -> x12, starting transfers between devices: 258 us -> 42.5 us  [from_behind(): return lax.ppermute(block, axis, route)]
    dot_general x353 -> x104, matrix products: 312 us -> 147 us  [matmul(): return jnp.matmul(left, right, precision=highest)]
    all_gather x1, waiting for transfers between devices: 0.03 us -> 39.8 us  [per_device(): lax.all_gather(smooth_gains, 'blk', axis=1, tiled=True)]
    all_gather x1, waiting for transfers between devices: 0.01 us -> 39.4 us  [per_device(): lax.all_gather(filt_cov, 'blk', axis=1, tiled=True)]
    dot_general x0 -> x19, matrix products: none -> 14.4 us  [matvec(): return jnp.einsum('...ij,...j->...i', left, right, precision=highest)]
  transfers between devices with their start and end apart: 65 -> 15, of which waited for: 63 -> 14; matrix products, arithmetic and copies ran while one was open for 9% -> 6% of each run, Pallas kernels for 0% -> 0%
where the time goes in v1:
time: 464 us; the launch traced here: 459 us
  waiting for transfers between devices  200 us (43%)
  matrix products  169 us (36%)
  starting transfers between devices  42.6 us (9%)
  between operations  15.3 us (3%)
  local copies, waits for them, and re-layouts  13.6 us (3%)
  blocking collectives  11 us (2%)
  other arithmetic  5.8 us (1%)
    dot_general x104, matrix products, matmul(): return jnp.matmul(left, right, precision=highest)  147 us
    ppermute x12, waiting for transfers between devices, from_behind(): return lax.ppermute(block, axis, route)  82.8 us
    ppermute x12, starting transfers between devices, from_behind(): return lax.ppermute(block, axis, route)  42.5 us
    all_gather x1, waiting for transfers between devices, per_device(): lax.all_gather(smooth_gains, 'blk', axis=1, tiled=True)  39.8 us
    all_gather x1, waiting for transfers between devices, per_device(): lax.all_gather(filt_cov, 'blk', axis=1, tiled=True)  39.4 us
    all_gather x1, waiting for transfers between devices, per_device(): lax.all_gather(map_rows, 'blk', axis=1, tiled=True)  37 us
    dot_general x19, matrix products, matvec(): return jnp.einsum('...ij,...j->...i', left, right, precision=highest)  14.4 us
    all_gather x1, blocking collectives, per_device(): lax.all_gather(shift_rows, 'blk', axis=1, tiled=True)  11 us
  transfers between devices with their start and end apart: 15, of which 14 were waited for; matrix products, arithmetic and copies ran while one was open for 6% of the time, Pallas kernels for 0%

profile of v1, /device:TPU:15, one launch (start us, length us, event | category | flops | bytes accessed | tf_op | source)
XLA Modules:
  0.0 458.9 jit_solution(17579235579486817808)
XLA Ops:
  12.2 2.0 fusion.37
  16.7 11.0 %all-gather = f32[4,64,16]{1,2,0:T(8,128)S(1)} all-gather(f32[1,64,16]{1,2,0:T(8,128)S(1)} %bitcast.289), channel_id=1, replica_groups=mesh['tm'=32,'blk'=4] {'blk'}, dimensions={0}, use_global_device_ids=true | all-gather | bytes 20480 | tf_op jit(solution)/shard_map/all_gather | solution.py:170
  28.0 37.0 %all-gather.9.cloned.1.call-done = f32[16,256,256]{2,1,0:T(8,128)} async-done(((f32[16,64,256]{2,1,0:T(8,128)}), f32[16,256,256]{2,1,0:T(8,128)}) %all-gather.9.cloned.1.call-update) | async-done | bytes 4194320 | tf_op jit(solution)/shard_map/all_gather | solution.py:169
  65.1 3.4 fusion.26
  68.5 4.3 fusion.19
  73.9 2.1 fusion.45
  76.1 39.4 %all-gather.7.cloned.1.call-done = f32[16,256,256]{2,1,0:T(8,128)} async-done(((f32[16,64,256]{2,1,0:T(8,128)}), f32[16,256,256]{2,1,0:T(8,128)}) %all-gather.7.cloned.1.call-update) | async-done | bytes 4194320 | tf_op jit(solution)/shard_map/all_gather | solution.py:172
  115.4 5.4 %fusion.96 = f32[256,16,256]{2,0,1:T(8,128)S(1)} fusion(f32[16,256,256]{2,1,0:T(8,128)} %all-gather.7.cloned.1.call-done, f32[256,256]{0,1:T(8,128)S(1)} %bitcast_multiply_fusion.1), kind=kOutput, calls=%fused_computation.137 | convolution fusion | flops 3221225472 | bytes 8650752 | tf_op jit(solution)/shard_map/dot_general | solution.py:22
  120.9 5.1 %fusion.15 = f32[16,256,256]{2,1,0:T(8,128)} fusion(f32[256,16,256]{2,0,1:T(8,128)S(1)} %fusion.96, f32[256,256]{0,1:T(8,128)S(1)} %bitcast_multiply_fusion.1), kind=kOutput, calls=%fused_computation.19 | convolution fusion | flops 3221225472 | bytes 8650752 | tf_op jit(solution)/shard_map/dot_general | solution.py:22
  126.0 39.8 %all-gather.5.cloned.1.call-done = f32[16,256,256]{2,1,0:T(8,128)} async-done(((f32[16,64,256]{2,1,0:T(8,128)}), f32[16,256,256]{2,1,0:T(8,128)}) %all-gather.5.cloned.1.call-update) | async-done | bytes 4194320 | tf_op jit(solution)/shard_map/all_gather | solution.py:171
  165.8 2.7 broadcast_select_fusion
  168.5 2.1 fusion.24
  170.6 1.6 copy-done.4
  172.2 4.5 fusion.17
  176.7 4.4 convolution_subtract_fusion
  181.2 2.4 fusion.21
  183.6 2.3 slice_add_fusion
  191.7 3.7 collective-permute-start
  196.1 2.7 collective-permute-done
  199.6 3.5 collective-permute-start.1
  203.8 4.3 collective-permute-done.1
  208.8 3.4 collective-permute-start.2
  212.8 4.7 %collective-permute-done.2 = f32[257,256]{1,0:T(8,128)S(1)} collective-permute-done((f32[257,256]{1,0:T(8,128)S(1)}, f32[257,256]{1,0:T(8,128)S(1)}, u32[]{:S(2)}, u32[]{:S(2)}) %collective-permute-start.2) | collective-permute-done | bytes 263200 | tf_op jit(solution)/shard_map/ppermute | solution.py:12
  218.3 2.5 collective-permute-start.3
  221.6 3.9 collective-permute-done.3
  225.8 2.3 collective-permute-start.4
  229.1 15.7 %collective-permute-start.5 = (f32[256]{0:T(256)S(1)}, f32[256]{0:T(256)S(1)}, u32[]{:S(2)}, u32[]{:S(2)}) collective-permute-start(f32[256]{0:T(256)S(1)} %add_select_fusion.5), channel_id=1, source_target_pairs={{0,4},{4,8},{8,12},{12,16},{16,20},{20,24},{24,28},{28,32},{32,36}... | collective-permute-start | bytes 3080 | tf_op jit(solution)/shard_map/ppermute | solution.py:12
  246.0 21.9 %while.32 = (s32[]{:T(128)}, f32[256]{0:T(256)S(1)}, f32[16,256]{1,0:T(8,128)S(1)}, f32[16,256,256]{2,1,0:T(8,128)}, f32[16,256]{1,0:T(8,128)S(1)}, /*index=5*/s32[]{:T(128)}, s32[]{:T(128)}) while((s32[]{:T(128)}, f32[256]{0:T(256)S(1)}, f32[16,256]{1,0:T(8,128)S(1)}, f32[16,256,256]{2,1,0:T(8,128)}, f32[16,256]{1,0:T(8,128)S(1)}, ...), condition=%wide.region_1.2_spmd, body=%wide.region_0.1_spmd.sunk | while | flops 786690 | bytes 271957 | solution.py:121
  269.0 5.8 %fusion.106 = f32[16,1,256]{2,1,0:T(1,128)S(1)} fusion(f32[16,256,256]{2,1,0:T(8,128)} %copy-done.2, f32[16,256,1]{1,0,2:T(8,128)S(1)} %convolution_bitcast_fusion.3), kind=kOutput, calls=%fused_computation.152 | convolution fusion | flops 12582912 | bytes 4227072 | tf_op jit(solution)/shard_map/tij,tj->ti/dot_general | solution.py:126
  274.8 3.4 fusion.29
  282.2 2.1 collective-permute-start.6
  284.3 10.7 %collective-permute-done.6 = f32[513,256]{1,0:T(8,128)S(1)} collective-permute-done((f32[513,256]{1,0:T(8,128)S(1)}, f32[513,256]{1,0:T(8,128)S(1)}, u32[]{:S(2)}, u32[]{:S(2)}) %collective-permute-start.6) | collective-permute-done | bytes 525344 | tf_op jit(solution)/shard_map/ppermute | solution.py:12
  295.4 1.4 fusion.42
  297.5 1.9 collective-permute-start.7
  299.5 12.5 %collective-permute-done.7 = f32[513,256]{1,0:T(8,128)S(1)} collective-permute-done((f32[513,256]{1,0:T(8,128)S(1)}, f32[513,256]{1,0:T(8,128)S(1)}, u32[]{:S(2)}, u32[]{:S(2)}) %collective-permute-start.7) | collective-permute-done | bytes 525344 | tf_op jit(solution)/shard_map/ppermute | solution.py:12
  313.5 1.9 collective-permute-start.8
  315.4 13.8 %collective-permute-done.8 = f32[513,256]{1,0:T(8,128)S(1)} collective-permute-done((f32[513,256]{1,0:T(8,128)S(1)}, f32[513,256]{1,0:T(8,128)S(1)}, u32[]{:S(2)}, u32[]{:S(2)}) %collective-permute-start.8) | collective-permute-done | bytes 525344 | tf_op jit(solution)/shard_map/ppermute | solution.py:12
  330.9 1.9 collective-permute-start.9
  332.8 12.5 %collective-permute-done.9 = f32[513,256]{1,0:T(8,128)S(1)} collective-permute-done((f32[513,256]{1,0:T(8,128)S(1)}, f32[513,256]{1,0:T(8,128)S(1)}, u32[]{:S(2)}, u32[]{:S(2)}) %collective-permute-start.9) | collective-permute-done | bytes 525344 | tf_op jit(solution)/shard_map/ppermute | solution.py:12
  348.2 9.9 %collective-permute-done.10 = f32[257,256]{1,0:T(8,128)S(1)} collective-permute-done((f32[257,256]{1,0:T(8,128)S(1)}, f32[257,256]{1,0:T(8,128)S(1)}, u32[]{:S(2)}, u32[]{:S(2)}) %collective-permute-start.10) | collective-permute-done | bytes 263200 | tf_op jit(solution)/shard_map/ppermute | solution.py:12
  359.2 2.3 collective-permute-start.11
  361.6 7.6 %collective-permute-done.11 = f32[257,256]{1,0:T(8,128)S(1)} collective-permute-done((f32[257,256]{1,0:T(8,128)S(1)}, f32[257,256]{1,0:T(8,128)S(1)}, u32[]{:S(2)}, u32[]{:S(2)}) %collective-permute-start.11) | collective-permute-done | bytes 263200 | tf_op jit(solution)/shard_map/ppermute | solution.py:12
  369.2 2.4 broadcast_in_dim.107
  371.6 77.6 %while.33 = (s32[]{:T(128)}, f32[256,256]{1,0:T(8,128)S(1)}, f32[256]{0:T(256)S(1)}, f32[16,256]{1,0:T(8,128)S(1)}, f32[16,256,256]{2,1,0:T(8,128)}, /*index=5*/...) while((s32[]{:T(128)}, f32[256,256]{1,0:T(8,128)S(1)}, ...), condition=%wide.region_3.4_spmd, body=%wide.region_2.3_spmd.sunk | while | flops 403505408 | bytes 2369673 | solution.py:138
  374.4 2.2 bitcast_dynamic-update-slice_fusion.2
  379.3 2.2 bitcast_dynamic-update-slice_fusion.2
  384.1 2.1 bitcast_dynamic-update-slice_fusion.2
  389.0 2.1 bitcast_dynamic-update-slice_fusion.2
  392.5 1.3 fusion.201
  393.8 2.1 bitcast_dynamic-update-slice_fusion.2
  398.6 2.2 bitcast_dynamic-update-slice_fusion.2
  403.5 2.2 bitcast_dynamic-update-slice_fusion.2
  408.3 2.2 bitcast_dynamic-update-slice_fusion.2
  413.2 2.1 bitcast_dynamic-update-slice_fusion.2
  416.7 1.3 fusion.201
  418.0 2.1 bitcast_dynamic-update-slice_fusion.2
  422.8 2.1 bitcast_dynamic-update-slice_fusion.2
  427.7 2.2 bitcast_dynamic-update-slice_fusion.2
  432.5 2.1 bitcast_dynamic-update-slice_fusion.2
  437.3 2.1 bitcast_dynamic-update-slice_fusion.2
  442.2 2.2 bitcast_dynamic-update-slice_fusion.2
  445.7 1.3 fusion.201
  447.0 2.2 bitcast_dynamic-update-slice_fusion.2
  449.2 2.3 constant_dynamic-slice_fusion.2
  (286 shorter events, 95.4 us)
Async XLA Ops:
  7.2 5.1 %copy-start = (f32[16,64,256]{2,1,0:T(8,128)S(1)}, f32[16,64,256]{2,1,0:T(8,128)}, u32[]{:S(2)}) copy-start(f32[16,64,256]{2,1,0:T(8,128)} %param.20) | copy-start | bytes 3145732
  7.2 57.9 %all-gather.9.cloned.1.call-start = ((), (), s32[]{:S(2)}) async-start(), calls=%async_computation.2 | async-start | bytes 5242880 | tf_op jit(solution)/shard_map/all_gather | solution.py:169
  9.3 6.4 %copy-start.9 = (f32[16,256]{1,0:T(8,128)S(1)}, f32[16,256]{1,0:T(8,128)}, u32[]{:S(2)}) copy-start(f32[16,256]{1,0:T(8,128)} %param.21) | copy-start | bytes 49156
  9.3 111.5 %copy-start.6 = (f32[256,256]{0,1:T(8,128)}, f32[256,256]{0,1:T(8,128)S(1)}, u32[]{:S(2)}) copy-start(f32[256,256]{0,1:T(8,128)S(1)} %bitcast_multiply_fusion.1) | copy-start | bytes 786436
  10.6 17.3 %copy-start.11 = (f32[256]{0:T(256)S(1)}, f32[256]{0:T(256)}, u32[]{:S(2)}) copy-start(f32[256]{0:T(256)} %param.18) | copy-start | bytes 3076
  14.2 101.2 %all-gather.7.cloned.1.call-start = ((), (), s32[]{:S(2)}) async-start(), calls=%async_computation.1 | async-start | bytes 5242880 | tf_op jit(solution)/shard_map/all_gather | solution.py:172
  15.0 150.8 %all-gather.5.cloned.1.call-start = ((), (), s32[]{:S(2)}) async-start(), calls=%async_computation | async-start | bytes 5242880 | tf_op jit(solution)/shard_map/all_gather | solution.py:171
  168.5 15.1 %copy-start.2 = (f32[16,256,256]{2,1,0:T(8,128)}, f32[16,256,256]{2,1,0:T(8,128)S(1)}, u32[]{:S(2)}) copy-start(f32[16,256,256]{2,1,0:T(8,128)S(1)} %broadcast_select_fusion) | copy-start | bytes 12582916
  168.5 3.7 copy-start.4
  172.2 4.6 copy-start.5
  181.2 4.7 %copy-start.3 = (f32[16,256,256]{2,1,0:T(8,128)}, f32[16,256,256]{2,1,0:T(8,128)S(1)}, u32[]{:S(2)}) copy-start(f32[16,256,256]{2,1,0:T(8,128)S(1)} %convolution_subtract_fusion) | copy-start | bytes 12582916
  187.0 2.4 copy-start.7
  188.2 3.2 copy-start.10
  191.7 7.1 %collective-permute-start = (f32[257,256]{1,0:T(8,128)S(1)}, f32[257,256]{1,0:T(8,128)S(1)}, u32[]{:S(2)}, u32[]{:S(2)}) collective-permute-start(f32[257,256]{1,0:T(8,128)S(1)} %pad_maximum_fusion.4), channel_id=1, source_target_pairs={{0,4},{4,8},{8,12},{12,16},{16,20},{20,24},{24,28},{28,32},{32,36}... | collective-permute-start | bytes 789512 | tf_op jit(solution)/shard_map/ppermute | solution.py:12
  199.6 8.5 %collective-permute-start.1 = (f32[257,256]{1,0:T(8,128)S(1)}, f32[257,256]{1,0:T(8,128)S(1)}, u32[]{:S(2)}, u32[]{:S(2)}) collective-permute-start(f32[257,256]{1,0:T(8,128)S(1)} %pad_maximum_fusion.5), channel_id=1, source_target_pairs={{0,8},{4,12},{8,16},{12,20},{16,24},{20,28},{24,32},{28,36},{32,40... | collective-permute-start | bytes 789512 | tf_op jit(solution)/shard_map/ppermute | solution.py:12
  208.8 8.7 %collective-permute-start.2 = (f32[257,256]{1,0:T(8,128)S(1)}, f32[257,256]{1,0:T(8,128)S(1)}, u32[]{:S(2)}, u32[]{:S(2)}) collective-permute-start(f32[257,256]{1,0:T(8,128)S(1)} %pad_maximum_fusion.6), channel_id=1, source_target_pairs={{0,16},{4,20},{8,24},{12,28},{16,32},{20,36},{24,40},{28,44},{32,4... | collective-permute-start | bytes 789512 | tf_op jit(solution)/shard_map/ppermute | solution.py:12
  212.8 32.0 %copy-start.8 = (f32[2,256,256]{2,1,0:T(8,128)}, f32[2,256,256]{2,1,0:T(8,128)S(1)}, u32[]{:S(2)}) copy-start(f32[2,256,256]{2,1,0:T(8,128)S(1)} %fusion.63) | copy-start | bytes 1572868
  218.3 7.2 %collective-permute-start.3 = (f32[257,256]{1,0:T(8,128)S(1)}, f32[257,256]{1,0:T(8,128)S(1)}, u32[]{:S(2)}, u32[]{:S(2)}) collective-permute-start(f32[257,256]{1,0:T(8,128)S(1)} %pad_maximum_fusion.7), channel_id=1, source_target_pairs={{0,32},{4,36},{8,40},{12,44},{16,48},{20,52},{24,56},{28,60},{32,6... | collective-permute-start | bytes 789512 | tf_op jit(solution)/shard_map/ppermute | solution.py:12
  225.8 3.0 collective-permute-start.4
  229.1 16.9 %collective-permute-start.5 = (f32[256]{0:T(256)S(1)}, f32[256]{0:T(256)S(1)}, u32[]{:S(2)}, u32[]{:S(2)}) collective-permute-start(f32[256]{0:T(256)S(1)} %add_select_fusion.5), channel_id=1, source_target_pairs={{0,4},{4,8},{8,12},{12,16},{16,20},{20,24},{24,28},{28,32},{32,36}... | collective-permute-start | bytes 3080 | tf_op jit(solution)/shard_map/ppermute | solution.py:12
  282.2 12.8 %collective-permute-start.6 = (f32[513,256]{1,0:T(8,128)S(1)}, f32[513,256]{1,0:T(8,128)S(1)}, u32[]{:S(2)}, u32[]{:S(2)}) collective-permute-start(f32[513,256]{1,0:T(8,128)S(1)} %pad_maximum_fusion), channel_id=1, source_target_pairs={{4,0},{8,4},{12,8},{16,12},{20,16},{24,20},{28,24},{32,28},{36,32}... | collective-permute-start | bytes 1575944 | tf_op jit(solution)/shard_map/ppermute | solution.py:12
  297.5 14.4 %collective-permute-start.7 = (f32[513,256]{1,0:T(8,128)S(1)}, f32[513,256]{1,0:T(8,128)S(1)}, u32[]{:S(2)}, u32[]{:S(2)}) collective-permute-start(f32[513,256]{1,0:T(8,128)S(1)} %pad_maximum_fusion.1), channel_id=1, source_target_pairs={{8,0},{12,4},{16,8},{20,12},{24,16},{28,20},{32,24},{36,28},{40,32... | collective-permute-start | bytes 1575944 | tf_op jit(solution)/shard_map/ppermute | solution.py:12
  313.5 15.8 %collective-permute-start.8 = (f32[513,256]{1,0:T(8,128)S(1)}, f32[513,256]{1,0:T(8,128)S(1)}, u32[]{:S(2)}, u32[]{:S(2)}) collective-permute-start(f32[513,256]{1,0:T(8,128)S(1)} %pad_maximum_fusion.2), channel_id=1, source_target_pairs={{16,0},{20,4},{24,8},{28,12},{32,16},{36,20},{40,24},{44,28},{48,3... | collective-permute-start | bytes 1575944 | tf_op jit(solution)/shard_map/ppermute | solution.py:12
  330.9 14.5 %collective-permute-start.9 = (f32[513,256]{1,0:T(8,128)S(1)}, f32[513,256]{1,0:T(8,128)S(1)}, u32[]{:S(2)}, u32[]{:S(2)}) collective-permute-start(f32[513,256]{1,0:T(8,128)S(1)} %pad_maximum_fusion.3), channel_id=1, source_target_pairs={{32,0},{36,4},{40,8},{44,12},{48,16},{52,20},{56,24},{60,28},{64,3... | collective-permute-start | bytes 1575944 | tf_op jit(solution)/shard_map/ppermute | solution.py:12
  346.5 11.6 %collective-permute-start.10 = (f32[257,256]{1,0:T(8,128)S(1)}, f32[257,256]{1,0:T(8,128)S(1)}, u32[]{:S(2)}, u32[]{:S(2)}) collective-permute-start(f32[257,256]{1,0:T(8,128)S(1)} %pad_maximum_fusion.8), channel_id=1, source_target_pairs={{64,0},{68,4},{72,8},{76,12},{80,16},{84,20},{88,24},{92,28},{96,3... | collective-permute-start | bytes 789512 | tf_op jit(solution)/shard_map/ppermute | solution.py:12
  359.2 9.9 %collective-permute-start.11 = (f32[257,256]{1,0:T(8,128)S(1)}, f32[257,256]{1,0:T(8,128)S(1)}, u32[]{:S(2)}, u32[]{:S(2)}) collective-permute-start(f32[257,256]{1,0:T(8,128)S(1)} %pad_maximum_fusion.9), channel_id=1, source_target_pairs={{4,0},{8,4},{12,8},{16,12},{20,16},{24,20},{28,24},{32,28},{36,32}... | collective-permute-start | bytes 789512 | tf_op jit(solution)/shard_map/ppermute | solution.py:12
  371.6 80.5 %copy-start.1 = (f32[16,64,256]{2,1,0:T(8,128)S(1)}, f32[16,64,256]{2,1,0:T(8,128)}, u32[]{:S(2)}) copy-start(f32[16,64,256]{2,1,0:T(8,128)} %param.20) | copy-start | bytes 3145732
Sparse Core Ops, SparseCore 0:
  14.3 50.6 all-gather.8
  66.7 48.6 all-gather.6
  117.1 48.6 all-gather.4

commit v2 on v1

--- a/solution.py
+++ b/solution.py
@@ -4,6 +4,7 @@
 from jax.sharding import PartitionSpec as P
 
 highest = lax.Precision.HIGHEST
+CHUNKS = ("tm", "blk")
 
 
 def from_behind(block, axis, distance):
@@ -56,15 +57,15 @@
     while distance < tm_count:
         has_left = tm_index >= distance
         if 2 * distance >= tm_count:
-            shift_left = from_behind(shift, "tm", distance)
+            shift_left = from_behind(shift, CHUNKS, distance)
             shift = jnp.where(has_left, matvec(cmap, shift_left) + shift, shift)
         else:
-            arrived = from_behind(jnp.concatenate([cmap, shift[None]], axis=0), "tm", distance)
+            arrived = from_behind(jnp.concatenate([cmap, shift[None]], axis=0), CHUNKS, distance)
             map_left, shift_left = arrived[:width], arrived[width]
             shift = jnp.where(has_left, matvec(cmap, shift_left) + shift, shift)
             cmap = jnp.where(has_left, matmul(cmap, map_left), cmap)
         distance *= 2
-    mean_in = from_behind(shift, "tm", 1)
+    mean_in = from_behind(shift, CHUNKS, 1)
     return jnp.where(first_window, initial_expectation, mean_in)
 
 
@@ -75,11 +76,11 @@
     while distance < tm_count:
         has_right = tm_index + distance < tm_count
         if 2 * distance >= tm_count:
-            arrived = from_behind(jnp.concatenate([resid, offset[None]], axis=0), "tm", -distance)
+            arrived = from_behind(jnp.concatenate([resid, offset[None]], axis=0), CHUNKS, -distance)
             resid_right, offset_right = arrived[:width], arrived[width]
         else:
             arrived = from_behind(
-                jnp.concatenate([gain, resid, offset[None]], axis=0), "tm", -distance
+                jnp.concatenate([gain, resid, offset[None]], axis=0), CHUNKS, -distance
             )
             gain_right = arrived[:width]
             resid_right = arrived[width : 2 * width]
@@ -90,7 +91,7 @@
         if 2 * distance < tm_count:
             gain = jnp.where(has_right, matmul(gain, gain_right), gain)
         distance *= 2
-    arrived = from_behind(jnp.concatenate([resid, offset[None]], axis=0), "tm", -1)
+    arrived = from_behind(jnp.concatenate([resid, offset[None]], axis=0), CHUNKS, -1)
     last_window = tm_index == tm_count - 1
     arrived = jnp.where(last_window, jnp.float32(0.0), arrived)
     return arrived[:width], arrived[width]
@@ -165,26 +166,24 @@
     own_rows = lax.dynamic_slice_in_dim(trans_map, row_start, row_count, 0)
     map_rows = own_rows[None] - matmul(filter_gains, obs_dyn)
     shift_rows = jnp.einsum("tro,to->tr", filter_gains, observations, precision=highest)
-    transition_operators, step_shifts, gain_full, cov_full = (
-        lax.all_gather(map_rows, "blk", axis=1, tiled=True),
-        lax.all_gather(shift_rows, "blk", axis=1, tiled=True),
-        lax.all_gather(smooth_gains, "blk", axis=1, tiled=True),
-        lax.all_gather(filt_cov, "blk", axis=1, tiled=True),
-    )
+    def steps_whole(rows):
+        return lax.all_to_all(rows, "blk", 0, 1, tiled=True)
+
+    def rows_of_steps(whole):
+        return lax.all_to_all(whole, "blk", 1, 0, tiled=True)
+
     means_out, cov_out = window_work(
         trans_map,
         process_noise,
         initial_expectation,
-        transition_operators,
-        step_shifts,
-        gain_full,
-        cov_full,
-        lax.axis_index("tm"),
-        lax.axis_size("tm"),
+        steps_whole(map_rows),
+        steps_whole(shift_rows),
+        steps_whole(smooth_gains),
+        steps_whole(filt_cov),
+        lax.axis_index(CHUNKS),
+        lax.axis_size(CHUNKS),
     )
-    means_rows = lax.dynamic_slice_in_dim(means_out, row_start, row_count, 1)
-    cov_rows = lax.dynamic_slice_in_dim(cov_out, row_start, row_count, 1)
-    return (means_rows, cov_rows)
+    return (rows_of_steps(means_out), rows_of_steps(cov_out))
 
 
 def solution(mesh):

time: 464 us -> 362 us (0.78)
  matrix products: 169 us -> 52.6 us
  waiting for transfers between devices: 200 us -> 149 us
  local copies, waits for them, and re-layouts: 13.6 us -> 47.7 us
  blocking collectives: 11 us -> 35.7 us
  starting transfers between devices: 42.6 us -> 62.3 us
  between operations: 15.3 us -> 2.16 us
    all_gather x3 -> x0, waiting for transfers between devices: 116 us -> none  [the longest x1 39.8 us: per_device(): lax.all_gather(smooth_gains, 'blk', axis=1, tiled=True)]
    dot_general x104 -> x56, matrix products: 147 us -> 41 us  [matmul(): return jnp.matmul(left, right, precision=highest)]
    ppermute x12 -> x16, waiting for transfers between devices: 82.8 us -> 129 us  [from_behind(): return lax.ppermute(block, axis, route)]
    all_to_all x0 -> x3, blocking collectives: none -> 35.7 us  [the longest x2 24.1 us: steps_whole(): return lax.all_to_all(rows, 'blk', 0, 1, tiled=True)]
    dynamic_update_slice x0 -> x8, local copies, waits for them, and re-layouts: none -> 27.7 us  [window_work(): lax.scan(smooth_walk, (cov_after, mean_after), (gain_full, residual_cov,...]
    all_to_all x0 -> x3, waiting for transfers between devices: none -> 19.9 us  [the longest x1 14 us: rows_of_steps(): return lax.all_to_all(whole, 'blk', 1, 0, tiled=True)]
    all_to_all x0 -> x3, starting transfers between devices: none -> 11.4 us  [the longest x2 7.89 us: steps_whole(): return lax.all_to_all(rows, 'blk', 0, 1, tiled=True)]
    all_gather x1 -> x0, blocking collectives: 11 us -> none  [per_device(): lax.all_gather(shift_rows, 'blk', axis=1, tiled=True)]
  transfers between devices with their start and end apart: 15 -> 19, of which waited for: 14 -> 19; matrix products, arithmetic and copies ran while one was open for 6% -> 8% of each run, Pallas kernels for 0% -> 0%
where the time goes in v2:
time: 362 us; the launch traced here: 359 us
  waiting for transfers between devices  149 us (41%)
  starting transfers between devices  62.3 us (17%)
  matrix products  52.6 us (15%)
  local copies, waits for them, and re-layouts  47.7 us (13%)
  blocking collectives  35.7 us (10%)
  other arithmetic  9.79 us (3%)
    ppermute x16, waiting for transfers between devices, from_behind(): return lax.ppermute(block, axis, route)  129 us
    ppermute x16, starting transfers between devices, from_behind(): return lax.ppermute(block, axis, route)  50.9 us
    dot_general x56, matrix products, matmul(): return jnp.matmul(left, right, precision=highest)  41 us
    dynamic_update_slice x8, local copies, waits for them, and re-layouts, window_work(): lax.scan(smooth_walk, (cov_after, mean_after), (gain_full, residual_cov,...  27.7 us
    all_to_all x2, blocking collectives, steps_whole(): return lax.all_to_all(rows, 'blk', 0, 1, tiled=True)  24.1 us
    all_to_all x1, waiting for transfers between devices, rows_of_steps(): return lax.all_to_all(whole, 'blk', 1, 0, tiled=True)  14 us
    unnamed x50, local copies, waits for them, and re-layouts  11.6 us
    all_to_all x1, blocking collectives, rows_of_steps(): return lax.all_to_all(whole, 'blk', 1, 0, tiled=True)  11.6 us
  transfers between devices with their start and end apart: 19, of which 19 were waited for; matrix products, arithmetic and copies ran while one was open for 8% of the time, Pallas kernels for 0%

profile of v2, /device:TPU:15, one launch (start us, length us, event | category | flops | bytes accessed | tf_op | source)
XLA Modules:
  0.0 359.4 jit_solution(2667771907331407574)
XLA Ops:
  1.9 1.7 fusion.79
  3.7 9.0 %all_to_all.110 = f32[4,1,256]{2,1,0:T(1,128)S(1)} all-to-all(f32[4,1,256]{2,1,0:T(1,128)S(1)} %reshape.112), channel_id=1, replica_groups=mesh['tm'=32,'blk'=4] {'blk'}, dimensions={0} | all-to-all | bytes 8192 | tf_op jit(solution)/shard_map/all_to_all | solution.py:170
  12.6 15.1 %all_to_all.111 = f32[16,64,256]{2,1,0:T(8,128)S(1)} all-to-all(f32[16,64,256]{2,1,0:T(8,128)S(1)} %copy-done.11), channel_id=1, replica_groups=mesh['tm'=32,'blk'=4] {'blk'}, dimensions={0} | all-to-all | bytes 2097152 | tf_op jit(solution)/shard_map/all_to_all | solution.py:170
  27.8 3.6 %all-to-all-start.1 = ((f32[16,64,256]{2,1,0:T(8,128)}), f32[16,64,256]{2,1,0:T(8,128)S(1)}, u32[]{:S(2)}, u32[]{:S(2)}) async-start(f32[16,64,256]{2,1,0:T(8,128)} %param.23), calls=%async_computation.1 | async-start | bytes 2097152 | tf_op jit(solution)/shard_map/all_to_all | solution.py:170
  34.3 1.8 copy.48
  38.2 2.0 fusion.15
  40.2 2.7 all-to-all-done.1
  42.9 4.2 %all-to-all-start.2 = ((f32[16,64,256]{2,1,0:T(8,128)}), f32[16,64,256]{2,1,0:T(8,128)}, u32[]{:S(2)}, u32[]{:S(2)}) async-start(f32[16,64,256]{2,1,0:T(8,128)} %fusion.15), calls=%async_computation.2 | async-start | bytes 2097152 | tf_op jit(solution)/shard_map/all_to_all | solution.py:170
  52.3 2.0 convolution_bitcast_fusion.1
  54.3 3.2 all-to-all-done.2
  57.5 1.3 copy.49
  61.9 2.3 collective-permute-start
  66.6 10.9 %collective-permute-done = f32[257,256]{1,0:T(8,128)S(1)} collective-permute-done((f32[257,256]{1,0:T(8,128)S(1)}, f32[257,256]{1,0:T(8,128)S(1)}, u32[]{:S(2)}, u32[]{:S(2)}) %collective-permute-start) | collective-permute-done | bytes 263200 | tf_op jit(solution)/shard_map/ppermute | solution.py:13
  78.2 1.9 collective-permute-start.1
  80.1 2.2 convolution_subtract_fusion
  82.3 8.1 %collective-permute-done.1 = f32[257,256]{1,0:T(8,128)S(1)} collective-permute-done((f32[257,256]{1,0:T(8,128)S(1)}, f32[257,256]{1,0:T(8,128)S(1)}, u32[]{:S(2)}, u32[]{:S(2)}) %collective-permute-start.1) | collective-permute-done | bytes 263200 | tf_op jit(solution)/shard_map/ppermute | solution.py:13
  91.1 5.6 %collective-permute-start.2 = (f32[257,256]{1,0:T(8,128)S(1)}, f32[257,256]{1,0:T(8,128)S(1)}, u32[]{:S(2)}, u32[]{:S(2)}) collective-permute-start(f32[257,256]{1,0:T(8,128)S(1)} %pad_maximum_fusion.8), channel_id=1, source_target_pairs={{0,4},{1,5},{2,6},{3,7},{4,8},{5,9},{6,10},{7,11},{8,12},{9,13},{1... | collective-permute-start | bytes 789512 | tf_op jit(solution)/shard_map/ppermute | solution.py:13
  96.7 1.7 fusion.27
  98.4 1.5 collective-permute-done.2
  100.7 1.9 collective-permute-start.3
  102.6 1.7 convolution_add_fusion.2
  104.3 5.1 %collective-permute-done.3 = f32[257,256]{1,0:T(8,128)S(1)} collective-permute-done((f32[257,256]{1,0:T(8,128)S(1)}, f32[257,256]{1,0:T(8,128)S(1)}, u32[]{:S(2)}, u32[]{:S(2)}) %collective-permute-start.3) | collective-permute-done | bytes 263200 | tf_op jit(solution)/shard_map/ppermute | solution.py:13
  110.2 1.9 collective-permute-start.4
  112.8 6.7 %collective-permute-done.4 = f32[257,256]{1,0:T(8,128)S(1)} collective-permute-done((f32[257,256]{1,0:T(8,128)S(1)}, f32[257,256]{1,0:T(8,128)S(1)}, u32[]{:S(2)}, u32[]{:S(2)}) %collective-permute-start.4) | collective-permute-done | bytes 263200 | tf_op jit(solution)/shard_map/ppermute | solution.py:13
  120.2 3.5 collective-permute-start.5
  124.5 2.9 collective-permute-done.5
  127.7 3.2 collective-permute-start.6
  132.0 2.5 collective-permute-start.7
  135.7 2.4 collective-permute-done.7
  138.1 1.6 while.32
  144.4 1.9 collective-permute-start.8
  146.3 8.4 %collective-permute-done.8 = f32[513,256]{1,0:T(8,128)} collective-permute-done((f32[513,256]{1,0:T(8,128)}, f32[513,256]{1,0:T(8,128)}, u32[]{:S(2)}, u32[]{:S(2)}) %collective-permute-start.8) | collective-permute-done | bytes 525344 | tf_op jit(solution)/shard_map/ppermute | solution.py:13
  154.7 1.3 fusion.56
  157.5 1.3 convolution_select_fusion.5
  159.6 6.6 %collective-permute-start.9 = (f32[513,256]{1,0:T(8,128)}, f32[513,256]{1,0:T(8,128)S(1)}, u32[]{:S(2)}, u32[]{:S(2)}) collective-permute-start(f32[513,256]{1,0:T(8,128)} %pad_maximum_fusion.1), channel_id=1, source_target_pairs={{2,0},{3,1},{4,2},{5,3},{6,4},{7,5},{8,6},{9,7},{10,8},{11,9},{12,... | collective-permute-start | bytes 1575944 | tf_op jit(solution)/shard_map/ppermute | solution.py:13
  166.3 17.8 %collective-permute-done.9 = f32[513,256]{1,0:T(8,128)S(1)} collective-permute-done((f32[513,256]{1,0:T(8,128)}, f32[513,256]{1,0:T(8,128)S(1)}, u32[]{:S(2)}, u32[]{:S(2)}) %collective-permute-start.9) | collective-permute-done | bytes 525344 | tf_op jit(solution)/shard_map/ppermute | solution.py:13
  186.4 2.1 collective-permute-start.10
  188.5 12.5 %collective-permute-done.10 = f32[513,256]{1,0:T(8,128)S(1)} collective-permute-done((f32[513,256]{1,0:T(8,128)}, f32[513,256]{1,0:T(8,128)S(1)}, u32[]{:S(2)}, u32[]{:S(2)}) %collective-permute-start.10) | collective-permute-done | bytes 525344 | tf_op jit(solution)/shard_map/ppermute | solution.py:13
  204.8 1.9 collective-permute-start.11
  206.8 12.9 %collective-permute-done.11 = f32[513,256]{1,0:T(8,128)} collective-permute-done((f32[513,256]{1,0:T(8,128)}, f32[513,256]{1,0:T(8,128)}, u32[]{:S(2)}, u32[]{:S(2)}) %collective-permute-start.11) | collective-permute-done | bytes 525344 | tf_op jit(solution)/shard_map/ppermute | solution.py:13
  219.6 1.3 fusion.47
  222.4 1.3 convolution_select_fusion.2
  224.6 1.9 collective-permute-start.12
  226.5 14.2 %collective-permute-done.12 = f32[513,256]{1,0:T(8,128)S(1)} collective-permute-done((f32[513,256]{1,0:T(8,128)}, f32[513,256]{1,0:T(8,128)S(1)}, u32[]{:S(2)}, u32[]{:S(2)}) %collective-permute-start.12) | collective-permute-done | bytes 525344 | tf_op jit(solution)/shard_map/ppermute | solution.py:13
  244.5 3.4 collective-permute-start.13
  247.8 13.3 %collective-permute-done.13 = f32[513,256]{1,0:T(8,128)} collective-permute-done((f32[513,256]{1,0:T(8,128)}, f32[513,256]{1,0:T(8,128)}, u32[]{:S(2)}, u32[]{:S(2)}) %collective-permute-start.13) | collective-permute-done | bytes 525344 | tf_op jit(solution)/shard_map/ppermute | solution.py:13
  261.1 1.3 fusion.41
  264.0 1.3 collective-permute-start.14
  265.3 1.3 convolution_select_fusion
  266.6 8.7 %collective-permute-done.14 = f32[257,256]{1,0:T(8,128)S(1)} collective-permute-done((f32[257,256]{1,0:T(8,128)S(1)}, f32[257,256]{1,0:T(8,128)S(1)}, u32[]{:S(2)}, u32[]{:S(2)}) %collective-permute-start.14) | collective-permute-done | bytes 263200 | tf_op jit(solution)/shard_map/ppermute | solution.py:13
  276.5 8.8 %collective-permute-start.15 = (f32[257,256]{1,0:T(8,128)S(1)}, f32[257,256]{1,0:T(8,128)S(1)}, u32[]{:S(2)}, u32[]{:S(2)}) collective-permute-start(f32[257,256]{1,0:T(8,128)S(1)} %pad_maximum_fusion.13), channel_id=1, source_target_pairs={{1,0},{2,1},{3,2},{4,3},{5,4},{6,5},{7,6},{8,7},{9,8},{10,9},{11,1... | collective-permute-start | bytes 789512 | tf_op jit(solution)/shard_map/ppermute | solution.py:13
  285.3 3.4 collective-permute-done.15
  291.2 36.4 %while.33 = (s32[]{:T(128)}, f32[256,256]{1,0:T(8,128)S(1)}, f32[256]{0:T(256)S(1)}, f32[4,256]{1,0:T(4,128)S(1)}, f32[4,256,256]{2,0,1:T(4,128)}, /*index=5*/f3...) while((s32[]{:T(128)}, f32[256,256]{1,0:T(8,128)S(1)}, ...), condition=%wide.region_3.4_spmd, body=%wide.region_2.3_spmd.sunk | while | flops 403505408 | bytes 3156109 | solution.py:139
  291.6 1.4 convolution_add_fusion.13
  293.2 6.7 %dynamic_update_slice.28 = f32[4,256,256]{2,0,1:T(4,128)} dynamic-update-slice(f32[4,256,256]{2,0,1:T(4,128)} %get-tuple-element.337, f32[1,256,256]{2,0,1:T(1,128)S(1)} %copy.82, s32[]{:T(128)S(6)} %sub.30, s32[]{:T(128)} %constant.73.clone.1..sunk.1, s32[]{:T(128)} %constant.73.clone.1..sunk.1) | dynamic-update-slice | bytes 524292 | tf_op jit(solution)/shard_map/while/body/jit(dynamic_update_index_in_dim)/dynamic_update_slice | solution.py:139
  300.7 1.4 convolution_add_fusion.13
  302.3 6.7 %dynamic_update_slice.28 = f32[4,256,256]{2,0,1:T(4,128)} dynamic-update-slice(f32[4,256,256]{2,0,1:T(4,128)} %get-tuple-element.337, f32[1,256,256]{2,0,1:T(1,128)S(1)} %copy.82, s32[]{:T(128)S(6)} %sub.30, s32[]{:T(128)} %constant.73.clone.1..sunk.1, s32[]{:T(128)} %constant.73.clone.1..sunk.1) | dynamic-update-slice | bytes 524292 | tf_op jit(solution)/shard_map/while/body/jit(dynamic_update_index_in_dim)/dynamic_update_slice | solution.py:139
  309.8 1.4 convolution_add_fusion.13
  311.4 6.7 %dynamic_update_slice.28 = f32[4,256,256]{2,0,1:T(4,128)} dynamic-update-slice(f32[4,256,256]{2,0,1:T(4,128)} %get-tuple-element.337, f32[1,256,256]{2,0,1:T(1,128)S(1)} %copy.82, s32[]{:T(128)S(6)} %sub.30, s32[]{:T(128)} %constant.73.clone.1..sunk.1, s32[]{:T(128)} %constant.73.clone.1..sunk.1) | dynamic-update-slice | bytes 524292 | tf_op jit(solution)/shard_map/while/body/jit(dynamic_update_index_in_dim)/dynamic_update_slice | solution.py:139
  318.9 1.4 convolution_add_fusion.13
  320.5 6.7 %dynamic_update_slice.28 = f32[4,256,256]{2,0,1:T(4,128)} dynamic-update-slice(f32[4,256,256]{2,0,1:T(4,128)} %get-tuple-element.337, f32[1,256,256]{2,0,1:T(1,128)S(1)} %copy.82, s32[]{:T(128)S(6)} %sub.30, s32[]{:T(128)} %constant.73.clone.1..sunk.1, s32[]{:T(128)} %constant.73.clone.1..sunk.1) | dynamic-update-slice | bytes 524292 | tf_op jit(solution)/shard_map/while/body/jit(dynamic_update_index_in_dim)/dynamic_update_slice | solution.py:139
  327.8 11.6 %all_to_all.112 = f32[4,1,256]{2,1,0:T(1,128)S(1)} all-to-all(f32[4,1,256]{2,1,0:T(1,128)S(1)} %reshape.114), channel_id=1, replica_groups=mesh['tm'=32,'blk'=4] {'blk'}, dimensions={0} | all-to-all | bytes 8192 | tf_op jit(solution)/shard_map/all_to_all | solution.py:173
  339.4 3.5 all-to-all-start.5
  344.3 14.0 %all-to-all-done.5 = f32[4,256,256]{2,0,1:T(4,128)S(1)} async-done(((f32[4,256,256]{2,0,1:T(4,128)}), f32[4,256,256]{2,0,1:T(4,128)S(1)}, u32[]{:S(2)}, u32[]{:S(2)}) %all-to-all-start.5) | async-done | bytes 1048608 | tf_op jit(solution)/shard_map/all_to_all | solution.py:173
  (209 shorter events, 55.9 us)
Async XLA Ops:
  0.6 1.2 copy-start
  0.6 12.0 %copy-start.11 = (f32[16,64,256]{2,1,0:T(8,128)S(1)}, f32[16,64,256]{2,1,0:T(8,128)}, u32[]{:S(2)}) copy-start(f32[16,64,256]{2,1,0:T(8,128)} %param.22) | copy-start | bytes 3145732
  27.8 3.7 %copy-start.17 = (f32[256,256]{1,0:T(8,128)S(1)}, f32[256,256]{1,0:T(8,128)}, u32[]{:S(2)}) copy-start(f32[256,256]{1,0:T(8,128)} %param.14) | copy-start | bytes 786436
  27.8 15.1 %all-to-all-start.1 = ((f32[16,64,256]{2,1,0:T(8,128)}), f32[16,64,256]{2,1,0:T(8,128)S(1)}, u32[]{:S(2)}, u32[]{:S(2)}) async-start(f32[16,64,256]{2,1,0:T(8,128)} %param.23), calls=%async_computation.1 | async-start | bytes 2097152 | tf_op jit(solution)/shard_map/all_to_all | solution.py:170
  31.4 0.9 copy-start.19
  33.5 30.9 %copy-start.3 = (f32[256,256]{0,1:T(8,128)}, f32[256,256]{0,1:T(8,128)S(1)}, u32[]{:S(2)}) copy-start(f32[256,256]{0,1:T(8,128)S(1)} %bitcast_multiply_fusion.1) | copy-start | bytes 786436
  34.3 1.8 copy-start.20
  37.3 0.8 copy-start.16
  42.9 14.6 %all-to-all-start.2 = ((f32[16,64,256]{2,1,0:T(8,128)}), f32[16,64,256]{2,1,0:T(8,128)}, u32[]{:S(2)}, u32[]{:S(2)}) async-start(f32[16,64,256]{2,1,0:T(8,128)} %fusion.15), calls=%async_computation.2 | async-start | bytes 2097152 | tf_op jit(solution)/shard_map/all_to_all | solution.py:170
  47.2 0.7 copy-start.21
  51.3 1.0 copy-start.1
  60.0 4.1 %copy-start.6 = (f32[4,4,64,256]{3,2,0,1:T(8,128)S(1)}, f32[4,4,64,256]{3,2,0,1:T(8,128)}, u32[]{:S(2)}) copy-start(f32[4,4,64,256]{3,2,0,1:T(8,128)} %copy.40) | copy-start | bytes 3145732
  60.8 0.7 copy-start.18
  61.8 2.5 copy-start.7
  61.8 2.5 copy-start.10
  61.9 15.6 %collective-permute-start = (f32[257,256]{1,0:T(8,128)S(1)}, f32[257,256]{1,0:T(8,128)S(1)}, u32[]{:S(2)}, u32[]{:S(2)}) collective-permute-start(f32[257,256]{1,0:T(8,128)S(1)} %pad_maximum_fusion.6), channel_id=1, source_target_pairs={{0,1},{1,2},{2,3},{3,4},{4,5},{5,6},{6,7},{7,8},{8,9},{9,10},{10,1... | collective-permute-start | bytes 789512 | tf_op jit(solution)/shard_map/ppermute | solution.py:13
  66.5 13.6 %copy-start.2 = (f32[4,4,64,256]{3,2,0,1:T(8,128)S(1)}, f32[4,4,64,256]{3,2,0,1:T(8,128)}, u32[]{:S(2)}) copy-start(f32[4,4,64,256]{3,2,0,1:T(8,128)} %copy-done.1) | copy-start | bytes 3145732
  78.2 12.2 %collective-permute-start.1 = (f32[257,256]{1,0:T(8,128)S(1)}, f32[257,256]{1,0:T(8,128)S(1)}, u32[]{:S(2)}, u32[]{:S(2)}) collective-permute-start(f32[257,256]{1,0:T(8,128)S(1)} %pad_maximum_fusion.7), channel_id=1, source_target_pairs={{0,2},{1,3},{2,4},{3,5},{4,6},{5,7},{6,8},{7,9},{8,10},{9,11},{10,... | collective-permute-start | bytes 789512 | tf_op jit(solution)/shard_map/ppermute | solution.py:13
  91.1 8.8 %collective-permute-start.2 = (f32[257,256]{1,0:T(8,128)S(1)}, f32[257,256]{1,0:T(8,128)S(1)}, u32[]{:S(2)}, u32[]{:S(2)}) collective-permute-start(f32[257,256]{1,0:T(8,128)S(1)} %pad_maximum_fusion.8), channel_id=1, source_target_pairs={{0,4},{1,5},{2,6},{3,7},{4,8},{5,9},{6,10},{7,11},{8,12},{9,13},{1... | collective-permute-start | bytes 789512 | tf_op jit(solution)/shard_map/ppermute | solution.py:13
  100.7 8.8 %collective-permute-start.3 = (f32[257,256]{1,0:T(8,128)S(1)}, f32[257,256]{1,0:T(8,128)S(1)}, u32[]{:S(2)}, u32[]{:S(2)}) collective-permute-start(f32[257,256]{1,0:T(8,128)S(1)} %pad_maximum_fusion.9), channel_id=1, source_target_pairs={{0,8},{1,9},{2,10},{3,11},{4,12},{5,13},{6,14},{7,15},{8,16},{9,17... | collective-permute-start | bytes 789512 | tf_op jit(solution)/shard_map/ppermute | solution.py:13
  110.2 9.3 %collective-permute-start.4 = (f32[257,256]{1,0:T(8,128)S(1)}, f32[257,256]{1,0:T(8,128)S(1)}, u32[]{:S(2)}, u32[]{:S(2)}) collective-permute-start(f32[257,256]{1,0:T(8,128)S(1)} %pad_maximum_fusion.10), channel_id=1, source_target_pairs={{0,16},{1,17},{2,18},{3,19},{4,20},{5,21},{6,22},{7,23},{8,24},{9,... | collective-permute-start | bytes 789512 | tf_op jit(solution)/shard_map/ppermute | solution.py:13
  112.8 21.8 %copy-start.4 = (f32[2,256,256]{2,1,0:T(8,128)}, f32[2,256,256]{2,1,0:T(8,128)S(1)}, u32[]{:S(2)}) copy-start(f32[2,256,256]{2,1,0:T(8,128)S(1)} %fusion.29) | copy-start | bytes 1572868
  120.2 7.2 %collective-permute-start.5 = (f32[257,256]{1,0:T(8,128)S(1)}, f32[257,256]{1,0:T(8,128)S(1)}, u32[]{:S(2)}, u32[]{:S(2)}) collective-permute-start(f32[257,256]{1,0:T(8,128)S(1)} %pad_maximum_fusion.11), channel_id=1, source_target_pairs={{0,32},{1,33},{2,34},{3,35},{4,36},{5,37},{6,38},{7,39},{8,40},{9,... | collective-permute-start | bytes 789512 | tf_op jit(solution)/shard_map/ppermute | solution.py:13
  127.7 3.9 %collective-permute-start.6 = (f32[256]{0:T(256)S(1)}, f32[256]{0:T(256)S(1)}, u32[]{:S(2)}, u32[]{:S(2)}) collective-permute-start(f32[256]{0:T(256)S(1)} %add_select_fusion.8), channel_id=1, source_target_pairs={{0,64},{1,65},{2,66},{3,67},{4,68},{5,69},{6,70},{7,71},{8,72},{9,... | collective-permute-start | bytes 3080 | tf_op jit(solution)/shard_map/ppermute | solution.py:13
  132.0 6.1 %collective-permute-start.7 = (f32[256]{0:T(256)S(1)}, f32[256]{0:T(256)S(1)}, u32[]{:S(2)}, u32[]{:S(2)}) collective-permute-start(f32[256]{0:T(256)S(1)} %add_select_fusion.7), channel_id=1, source_target_pairs={{0,1},{1,2},{2,3},{3,4},{4,5},{5,6},{6,7},{7,8},{8,9},{9,10},{10,1... | collective-permute-start | bytes 3080 | tf_op jit(solution)/shard_map/ppermute | solution.py:13
  141.9 1.1 copy-start.5
  142.5 1.0 copy-start.8
  144.4 10.3 %collective-permute-start.8 = (f32[513,256]{1,0:T(8,128)}, f32[513,256]{1,0:T(8,128)}, u32[]{:S(2)}, u32[]{:S(2)}) collective-permute-start(f32[513,256]{1,0:T(8,128)} %pad_maximum_fusion), channel_id=1, source_target_pairs={{1,0},{2,1},{3,2},{4,3},{5,4},{6,5},{7,6},{8,7},{9,8},{10,9},{11,1... | collective-permute-start | bytes 1575944 | tf_op jit(solution)/shard_map/ppermute | solution.py:13
  159.6 24.4 %collective-permute-start.9 = (f32[513,256]{1,0:T(8,128)}, f32[513,256]{1,0:T(8,128)S(1)}, u32[]{:S(2)}, u32[]{:S(2)}) collective-permute-start(f32[513,256]{1,0:T(8,128)} %pad_maximum_fusion.1), channel_id=1, source_target_pairs={{2,0},{3,1},{4,2},{5,3},{6,4},{7,5},{8,6},{9,7},{10,8},{11,9},{12,... | collective-permute-start | bytes 1575944 | tf_op jit(solution)/shard_map/ppermute | solution.py:13
  186.4 14.6 %collective-permute-start.10 = (f32[513,256]{1,0:T(8,128)}, f32[513,256]{1,0:T(8,128)S(1)}, u32[]{:S(2)}, u32[]{:S(2)}) collective-permute-start(f32[513,256]{1,0:T(8,128)} %pad_maximum_fusion.2), channel_id=1, source_target_pairs={{4,0},{5,1},{6,2},{7,3},{8,4},{9,5},{10,6},{11,7},{12,8},{13,9},{1... | collective-permute-start | bytes 1575944 | tf_op jit(solution)/shard_map/ppermute | solution.py:13
  201.0 0.8 copy-start.12
  202.2 1.0 copy-start.13
  204.8 14.8 %collective-permute-start.11 = (f32[513,256]{1,0:T(8,128)}, f32[513,256]{1,0:T(8,128)}, u32[]{:S(2)}, u32[]{:S(2)}) collective-permute-start(f32[513,256]{1,0:T(8,128)} %pad_maximum_fusion.3), channel_id=1, source_target_pairs={{8,0},{9,1},{10,2},{11,3},{12,4},{13,5},{14,6},{15,7},{16,8},{17,9... | collective-permute-start | bytes 1575944 | tf_op jit(solution)/shard_map/ppermute | solution.py:13
  224.6 16.1 %collective-permute-start.12 = (f32[513,256]{1,0:T(8,128)}, f32[513,256]{1,0:T(8,128)S(1)}, u32[]{:S(2)}, u32[]{:S(2)}) collective-permute-start(f32[513,256]{1,0:T(8,128)} %pad_maximum_fusion.4), channel_id=1, source_target_pairs={{16,0},{17,1},{18,2},{19,3},{20,4},{21,5},{22,6},{23,7},{24,8},{25... | collective-permute-start | bytes 1575944 | tf_op jit(solution)/shard_map/ppermute | solution.py:13
  240.7 0.8 copy-start.14
  241.9 1.0 copy-start.15
  244.5 16.7 %collective-permute-start.13 = (f32[513,256]{1,0:T(8,128)}, f32[513,256]{1,0:T(8,128)}, u32[]{:S(2)}, u32[]{:S(2)}) collective-permute-start(f32[513,256]{1,0:T(8,128)} %pad_maximum_fusion.5), channel_id=1, source_target_pairs={{32,0},{33,1},{34,2},{35,3},{36,4},{37,5},{38,6},{39,7},{40,8},{41... | collective-permute-start | bytes 1575944 | tf_op jit(solution)/shard_map/ppermute | solution.py:13
  264.0 11.3 %collective-permute-start.14 = (f32[257,256]{1,0:T(8,128)S(1)}, f32[257,256]{1,0:T(8,128)S(1)}, u32[]{:S(2)}, u32[]{:S(2)}) collective-permute-start(f32[257,256]{1,0:T(8,128)S(1)} %pad_maximum_fusion.12), channel_id=1, source_target_pairs={{64,0},{65,1},{66,2},{67,3},{68,4},{69,5},{70,6},{71,7},{72,8},{73... | collective-permute-start | bytes 789512 | tf_op jit(solution)/shard_map/ppermute | solution.py:13
  276.5 12.2 %collective-permute-start.15 = (f32[257,256]{1,0:T(8,128)S(1)}, f32[257,256]{1,0:T(8,128)S(1)}, u32[]{:S(2)}, u32[]{:S(2)}) collective-permute-start(f32[257,256]{1,0:T(8,128)S(1)} %pad_maximum_fusion.13), channel_id=1, source_target_pairs={{1,0},{2,1},{3,2},{4,3},{5,4},{6,5},{7,6},{8,7},{9,8},{10,9},{11,1... | collective-permute-start | bytes 789512 | tf_op jit(solution)/shard_map/ppermute | solution.py:13
  288.7 0.7 copy-start.9
  290.5 0.7 slice-start
  339.4 18.8 %all-to-all-start.5 = ((f32[4,256,256]{2,0,1:T(4,128)}), f32[4,256,256]{2,0,1:T(4,128)S(1)}, u32[]{:S(2)}, u32[]{:S(2)}) async-start(f32[4,256,256]{2,0,1:T(4,128)} %get-tuple-element.192), calls=%async_computation.5 | async-start | bytes 2097152 | tf_op jit(solution)/shard_map/all_to_all | solution.py:173

commit v3 on v2

--- a/solution.py
+++ b/solution.py
@@ -115,11 +115,12 @@
     window_map, window_shift = filter_tree(transition_operators, step_shifts)
     mean_in = filter_scan(window_map, window_shift, initial_expectation, tm_index, tm_count)
 
-    def filter_walk(current, step_parts):
-        current = matmul(step_parts[0], current) + step_parts[1]
-        return (current, current)
-
-    filt_means = lax.scan(filter_walk, mean_in, (transition_operators, step_shifts))[1]
+    filt_steps = []
+    current = mean_in
+    for step in range(step_count):
+        current = matvec(transition_operators[step], current) + step_shifts[step]
+        filt_steps.append(current)
+    filt_means = jnp.stack(filt_steps)
     predicted = matmul(matmul(trans_map, cov_full), trans_map.T) + jnp.diag(process_noise)
     gain_trans = jnp.swapaxes(gain_full, 1, 2)
     residual_cov = cov_full - matmul(matmul(gain_full, predicted), gain_trans)
@@ -129,19 +130,16 @@
     window_gain, window_resid, window_offset = smooth_tree(gain_full, residual_cov, offsets)
     cov_after, mean_after = smooth_scan(window_gain, window_resid, window_offset, tm_index, tm_count)
 
-    def smooth_walk(current, step_parts):
-        cov_next, mean_next = current
-        gain_now, resid_now, offset_now = step_parts
-        cov_now = matmul(matmul(gain_now, cov_next), gain_now.T) + resid_now
-        current_mean = matmul(gain_now, mean_next) + offset_now
-        return ((cov_now, current_mean), (current_mean, cov_now))
-
-    return lax.scan(
-        smooth_walk,
-        (cov_after, mean_after),
-        (gain_full, residual_cov, offsets),
-        reverse=True,
-    )[1]
+    cov_steps = [None] * step_count
+    mean_steps = [None] * step_count
+    cov_next, mean_next = cov_after, mean_after
+    for step in reversed(range(step_count)):
+        gain_now = gain_full[step]
+        cov_next = matmul(matmul(gain_now, cov_next), gain_now.T) + residual_cov[step]
+        mean_next = matvec(gain_now, mean_next) + offsets[step]
+        cov_steps[step] = cov_next
+        mean_steps[step] = mean_next
+    return jnp.stack(mean_steps), jnp.stack(cov_steps)
 
 
 def per_device(

time: 362 us -> 319 us (0.88)
  local copies, waits for them, and re-layouts: 47.7 us -> 15.9 us
  blocking collectives: 35.7 us -> 8.97 us
  starting transfers between devices: 62.3 us -> 76.2 us
  waiting for transfers between devices: 149 us -> 159 us
  matrix products: 52.6 us -> 46.7 us
    dynamic_update_slice x16 -> x0, local copies, waits for them, and re-layouts: 28.1 us -> none  [the longest x8 27.7 us: window_work(): lax.scan(smooth_walk, (cov_after, mean_after), (gain_full, residual_cov,...]
    all_to_all x2 -> x1, blocking collectives: 24.1 us -> 8.97 us  [steps_whole(): return lax.all_to_all(rows, 'blk', 0, 1, tiled=True)]
    all_to_all x2 -> x3, waiting for transfers between devices: 5.92 us -> 19.1 us  [steps_whole(): return lax.all_to_all(rows, 'blk', 0, 1, tiled=True)]
    all_to_all x1 -> x0, blocking collectives: 11.6 us -> none  [rows_of_steps(): return lax.all_to_all(whole, 'blk', 1, 0, tiled=True)]
    all_to_all x1 -> x2, starting transfers between devices: 3.52 us -> 11.9 us  [rows_of_steps(): return lax.all_to_all(whole, 'blk', 1, 0, tiled=True)]
    dot_general x56 -> x48, matrix products: 41 us -> 33.1 us  [matmul(): return jnp.matmul(left, right, precision=highest)]
    all_to_all x2 -> x3, starting transfers between devices: 7.89 us -> 11.4 us  [steps_whole(): return lax.all_to_all(rows, 'blk', 0, 1, tiled=True)]
    unnamed x50 -> x44, local copies, waits for them, and re-layouts: 11.6 us -> 8.26 us
  transfers between devices with their start and end apart: 19 -> 21, of which waited for: 19 -> 20; matrix products, arithmetic and copies ran while one was open for 8% -> 8% of each run, Pallas kernels for 0% -> 0%
where the time goes in v3:
time: 319 us; the launch traced here: 317 us
  waiting for transfers between devices  159 us (50%)
  starting transfers between devices  76.2 us (24%)
  matrix products  46.7 us (15%)
  local copies, waits for them, and re-layouts  15.9 us (5%)
  blocking collectives  8.97 us (3%)
  other arithmetic  8.1 us (3%)
    ppermute x16, waiting for transfers between devices, from_behind(): return lax.ppermute(block, axis, route)  126 us
    ppermute x16, starting transfers between devices, from_behind(): return lax.ppermute(block, axis, route)  52.9 us
    dot_general x48, matrix products, matmul(): return jnp.matmul(left, right, precision=highest)  33.1 us
    all_to_all x3, waiting for transfers between devices, steps_whole(): return lax.all_to_all(rows, 'blk', 0, 1, tiled=True)  19.1 us
    all_to_all x2, waiting for transfers between devices, rows_of_steps(): return lax.all_to_all(whole, 'blk', 1, 0, tiled=True)  14 us
    all_to_all x2, starting transfers between devices, rows_of_steps(): return lax.all_to_all(whole, 'blk', 1, 0, tiled=True)  11.9 us
    all_to_all x3, starting transfers between devices, steps_whole(): return lax.all_to_all(rows, 'blk', 0, 1, tiled=True)  11.4 us
    dot_general x27, matrix products, matvec(): return jnp.einsum('...ij,...j->...i', left, right, precision=highest)  10.8 us
  transfers between devices with their start and end apart: 21, of which 20 were waited for; matrix products, arithmetic and copies ran while one was open for 8% of the time, Pallas kernels for 0%

profile of v3, /device:TPU:15, one launch (start us, length us, event | category | flops | bytes accessed | tf_op | source)
XLA Modules:
  0.0 317.1 jit_solution(15208053824209496789)
XLA Ops:
  0.6 1.2 copy-done
  1.9 1.7 fusion.74
  3.7 9.0 %all_to_all.107 = f32[4,1,256]{2,1,0:T(1,128)S(1)} all-to-all(f32[4,1,256]{2,1,0:T(1,128)S(1)} %reshape.170), channel_id=1, replica_groups=mesh['tm'=32,'blk'=4] {'blk'}, dimensions={0} | all-to-all | bytes 8192 | tf_op jit(solution)/shard_map/all_to_all | solution.py:168
  12.6 3.6 %all-to-all-start = ((f32[16,64,256]{2,1,0:T(8,128)}), f32[16,64,256]{2,1,0:T(8,128)S(1)}, u32[]{:S(2)}, u32[]{:S(2)}) async-start(f32[16,64,256]{2,1,0:T(8,128)} %param.18), calls=%async_computation | async-start | bytes 2097152 | tf_op jit(solution)/shard_map/all_to_all | solution.py:168
  19.1 2.0 fusion
  21.0 8.2 %all-to-all-done = f32[16,64,256]{2,1,0:T(8,128)S(1)} async-done(((f32[16,64,256]{2,1,0:T(8,128)}), f32[16,64,256]{2,1,0:T(8,128)S(1)}, u32[]{:S(2)}, u32[]{:S(2)}) %all-to-all-start) | async-done | bytes 1048608 | tf_op jit(solution)/shard_map/all_to_all | solution.py:168
  29.3 3.5 %all-to-all-start.2 = ((f32[16,64,256]{2,1,0:T(8,128)}), f32[16,64,256]{2,1,0:T(8,128)S(1)}, u32[]{:S(2)}, u32[]{:S(2)}) async-start(f32[16,64,256]{2,1,0:T(8,128)} %fusion), calls=%async_computation.2 | async-start | bytes 2097152 | tf_op jit(solution)/shard_map/all_to_all | solution.py:168
  36.1 1.1 copy.37
  37.2 7.4 %all-to-all-done.2 = f32[16,64,256]{2,1,0:T(8,128)S(1)} async-done(((f32[16,64,256]{2,1,0:T(8,128)}), f32[16,64,256]{2,1,0:T(8,128)S(1)}, u32[]{:S(2)}, u32[]{:S(2)}) %all-to-all-start.2) | async-done | bytes 1048608 | tf_op jit(solution)/shard_map/all_to_all | solution.py:168
  44.6 4.2 %all-to-all-start.1 = ((f32[16,64,256]{2,1,0:T(8,128)}), f32[16,64,256]{2,1,0:T(8,128)}, u32[]{:S(2)}, u32[]{:S(2)}) async-start(f32[16,64,256]{2,1,0:T(8,128)} %param.19), calls=%async_computation.1 | async-start | bytes 2097152 | tf_op jit(solution)/shard_map/all_to_all | solution.py:168
  52.7 3.3 %collective-permute-start = (f32[257,256]{1,0:T(8,128)}, f32[257,256]{1,0:T(8,128)}, u32[]{:S(2)}, u32[]{:S(2)}) collective-permute-start(f32[257,256]{1,0:T(8,128)} %pad_maximum_fusion.7), channel_id=1, source_target_pairs={{0,1},{1,2},{2,3},{3,4},{4,5},{5,6},{6,7},{7,8},{8,9},{9,10},{10,1... | collective-permute-start | bytes 789512 | tf_op jit(solution)/shard_map/ppermute | solution.py:13
  56.0 3.5 %all-to-all-done.1 = f32[16,64,256]{2,1,0:T(8,128)} async-done(((f32[16,64,256]{2,1,0:T(8,128)}), f32[16,64,256]{2,1,0:T(8,128)}, u32[]{:S(2)}, u32[]{:S(2)}) %all-to-all-start.1) | async-done | bytes 1048608 | tf_op jit(solution)/shard_map/all_to_all | solution.py:168
  59.5 1.3 copy.38
  60.8 1.0 convolution_bitcast_fusion.1
  62.9 1.0 convolution_add_fusion
  63.9 1.1 fusion.97
  65.1 6.6 %collective-permute-done = f32[257,256]{1,0:T(8,128)} collective-permute-done((f32[257,256]{1,0:T(8,128)}, f32[257,256]{1,0:T(8,128)}, u32[]{:S(2)}, u32[]{:S(2)}) %collective-permute-start) | collective-permute-done | bytes 263200 | tf_op jit(solution)/shard_map/ppermute | solution.py:13
  71.7 1.0 fusion.92
  72.8 1.3 convolution_select_fusion.11
  74.1 1.9 collective-permute-start.1
  76.1 1.2 convolution_subtract_fusion
  77.2 6.2 %collective-permute-done.1 = f32[257,256]{1,0:T(8,128)S(1)} collective-permute-done((f32[257,256]{1,0:T(8,128)S(1)}, f32[257,256]{1,0:T(8,128)S(1)}, u32[]{:S(2)}, u32[]{:S(2)}) %collective-permute-start.1) | collective-permute-done | bytes 263200 | tf_op jit(solution)/shard_map/ppermute | solution.py:13
  84.2 9.8 %collective-permute-start.2 = (f32[257,256]{1,0:T(8,128)S(1)}, f32[257,256]{1,0:T(8,128)S(1)}, u32[]{:S(2)}, u32[]{:S(2)}) collective-permute-start(f32[257,256]{1,0:T(8,128)S(1)} %pad_maximum_fusion.9), channel_id=1, source_target_pairs={{0,4},{1,5},{2,6},{3,7},{4,8},{5,9},{6,10},{7,11},{8,12},{9,13},{1... | collective-permute-start | bytes 789512 | tf_op jit(solution)/shard_map/ppermute | solution.py:13
  95.0 2.1 collective-permute-done.2
  97.9 1.9 collective-permute-start.3
  100.5 7.7 %collective-permute-done.3 = f32[257,256]{1,0:T(8,128)S(1)} collective-permute-done((f32[257,256]{1,0:T(8,128)S(1)}, f32[257,256]{1,0:T(8,128)S(1)}, u32[]{:S(2)}, u32[]{:S(2)}) %collective-permute-start.3) | collective-permute-done | bytes 263200 | tf_op jit(solution)/shard_map/ppermute | solution.py:13
  108.9 1.9 collective-permute-start.4
  111.5 8.2 %collective-permute-done.4 = f32[257,256]{1,0:T(8,128)S(1)} collective-permute-done((f32[257,256]{1,0:T(8,128)S(1)}, f32[257,256]{1,0:T(8,128)S(1)}, u32[]{:S(2)}, u32[]{:S(2)}) %collective-permute-start.4) | collective-permute-done | bytes 263200 | tf_op jit(solution)/shard_map/ppermute | solution.py:13
  120.5 2.8 collective-permute-start.5
  123.7 5.1 %collective-permute-done.5 = f32[257,256]{1,0:T(8,128)S(1)} collective-permute-done((f32[257,256]{1,0:T(8,128)S(1)}, f32[257,256]{1,0:T(8,128)S(1)}, u32[]{:S(2)}, u32[]{:S(2)}) %collective-permute-start.5) | collective-permute-done | bytes 263200 | tf_op jit(solution)/shard_map/ppermute | solution.py:13
  129.2 2.7 collective-permute-start.6
  132.9 1.9 collective-permute-start.7
  135.3 3.7 %collective-permute-done.7 = f32[256]{0:T(256)S(1)} collective-permute-done((f32[256]{0:T(256)S(1)}, f32[256]{0:T(256)S(1)}, u32[]{:S(2)}, u32[]{:S(2)}) %collective-permute-start.7) | collective-permute-done | bytes 1056 | tf_op jit(solution)/shard_map/ppermute | solution.py:13
  140.8 1.0 fusion.76
  143.3 2.0 collective-permute-start.8
  145.3 9.7 %collective-permute-done.8 = f32[513,256]{1,0:T(8,128)} collective-permute-done((f32[513,256]{1,0:T(8,128)S(1)}, f32[513,256]{1,0:T(8,128)}, u32[]{:S(2)}, u32[]{:S(2)}) %collective-permute-start.8) | collective-permute-done | bytes 525344 | tf_op jit(solution)/shard_map/ppermute | solution.py:13
  154.9 1.3 fusion.44
  156.7 1.0 fusion.86
  157.7 1.3 convolution_select_fusion.5
  159.9 4.4 %collective-permute-start.9 = (f32[513,256]{1,0:T(8,128)}, f32[513,256]{1,0:T(8,128)S(1)}, u32[]{:S(2)}, u32[]{:S(2)}) collective-permute-start(f32[513,256]{1,0:T(8,128)} %pad_maximum_fusion.2), channel_id=1, source_target_pairs={{2,0},{3,1},{4,2},{5,3},{6,4},{7,5},{8,6},{9,7},{10,8},{11,9},{12,... | collective-permute-start | bytes 1575944 | tf_op jit(solution)/shard_map/ppermute | solution.py:13
  164.3 13.0 %collective-permute-done.9 = f32[513,256]{1,0:T(8,128)S(1)} collective-permute-done((f32[513,256]{1,0:T(8,128)}, f32[513,256]{1,0:T(8,128)S(1)}, u32[]{:S(2)}, u32[]{:S(2)}) %collective-permute-start.9) | collective-permute-done | bytes 525344 | tf_op jit(solution)/shard_map/ppermute | solution.py:13
  179.7 5.4 %collective-permute-start.10 = (f32[513,256]{1,0:T(8,128)}, f32[513,256]{1,0:T(8,128)S(1)}, u32[]{:S(2)}, u32[]{:S(2)}) collective-permute-start(f32[513,256]{1,0:T(8,128)} %pad_maximum_fusion.3), channel_id=1, source_target_pairs={{4,0},{5,1},{6,2},{7,3},{8,4},{9,5},{10,6},{11,7},{12,8},{13,9},{1... | collective-permute-start | bytes 1575944 | tf_op jit(solution)/shard_map/ppermute | solution.py:13
  185.1 10.1 %collective-permute-done.10 = f32[513,256]{1,0:T(8,128)S(1)} collective-permute-done((f32[513,256]{1,0:T(8,128)}, f32[513,256]{1,0:T(8,128)S(1)}, u32[]{:S(2)}, u32[]{:S(2)}) %collective-permute-start.10) | collective-permute-done | bytes 525344 | tf_op jit(solution)/shard_map/ppermute | solution.py:13
  196.8 1.3 convolution_select_fusion.3
  199.0 1.9 collective-permute-start.11
  200.9 13.4 %collective-permute-done.11 = f32[513,256]{1,0:T(8,128)} collective-permute-done((f32[513,256]{1,0:T(8,128)}, f32[513,256]{1,0:T(8,128)}, u32[]{:S(2)}, u32[]{:S(2)}) %collective-permute-start.11) | collective-permute-done | bytes 525344 | tf_op jit(solution)/shard_map/ppermute | solution.py:13
  215.4 1.3 fusion.35
  217.1 1.3 convolution_select_fusion.2
  219.3 1.9 collective-permute-start.12
  221.2 14.7 %collective-permute-done.12 = f32[513,256]{1,0:T(8,128)S(1)} collective-permute-done((f32[513,256]{1,0:T(8,128)}, f32[513,256]{1,0:T(8,128)S(1)}, u32[]{:S(2)}, u32[]{:S(2)}) %collective-permute-start.12) | collective-permute-done | bytes 525344 | tf_op jit(solution)/shard_map/ppermute | solution.py:13
  237.5 1.3 convolution_select_fusion.1
  239.7 4.3 %collective-permute-start.13 = (f32[513,256]{1,0:T(8,128)}, f32[513,256]{1,0:T(8,128)}, u32[]{:S(2)}, u32[]{:S(2)}) collective-permute-start(f32[513,256]{1,0:T(8,128)} %pad_maximum_fusion.6), channel_id=1, source_target_pairs={{32,0},{33,1},{34,2},{35,3},{36,4},{37,5},{38,6},{39,7},{40,8},{41... | collective-permute-start | bytes 1575944 | tf_op jit(solution)/shard_map/ppermute | solution.py:13
  244.0 13.3 %collective-permute-done.13 = f32[513,256]{1,0:T(8,128)} collective-permute-done((f32[513,256]{1,0:T(8,128)}, f32[513,256]{1,0:T(8,128)}, u32[]{:S(2)}, u32[]{:S(2)}) %collective-permute-start.13) | collective-permute-done | bytes 525344 | tf_op jit(solution)/shard_map/ppermute | solution.py:13
  258.4 1.3 fusion.29
  260.2 1.3 collective-permute-start.14
  261.5 1.3 convolution_select_fusion
  262.8 8.3 %collective-permute-done.14 = f32[257,256]{1,0:T(8,128)S(1)} collective-permute-done((f32[257,256]{1,0:T(8,128)S(1)}, f32[257,256]{1,0:T(8,128)S(1)}, u32[]{:S(2)}, u32[]{:S(2)}) %collective-permute-start.14) | collective-permute-done | bytes 263200 | tf_op jit(solution)/shard_map/ppermute | solution.py:13
  272.3 5.6 %collective-permute-start.15 = (f32[257,256]{1,0:T(8,128)S(1)}, f32[257,256]{1,0:T(8,128)S(1)}, u32[]{:S(2)}, u32[]{:S(2)}) collective-permute-start(f32[257,256]{1,0:T(8,128)S(1)} %pad_maximum_fusion.14), channel_id=1, source_target_pairs={{1,0},{2,1},{3,2},{4,3},{5,4},{6,5},{7,6},{8,7},{9,8},{10,9},{11,1... | collective-permute-start | bytes 789512 | tf_op jit(solution)/shard_map/ppermute | solution.py:13
  277.9 3.4 %collective-permute-done.15 = f32[257,256]{1,0:T(8,128)S(1)} collective-permute-done((f32[257,256]{1,0:T(8,128)S(1)}, f32[257,256]{1,0:T(8,128)S(1)}, u32[]{:S(2)}, u32[]{:S(2)}) %collective-permute-start.15) | collective-permute-done | bytes 263200 | tf_op jit(solution)/shard_map/ppermute | solution.py:13
  284.1 7.7 %all-to-all-start.4 = ((f32[4,1,256]{2,1,0:T(1,128)}), f32[4,1,256]{2,1,0:T(1,128)S(1)}, u32[]{:S(2)}, u32[]{:S(2)}) async-start(f32[4,1,256]{2,1,0:T(1,128)} %reshape.172), calls=%async_computation.4 | async-start | bytes 8192 | tf_op jit(solution)/shard_map/all_to_all | solution.py:171
  294.7 1.6 copy.48
  296.4 4.2 %all-to-all-start.5 = ((f32[4,256,256]{2,0,1:T(4,128)}), f32[4,256,256]{2,0,1:T(4,128)S(1)}, u32[]{:S(2)}, u32[]{:S(2)}) async-start(f32[4,256,256]{2,0,1:T(4,128)} %copy.48), calls=%async_computation.5 | async-start | bytes 2097152 | tf_op jit(solution)/shard_map/all_to_all | solution.py:171
  301.9 14.0 %all-to-all-done.5 = f32[4,256,256]{2,0,1:T(4,128)S(1)} async-done(((f32[4,256,256]{2,0,1:T(4,128)}), f32[4,256,256]{2,0,1:T(4,128)S(1)}, u32[]{:S(2)}, u32[]{:S(2)}) %all-to-all-start.5) | async-done | bytes 1048608 | tf_op jit(solution)/shard_map/all_to_all | solution.py:171
  315.9 1.2 copy.49
  (185 shorter events, 41.7 us)
Async XLA Ops:
  0.6 1.2 copy-start
  12.6 3.7 %copy-start.13 = (f32[256,256]{1,0:T(8,128)S(1)}, f32[256,256]{1,0:T(8,128)}, u32[]{:S(2)}) copy-start(f32[256,256]{1,0:T(8,128)} %param.10) | copy-start | bytes 786436
  12.6 16.6 %all-to-all-start = ((f32[16,64,256]{2,1,0:T(8,128)}), f32[16,64,256]{2,1,0:T(8,128)S(1)}, u32[]{:S(2)}, u32[]{:S(2)}) async-start(f32[16,64,256]{2,1,0:T(8,128)} %param.18), calls=%async_computation | async-start | bytes 2097152 | tf_op jit(solution)/shard_map/all_to_all | solution.py:168
  16.3 0.7 copy-start.16
  16.3 1.0 copy-start.14
  17.3 0.7 copy-start.17
  18.2 43.9 %copy-start.3 = (f32[256,256]{0,1:T(8,128)}, f32[256,256]{0,1:T(8,128)S(1)}, u32[]{:S(2)}) copy-start(f32[256,256]{0,1:T(8,128)S(1)} %bitcast_multiply_fusion.1) | copy-start | bytes 786436
  29.3 15.3 %all-to-all-start.2 = ((f32[16,64,256]{2,1,0:T(8,128)}), f32[16,64,256]{2,1,0:T(8,128)S(1)}, u32[]{:S(2)}, u32[]{:S(2)}) async-start(f32[16,64,256]{2,1,0:T(8,128)} %fusion), calls=%async_computation.2 | async-start | bytes 2097152 | tf_op jit(solution)/shard_map/all_to_all | solution.py:168
  32.8 0.7 copy-start.18
  44.6 14.9 %all-to-all-start.1 = ((f32[16,64,256]{2,1,0:T(8,128)}), f32[16,64,256]{2,1,0:T(8,128)}, u32[]{:S(2)}, u32[]{:S(2)}) async-start(f32[16,64,256]{2,1,0:T(8,128)} %param.19), calls=%async_computation.1 | async-start | bytes 2097152 | tf_op jit(solution)/shard_map/all_to_all | solution.py:168
  50.5 1.4 copy-start.8
  50.5 0.7 copy-start.15
  52.7 19.1 %collective-permute-start = (f32[257,256]{1,0:T(8,128)}, f32[257,256]{1,0:T(8,128)}, u32[]{:S(2)}, u32[]{:S(2)}) collective-permute-start(f32[257,256]{1,0:T(8,128)} %pad_maximum_fusion.7), channel_id=1, source_target_pairs={{0,1},{1,2},{2,3},{3,4},{4,5},{5,6},{6,7},{7,8},{8,9},{9,10},{10,1... | collective-permute-start | bytes 789512 | tf_op jit(solution)/shard_map/ppermute | solution.py:13
  60.8 1.2 copy-start.7
  62.0 0.9 copy-start.10
  63.9 7.8 %copy-start.9 = (f32[256,256]{1,0:T(8,128)S(1)}, f32[256,256]{1,0:T(8,128)}, u32[]{:S(2)}) copy-start(f32[256,256]{1,0:T(8,128)} %copy-done.8) | copy-start | bytes 786436
  74.1 9.3 %collective-permute-start.1 = (f32[257,256]{1,0:T(8,128)S(1)}, f32[257,256]{1,0:T(8,128)S(1)}, u32[]{:S(2)}, u32[]{:S(2)}) collective-permute-start(f32[257,256]{1,0:T(8,128)S(1)} %pad_maximum_fusion.8), channel_id=1, source_target_pairs={{0,2},{1,3},{2,4},{3,5},{4,6},{5,7},{6,8},{7,9},{8,10},{9,11},{10,... | collective-permute-start | bytes 789512 | tf_op jit(solution)/shard_map/ppermute | solution.py:13
  77.2 33.6 %copy-start.1 = (f32[4,256,256]{2,1,0:T(8,128)}, f32[4,256,256]{2,1,0:T(8,128)S(1)}, u32[]{:S(2)}) copy-start(f32[4,256,256]{2,1,0:T(8,128)S(1)} %convolution_subtract_fusion) | copy-start | bytes 3145732
  84.2 13.0 %collective-permute-start.2 = (f32[257,256]{1,0:T(8,128)S(1)}, f32[257,256]{1,0:T(8,128)S(1)}, u32[]{:S(2)}, u32[]{:S(2)}) collective-permute-start(f32[257,256]{1,0:T(8,128)S(1)} %pad_maximum_fusion.9), channel_id=1, source_target_pairs={{0,4},{1,5},{2,6},{3,7},{4,8},{5,9},{6,10},{7,11},{8,12},{9,13},{1... | collective-permute-start | bytes 789512 | tf_op jit(solution)/shard_map/ppermute | solution.py:13
  94.6 40.2 %copy-start.5 = (f32[2,256,256]{2,1,0:T(8,128)}, f32[2,256,256]{2,1,0:T(8,128)S(1)}, u32[]{:S(2)}) copy-start(f32[2,256,256]{2,1,0:T(8,128)S(1)} %fusion.15) | copy-start | bytes 1572868
  97.9 10.2 %collective-permute-start.3 = (f32[257,256]{1,0:T(8,128)S(1)}, f32[257,256]{1,0:T(8,128)S(1)}, u32[]{:S(2)}, u32[]{:S(2)}) collective-permute-start(f32[257,256]{1,0:T(8,128)S(1)} %pad_maximum_fusion.10), channel_id=1, source_target_pairs={{0,8},{1,9},{2,10},{3,11},{4,12},{5,13},{6,14},{7,15},{8,16},{9,17... | collective-permute-start | bytes 789512 | tf_op jit(solution)/shard_map/ppermute | solution.py:13
  108.9 10.8 %collective-permute-start.4 = (f32[257,256]{1,0:T(8,128)S(1)}, f32[257,256]{1,0:T(8,128)S(1)}, u32[]{:S(2)}, u32[]{:S(2)}) collective-permute-start(f32[257,256]{1,0:T(8,128)S(1)} %pad_maximum_fusion.11), channel_id=1, source_target_pairs={{0,16},{1,17},{2,18},{3,19},{4,20},{5,21},{6,22},{7,23},{8,24},{9,... | collective-permute-start | bytes 789512 | tf_op jit(solution)/shard_map/ppermute | solution.py:13
  120.5 8.4 %collective-permute-start.5 = (f32[257,256]{1,0:T(8,128)S(1)}, f32[257,256]{1,0:T(8,128)S(1)}, u32[]{:S(2)}, u32[]{:S(2)}) collective-permute-start(f32[257,256]{1,0:T(8,128)S(1)} %pad_maximum_fusion.12), channel_id=1, source_target_pairs={{0,32},{1,33},{2,34},{3,35},{4,36},{5,37},{6,38},{7,39},{8,40},{9,... | collective-permute-start | bytes 789512 | tf_op jit(solution)/shard_map/ppermute | solution.py:13
  129.2 3.4 %collective-permute-start.6 = (f32[256]{0:T(256)S(1)}, f32[256]{0:T(256)S(1)}, u32[]{:S(2)}, u32[]{:S(2)}) collective-permute-start(f32[256]{0:T(256)S(1)} %add_select_fusion.8), channel_id=1, source_target_pairs={{0,64},{1,65},{2,66},{3,67},{4,68},{5,69},{6,70},{7,71},{8,72},{9,... | collective-permute-start | bytes 3080 | tf_op jit(solution)/shard_map/ppermute | solution.py:13
  132.9 6.1 %collective-permute-start.7 = (f32[256]{0:T(256)S(1)}, f32[256]{0:T(256)S(1)}, u32[]{:S(2)}, u32[]{:S(2)}) collective-permute-start(f32[256]{0:T(256)S(1)} %add_select_fusion.7), channel_id=1, source_target_pairs={{0,1},{1,2},{2,3},{3,4},{4,5},{5,6},{6,7},{7,8},{8,9},{9,10},{10,1... | collective-permute-start | bytes 3080 | tf_op jit(solution)/shard_map/ppermute | solution.py:13
  139.6 1.0 copy-start.4
  141.9 1.1 copy-start.6
  143.3 11.6 %collective-permute-start.8 = (f32[513,256]{1,0:T(8,128)S(1)}, f32[513,256]{1,0:T(8,128)}, u32[]{:S(2)}, u32[]{:S(2)}) collective-permute-start(f32[513,256]{1,0:T(8,128)S(1)} %pad_maximum_fusion.1), channel_id=1, source_target_pairs={{1,0},{2,1},{3,2},{4,3},{5,4},{6,5},{7,6},{8,7},{9,8},{10,9},{11,1... | collective-permute-start | bytes 1575944 | tf_op jit(solution)/shard_map/ppermute | solution.py:13
  159.9 17.4 %collective-permute-start.9 = (f32[513,256]{1,0:T(8,128)}, f32[513,256]{1,0:T(8,128)S(1)}, u32[]{:S(2)}, u32[]{:S(2)}) collective-permute-start(f32[513,256]{1,0:T(8,128)} %pad_maximum_fusion.2), channel_id=1, source_target_pairs={{2,0},{3,1},{4,2},{5,3},{6,4},{7,5},{8,6},{9,7},{10,8},{11,9},{12,... | collective-permute-start | bytes 1575944 | tf_op jit(solution)/shard_map/ppermute | solution.py:13
  179.7 15.5 %collective-permute-start.10 = (f32[513,256]{1,0:T(8,128)}, f32[513,256]{1,0:T(8,128)S(1)}, u32[]{:S(2)}, u32[]{:S(2)}) collective-permute-start(f32[513,256]{1,0:T(8,128)} %pad_maximum_fusion.3), channel_id=1, source_target_pairs={{4,0},{5,1},{6,2},{7,3},{8,4},{9,5},{10,6},{11,7},{12,8},{13,9},{1... | collective-permute-start | bytes 1575944 | tf_op jit(solution)/shard_map/ppermute | solution.py:13
  195.2 0.8 copy-start.11
  199.0 15.3 %collective-permute-start.11 = (f32[513,256]{1,0:T(8,128)}, f32[513,256]{1,0:T(8,128)}, u32[]{:S(2)}, u32[]{:S(2)}) collective-permute-start(f32[513,256]{1,0:T(8,128)} %pad_maximum_fusion.4), channel_id=1, source_target_pairs={{8,0},{9,1},{10,2},{11,3},{12,4},{13,5},{14,6},{15,7},{16,8},{17,9... | collective-permute-start | bytes 1575944 | tf_op jit(solution)/shard_map/ppermute | solution.py:13
  219.3 16.6 %collective-permute-start.12 = (f32[513,256]{1,0:T(8,128)}, f32[513,256]{1,0:T(8,128)S(1)}, u32[]{:S(2)}, u32[]{:S(2)}) collective-permute-start(f32[513,256]{1,0:T(8,128)} %pad_maximum_fusion.5), channel_id=1, source_target_pairs={{16,0},{17,1},{18,2},{19,3},{20,4},{21,5},{22,6},{23,7},{24,8},{25... | collective-permute-start | bytes 1575944 | tf_op jit(solution)/shard_map/ppermute | solution.py:13
  235.9 0.8 copy-start.12
  239.7 17.7 %collective-permute-start.13 = (f32[513,256]{1,0:T(8,128)}, f32[513,256]{1,0:T(8,128)}, u32[]{:S(2)}, u32[]{:S(2)}) collective-permute-start(f32[513,256]{1,0:T(8,128)} %pad_maximum_fusion.6), channel_id=1, source_target_pairs={{32,0},{33,1},{34,2},{35,3},{36,4},{37,5},{38,6},{39,7},{40,8},{41... | collective-permute-start | bytes 1575944 | tf_op jit(solution)/shard_map/ppermute | solution.py:13
  260.2 10.9 %collective-permute-start.14 = (f32[257,256]{1,0:T(8,128)S(1)}, f32[257,256]{1,0:T(8,128)S(1)}, u32[]{:S(2)}, u32[]{:S(2)}) collective-permute-start(f32[257,256]{1,0:T(8,128)S(1)} %pad_maximum_fusion.13), channel_id=1, source_target_pairs={{64,0},{65,1},{66,2},{67,3},{68,4},{69,5},{70,6},{71,7},{72,8},{73... | collective-permute-start | bytes 789512 | tf_op jit(solution)/shard_map/ppermute | solution.py:13
  272.3 9.0 %collective-permute-start.15 = (f32[257,256]{1,0:T(8,128)S(1)}, f32[257,256]{1,0:T(8,128)S(1)}, u32[]{:S(2)}, u32[]{:S(2)}) collective-permute-start(f32[257,256]{1,0:T(8,128)S(1)} %pad_maximum_fusion.14), channel_id=1, source_target_pairs={{1,0},{2,1},{3,2},{4,3},{5,4},{6,5},{7,6},{8,7},{9,8},{10,9},{11,1... | collective-permute-start | bytes 789512 | tf_op jit(solution)/shard_map/ppermute | solution.py:13
  281.3 10.5 %copy-start.2 = (f32[4,256,256]{2,1,0:T(8,128)S(1)}, f32[4,256,256]{2,1,0:T(8,128)}, u32[]{:S(2)}) copy-start(f32[4,256,256]{2,1,0:T(8,128)} %copy-done.1) | copy-start | bytes 3145732
  284.1 12.3 %all-to-all-start.4 = ((f32[4,1,256]{2,1,0:T(1,128)}), f32[4,1,256]{2,1,0:T(1,128)S(1)}, u32[]{:S(2)}, u32[]{:S(2)}) async-start(f32[4,1,256]{2,1,0:T(1,128)} %reshape.172), calls=%async_computation.4 | async-start | bytes 8192 | tf_op jit(solution)/shard_map/all_to_all | solution.py:171
  296.4 19.5 %all-to-all-start.5 = ((f32[4,256,256]{2,0,1:T(4,128)}), f32[4,256,256]{2,0,1:T(4,128)S(1)}, u32[]{:S(2)}, u32[]{:S(2)}) async-start(f32[4,256,256]{2,0,1:T(4,128)} %copy.48), calls=%async_computation.5 | async-start | bytes 2097152 | tf_op jit(solution)/shard_map/all_to_all | solution.py:171

commit v4 on v3

--- a/solution.py
+++ b/solution.py
@@ -39,13 +39,20 @@
     return maps[0], shifts[0]
 
 
-def smooth_tree(gains, resids, offsets):
+def smooth_tree(gains, resids):
+    levels = []
     while gains.shape[0] > 1:
         outer, inner = gains[0::2], gains[1::2]
+        levels.append(outer)
         resids = matmul(matmul(outer, resids[1::2]), transpose(outer)) + resids[0::2]
+        gains = matmul(outer, inner)
+    return gains[0], resids[0], levels
+
+
+def offset_tree(levels, offsets):
+    for outer in levels:
         offsets = matvec(outer, offsets[1::2]) + offsets[0::2]
-        gains = matmul(outer, inner)
-    return gains[0], resids[0], offsets[0]
+    return offsets[0]
 
 
 def filter_scan(window_map, window_shift, initial_expectation, tm_index, tm_count):
@@ -69,32 +76,37 @@
     return jnp.where(first_window, initial_expectation, mean_in)
 
 
-def smooth_scan(window_gain, window_resid, window_offset, tm_index, tm_count):
-    width = window_gain.shape[0]
-    gain, resid, offset = window_gain, window_resid, window_offset
+def cov_scan(window_gain, window_resid, tm_index, tm_count):
+    gain, resid = window_gain, window_resid
+    round_gains = []
     distance = 1
     while distance < tm_count:
         has_right = tm_index + distance < tm_count
+        round_gains.append(gain)
         if 2 * distance >= tm_count:
-            arrived = from_behind(jnp.concatenate([resid, offset[None]], axis=0), CHUNKS, -distance)
-            resid_right, offset_right = arrived[:width], arrived[width]
+            resid_right = from_behind(resid, CHUNKS, -distance)
         else:
-            arrived = from_behind(
-                jnp.concatenate([gain, resid, offset[None]], axis=0), CHUNKS, -distance
-            )
-            gain_right = arrived[:width]
-            resid_right = arrived[width : 2 * width]
-            offset_right = arrived[2 * width]
+            arrived = from_behind(jnp.concatenate([gain, resid], axis=0), CHUNKS, -distance)
+            gain_right, resid_right = jnp.split(arrived, 2, axis=0)
         new_resid = matmul(matmul(gain, resid_right), gain.T) + resid
-        offset = jnp.where(has_right, matvec(gain, offset_right) + offset, offset)
         resid = jnp.where(has_right, new_resid, resid)
         if 2 * distance < tm_count:
             gain = jnp.where(has_right, matmul(gain, gain_right), gain)
         distance *= 2
-    arrived = from_behind(jnp.concatenate([resid, offset[None]], axis=0), CHUNKS, -1)
-    last_window = tm_index == tm_count - 1
-    arrived = jnp.where(last_window, jnp.float32(0.0), arrived)
-    return arrived[:width], arrived[width]
+    cov_after = from_behind(resid, CHUNKS, -1)
+    return jnp.where(tm_index == tm_count - 1, jnp.float32(0.0), cov_after), round_gains
+
+
+def offset_scan(window_offset, round_gains, tm_index, tm_count):
+    offset = window_offset
+    distance = 1
+    for gain in round_gains:
+        has_right = tm_index + distance < tm_count
+        offset_right = from_behind(offset, CHUNKS, -distance)
+        offset = jnp.where(has_right, matvec(gain, offset_right) + offset, offset)
+        distance *= 2
+    mean_after = from_behind(offset, CHUNKS, -1)
+    return jnp.where(tm_index == tm_count - 1, jnp.float32(0.0), mean_after)
 
 
 def window_work(
@@ -112,6 +124,12 @@
     final_step = jnp.logical_and(tm_index == tm_count - 1, jnp.arange(step_count) == step_count - 1)
     gain_full = jnp.where(final_step[:, None, None], jnp.float32(0.0), gain_full)
 
+    predicted = matmul(matmul(trans_map, cov_full), trans_map.T) + jnp.diag(process_noise)
+    gain_trans = jnp.swapaxes(gain_full, 1, 2)
+    residual_cov = cov_full - matmul(matmul(gain_full, predicted), gain_trans)
+    window_gain, window_resid, gain_levels = smooth_tree(gain_full, residual_cov)
+    cov_after, round_gains = cov_scan(window_gain, window_resid, tm_index, tm_count)
+
     window_map, window_shift = filter_tree(transition_operators, step_shifts)
     mean_in = filter_scan(window_map, window_shift, initial_expectation, tm_index, tm_count)
 
@@ -121,14 +139,9 @@
         current = matvec(transition_operators[step], current) + step_shifts[step]
         filt_steps.append(current)
     filt_means = jnp.stack(filt_steps)
-    predicted = matmul(matmul(trans_map, cov_full), trans_map.T) + jnp.diag(process_noise)
-    gain_trans = jnp.swapaxes(gain_full, 1, 2)
-    residual_cov = cov_full - matmul(matmul(gain_full, predicted), gain_trans)
     moved_means = jnp.einsum("ij,tj->ti", trans_map, filt_means, precision=highest)
     offsets = filt_means - jnp.einsum("tij,tj->ti", gain_full, moved_means, precision=highest)
-
-    window_gain, window_resid, window_offset = smooth_tree(gain_full, residual_cov, offsets)
-    cov_after, mean_after = smooth_scan(window_gain, window_resid, window_offset, tm_index, tm_count)
+    mean_after = offset_scan(offset_tree(gain_levels, offsets), round_gains, tm_index, tm_count)
 
     cov_steps = [None] * step_count
     mean_steps = [None] * step_count

time: 319 us -> 285 us (0.89)
  waiting for transfers between devices: 159 us -> 109 us
  starting transfers between devices: 76.2 us -> 99.3 us
  matrix products: 46.7 us -> 42.1 us
    ppermute x16 -> x24, waiting for transfers between devices: 126 us -> 79.7 us  [from_behind(): return lax.ppermute(block, axis, route)]
    ppermute x16 -> x24, starting transfers between devices: 52.9 us -> 81.1 us  [from_behind(): return lax.ppermute(block, axis, route)]
    all_to_all x2, starting transfers between devices: 11.9 us -> 6.76 us  [rows_of_steps(): return lax.all_to_all(whole, 'blk', 1, 0, tiled=True)]
    unnamed x44 -> x52, local copies, waits for them, and re-layouts: 8.26 us -> 6.72 us
  transfers between devices with their start and end apart: 21 -> 29, of which waited for: 20 -> 22; matrix products, arithmetic and copies ran while one was open for 8% -> 14% of each run, Pallas kernels for 0% -> 0%
where the time goes in v4:
time: 285 us; the launch traced here: 281 us
  waiting for transfers between devices  109 us (38%)
  starting transfers between devices  99.3 us (35%)
  matrix products  42.1 us (15%)
  local copies, waits for them, and re-layouts  14.3 us (5%)
  blocking collectives  8.97 us (3%)
  other arithmetic  5.26 us (2%)
    ppermute x24, starting transfers between devices, from_behind(): return lax.ppermute(block, axis, route)  81.1 us
    ppermute x24, waiting for transfers between devices, from_behind(): return lax.ppermute(block, axis, route)  79.7 us
    dot_general x48, matrix products, matmul(): return jnp.matmul(left, right, precision=highest)  30.5 us
    all_to_all x3, waiting for transfers between devices, steps_whole(): return lax.all_to_all(rows, 'blk', 0, 1, tiled=True)  17.4 us
    all_to_all x2, waiting for transfers between devices, rows_of_steps(): return lax.all_to_all(whole, 'blk', 1, 0, tiled=True)  12.1 us
    all_to_all x3, starting transfers between devices, steps_whole(): return lax.all_to_all(rows, 'blk', 0, 1, tiled=True)  11.4 us
    all_to_all x1, blocking collectives, steps_whole(): return lax.all_to_all(rows, 'blk', 0, 1, tiled=True)  8.97 us
    dot_general x27, matrix products, matvec(): return jnp.einsum('...ij,...j->...i', left, right, precision=highest)  8.62 us
  transfers between devices with their start and end apart: 29, of which 22 were waited for; matrix products, arithmetic and copies ran while one was open for 14% of the time, Pallas kernels for 0%

profile of v4, /device:TPU:15, one launch (start us, length us, event | category | flops | bytes accessed | tf_op | source)
XLA Modules:
  0.0 281.5 jit_solution(8437689593725085287)
XLA Ops:
  0.6 1.2 copy-done
  1.9 1.7 fusion.74
  3.7 9.0 %all_to_all.107 = f32[4,1,256]{2,1,0:T(1,128)S(1)} all-to-all(f32[4,1,256]{2,1,0:T(1,128)S(1)} %reshape.170), channel_id=1, replica_groups=mesh['tm'=32,'blk'=4] {'blk'}, dimensions={0} | all-to-all | bytes 8192 | tf_op jit(solution)/shard_map/all_to_all | solution.py:181
  12.6 3.6 %all-to-all-start = ((f32[16,64,256]{2,1,0:T(8,128)}), f32[16,64,256]{2,1,0:T(8,128)S(1)}, u32[]{:S(2)}, u32[]{:S(2)}) async-start(f32[16,64,256]{2,1,0:T(8,128)} %param.18), calls=%async_computation | async-start | bytes 2097152 | tf_op jit(solution)/shard_map/all_to_all | solution.py:181
  19.1 2.0 fusion
  21.1 8.2 %all-to-all-done = f32[16,64,256]{2,1,0:T(8,128)S(1)} async-done(((f32[16,64,256]{2,1,0:T(8,128)}), f32[16,64,256]{2,1,0:T(8,128)S(1)}, u32[]{:S(2)}, u32[]{:S(2)}) %all-to-all-start) | async-done | bytes 1048608 | tf_op jit(solution)/shard_map/all_to_all | solution.py:181
  29.3 3.5 %all-to-all-start.2 = ((f32[16,64,256]{2,1,0:T(8,128)}), f32[16,64,256]{2,1,0:T(8,128)S(1)}, u32[]{:S(2)}, u32[]{:S(2)}) async-start(f32[16,64,256]{2,1,0:T(8,128)} %fusion), calls=%async_computation.2 | async-start | bytes 2097152 | tf_op jit(solution)/shard_map/all_to_all | solution.py:181
  37.1 7.5 %all-to-all-done.2 = f32[16,64,256]{2,1,0:T(8,128)S(1)} async-done(((f32[16,64,256]{2,1,0:T(8,128)}), f32[16,64,256]{2,1,0:T(8,128)S(1)}, u32[]{:S(2)}, u32[]{:S(2)}) %all-to-all-start.2) | async-done | bytes 1048608 | tf_op jit(solution)/shard_map/all_to_all | solution.py:181
  44.6 4.2 %all-to-all-start.1 = ((f32[16,64,256]{2,1,0:T(8,128)}), f32[16,64,256]{2,1,0:T(8,128)}, u32[]{:S(2)}, u32[]{:S(2)}) async-start(f32[16,64,256]{2,1,0:T(8,128)} %param.19), calls=%async_computation.1 | async-start | bytes 2097152 | tf_op jit(solution)/shard_map/all_to_all | solution.py:181
  52.6 3.5 %collective-permute-start.6 = (f32[257,256]{1,0:T(8,128)}, f32[257,256]{1,0:T(8,128)}, u32[]{:S(2)}, u32[]{:S(2)}) collective-permute-start(f32[257,256]{1,0:T(8,128)} %pad_maximum_fusion.7), channel_id=1, source_target_pairs={{0,1},{1,2},{2,3},{3,4},{4,5},{5,6},{6,7},{7,8},{8,9},{9,10},{10,1... | collective-permute-start | bytes 789512 | tf_op jit(solution)/shard_map/ppermute | solution.py:13
  56.3 1.5 fusion.15
  57.8 1.7 all-to-all-done.1
  59.5 1.3 copy.38
  62.8 1.1 fusion.91
  64.0 1.2 convolution_subtract_fusion
  68.1 3.7 %collective-permute-done.6 = f32[257,256]{1,0:T(8,128)} collective-permute-done((f32[257,256]{1,0:T(8,128)}, f32[257,256]{1,0:T(8,128)}, u32[]{:S(2)}, u32[]{:S(2)}) %collective-permute-start.6) | collective-permute-done | bytes 263200 | tf_op jit(solution)/shard_map/ppermute | solution.py:13
  72.8 1.3 convolution_select_fusion.5
  74.1 1.9 collective-permute-start.7
  76.1 5.0 %collective-permute-start = (f32[512,256]{1,0:T(8,128)S(1)}, f32[512,256]{1,0:T(8,128)S(1)}, u32[]{:S(2)}, u32[]{:S(2)}) collective-permute-start(f32[512,256]{1,0:T(8,128)S(1)} %pad_maximum_fusion.1), channel_id=1, source_target_pairs={{1,0},{2,1},{3,2},{4,3},{5,4},{6,5},{7,6},{8,7},{9,8},{10,9},{11,1... | collective-permute-start | bytes 1572872 | tf_op jit(solution)/shard_map/ppermute | solution.py:13
  81.2 4.6 %collective-permute-done.7 = f32[257,256]{1,0:T(8,128)S(1)} collective-permute-done((f32[257,256]{1,0:T(8,128)S(1)}, f32[257,256]{1,0:T(8,128)S(1)}, u32[]{:S(2)}, u32[]{:S(2)}) %collective-permute-start.7) | collective-permute-done | bytes 263200 | tf_op jit(solution)/shard_map/ppermute | solution.py:13
  86.6 10.6 %collective-permute-start.8 = (f32[257,256]{1,0:T(8,128)S(1)}, f32[257,256]{1,0:T(8,128)S(1)}, u32[]{:S(2)}, u32[]{:S(2)}) collective-permute-start(f32[257,256]{1,0:T(8,128)S(1)} %pad_maximum_fusion.9), channel_id=1, source_target_pairs={{0,4},{1,5},{2,6},{3,7},{4,8},{5,9},{6,10},{7,11},{8,12},{9,13},{1... | collective-permute-start | bytes 789512 | tf_op jit(solution)/shard_map/ppermute | solution.py:13
  98.1 2.6 collective-permute-done.8
  101.4 1.9 collective-permute-start.9
  103.8 4.1 %collective-permute-start.1 = (f32[512,256]{1,0:T(8,128)S(1)}, f32[512,256]{1,0:T(8,128)S(1)}, u32[]{:S(2)}, u32[]{:S(2)}) collective-permute-start(f32[512,256]{1,0:T(8,128)S(1)} %pad_maximum_fusion.2), channel_id=1, source_target_pairs={{2,0},{3,1},{4,2},{5,3},{6,4},{7,5},{8,6},{9,7},{10,8},{11,9},{12,... | collective-permute-start | bytes 1572872 | tf_op jit(solution)/shard_map/ppermute | solution.py:13
  107.8 3.8 %collective-permute-done.9 = f32[257,256]{1,0:T(8,128)S(1)} collective-permute-done((f32[257,256]{1,0:T(8,128)S(1)}, f32[257,256]{1,0:T(8,128)S(1)}, u32[]{:S(2)}, u32[]{:S(2)}) %collective-permute-start.9) | collective-permute-done | bytes 263200 | tf_op jit(solution)/shard_map/ppermute | solution.py:13
  112.4 2.1 collective-permute-start.10
  114.5 5.0 %collective-permute-done.1 = f32[512,256]{1,0:T(8,128)S(1)} collective-permute-done((f32[512,256]{1,0:T(8,128)S(1)}, f32[512,256]{1,0:T(8,128)S(1)}, u32[]{:S(2)}, u32[]{:S(2)}) %collective-permute-start.1) | collective-permute-done | bytes 524320 | tf_op jit(solution)/shard_map/ppermute | solution.py:13
  120.4 2.8 %collective-permute-done.10 = f32[257,256]{1,0:T(8,128)S(1)} collective-permute-done((f32[257,256]{1,0:T(8,128)S(1)}, f32[257,256]{1,0:T(8,128)S(1)}, u32[]{:S(2)}, u32[]{:S(2)}) %collective-permute-start.10) | collective-permute-done | bytes 263200 | tf_op jit(solution)/shard_map/ppermute | solution.py:13
  124.0 2.8 collective-permute-start.11
  127.2 3.7 %collective-permute-start.2 = (f32[512,256]{1,0:T(8,128)S(1)}, f32[512,256]{1,0:T(8,128)S(1)}, u32[]{:S(2)}, u32[]{:S(2)}) collective-permute-start(f32[512,256]{1,0:T(8,128)S(1)} %pad_maximum_fusion.3), channel_id=1, source_target_pairs={{4,0},{5,1},{6,2},{7,3},{8,4},{9,5},{10,6},{11,7},{12,8},{13,9},{1... | collective-permute-start | bytes 1572872 | tf_op jit(solution)/shard_map/ppermute | solution.py:13
  131.0 1.4 collective-permute-done.11
  132.7 2.8 collective-permute-start.12
  136.5 1.9 collective-permute-start.13
  138.4 2.9 %collective-permute-done.2 = f32[512,256]{1,0:T(8,128)S(1)} collective-permute-done((f32[512,256]{1,0:T(8,128)S(1)}, f32[512,256]{1,0:T(8,128)S(1)}, u32[]{:S(2)}, u32[]{:S(2)}) %collective-permute-start.2) | collective-permute-done | bytes 524320 | tf_op jit(solution)/shard_map/ppermute | solution.py:13
  141.2 1.1 fusion.41
  146.7 3.9 %collective-permute-start.14 = (f32[256]{0:T(256)S(1)}, f32[256]{0:T(256)S(1)}, u32[]{:S(2)}, u32[]{:S(2)}) collective-permute-start(f32[256]{0:T(256)S(1)} %bitcast.370), channel_id=1, source_target_pairs={{1,0},{2,1},{3,2},{4,3},{5,4},{6,5},{7,6},{8,7},{9,8},{10,9},{11,1... | collective-permute-start | bytes 3080 | tf_op jit(solution)/shard_map/ppermute | solution.py:13
  150.6 1.4 fusion.6
  152.3 4.2 %collective-permute-start.15 = (f32[256]{0:T(256)S(1)}, f32[256]{0:T(256)S(1)}, u32[]{:S(2)}, u32[]{:S(2)}) collective-permute-start(f32[256]{0:T(256)S(1)} %add_select_fusion.6), channel_id=1, source_target_pairs={{2,0},{3,1},{4,2},{5,3},{6,4},{7,5},{8,6},{9,7},{10,8},{11,9},{12,... | collective-permute-start | bytes 3080 | tf_op jit(solution)/shard_map/ppermute | solution.py:13
  157.0 4.8 %collective-permute-done.15 = f32[256]{0:T(256)S(1)} collective-permute-done((f32[256]{0:T(256)S(1)}, f32[256]{0:T(256)S(1)}, u32[]{:S(2)}, u32[]{:S(2)}) %collective-permute-start.15) | collective-permute-done | bytes 1056 | tf_op jit(solution)/shard_map/ppermute | solution.py:13
  162.1 3.7 %collective-permute-start.16 = (f32[256]{0:T(256)S(1)}, f32[256]{0:T(256)S(1)}, u32[]{:S(2)}, u32[]{:S(2)}) collective-permute-start(f32[256]{0:T(256)S(1)} %add_select_fusion.5), channel_id=1, source_target_pairs={{4,0},{5,1},{6,2},{7,3},{8,4},{9,5},{10,6},{11,7},{12,8},{13,9},{1... | collective-permute-start | bytes 3080 | tf_op jit(solution)/shard_map/ppermute | solution.py:13
  166.7 1.9 collective-permute-start.3
  168.6 5.9 %collective-permute-done.16 = f32[256]{0:T(256)S(1)} collective-permute-done((f32[256]{0:T(256)S(1)}, f32[256]{0:T(256)S(1)}, u32[]{:S(2)}, u32[]{:S(2)}) %collective-permute-start.16) | collective-permute-done | bytes 1056 | tf_op jit(solution)/shard_map/ppermute | solution.py:13
  174.8 1.9 collective-permute-start.17
  176.8 11.9 %collective-permute-done.17 = f32[256]{0:T(256)S(1)} collective-permute-done((f32[256]{0:T(256)S(1)}, f32[256]{0:T(256)S(1)}, u32[]{:S(2)}, u32[]{:S(2)}) %collective-permute-start.17) | collective-permute-done | bytes 1056 | tf_op jit(solution)/shard_map/ppermute | solution.py:13
  189.0 1.4 fusion.38
  190.8 1.3 convolution_select_fusion.8
  193.0 1.9 collective-permute-start.4
  194.9 3.3 %collective-permute-start.18 = (f32[256]{0:T(256)S(1)}, f32[256]{0:T(256)S(1)}, u32[]{:S(2)}, u32[]{:S(2)}) collective-permute-start(f32[256]{0:T(256)S(1)} %add_select_fusion.3), channel_id=1, source_target_pairs={{16,0},{17,1},{18,2},{19,3},{20,4},{21,5},{22,6},{23,7},{24,8},{25... | collective-permute-start | bytes 3080 | tf_op jit(solution)/shard_map/ppermute | solution.py:13
  198.2 12.2 %collective-permute-done.18 = f32[256]{0:T(256)S(1)} collective-permute-done((f32[256]{0:T(256)S(1)}, f32[256]{0:T(256)S(1)}, u32[]{:S(2)}, u32[]{:S(2)}) %collective-permute-start.18) | collective-permute-done | bytes 1056 | tf_op jit(solution)/shard_map/ppermute | solution.py:13
  210.7 1.9 collective-permute-start.19
  213.9 1.9 collective-permute-start.5
  216.1 1.3 collective-permute-start.20
  217.4 10.2 %collective-permute-done.5 = f32[512,256]{1,0:T(8,128)S(1)} collective-permute-done((f32[512,256]{1,0:T(8,128)S(1)}, f32[512,256]{1,0:T(8,128)S(1)}, u32[]{:S(2)}, u32[]{:S(2)}) %collective-permute-start.5) | collective-permute-done | bytes 524320 | tf_op jit(solution)/shard_map/ppermute | solution.py:13
  228.6 10.1 %collective-permute-start.21 = (f32[256]{0:T(256)S(1)}, f32[256]{0:T(256)S(1)}, u32[]{:S(2)}, u32[]{:S(2)}) collective-permute-start(f32[256]{0:T(256)S(1)} %add_select_fusion), channel_id=1, source_target_pairs={{1,0},{2,1},{3,2},{4,3},{5,4},{6,5},{7,6},{8,7},{9,8},{10,9},{11,1... | collective-permute-start | bytes 3080 | tf_op jit(solution)/shard_map/ppermute | solution.py:13
  239.5 1.6 collective-permute-start.22
  242.4 5.8 %collective-permute-done.22 = f32[256,256]{1,0:T(8,128)S(1)} collective-permute-done((f32[256,256]{1,0:T(8,128)S(1)}, f32[256,256]{1,0:T(8,128)S(1)}, u32[]{:S(2)}, u32[]{:S(2)}) %collective-permute-start.22) | collective-permute-done | bytes 262176 | tf_op jit(solution)/shard_map/ppermute | solution.py:13
  248.6 1.1 fusion.2
  249.7 3.1 %collective-permute-start.23 = (f32[256,256]{1,0:T(8,128)}, f32[256,256]{1,0:T(8,128)S(1)}, u32[]{:S(2)}, u32[]{:S(2)}) collective-permute-start(f32[256,256]{1,0:T(8,128)} %fusion.2), channel_id=1, source_target_pairs={{1,0},{2,1},{3,2},{4,3},{5,4},{6,5},{7,6},{8,7},{9,8},{10,9},{11,1... | collective-permute-start | bytes 786440 | tf_op jit(solution)/shard_map/ppermute | solution.py:13
  253.9 3.2 %all-to-all-start.4 = ((f32[4,1,256]{2,1,0:T(1,128)}), f32[4,1,256]{2,1,0:T(1,128)S(1)}, u32[]{:S(2)}, u32[]{:S(2)}) async-start(f32[4,1,256]{2,1,0:T(1,128)} %reshape.172), calls=%async_computation.4 | async-start | bytes 8192 | tf_op jit(solution)/shard_map/all_to_all | solution.py:184
  257.1 1.3 collective-permute-done.23
  261.8 1.6 copy.48
  263.4 3.5 %all-to-all-start.5 = ((f32[4,256,256]{2,0,1:T(4,128)}), f32[4,256,256]{2,0,1:T(4,128)S(1)}, u32[]{:S(2)}, u32[]{:S(2)}) async-start(f32[4,256,256]{2,0,1:T(4,128)} %copy.48), calls=%async_computation.5 | async-start | bytes 2097152 | tf_op jit(solution)/shard_map/all_to_all | solution.py:184
  268.2 12.1 %all-to-all-done.5 = f32[4,256,256]{2,0,1:T(4,128)S(1)} async-done(((f32[4,256,256]{2,0,1:T(4,128)}), f32[4,256,256]{2,0,1:T(4,128)S(1)}, u32[]{:S(2)}, u32[]{:S(2)}) %all-to-all-start.5) | async-done | bytes 1048608 | tf_op jit(solution)/shard_map/all_to_all | solution.py:184
  280.3 1.2 copy.49
  (207 shorter events, 42.0 us)
Async XLA Ops:
  0.6 1.2 copy-start
  12.6 3.7 %copy-start.17 = (f32[256,256]{1,0:T(8,128)S(1)}, f32[256,256]{1,0:T(8,128)}, u32[]{:S(2)}) copy-start(f32[256,256]{1,0:T(8,128)} %param.10) | copy-start | bytes 786436
  12.6 16.6 %all-to-all-start = ((f32[16,64,256]{2,1,0:T(8,128)}), f32[16,64,256]{2,1,0:T(8,128)S(1)}, u32[]{:S(2)}, u32[]{:S(2)}) async-start(f32[16,64,256]{2,1,0:T(8,128)} %param.18), calls=%async_computation | async-start | bytes 2097152 | tf_op jit(solution)/shard_map/all_to_all | solution.py:181
  16.3 0.7 copy-start.20
  16.3 1.0 copy-start.18
  17.3 0.7 copy-start.21
  18.2 43.6 %copy-start.3 = (f32[256,256]{0,1:T(8,128)}, f32[256,256]{0,1:T(8,128)S(1)}, u32[]{:S(2)}) copy-start(f32[256,256]{0,1:T(8,128)S(1)} %bitcast_multiply_fusion.1) | copy-start | bytes 786436
  29.3 15.3 %all-to-all-start.2 = ((f32[16,64,256]{2,1,0:T(8,128)}), f32[16,64,256]{2,1,0:T(8,128)S(1)}, u32[]{:S(2)}, u32[]{:S(2)}) async-start(f32[16,64,256]{2,1,0:T(8,128)} %fusion), calls=%async_computation.2 | async-start | bytes 2097152 | tf_op jit(solution)/shard_map/all_to_all | solution.py:181
  32.8 0.7 copy-start.22
  44.6 14.9 %all-to-all-start.1 = ((f32[16,64,256]{2,1,0:T(8,128)}), f32[16,64,256]{2,1,0:T(8,128)}, u32[]{:S(2)}, u32[]{:S(2)}) async-start(f32[16,64,256]{2,1,0:T(8,128)} %param.19), calls=%async_computation.1 | async-start | bytes 2097152 | tf_op jit(solution)/shard_map/all_to_all | solution.py:181
  50.1 6.0 %copy-start.7 = (f32[4,4,64,256]{3,2,0,1:T(8,128)S(1)}, f32[4,4,64,256]{3,2,0,1:T(8,128)}, u32[]{:S(2)}) copy-start(f32[4,4,64,256]{3,2,0,1:T(8,128)} %copy.37) | copy-start | bytes 3145732
  50.9 1.8 copy-start.8
  50.9 0.7 copy-start.19
  52.6 19.1 %collective-permute-start.6 = (f32[257,256]{1,0:T(8,128)}, f32[257,256]{1,0:T(8,128)}, u32[]{:S(2)}, u32[]{:S(2)}) collective-permute-start(f32[257,256]{1,0:T(8,128)} %pad_maximum_fusion.7), channel_id=1, source_target_pairs={{0,1},{1,2},{2,3},{3,4},{4,5},{5,6},{6,7},{7,8},{8,9},{9,10},{10,1... | collective-permute-start | bytes 789512 | tf_op jit(solution)/shard_map/ppermute | solution.py:13
  60.8 1.1 copy-start.12
  65.2 1.4 copy-start.1
  65.8 1.0 copy-start.5
  67.7 4.1 %copy-start.9 = (f32[256,256]{1,0:T(8,128)S(1)}, f32[256,256]{1,0:T(8,128)}, u32[]{:S(2)}) copy-start(f32[256,256]{1,0:T(8,128)} %copy-done.8) | copy-start | bytes 786436
  74.1 11.7 %collective-permute-start.7 = (f32[257,256]{1,0:T(8,128)S(1)}, f32[257,256]{1,0:T(8,128)S(1)}, u32[]{:S(2)}, u32[]{:S(2)}) collective-permute-start(f32[257,256]{1,0:T(8,128)S(1)} %pad_maximum_fusion.8), channel_id=1, source_target_pairs={{0,2},{1,3},{2,4},{3,5},{4,6},{5,7},{6,8},{7,9},{8,10},{9,11},{10,... | collective-permute-start | bytes 789512 | tf_op jit(solution)/shard_map/ppermute | solution.py:13
  76.1 21.2 %collective-permute-start = (f32[512,256]{1,0:T(8,128)S(1)}, f32[512,256]{1,0:T(8,128)S(1)}, u32[]{:S(2)}, u32[]{:S(2)}) collective-permute-start(f32[512,256]{1,0:T(8,128)S(1)} %pad_maximum_fusion.1), channel_id=1, source_target_pairs={{1,0},{2,1},{3,2},{4,3},{5,4},{6,5},{7,6},{8,7},{9,8},{10,9},{11,1... | collective-permute-start | bytes 1572872 | tf_op jit(solution)/shard_map/ppermute | solution.py:13
  86.6 14.0 %collective-permute-start.8 = (f32[257,256]{1,0:T(8,128)S(1)}, f32[257,256]{1,0:T(8,128)S(1)}, u32[]{:S(2)}, u32[]{:S(2)}) collective-permute-start(f32[257,256]{1,0:T(8,128)S(1)} %pad_maximum_fusion.9), channel_id=1, source_target_pairs={{0,4},{1,5},{2,6},{3,7},{4,8},{5,9},{6,10},{7,11},{8,12},{9,13},{1... | collective-permute-start | bytes 789512 | tf_op jit(solution)/shard_map/ppermute | solution.py:13
  101.4 10.2 %collective-permute-start.9 = (f32[257,256]{1,0:T(8,128)S(1)}, f32[257,256]{1,0:T(8,128)S(1)}, u32[]{:S(2)}, u32[]{:S(2)}) collective-permute-start(f32[257,256]{1,0:T(8,128)S(1)} %pad_maximum_fusion.10), channel_id=1, source_target_pairs={{0,8},{1,9},{2,10},{3,11},{4,12},{5,13},{6,14},{7,15},{8,16},{9,17... | collective-permute-start | bytes 789512 | tf_op jit(solution)/shard_map/ppermute | solution.py:13
  103.8 15.8 %collective-permute-start.1 = (f32[512,256]{1,0:T(8,128)S(1)}, f32[512,256]{1,0:T(8,128)S(1)}, u32[]{:S(2)}, u32[]{:S(2)}) collective-permute-start(f32[512,256]{1,0:T(8,128)S(1)} %pad_maximum_fusion.2), channel_id=1, source_target_pairs={{2,0},{3,1},{4,2},{5,3},{6,4},{7,5},{8,6},{9,7},{10,8},{11,9},{12,... | collective-permute-start | bytes 1572872 | tf_op jit(solution)/shard_map/ppermute | solution.py:13
  112.4 10.8 %collective-permute-start.10 = (f32[257,256]{1,0:T(8,128)S(1)}, f32[257,256]{1,0:T(8,128)S(1)}, u32[]{:S(2)}, u32[]{:S(2)}) collective-permute-start(f32[257,256]{1,0:T(8,128)S(1)} %pad_maximum_fusion.11), channel_id=1, source_target_pairs={{0,16},{1,17},{2,18},{3,19},{4,20},{5,21},{6,22},{7,23},{8,24},{9,... | collective-permute-start | bytes 789512 | tf_op jit(solution)/shard_map/ppermute | solution.py:13
  120.4 6.8 %copy-start.10 = (f32[256,256]{1,0:T(8,128)}, f32[256,256]{1,0:T(8,128)S(1)}, u32[]{:S(2)}) copy-start(f32[256,256]{1,0:T(8,128)S(1)} %fusion.7) | copy-start | bytes 786436
  124.0 8.4 %collective-permute-start.11 = (f32[257,256]{1,0:T(8,128)S(1)}, f32[257,256]{1,0:T(8,128)S(1)}, u32[]{:S(2)}, u32[]{:S(2)}) collective-permute-start(f32[257,256]{1,0:T(8,128)S(1)} %pad_maximum_fusion.12), channel_id=1, source_target_pairs={{0,32},{1,33},{2,34},{3,35},{4,36},{5,37},{6,38},{7,39},{8,40},{9,... | collective-permute-start | bytes 789512 | tf_op jit(solution)/shard_map/ppermute | solution.py:13
  127.2 14.0 %collective-permute-start.2 = (f32[512,256]{1,0:T(8,128)S(1)}, f32[512,256]{1,0:T(8,128)S(1)}, u32[]{:S(2)}, u32[]{:S(2)}) collective-permute-start(f32[512,256]{1,0:T(8,128)S(1)} %pad_maximum_fusion.3), channel_id=1, source_target_pairs={{4,0},{5,1},{6,2},{7,3},{8,4},{9,5},{10,6},{11,7},{12,8},{13,9},{1... | collective-permute-start | bytes 1572872 | tf_op jit(solution)/shard_map/ppermute | solution.py:13
  132.7 3.5 %collective-permute-start.12 = (f32[256]{0:T(256)S(1)}, f32[256]{0:T(256)S(1)}, u32[]{:S(2)}, u32[]{:S(2)}) collective-permute-start(f32[256]{0:T(256)S(1)} %add_select_fusion.8), channel_id=1, source_target_pairs={{0,64},{1,65},{2,66},{3,67},{4,68},{5,69},{6,70},{7,71},{8,72},{9,... | collective-permute-start | bytes 3080 | tf_op jit(solution)/shard_map/ppermute | solution.py:13
  136.5 6.1 %collective-permute-start.13 = (f32[256]{0:T(256)S(1)}, f32[256]{0:T(256)S(1)}, u32[]{:S(2)}, u32[]{:S(2)}) collective-permute-start(f32[256]{0:T(256)S(1)} %add_select_fusion.7), channel_id=1, source_target_pairs={{0,1},{1,2},{2,3},{3,4},{4,5},{5,6},{6,7},{7,8},{8,9},{9,10},{10,1... | collective-permute-start | bytes 3080 | tf_op jit(solution)/shard_map/ppermute | solution.py:13
  141.2 1.6 copy-start.15
  143.2 1.0 copy-start.4
  145.4 1.1 copy-start.6
  146.0 4.6 %copy-start.11 = (f32[256,256]{1,0:T(8,128)S(1)}, f32[256,256]{1,0:T(8,128)}, u32[]{:S(2)}) copy-start(f32[256,256]{1,0:T(8,128)} %copy-done.10) | copy-start | bytes 786436
  146.7 9.8 %copy-start.16 = (f32[512,256]{1,0:T(8,128)S(1)}, f32[512,256]{1,0:T(8,128)}, u32[]{:S(2)}) copy-start(f32[512,256]{1,0:T(8,128)} %copy-done.15) | copy-start | bytes 1572868
  146.7 5.3 %collective-permute-start.14 = (f32[256]{0:T(256)S(1)}, f32[256]{0:T(256)S(1)}, u32[]{:S(2)}, u32[]{:S(2)}) collective-permute-start(f32[256]{0:T(256)S(1)} %bitcast.370), channel_id=1, source_target_pairs={{1,0},{2,1},{3,2},{4,3},{5,4},{6,5},{7,6},{8,7},{9,8},{10,9},{11,1... | collective-permute-start | bytes 3080 | tf_op jit(solution)/shard_map/ppermute | solution.py:13
  152.3 9.5 %collective-permute-start.15 = (f32[256]{0:T(256)S(1)}, f32[256]{0:T(256)S(1)}, u32[]{:S(2)}, u32[]{:S(2)}) collective-permute-start(f32[256]{0:T(256)S(1)} %add_select_fusion.6), channel_id=1, source_target_pairs={{2,0},{3,1},{4,2},{5,3},{6,4},{7,5},{8,6},{9,7},{10,8},{11,9},{12,... | collective-permute-start | bytes 3080 | tf_op jit(solution)/shard_map/ppermute | solution.py:13
  162.1 12.4 %collective-permute-start.16 = (f32[256]{0:T(256)S(1)}, f32[256]{0:T(256)S(1)}, u32[]{:S(2)}, u32[]{:S(2)}) collective-permute-start(f32[256]{0:T(256)S(1)} %add_select_fusion.5), channel_id=1, source_target_pairs={{4,0},{5,1},{6,2},{7,3},{8,4},{9,5},{10,6},{11,7},{12,8},{13,9},{1... | collective-permute-start | bytes 3080 | tf_op jit(solution)/shard_map/ppermute | solution.py:13
  166.7 22.3 %collective-permute-start.3 = (f32[512,256]{1,0:T(8,128)}, f32[512,256]{1,0:T(8,128)}, u32[]{:S(2)}, u32[]{:S(2)}) collective-permute-start(f32[512,256]{1,0:T(8,128)} %pad_maximum_fusion.4), channel_id=1, source_target_pairs={{8,0},{9,1},{10,2},{11,3},{12,4},{13,5},{14,6},{15,7},{16,8},{17,9... | collective-permute-start | bytes 1572872 | tf_op jit(solution)/shard_map/ppermute | solution.py:13
  174.8 13.9 %collective-permute-start.17 = (f32[256]{0:T(256)S(1)}, f32[256]{0:T(256)S(1)}, u32[]{:S(2)}, u32[]{:S(2)}) collective-permute-start(f32[256]{0:T(256)S(1)} %add_select_fusion.4), channel_id=1, source_target_pairs={{8,0},{9,1},{10,2},{11,3},{12,4},{13,5},{14,6},{15,7},{16,8},{17,9... | collective-permute-start | bytes 3080 | tf_op jit(solution)/shard_map/ppermute | solution.py:13
  193.0 19.7 %collective-permute-start.4 = (f32[512,256]{1,0:T(8,128)}, f32[512,256]{1,0:T(8,128)S(1)}, u32[]{:S(2)}, u32[]{:S(2)}) collective-permute-start(f32[512,256]{1,0:T(8,128)} %pad_maximum_fusion.5), channel_id=1, source_target_pairs={{16,0},{17,1},{18,2},{19,3},{20,4},{21,5},{22,6},{23,7},{24,8},{25... | collective-permute-start | bytes 1572872 | tf_op jit(solution)/shard_map/ppermute | solution.py:13
  194.9 15.5 %collective-permute-start.18 = (f32[256]{0:T(256)S(1)}, f32[256]{0:T(256)S(1)}, u32[]{:S(2)}, u32[]{:S(2)}) collective-permute-start(f32[256]{0:T(256)S(1)} %add_select_fusion.3), channel_id=1, source_target_pairs={{16,0},{17,1},{18,2},{19,3},{20,4},{21,5},{22,6},{23,7},{24,8},{25... | collective-permute-start | bytes 3080 | tf_op jit(solution)/shard_map/ppermute | solution.py:13
  210.7 5.1 %collective-permute-start.19 = (f32[256]{0:T(256)S(1)}, f32[256]{0:T(256)S(1)}, u32[]{:S(2)}, u32[]{:S(2)}) collective-permute-start(f32[256]{0:T(256)S(1)} %add_select_fusion.2), channel_id=1, source_target_pairs={{32,0},{33,1},{34,2},{35,3},{36,4},{37,5},{38,6},{39,7},{40,8},{41... | collective-permute-start | bytes 3080 | tf_op jit(solution)/shard_map/ppermute | solution.py:13
  213.9 13.8 %collective-permute-start.5 = (f32[512,256]{1,0:T(8,128)S(1)}, f32[512,256]{1,0:T(8,128)S(1)}, u32[]{:S(2)}, u32[]{:S(2)}) collective-permute-start(f32[512,256]{1,0:T(8,128)S(1)} %pad_maximum_fusion.6), channel_id=1, source_target_pairs={{32,0},{33,1},{34,2},{35,3},{36,4},{37,5},{38,6},{39,7},{40,8},{41... | collective-permute-start | bytes 1572872 | tf_op jit(solution)/shard_map/ppermute | solution.py:13
  216.1 12.1 %collective-permute-start.20 = (f32[256]{0:T(256)S(1)}, f32[256]{0:T(256)S(1)}, u32[]{:S(2)}, u32[]{:S(2)}) collective-permute-start(f32[256]{0:T(256)S(1)} %add_select_fusion.1), channel_id=1, source_target_pairs={{64,0},{65,1},{66,2},{67,3},{68,4},{69,5},{70,6},{71,7},{72,8},{73... | collective-permute-start | bytes 3080 | tf_op jit(solution)/shard_map/ppermute | solution.py:13
  228.6 12.5 %collective-permute-start.21 = (f32[256]{0:T(256)S(1)}, f32[256]{0:T(256)S(1)}, u32[]{:S(2)}, u32[]{:S(2)}) collective-permute-start(f32[256]{0:T(256)S(1)} %add_select_fusion), channel_id=1, source_target_pairs={{1,0},{2,1},{3,2},{4,3},{5,4},{6,5},{7,6},{8,7},{9,8},{10,9},{11,1... | collective-permute-start | bytes 3080 | tf_op jit(solution)/shard_map/ppermute | solution.py:13
  239.5 2.2 copy-start.13
  239.5 8.6 %collective-permute-start.22 = (f32[256,256]{1,0:T(8,128)S(1)}, f32[256,256]{1,0:T(8,128)S(1)}, u32[]{:S(2)}, u32[]{:S(2)}) collective-permute-start(f32[256,256]{1,0:T(8,128)S(1)} %fusion.3), channel_id=1, source_target_pairs={{64,0},{65,1},{66,2},{67,3},{68,4},{69,5},{70,6},{71,7},{72,8},{73... | collective-permute-start | bytes 786440 | tf_op jit(solution)/shard_map/ppermute | solution.py:13
  242.4 6.2 %copy-start.14 = (f32[256,256]{1,0:T(8,128)S(1)}, f32[256,256]{1,0:T(8,128)}, u32[]{:S(2)}) copy-start(f32[256,256]{1,0:T(8,128)} %copy-done.13) | copy-start | bytes 786436
  248.6 10.3 %copy-start.2 = (f32[4,256,256]{2,1,0:T(8,128)S(1)}, f32[4,256,256]{2,1,0:T(8,128)}, u32[]{:S(2)}) copy-start(f32[4,256,256]{2,1,0:T(8,128)} %copy-done.1) | copy-start | bytes 3145732
  249.7 8.7 %collective-permute-start.23 = (f32[256,256]{1,0:T(8,128)}, f32[256,256]{1,0:T(8,128)S(1)}, u32[]{:S(2)}, u32[]{:S(2)}) collective-permute-start(f32[256,256]{1,0:T(8,128)} %fusion.2), channel_id=1, source_target_pairs={{1,0},{2,1},{3,2},{4,3},{5,4},{6,5},{7,6},{8,7},{9,8},{10,9},{11,1... | collective-permute-start | bytes 786440 | tf_op jit(solution)/shard_map/ppermute | solution.py:13
  253.9 9.5 %all-to-all-start.4 = ((f32[4,1,256]{2,1,0:T(1,128)}), f32[4,1,256]{2,1,0:T(1,128)S(1)}, u32[]{:S(2)}, u32[]{:S(2)}) async-start(f32[4,1,256]{2,1,0:T(1,128)} %reshape.172), calls=%async_computation.4 | async-start | bytes 8192 | tf_op jit(solution)/shard_map/all_to_all | solution.py:184
  263.4 16.9 %all-to-all-start.5 = ((f32[4,256,256]{2,0,1:T(4,128)}), f32[4,256,256]{2,0,1:T(4,128)S(1)}, u32[]{:S(2)}, u32[]{:S(2)}) async-start(f32[4,256,256]{2,0,1:T(4,128)} %copy.48), calls=%async_computation.5 | async-start | bytes 2097152 | tf_op jit(solution)/shard_map/all_to_all | solution.py:184

commit v5 on v4

--- a/solution.py
+++ b/solution.py
@@ -80,20 +80,24 @@
     gain, resid = window_gain, window_resid
     round_gains = []
     distance = 1
-    while distance < tm_count:
+    while 2 * distance < tm_count:
         has_right = tm_index + distance < tm_count
         round_gains.append(gain)
-        if 2 * distance >= tm_count:
-            resid_right = from_behind(resid, CHUNKS, -distance)
-        else:
-            arrived = from_behind(jnp.concatenate([gain, resid], axis=0), CHUNKS, -distance)
-            gain_right, resid_right = jnp.split(arrived, 2, axis=0)
+        arrived = from_behind(jnp.concatenate([gain, resid], axis=0), CHUNKS, -distance)
+        gain_right, resid_right = jnp.split(arrived, 2, axis=0)
         new_resid = matmul(matmul(gain, resid_right), gain.T) + resid
         resid = jnp.where(has_right, new_resid, resid)
-        if 2 * distance < tm_count:
-            gain = jnp.where(has_right, matmul(gain, gain_right), gain)
+        gain = jnp.where(has_right, matmul(gain, gain_right), gain)
         distance *= 2
-    cov_after = from_behind(resid, CHUNKS, -1)
+    round_gains.append(gain)
+    gain_next, resid_next = jnp.split(
+        from_behind(jnp.concatenate([gain, resid], axis=0), CHUNKS, -1), 2, axis=0
+    )
+    resid_far = from_behind(resid, CHUNKS, -(distance + 1))
+    has_far = tm_index + distance + 1 < tm_count
+    cov_after = jnp.where(
+        has_far, matmul(matmul(gain_next, resid_far), gain_next.T) + resid_next, resid_next
+    )
     return jnp.where(tm_index == tm_count - 1, jnp.float32(0.0), cov_after), round_gains
 
 

time: 285 us -> 287 us (level)
  transfers between devices with their start and end apart: 29 -> 29, of which waited for: 22 -> 22; matrix products, arithmetic and copies ran while one was open for 14% -> 15% of each run, Pallas kernels for 0% -> 0%
where the time goes in v5:
time: 287 us; the launch traced here: 281 us
  waiting for transfers between devices  110 us (38%)
  starting transfers between devices  98.2 us (34%)
  matrix products  40.3 us (14%)
  local copies, waits for them, and re-layouts  15.7 us (5%)
  blocking collectives  8.97 us (3%)
  other arithmetic  5.3 us (2%)
    ppermute x24, waiting for transfers between devices, from_behind(): return lax.ppermute(block, axis, route)  81.1 us
    ppermute x24, starting transfers between devices, from_behind(): return lax.ppermute(block, axis, route)  80 us
    dot_general x48, matrix products, matmul(): return jnp.matmul(left, right, precision=highest)  28.8 us
    all_to_all x3, waiting for transfers between devices, steps_whole(): return lax.all_to_all(rows, 'blk', 0, 1, tiled=True)  17.4 us
    all_to_all x2, waiting for transfers between devices, rows_of_steps(): return lax.all_to_all(whole, 'blk', 1, 0, tiled=True)  12 us
    all_to_all x3, starting transfers between devices, steps_whole(): return lax.all_to_all(rows, 'blk', 0, 1, tiled=True)  11.4 us
    all_to_all x1, blocking collectives, steps_whole(): return lax.all_to_all(rows, 'blk', 0, 1, tiled=True)  8.97 us
    dot_general x27, matrix products, matvec(): return jnp.einsum('...ij,...j->...i', left, right, precision=highest)  8.59 us
  transfers between devices with their start and end apart: 29, of which 22 were waited for; matrix products, arithmetic and copies ran while one was open for 15% of the time, Pallas kernels for 0%

profile of v5, /device:TPU:15, one launch (start us, length us, event | category | flops | bytes accessed | tf_op | source)
XLA Modules:
  0.0 281.4 jit_solution(7863760656114669106)
XLA Ops:
  0.6 1.2 copy-done
  1.9 1.7 fusion.75
  3.7 9.0 %all_to_all.107 = f32[4,1,256]{2,1,0:T(1,128)S(1)} all-to-all(f32[4,1,256]{2,1,0:T(1,128)S(1)} %reshape.170), channel_id=1, replica_groups=mesh['tm'=32,'blk'=4] {'blk'}, dimensions={0} | all-to-all | bytes 8192 | tf_op jit(solution)/shard_map/all_to_all | solution.py:185
  12.6 3.6 %all-to-all-start = ((f32[16,64,256]{2,1,0:T(8,128)}), f32[16,64,256]{2,1,0:T(8,128)S(1)}, u32[]{:S(2)}, u32[]{:S(2)}) async-start(f32[16,64,256]{2,1,0:T(8,128)} %param.18), calls=%async_computation | async-start | bytes 2097152 | tf_op jit(solution)/shard_map/all_to_all | solution.py:185
  19.1 2.0 fusion
  21.1 8.2 %all-to-all-done = f32[16,64,256]{2,1,0:T(8,128)S(1)} async-done(((f32[16,64,256]{2,1,0:T(8,128)}), f32[16,64,256]{2,1,0:T(8,128)S(1)}, u32[]{:S(2)}, u32[]{:S(2)}) %all-to-all-start) | async-done | bytes 1048608 | tf_op jit(solution)/shard_map/all_to_all | solution.py:185
  29.3 3.5 %all-to-all-start.2 = ((f32[16,64,256]{2,1,0:T(8,128)}), f32[16,64,256]{2,1,0:T(8,128)S(1)}, u32[]{:S(2)}, u32[]{:S(2)}) async-start(f32[16,64,256]{2,1,0:T(8,128)} %fusion), calls=%async_computation.2 | async-start | bytes 2097152 | tf_op jit(solution)/shard_map/all_to_all | solution.py:185
  36.0 1.1 copy.37
  37.1 7.5 %all-to-all-done.2 = f32[16,64,256]{2,1,0:T(8,128)S(1)} async-done(((f32[16,64,256]{2,1,0:T(8,128)}), f32[16,64,256]{2,1,0:T(8,128)S(1)}, u32[]{:S(2)}, u32[]{:S(2)}) %all-to-all-start.2) | async-done | bytes 1048608 | tf_op jit(solution)/shard_map/all_to_all | solution.py:185
  44.6 4.2 %all-to-all-start.1 = ((f32[16,64,256]{2,1,0:T(8,128)}), f32[16,64,256]{2,1,0:T(8,128)}, u32[]{:S(2)}, u32[]{:S(2)}) async-start(f32[16,64,256]{2,1,0:T(8,128)} %param.19), calls=%async_computation.1 | async-start | bytes 2097152 | tf_op jit(solution)/shard_map/all_to_all | solution.py:185
  52.6 3.5 %collective-permute-start.6 = (f32[257,256]{1,0:T(8,128)}, f32[257,256]{1,0:T(8,128)}, u32[]{:S(2)}, u32[]{:S(2)}) collective-permute-start(f32[257,256]{1,0:T(8,128)} %pad_maximum_fusion.8), channel_id=1, source_target_pairs={{0,1},{1,2},{2,3},{3,4},{4,5},{5,6},{6,7},{7,8},{8,9},{9,10},{10,1... | collective-permute-start | bytes 789512 | tf_op jit(solution)/shard_map/ppermute | solution.py:13
  56.3 1.5 fusion.16
  57.8 1.7 all-to-all-done.1
  59.5 1.3 copy.38
  60.8 1.0 convolution_bitcast_fusion.1
  62.8 1.1 fusion.91
  64.0 1.2 convolution_subtract_fusion
  68.1 3.7 %collective-permute-done.6 = f32[257,256]{1,0:T(8,128)} collective-permute-done((f32[257,256]{1,0:T(8,128)}, f32[257,256]{1,0:T(8,128)}, u32[]{:S(2)}, u32[]{:S(2)}) %collective-permute-start.6) | collective-permute-done | bytes 263200 | tf_op jit(solution)/shard_map/ppermute | solution.py:13
  72.8 1.3 convolution_select_fusion.5
  74.1 1.9 collective-permute-start.7
  76.1 5.0 %collective-permute-start = (f32[512,256]{1,0:T(8,128)S(1)}, f32[512,256]{1,0:T(8,128)S(1)}, u32[]{:S(2)}, u32[]{:S(2)}) collective-permute-start(f32[512,256]{1,0:T(8,128)S(1)} %pad_maximum_fusion.1), channel_id=1, source_target_pairs={{1,0},{2,1},{3,2},{4,3},{5,4},{6,5},{7,6},{8,7},{9,8},{10,9},{11,1... | collective-permute-start | bytes 1572872 | tf_op jit(solution)/shard_map/ppermute | solution.py:13
  81.2 4.6 %collective-permute-done.7 = f32[257,256]{1,0:T(8,128)S(1)} collective-permute-done((f32[257,256]{1,0:T(8,128)S(1)}, f32[257,256]{1,0:T(8,128)S(1)}, u32[]{:S(2)}, u32[]{:S(2)}) %collective-permute-start.7) | collective-permute-done | bytes 263200 | tf_op jit(solution)/shard_map/ppermute | solution.py:13
  86.6 10.6 %collective-permute-start.8 = (f32[257,256]{1,0:T(8,128)S(1)}, f32[257,256]{1,0:T(8,128)S(1)}, u32[]{:S(2)}, u32[]{:S(2)}) collective-permute-start(f32[257,256]{1,0:T(8,128)S(1)} %pad_maximum_fusion.10), channel_id=1, source_target_pairs={{0,4},{1,5},{2,6},{3,7},{4,8},{5,9},{6,10},{7,11},{8,12},{9,13},{1... | collective-permute-start | bytes 789512 | tf_op jit(solution)/shard_map/ppermute | solution.py:13
  98.1 2.6 collective-permute-done.8
  101.4 1.9 collective-permute-start.9
  103.8 4.1 %collective-permute-start.1 = (f32[512,256]{1,0:T(8,128)S(1)}, f32[512,256]{1,0:T(8,128)S(1)}, u32[]{:S(2)}, u32[]{:S(2)}) collective-permute-start(f32[512,256]{1,0:T(8,128)S(1)} %pad_maximum_fusion.2), channel_id=1, source_target_pairs={{2,0},{3,1},{4,2},{5,3},{6,4},{7,5},{8,6},{9,7},{10,8},{11,9},{12,... | collective-permute-start | bytes 1572872 | tf_op jit(solution)/shard_map/ppermute | solution.py:13
  107.8 3.8 %collective-permute-done.9 = f32[257,256]{1,0:T(8,128)S(1)} collective-permute-done((f32[257,256]{1,0:T(8,128)S(1)}, f32[257,256]{1,0:T(8,128)S(1)}, u32[]{:S(2)}, u32[]{:S(2)}) %collective-permute-start.9) | collective-permute-done | bytes 263200 | tf_op jit(solution)/shard_map/ppermute | solution.py:13
  112.4 2.1 collective-permute-start.10
  114.5 5.0 %collective-permute-done.1 = f32[512,256]{1,0:T(8,128)S(1)} collective-permute-done((f32[512,256]{1,0:T(8,128)S(1)}, f32[512,256]{1,0:T(8,128)S(1)}, u32[]{:S(2)}, u32[]{:S(2)}) %collective-permute-start.1) | collective-permute-done | bytes 524320 | tf_op jit(solution)/shard_map/ppermute | solution.py:13
  120.4 2.8 %collective-permute-done.10 = f32[257,256]{1,0:T(8,128)S(1)} collective-permute-done((f32[257,256]{1,0:T(8,128)S(1)}, f32[257,256]{1,0:T(8,128)S(1)}, u32[]{:S(2)}, u32[]{:S(2)}) %collective-permute-start.10) | collective-permute-done | bytes 263200 | tf_op jit(solution)/shard_map/ppermute | solution.py:13
  124.0 2.8 collective-permute-start.11
  127.2 3.7 %collective-permute-start.2 = (f32[512,256]{1,0:T(8,128)S(1)}, f32[512,256]{1,0:T(8,128)S(1)}, u32[]{:S(2)}, u32[]{:S(2)}) collective-permute-start(f32[512,256]{1,0:T(8,128)S(1)} %pad_maximum_fusion.3), channel_id=1, source_target_pairs={{4,0},{5,1},{6,2},{7,3},{8,4},{9,5},{10,6},{11,7},{12,8},{13,9},{1... | collective-permute-start | bytes 1572872 | tf_op jit(solution)/shard_map/ppermute | solution.py:13
  131.0 1.4 collective-permute-done.11
  132.7 2.8 collective-permute-start.12
  136.5 1.9 collective-permute-start.13
  138.4 2.9 %collective-permute-done.2 = f32[512,256]{1,0:T(8,128)S(1)} collective-permute-done((f32[512,256]{1,0:T(8,128)S(1)}, f32[512,256]{1,0:T(8,128)S(1)}, u32[]{:S(2)}, u32[]{:S(2)}) %collective-permute-start.2) | collective-permute-done | bytes 524320 | tf_op jit(solution)/shard_map/ppermute | solution.py:13
  141.2 1.1 fusion.42
  144.4 1.0 fusion.77
  146.7 3.9 %collective-permute-start.14 = (f32[256]{0:T(256)S(1)}, f32[256]{0:T(256)S(1)}, u32[]{:S(2)}, u32[]{:S(2)}) collective-permute-start(f32[256]{0:T(256)S(1)} %bitcast.369), channel_id=1, source_target_pairs={{1,0},{2,1},{3,2},{4,3},{5,4},{6,5},{7,6},{8,7},{9,8},{10,9},{11,1... | collective-permute-start | bytes 3080 | tf_op jit(solution)/shard_map/ppermute | solution.py:13
  150.6 1.4 fusion.6
  152.3 4.2 %collective-permute-start.15 = (f32[256]{0:T(256)S(1)}, f32[256]{0:T(256)S(1)}, u32[]{:S(2)}, u32[]{:S(2)}) collective-permute-start(f32[256]{0:T(256)S(1)} %add_select_fusion.6), channel_id=1, source_target_pairs={{2,0},{3,1},{4,2},{5,3},{6,4},{7,5},{8,6},{9,7},{10,8},{11,9},{12,... | collective-permute-start | bytes 3080 | tf_op jit(solution)/shard_map/ppermute | solution.py:13
  157.0 4.8 %collective-permute-done.15 = f32[256]{0:T(256)S(1)} collective-permute-done((f32[256]{0:T(256)S(1)}, f32[256]{0:T(256)S(1)}, u32[]{:S(2)}, u32[]{:S(2)}) %collective-permute-start.15) | collective-permute-done | bytes 1056 | tf_op jit(solution)/shard_map/ppermute | solution.py:13
  162.1 3.7 %collective-permute-start.16 = (f32[256]{0:T(256)S(1)}, f32[256]{0:T(256)S(1)}, u32[]{:S(2)}, u32[]{:S(2)}) collective-permute-start(f32[256]{0:T(256)S(1)} %add_select_fusion.5), channel_id=1, source_target_pairs={{4,0},{5,1},{6,2},{7,3},{8,4},{9,5},{10,6},{11,7},{12,8},{13,9},{1... | collective-permute-start | bytes 3080 | tf_op jit(solution)/shard_map/ppermute | solution.py:13
  166.7 1.9 collective-permute-start.3
  168.6 5.9 %collective-permute-done.16 = f32[256]{0:T(256)S(1)} collective-permute-done((f32[256]{0:T(256)S(1)}, f32[256]{0:T(256)S(1)}, u32[]{:S(2)}, u32[]{:S(2)}) %collective-permute-start.16) | collective-permute-done | bytes 1056 | tf_op jit(solution)/shard_map/ppermute | solution.py:13
  174.8 1.9 collective-permute-start.17
  176.8 11.8 %collective-permute-done.17 = f32[256]{0:T(256)S(1)} collective-permute-done((f32[256]{0:T(256)S(1)}, f32[256]{0:T(256)S(1)}, u32[]{:S(2)}, u32[]{:S(2)}) %collective-permute-start.17) | collective-permute-done | bytes 1056 | tf_op jit(solution)/shard_map/ppermute | solution.py:13
  192.3 1.9 collective-permute-start.4
  194.3 3.3 %collective-permute-start.18 = (f32[256]{0:T(256)S(1)}, f32[256]{0:T(256)S(1)}, u32[]{:S(2)}, u32[]{:S(2)}) collective-permute-start(f32[256]{0:T(256)S(1)} %add_select_fusion.3), channel_id=1, source_target_pairs={{16,0},{17,1},{18,2},{19,3},{20,4},{21,5},{22,6},{23,7},{24,8},{25... | collective-permute-start | bytes 3080 | tf_op jit(solution)/shard_map/ppermute | solution.py:13
  197.6 12.1 %collective-permute-done.18 = f32[256]{0:T(256)S(1)} collective-permute-done((f32[256]{0:T(256)S(1)}, f32[256]{0:T(256)S(1)}, u32[]{:S(2)}, u32[]{:S(2)}) %collective-permute-start.18) | collective-permute-done | bytes 1056 | tf_op jit(solution)/shard_map/ppermute | solution.py:13
  210.0 1.9 collective-permute-start.19
  213.2 1.9 collective-permute-start.5
  215.5 1.3 collective-permute-start.20
  216.8 10.2 %collective-permute-done.5 = f32[512,256]{1,0:T(8,128)S(1)} collective-permute-done((f32[512,256]{1,0:T(8,128)S(1)}, f32[512,256]{1,0:T(8,128)S(1)}, u32[]{:S(2)}, u32[]{:S(2)}) %collective-permute-start.5) | collective-permute-done | bytes 524320 | tf_op jit(solution)/shard_map/ppermute | solution.py:13
  227.9 10.1 %collective-permute-start.21 = (f32[256]{0:T(256)S(1)}, f32[256]{0:T(256)S(1)}, u32[]{:S(2)}, u32[]{:S(2)}) collective-permute-start(f32[256]{0:T(256)S(1)} %add_select_fusion), channel_id=1, source_target_pairs={{1,0},{2,1},{3,2},{4,3},{5,4},{6,5},{7,6},{8,7},{9,8},{10,9},{11,1... | collective-permute-start | bytes 3080 | tf_op jit(solution)/shard_map/ppermute | solution.py:13
  238.9 1.3 collective-permute-start.23
  240.2 2.2 collective-permute-start.22
  244.8 3.2 %all-to-all-start.4 = ((f32[4,1,256]{2,1,0:T(1,128)}), f32[4,1,256]{2,1,0:T(1,128)S(1)}, u32[]{:S(2)}, u32[]{:S(2)}) async-start(f32[4,1,256]{2,1,0:T(1,128)} %reshape.172), calls=%async_computation.4 | async-start | bytes 8192 | tf_op jit(solution)/shard_map/all_to_all | solution.py:188
  248.6 8.1 %collective-permute-done.22 = f32[512,256]{1,0:T(8,128)S(1)} collective-permute-done((f32[512,256]{1,0:T(8,128)S(1)}, f32[512,256]{1,0:T(8,128)S(1)}, u32[]{:S(2)}, u32[]{:S(2)}) %collective-permute-start.22) | collective-permute-done | bytes 524320 | tf_op jit(solution)/shard_map/ppermute | solution.py:13
  256.7 1.3 fusion.61
  261.8 1.6 copy.48
  263.5 3.5 %all-to-all-start.5 = ((f32[4,256,256]{2,0,1:T(4,128)}), f32[4,256,256]{2,0,1:T(4,128)S(1)}, u32[]{:S(2)}, u32[]{:S(2)}) async-start(f32[4,256,256]{2,0,1:T(4,128)} %copy.48), calls=%async_computation.5 | async-start | bytes 2097152 | tf_op jit(solution)/shard_map/all_to_all | solution.py:188
  268.3 12.0 %all-to-all-done.5 = f32[4,256,256]{2,0,1:T(4,128)S(1)} async-done(((f32[4,256,256]{2,0,1:T(4,128)}), f32[4,256,256]{2,0,1:T(4,128)S(1)}, u32[]{:S(2)}, u32[]{:S(2)}) %all-to-all-start.5) | async-done | bytes 1048608 | tf_op jit(solution)/shard_map/all_to_all | solution.py:188
  280.2 1.2 copy.49
  (208 shorter events, 41.7 us)
Async XLA Ops:
  0.6 1.2 copy-start
  12.6 3.7 %copy-start.17 = (f32[256,256]{1,0:T(8,128)S(1)}, f32[256,256]{1,0:T(8,128)}, u32[]{:S(2)}) copy-start(f32[256,256]{1,0:T(8,128)} %param.10) | copy-start | bytes 786436
  12.6 16.6 %all-to-all-start = ((f32[16,64,256]{2,1,0:T(8,128)}), f32[16,64,256]{2,1,0:T(8,128)S(1)}, u32[]{:S(2)}, u32[]{:S(2)}) async-start(f32[16,64,256]{2,1,0:T(8,128)} %param.18), calls=%async_computation | async-start | bytes 2097152 | tf_op jit(solution)/shard_map/all_to_all | solution.py:185
  16.3 0.7 copy-start.20
  16.3 1.0 copy-start.18
  17.3 0.7 copy-start.21
  18.2 43.6 %copy-start.3 = (f32[256,256]{0,1:T(8,128)}, f32[256,256]{0,1:T(8,128)S(1)}, u32[]{:S(2)}) copy-start(f32[256,256]{0,1:T(8,128)S(1)} %bitcast_multiply_fusion.1) | copy-start | bytes 786436
  29.3 15.3 %all-to-all-start.2 = ((f32[16,64,256]{2,1,0:T(8,128)}), f32[16,64,256]{2,1,0:T(8,128)S(1)}, u32[]{:S(2)}, u32[]{:S(2)}) async-start(f32[16,64,256]{2,1,0:T(8,128)} %fusion), calls=%async_computation.2 | async-start | bytes 2097152 | tf_op jit(solution)/shard_map/all_to_all | solution.py:185
  32.8 0.7 copy-start.22
  44.6 14.9 %all-to-all-start.1 = ((f32[16,64,256]{2,1,0:T(8,128)}), f32[16,64,256]{2,1,0:T(8,128)}, u32[]{:S(2)}, u32[]{:S(2)}) async-start(f32[16,64,256]{2,1,0:T(8,128)} %param.19), calls=%async_computation.1 | async-start | bytes 2097152 | tf_op jit(solution)/shard_map/all_to_all | solution.py:185
  50.1 6.0 %copy-start.7 = (f32[4,4,64,256]{3,2,0,1:T(8,128)S(1)}, f32[4,4,64,256]{3,2,0,1:T(8,128)}, u32[]{:S(2)}) copy-start(f32[4,4,64,256]{3,2,0,1:T(8,128)} %copy.37) | copy-start | bytes 3145732
  50.9 1.8 copy-start.8
  50.9 0.7 copy-start.19
  52.6 19.1 %collective-permute-start.6 = (f32[257,256]{1,0:T(8,128)}, f32[257,256]{1,0:T(8,128)}, u32[]{:S(2)}, u32[]{:S(2)}) collective-permute-start(f32[257,256]{1,0:T(8,128)} %pad_maximum_fusion.8), channel_id=1, source_target_pairs={{0,1},{1,2},{2,3},{3,4},{4,5},{5,6},{6,7},{7,8},{8,9},{9,10},{10,1... | collective-permute-start | bytes 789512 | tf_op jit(solution)/shard_map/ppermute | solution.py:13
  60.8 1.1 copy-start.12
  65.2 1.4 copy-start.1
  65.8 1.0 copy-start.5
  67.7 4.1 %copy-start.9 = (f32[256,256]{1,0:T(8,128)S(1)}, f32[256,256]{1,0:T(8,128)}, u32[]{:S(2)}) copy-start(f32[256,256]{1,0:T(8,128)} %copy-done.8) | copy-start | bytes 786436
  74.1 11.7 %collective-permute-start.7 = (f32[257,256]{1,0:T(8,128)S(1)}, f32[257,256]{1,0:T(8,128)S(1)}, u32[]{:S(2)}, u32[]{:S(2)}) collective-permute-start(f32[257,256]{1,0:T(8,128)S(1)} %pad_maximum_fusion.9), channel_id=1, source_target_pairs={{0,2},{1,3},{2,4},{3,5},{4,6},{5,7},{6,8},{7,9},{8,10},{9,11},{10,... | collective-permute-start | bytes 789512 | tf_op jit(solution)/shard_map/ppermute | solution.py:13
  76.1 21.2 %collective-permute-start = (f32[512,256]{1,0:T(8,128)S(1)}, f32[512,256]{1,0:T(8,128)S(1)}, u32[]{:S(2)}, u32[]{:S(2)}) collective-permute-start(f32[512,256]{1,0:T(8,128)S(1)} %pad_maximum_fusion.1), channel_id=1, source_target_pairs={{1,0},{2,1},{3,2},{4,3},{5,4},{6,5},{7,6},{8,7},{9,8},{10,9},{11,1... | collective-permute-start | bytes 1572872 | tf_op jit(solution)/shard_map/ppermute | solution.py:13
  86.6 14.0 %collective-permute-start.8 = (f32[257,256]{1,0:T(8,128)S(1)}, f32[257,256]{1,0:T(8,128)S(1)}, u32[]{:S(2)}, u32[]{:S(2)}) collective-permute-start(f32[257,256]{1,0:T(8,128)S(1)} %pad_maximum_fusion.10), channel_id=1, source_target_pairs={{0,4},{1,5},{2,6},{3,7},{4,8},{5,9},{6,10},{7,11},{8,12},{9,13},{1... | collective-permute-start | bytes 789512 | tf_op jit(solution)/shard_map/ppermute | solution.py:13
  101.4 10.2 %collective-permute-start.9 = (f32[257,256]{1,0:T(8,128)S(1)}, f32[257,256]{1,0:T(8,128)S(1)}, u32[]{:S(2)}, u32[]{:S(2)}) collective-permute-start(f32[257,256]{1,0:T(8,128)S(1)} %pad_maximum_fusion.11), channel_id=1, source_target_pairs={{0,8},{1,9},{2,10},{3,11},{4,12},{5,13},{6,14},{7,15},{8,16},{9,17... | collective-permute-start | bytes 789512 | tf_op jit(solution)/shard_map/ppermute | solution.py:13
  103.8 15.8 %collective-permute-start.1 = (f32[512,256]{1,0:T(8,128)S(1)}, f32[512,256]{1,0:T(8,128)S(1)}, u32[]{:S(2)}, u32[]{:S(2)}) collective-permute-start(f32[512,256]{1,0:T(8,128)S(1)} %pad_maximum_fusion.2), channel_id=1, source_target_pairs={{2,0},{3,1},{4,2},{5,3},{6,4},{7,5},{8,6},{9,7},{10,8},{11,9},{12,... | collective-permute-start | bytes 1572872 | tf_op jit(solution)/shard_map/ppermute | solution.py:13
  112.4 10.8 %collective-permute-start.10 = (f32[257,256]{1,0:T(8,128)S(1)}, f32[257,256]{1,0:T(8,128)S(1)}, u32[]{:S(2)}, u32[]{:S(2)}) collective-permute-start(f32[257,256]{1,0:T(8,128)S(1)} %pad_maximum_fusion.12), channel_id=1, source_target_pairs={{0,16},{1,17},{2,18},{3,19},{4,20},{5,21},{6,22},{7,23},{8,24},{9,... | collective-permute-start | bytes 789512 | tf_op jit(solution)/shard_map/ppermute | solution.py:13
  120.4 6.8 %copy-start.10 = (f32[256,256]{1,0:T(8,128)}, f32[256,256]{1,0:T(8,128)S(1)}, u32[]{:S(2)}) copy-start(f32[256,256]{1,0:T(8,128)S(1)} %fusion.7) | copy-start | bytes 786436
  124.0 8.4 %collective-permute-start.11 = (f32[257,256]{1,0:T(8,128)S(1)}, f32[257,256]{1,0:T(8,128)S(1)}, u32[]{:S(2)}, u32[]{:S(2)}) collective-permute-start(f32[257,256]{1,0:T(8,128)S(1)} %pad_maximum_fusion.13), channel_id=1, source_target_pairs={{0,32},{1,33},{2,34},{3,35},{4,36},{5,37},{6,38},{7,39},{8,40},{9,... | collective-permute-start | bytes 789512 | tf_op jit(solution)/shard_map/ppermute | solution.py:13
  127.2 14.0 %collective-permute-start.2 = (f32[512,256]{1,0:T(8,128)S(1)}, f32[512,256]{1,0:T(8,128)S(1)}, u32[]{:S(2)}, u32[]{:S(2)}) collective-permute-start(f32[512,256]{1,0:T(8,128)S(1)} %pad_maximum_fusion.3), channel_id=1, source_target_pairs={{4,0},{5,1},{6,2},{7,3},{8,4},{9,5},{10,6},{11,7},{12,8},{13,9},{1... | collective-permute-start | bytes 1572872 | tf_op jit(solution)/shard_map/ppermute | solution.py:13
  132.7 3.5 %collective-permute-start.12 = (f32[256]{0:T(256)S(1)}, f32[256]{0:T(256)S(1)}, u32[]{:S(2)}, u32[]{:S(2)}) collective-permute-start(f32[256]{0:T(256)S(1)} %add_select_fusion.8), channel_id=1, source_target_pairs={{0,64},{1,65},{2,66},{3,67},{4,68},{5,69},{6,70},{7,71},{8,72},{9,... | collective-permute-start | bytes 3080 | tf_op jit(solution)/shard_map/ppermute | solution.py:13
  136.5 6.1 %collective-permute-start.13 = (f32[256]{0:T(256)S(1)}, f32[256]{0:T(256)S(1)}, u32[]{:S(2)}, u32[]{:S(2)}) collective-permute-start(f32[256]{0:T(256)S(1)} %add_select_fusion.7), channel_id=1, source_target_pairs={{0,1},{1,2},{2,3},{3,4},{4,5},{5,6},{6,7},{7,8},{8,9},{9,10},{10,1... | collective-permute-start | bytes 3080 | tf_op jit(solution)/shard_map/ppermute | solution.py:13
  141.2 1.6 copy-start.13
  143.2 1.0 copy-start.4
  145.4 1.1 copy-start.6
  146.0 4.6 %copy-start.11 = (f32[256,256]{1,0:T(8,128)S(1)}, f32[256,256]{1,0:T(8,128)}, u32[]{:S(2)}) copy-start(f32[256,256]{1,0:T(8,128)} %copy-done.10) | copy-start | bytes 786436
  146.7 9.8 %copy-start.14 = (f32[512,256]{1,0:T(8,128)S(1)}, f32[512,256]{1,0:T(8,128)}, u32[]{:S(2)}) copy-start(f32[512,256]{1,0:T(8,128)} %copy-done.13) | copy-start | bytes 1572868
  146.7 5.3 %collective-permute-start.14 = (f32[256]{0:T(256)S(1)}, f32[256]{0:T(256)S(1)}, u32[]{:S(2)}, u32[]{:S(2)}) collective-permute-start(f32[256]{0:T(256)S(1)} %bitcast.369), channel_id=1, source_target_pairs={{1,0},{2,1},{3,2},{4,3},{5,4},{6,5},{7,6},{8,7},{9,8},{10,9},{11,1... | collective-permute-start | bytes 3080 | tf_op jit(solution)/shard_map/ppermute | solution.py:13
  152.3 9.5 %collective-permute-start.15 = (f32[256]{0:T(256)S(1)}, f32[256]{0:T(256)S(1)}, u32[]{:S(2)}, u32[]{:S(2)}) collective-permute-start(f32[256]{0:T(256)S(1)} %add_select_fusion.6), channel_id=1, source_target_pairs={{2,0},{3,1},{4,2},{5,3},{6,4},{7,5},{8,6},{9,7},{10,8},{11,9},{12,... | collective-permute-start | bytes 3080 | tf_op jit(solution)/shard_map/ppermute | solution.py:13
  162.1 12.4 %collective-permute-start.16 = (f32[256]{0:T(256)S(1)}, f32[256]{0:T(256)S(1)}, u32[]{:S(2)}, u32[]{:S(2)}) collective-permute-start(f32[256]{0:T(256)S(1)} %add_select_fusion.5), channel_id=1, source_target_pairs={{4,0},{5,1},{6,2},{7,3},{8,4},{9,5},{10,6},{11,7},{12,8},{13,9},{1... | collective-permute-start | bytes 3080 | tf_op jit(solution)/shard_map/ppermute | solution.py:13
  166.7 22.2 %collective-permute-start.3 = (f32[512,256]{1,0:T(8,128)}, f32[512,256]{1,0:T(8,128)S(1)}, u32[]{:S(2)}, u32[]{:S(2)}) collective-permute-start(f32[512,256]{1,0:T(8,128)} %pad_maximum_fusion.4), channel_id=1, source_target_pairs={{8,0},{9,1},{10,2},{11,3},{12,4},{13,5},{14,6},{15,7},{16,8},{17,9... | collective-permute-start | bytes 1572872 | tf_op jit(solution)/shard_map/ppermute | solution.py:13
  174.8 13.8 %collective-permute-start.17 = (f32[256]{0:T(256)S(1)}, f32[256]{0:T(256)S(1)}, u32[]{:S(2)}, u32[]{:S(2)}) collective-permute-start(f32[256]{0:T(256)S(1)} %add_select_fusion.4), channel_id=1, source_target_pairs={{8,0},{9,1},{10,2},{11,3},{12,4},{13,5},{14,6},{15,7},{16,8},{17,9... | collective-permute-start | bytes 3080 | tf_op jit(solution)/shard_map/ppermute | solution.py:13
  188.9 0.8 copy-start.15
  190.1 1.0 copy-start.16
  192.3 19.6 %collective-permute-start.4 = (f32[512,256]{1,0:T(8,128)}, f32[512,256]{1,0:T(8,128)S(1)}, u32[]{:S(2)}, u32[]{:S(2)}) collective-permute-start(f32[512,256]{1,0:T(8,128)} %pad_maximum_fusion.5), channel_id=1, source_target_pairs={{16,0},{17,1},{18,2},{19,3},{20,4},{21,5},{22,6},{23,7},{24,8},{25... | collective-permute-start | bytes 1572872 | tf_op jit(solution)/shard_map/ppermute | solution.py:13
  194.3 15.4 %collective-permute-start.18 = (f32[256]{0:T(256)S(1)}, f32[256]{0:T(256)S(1)}, u32[]{:S(2)}, u32[]{:S(2)}) collective-permute-start(f32[256]{0:T(256)S(1)} %add_select_fusion.3), channel_id=1, source_target_pairs={{16,0},{17,1},{18,2},{19,3},{20,4},{21,5},{22,6},{23,7},{24,8},{25... | collective-permute-start | bytes 3080 | tf_op jit(solution)/shard_map/ppermute | solution.py:13
  210.0 5.1 %collective-permute-start.19 = (f32[256]{0:T(256)S(1)}, f32[256]{0:T(256)S(1)}, u32[]{:S(2)}, u32[]{:S(2)}) collective-permute-start(f32[256]{0:T(256)S(1)} %add_select_fusion.2), channel_id=1, source_target_pairs={{32,0},{33,1},{34,2},{35,3},{36,4},{37,5},{38,6},{39,7},{40,8},{41... | collective-permute-start | bytes 3080 | tf_op jit(solution)/shard_map/ppermute | solution.py:13
  213.2 13.8 %collective-permute-start.5 = (f32[512,256]{1,0:T(8,128)S(1)}, f32[512,256]{1,0:T(8,128)S(1)}, u32[]{:S(2)}, u32[]{:S(2)}) collective-permute-start(f32[512,256]{1,0:T(8,128)S(1)} %pad_maximum_fusion.6), channel_id=1, source_target_pairs={{32,0},{33,1},{34,2},{35,3},{36,4},{37,5},{38,6},{39,7},{40,8},{41... | collective-permute-start | bytes 1572872 | tf_op jit(solution)/shard_map/ppermute | solution.py:13
  215.5 12.1 %collective-permute-start.20 = (f32[256]{0:T(256)S(1)}, f32[256]{0:T(256)S(1)}, u32[]{:S(2)}, u32[]{:S(2)}) collective-permute-start(f32[256]{0:T(256)S(1)} %add_select_fusion.1), channel_id=1, source_target_pairs={{64,0},{65,1},{66,2},{67,3},{68,4},{69,5},{70,6},{71,7},{72,8},{73... | collective-permute-start | bytes 3080 | tf_op jit(solution)/shard_map/ppermute | solution.py:13
  227.9 14.5 %collective-permute-start.21 = (f32[256]{0:T(256)S(1)}, f32[256]{0:T(256)S(1)}, u32[]{:S(2)}, u32[]{:S(2)}) collective-permute-start(f32[256]{0:T(256)S(1)} %add_select_fusion), channel_id=1, source_target_pairs={{1,0},{2,1},{3,2},{4,3},{5,4},{6,5},{7,6},{8,7},{9,8},{10,9},{11,1... | collective-permute-start | bytes 3080 | tf_op jit(solution)/shard_map/ppermute | solution.py:13
  238.9 9.7 %collective-permute-start.23 = (f32[256,256]{1,0:T(8,128)S(1)}, f32[256,256]{1,0:T(8,128)}, u32[]{:S(2)}, u32[]{:S(2)}) collective-permute-start(f32[256,256]{1,0:T(8,128)S(1)} %fusion.3), channel_id=1, source_target_pairs={{65,0},{66,1},{67,2},{68,3},{69,4},{70,5},{71,6},{72,7},{73,8},{74... | collective-permute-start | bytes 786440 | tf_op jit(solution)/shard_map/ppermute | solution.py:13
  240.2 16.5 %collective-permute-start.22 = (f32[512,256]{1,0:T(8,128)S(1)}, f32[512,256]{1,0:T(8,128)S(1)}, u32[]{:S(2)}, u32[]{:S(2)}) collective-permute-start(f32[512,256]{1,0:T(8,128)S(1)} %pad_maximum_fusion.7), channel_id=1, source_target_pairs={{1,0},{2,1},{3,2},{4,3},{5,4},{6,5},{7,6},{8,7},{9,8},{10,9},{11,1... | collective-permute-start | bytes 1572872 | tf_op jit(solution)/shard_map/ppermute | solution.py:13
  244.8 18.6 %all-to-all-start.4 = ((f32[4,1,256]{2,1,0:T(1,128)}), f32[4,1,256]{2,1,0:T(1,128)S(1)}, u32[]{:S(2)}, u32[]{:S(2)}) async-start(f32[4,1,256]{2,1,0:T(1,128)} %reshape.172), calls=%async_computation.4 | async-start | bytes 8192 | tf_op jit(solution)/shard_map/all_to_all | solution.py:188
  248.1 10.8 %copy-start.2 = (f32[4,256,256]{2,1,0:T(8,128)S(1)}, f32[4,256,256]{2,1,0:T(8,128)}, u32[]{:S(2)}) copy-start(f32[4,256,256]{2,1,0:T(8,128)} %copy-done.1) | copy-start | bytes 3145732
  263.5 16.8 %all-to-all-start.5 = ((f32[4,256,256]{2,0,1:T(4,128)}), f32[4,256,256]{2,0,1:T(4,128)S(1)}, u32[]{:S(2)}, u32[]{:S(2)}) async-start(f32[4,256,256]{2,0,1:T(4,128)} %copy.48), calls=%async_computation.5 | async-start | bytes 2097152 | tf_op jit(solution)/shard_map/all_to_all | solution.py:188

commit v6 on v5

--- a/solution.py
+++ b/solution.py
@@ -76,11 +76,10 @@
     return jnp.where(first_window, initial_expectation, mean_in)
 
 
-def cov_scan(window_gain, window_resid, tm_index, tm_count):
-    gain, resid = window_gain, window_resid
+def cov_rounds(gain, resid, tm_index, tm_count, stop):
     round_gains = []
     distance = 1
-    while 2 * distance < tm_count:
+    while distance < stop and 2 * distance < tm_count:
         has_right = tm_index + distance < tm_count
         round_gains.append(gain)
         arrived = from_behind(jnp.concatenate([gain, resid], axis=0), CHUNKS, -distance)
@@ -89,28 +88,49 @@
         resid = jnp.where(has_right, new_resid, resid)
         gain = jnp.where(has_right, matmul(gain, gain_right), gain)
         distance *= 2
-    round_gains.append(gain)
-    gain_next, resid_next = jnp.split(
-        from_behind(jnp.concatenate([gain, resid], axis=0), CHUNKS, -1), 2, axis=0
-    )
-    resid_far = from_behind(resid, CHUNKS, -(distance + 1))
-    has_far = tm_index + distance + 1 < tm_count
-    cov_after = jnp.where(
-        has_far, matmul(matmul(gain_next, resid_far), gain_next.T) + resid_next, resid_next
-    )
-    return jnp.where(tm_index == tm_count - 1, jnp.float32(0.0), cov_after), round_gains
-
-
-def offset_scan(window_offset, round_gains, tm_index, tm_count):
-    offset = window_offset
+    return gain, resid, round_gains, distance
+
+
+def offset_rounds(offset, round_gains, tm_index, tm_count):
     distance = 1
     for gain in round_gains:
         has_right = tm_index + distance < tm_count
         offset_right = from_behind(offset, CHUNKS, -distance)
         offset = jnp.where(has_right, matvec(gain, offset_right) + offset, offset)
         distance *= 2
-    mean_after = from_behind(offset, CHUNKS, -1)
-    return jnp.where(tm_index == tm_count - 1, jnp.float32(0.0), mean_after)
+    return offset
+
+
+def joint_rounds(gain, resid, offset, tm_index, tm_count, distance):
+    width = gain.shape[0]
+    while 2 * distance < tm_count:
+        has_right = tm_index + distance < tm_count
+        arrived = from_behind(
+            jnp.concatenate([gain, resid, offset[None]], axis=0), CHUNKS, -distance
+        )
+        gain_right = arrived[:width]
+        resid_right = arrived[width : 2 * width]
+        offset_right = arrived[2 * width]
+        new_resid = matmul(matmul(gain, resid_right), gain.T) + resid
+        resid = jnp.where(has_right, new_resid, resid)
+        offset = jnp.where(has_right, matvec(gain, offset_right) + offset, offset)
+        gain = jnp.where(has_right, matmul(gain, gain_right), gain)
+        distance *= 2
+    arrived = from_behind(jnp.concatenate([gain, resid, offset[None]], axis=0), CHUNKS, -1)
+    gain_next = arrived[:width]
+    resid_next = arrived[width : 2 * width]
+    offset_next = arrived[2 * width]
+    far = from_behind(jnp.concatenate([resid, offset[None]], axis=0), CHUNKS, -(distance + 1))
+    has_far = tm_index + distance + 1 < tm_count
+    cov_after = jnp.where(
+        has_far, matmul(matmul(gain_next, far[:width]), gain_next.T) + resid_next, resid_next
+    )
+    mean_after = jnp.where(has_far, matvec(gain_next, far[width]) + offset_next, offset_next)
+    last_chunk = tm_index == tm_count - 1
+    return (
+        jnp.where(last_chunk, jnp.float32(0.0), cov_after),
+        jnp.where(last_chunk, jnp.float32(0.0), mean_after),
+    )
 
 
 def window_work(
@@ -132,7 +152,9 @@
     gain_trans = jnp.swapaxes(gain_full, 1, 2)
     residual_cov = cov_full - matmul(matmul(gain_full, predicted), gain_trans)
     window_gain, window_resid, gain_levels = smooth_tree(gain_full, residual_cov)
-    cov_after, round_gains = cov_scan(window_gain, window_resid, tm_index, tm_count)
+    scan_gain, scan_resid, round_gains, distance = cov_rounds(
+        window_gain, window_resid, tm_index, tm_count, 8
+    )
 
     window_map, window_shift = filter_tree(transition_operators, step_shifts)
     mean_in = filter_scan(window_map, window_shift, initial_expectation, tm_index, tm_count)
@@ -145,7 +167,10 @@
     filt_means = jnp.stack(filt_steps)
     moved_means = jnp.einsum("ij,tj->ti", trans_map, filt_means, precision=highest)
     offsets = filt_means - jnp.einsum("tij,tj->ti", gain_full, moved_means, precision=highest)
-    mean_after = offset_scan(offset_tree(gain_levels, offsets), round_gains, tm_index, tm_count)
+    scan_offset = offset_rounds(offset_tree(gain_levels, offsets), round_gains, tm_index, tm_count)
+    cov_after, mean_after = joint_rounds(
+        scan_gain, scan_resid, scan_offset, tm_index, tm_count, distance
+    )
 
     cov_steps = [None] * step_count
     mean_steps = [None] * step_count

time: 287 us -> 293 us (1.021)
  waiting for transfers between devices: 110 us -> 124 us
  starting transfers between devices: 98.2 us -> 89.4 us
  matrix products: 40.3 us -> 43.3 us
    ppermute x24 -> x19, waiting for transfers between devices: 81.1 us -> 93.6 us  [from_behind(): return lax.ppermute(block, axis, route)]
    ppermute x24 -> x19, starting transfers between devices: 80 us -> 67.5 us  [from_behind(): return lax.ppermute(block, axis, route)]
    all_to_all x2, starting transfers between devices: 6.76 us -> 10.5 us  [rows_of_steps(): return lax.all_to_all(whole, 'blk', 1, 0, tiled=True)]
    unnamed x52 -> x50, local copies, waits for them, and re-layouts: 8.15 us -> 7.22 us
  transfers between devices with their start and end apart: 29 -> 24, of which waited for: 22 -> 19; matrix products, arithmetic and copies ran while one was open for 15% -> 13% of each run, Pallas kernels for 0% -> 0%
where the time goes in v6:
time: 293 us; the launch traced here: 290 us
  waiting for transfers between devices  124 us (42%)
  starting transfers between devices  89.4 us (31%)
  matrix products  43.3 us (15%)
  local copies, waits for them, and re-layouts  14.8 us (5%)
  blocking collectives  8.97 us (3%)
  other arithmetic  7.71 us (3%)
    ppermute x19, waiting for transfers between devices, from_behind(): return lax.ppermute(block, axis, route)  93.6 us
    ppermute x19, starting transfers between devices, from_behind(): return lax.ppermute(block, axis, route)  67.5 us
    dot_general x48, matrix products, matmul(): return jnp.matmul(left, right, precision=highest)  31 us
    all_to_all x3, waiting for transfers between devices, steps_whole(): return lax.all_to_all(rows, 'blk', 0, 1, tiled=True)  17.4 us
    all_to_all x2, waiting for transfers between devices, rows_of_steps(): return lax.all_to_all(whole, 'blk', 1, 0, tiled=True)  12.6 us
    all_to_all x3, starting transfers between devices, steps_whole(): return lax.all_to_all(rows, 'blk', 0, 1, tiled=True)  11.4 us
    all_to_all x2, starting transfers between devices, rows_of_steps(): return lax.all_to_all(whole, 'blk', 1, 0, tiled=True)  10.5 us
    dot_general x27, matrix products, matvec(): return jnp.einsum('...ij,...j->...i', left, right, precision=highest)  9.34 us
  transfers between devices with their start and end apart: 24, of which 19 were waited for; matrix products, arithmetic and copies ran while one was open for 13% of the time, Pallas kernels for 0%

profile of v6, /device:TPU:15, one launch (start us, length us, event | category | flops | bytes accessed | tf_op | source)
XLA Modules:
  0.0 290.1 jit_solution(14329631992640404601)
XLA Ops:
  0.6 1.2 copy-done
  1.9 1.7 fusion.78
  3.7 9.0 %all_to_all.107 = f32[4,1,256]{2,1,0:T(1,128)S(1)} all-to-all(f32[4,1,256]{2,1,0:T(1,128)S(1)} %reshape.170), channel_id=1, replica_groups=mesh['tm'=32,'blk'=4] {'blk'}, dimensions={0} | all-to-all | bytes 8192 | tf_op jit(solution)/shard_map/all_to_all | solution.py:210
  12.6 3.6 %all-to-all-start = ((f32[16,64,256]{2,1,0:T(8,128)}), f32[16,64,256]{2,1,0:T(8,128)S(1)}, u32[]{:S(2)}, u32[]{:S(2)}) async-start(f32[16,64,256]{2,1,0:T(8,128)} %param.18), calls=%async_computation | async-start | bytes 2097152 | tf_op jit(solution)/shard_map/all_to_all | solution.py:210
  19.1 2.0 fusion
  21.0 8.2 %all-to-all-done = f32[16,64,256]{2,1,0:T(8,128)S(1)} async-done(((f32[16,64,256]{2,1,0:T(8,128)}), f32[16,64,256]{2,1,0:T(8,128)S(1)}, u32[]{:S(2)}, u32[]{:S(2)}) %all-to-all-start) | async-done | bytes 1048608 | tf_op jit(solution)/shard_map/all_to_all | solution.py:210
  29.3 3.5 %all-to-all-start.2 = ((f32[16,64,256]{2,1,0:T(8,128)}), f32[16,64,256]{2,1,0:T(8,128)S(1)}, u32[]{:S(2)}, u32[]{:S(2)}) async-start(f32[16,64,256]{2,1,0:T(8,128)} %fusion), calls=%async_computation.2 | async-start | bytes 2097152 | tf_op jit(solution)/shard_map/all_to_all | solution.py:210
  36.0 1.1 copy.37
  37.1 7.5 %all-to-all-done.2 = f32[16,64,256]{2,1,0:T(8,128)S(1)} async-done(((f32[16,64,256]{2,1,0:T(8,128)}), f32[16,64,256]{2,1,0:T(8,128)S(1)}, u32[]{:S(2)}, u32[]{:S(2)}) %all-to-all-start.2) | async-done | bytes 1048608 | tf_op jit(solution)/shard_map/all_to_all | solution.py:210
  44.6 4.2 %all-to-all-start.1 = ((f32[16,64,256]{2,1,0:T(8,128)}), f32[16,64,256]{2,1,0:T(8,128)}, u32[]{:S(2)}, u32[]{:S(2)}) async-start(f32[16,64,256]{2,1,0:T(8,128)} %param.19), calls=%async_computation.1 | async-start | bytes 2097152 | tf_op jit(solution)/shard_map/all_to_all | solution.py:210
  52.6 3.5 %collective-permute-start.3 = (f32[257,256]{1,0:T(8,128)}, f32[257,256]{1,0:T(8,128)}, u32[]{:S(2)}, u32[]{:S(2)}) collective-permute-start(f32[257,256]{1,0:T(8,128)} %pad_maximum_fusion.8), channel_id=1, source_target_pairs={{0,1},{1,2},{2,3},{3,4},{4,5},{5,6},{6,7},{7,8},{8,9},{9,10},{10,1... | collective-permute-start | bytes 789512 | tf_op jit(solution)/shard_map/ppermute | solution.py:13
  56.3 1.4 fusion.16
  57.8 1.7 all-to-all-done.1
  59.5 1.3 copy.38
  60.8 1.0 convolution_bitcast_fusion.1
  61.8 1.0 convolution_add_fusion
  62.8 1.1 fusion.98
  64.0 1.2 convolution_subtract_fusion
  67.6 4.1 %collective-permute-done.3 = f32[257,256]{1,0:T(8,128)} collective-permute-done((f32[257,256]{1,0:T(8,128)}, f32[257,256]{1,0:T(8,128)}, u32[]{:S(2)}, u32[]{:S(2)}) %collective-permute-start.3) | collective-permute-done | bytes 263200 | tf_op jit(solution)/shard_map/ppermute | solution.py:13
  71.7 1.0 fusion.93
  72.8 1.3 convolution_select_fusion.8
  74.1 1.9 collective-permute-start.4
  76.5 4.6 %collective-permute-start = (f32[512,256]{1,0:T(8,128)S(1)}, f32[512,256]{1,0:T(8,128)S(1)}, u32[]{:S(2)}, u32[]{:S(2)}) collective-permute-start(f32[512,256]{1,0:T(8,128)S(1)} %pad_maximum_fusion.5), channel_id=1, source_target_pairs={{1,0},{2,1},{3,2},{4,3},{5,4},{6,5},{7,6},{8,7},{9,8},{10,9},{11,1... | collective-permute-start | bytes 1572872 | tf_op jit(solution)/shard_map/ppermute | solution.py:13
  81.1 4.3 %collective-permute-done.4 = f32[257,256]{1,0:T(8,128)S(1)} collective-permute-done((f32[257,256]{1,0:T(8,128)S(1)}, f32[257,256]{1,0:T(8,128)S(1)}, u32[]{:S(2)}, u32[]{:S(2)}) %collective-permute-start.4) | collective-permute-done | bytes 263200 | tf_op jit(solution)/shard_map/ppermute | solution.py:13
  86.2 10.6 %collective-permute-start.5 = (f32[257,256]{1,0:T(8,128)S(1)}, f32[257,256]{1,0:T(8,128)S(1)}, u32[]{:S(2)}, u32[]{:S(2)}) collective-permute-start(f32[257,256]{1,0:T(8,128)S(1)} %pad_maximum_fusion.10), channel_id=1, source_target_pairs={{0,4},{1,5},{2,6},{3,7},{4,8},{5,9},{6,10},{7,11},{8,12},{9,13},{1... | collective-permute-start | bytes 789512 | tf_op jit(solution)/shard_map/ppermute | solution.py:13
  97.6 2.6 collective-permute-done.5
  101.0 1.9 collective-permute-start.6
  103.3 4.1 %collective-permute-start.1 = (f32[512,256]{1,0:T(8,128)S(1)}, f32[512,256]{1,0:T(8,128)S(1)}, u32[]{:S(2)}, u32[]{:S(2)}) collective-permute-start(f32[512,256]{1,0:T(8,128)S(1)} %pad_maximum_fusion.6), channel_id=1, source_target_pairs={{2,0},{3,1},{4,2},{5,3},{6,4},{7,5},{8,6},{9,7},{10,8},{11,9},{12,... | collective-permute-start | bytes 1572872 | tf_op jit(solution)/shard_map/ppermute | solution.py:13
  107.4 3.8 %collective-permute-done.6 = f32[257,256]{1,0:T(8,128)S(1)} collective-permute-done((f32[257,256]{1,0:T(8,128)S(1)}, f32[257,256]{1,0:T(8,128)S(1)}, u32[]{:S(2)}, u32[]{:S(2)}) %collective-permute-start.6) | collective-permute-done | bytes 263200 | tf_op jit(solution)/shard_map/ppermute | solution.py:13
  112.0 2.1 collective-permute-start.7
  114.2 4.9 %collective-permute-done.1 = f32[512,256]{1,0:T(8,128)S(1)} collective-permute-done((f32[512,256]{1,0:T(8,128)S(1)}, f32[512,256]{1,0:T(8,128)S(1)}, u32[]{:S(2)}, u32[]{:S(2)}) %collective-permute-start.1) | collective-permute-done | bytes 524320 | tf_op jit(solution)/shard_map/ppermute | solution.py:13
  119.5 3.3 %collective-permute-done.7 = f32[257,256]{1,0:T(8,128)S(1)} collective-permute-done((f32[257,256]{1,0:T(8,128)S(1)}, f32[257,256]{1,0:T(8,128)S(1)}, u32[]{:S(2)}, u32[]{:S(2)}) %collective-permute-start.7) | collective-permute-done | bytes 263200 | tf_op jit(solution)/shard_map/ppermute | solution.py:13
  123.6 2.7 collective-permute-start.8
  127.1 4.9 %collective-permute-done.8 = f32[257,256]{1,0:T(8,128)S(1)} collective-permute-done((f32[257,256]{1,0:T(8,128)S(1)}, f32[257,256]{1,0:T(8,128)S(1)}, u32[]{:S(2)}, u32[]{:S(2)}) %collective-permute-start.8) | collective-permute-done | bytes 263200 | tf_op jit(solution)/shard_map/ppermute | solution.py:13
  132.3 2.6 collective-permute-start.9
  135.9 1.9 collective-permute-start.10
  138.7 5.0 %collective-permute-start.2 = (f32[512,256]{1,0:T(8,128)}, f32[512,256]{1,0:T(8,128)}, u32[]{:S(2)}, u32[]{:S(2)}) collective-permute-start(f32[512,256]{1,0:T(8,128)} %pad_maximum_fusion.7), channel_id=1, source_target_pairs={{4,0},{5,1},{6,2},{7,3},{8,4},{9,5},{10,6},{11,7},{12,8},{13,9},{1... | collective-permute-start | bytes 1572872 | tf_op jit(solution)/shard_map/ppermute | solution.py:13
  145.5 1.0 fusion.80
  147.9 6.0 %collective-permute-start.11 = (f32[256]{0:T(256)S(1)}, f32[256]{0:T(256)S(1)}, u32[]{:S(2)}, u32[]{:S(2)}) collective-permute-start(f32[256]{0:T(256)S(1)} %bitcast.384), channel_id=1, source_target_pairs={{1,0},{2,1},{3,2},{4,3},{5,4},{6,5},{7,6},{8,7},{9,8},{10,9},{11,1... | collective-permute-start | bytes 3080 | tf_op jit(solution)/shard_map/ppermute | solution.py:13
  153.8 4.4 %collective-permute-done.2 = f32[512,256]{1,0:T(8,128)} collective-permute-done((f32[512,256]{1,0:T(8,128)}, f32[512,256]{1,0:T(8,128)}, u32[]{:S(2)}, u32[]{:S(2)}) %collective-permute-start.2) | collective-permute-done | bytes 524320 | tf_op jit(solution)/shard_map/ppermute | solution.py:13
  158.2 1.3 fusion.44
  159.9 2.1 collective-permute-start.12
  162.4 3.5 %collective-permute-done.12 = f32[256]{0:T(256)S(1)} collective-permute-done((f32[256]{0:T(256)S(1)}, f32[256]{0:T(256)S(1)}, u32[]{:S(2)}, u32[]{:S(2)}) %collective-permute-start.12) | collective-permute-done | bytes 1056 | tf_op jit(solution)/shard_map/ppermute | solution.py:13
  166.2 1.9 collective-permute-start.13
  168.1 1.3 convolution_select_fusion.9
  169.5 4.6 %collective-permute-done.13 = f32[256]{0:T(256)S(1)} collective-permute-done((f32[256]{0:T(256)S(1)}, f32[256]{0:T(256)S(1)}, u32[]{:S(2)}, u32[]{:S(2)}) %collective-permute-start.13) | collective-permute-done | bytes 1056 | tf_op jit(solution)/shard_map/ppermute | solution.py:13
  175.2 1.9 collective-permute-start.14
  177.2 13.0 %collective-permute-done.14 = f32[513,256]{1,0:T(8,128)S(1)} collective-permute-done((f32[513,256]{1,0:T(8,128)}, f32[513,256]{1,0:T(8,128)S(1)}, u32[]{:S(2)}, u32[]{:S(2)}) %collective-permute-start.14) | collective-permute-done | bytes 525344 | tf_op jit(solution)/shard_map/ppermute | solution.py:13
  191.7 1.3 convolution_select_fusion.2
  193.9 1.9 collective-permute-start.15
  195.8 14.4 %collective-permute-done.15 = f32[513,256]{1,0:T(8,128)} collective-permute-done((f32[513,256]{1,0:T(8,128)}, f32[513,256]{1,0:T(8,128)}, u32[]{:S(2)}, u32[]{:S(2)}) %collective-permute-start.15) | collective-permute-done | bytes 525344 | tf_op jit(solution)/shard_map/ppermute | solution.py:13
  210.3 1.0 fusion.86
  211.3 1.3 fusion.31
  213.1 1.3 convolution_select_fusion.1
  215.3 1.9 collective-permute-start.16
  217.2 13.0 %collective-permute-done.16 = f32[513,256]{1,0:T(8,128)S(1)} collective-permute-done((f32[513,256]{1,0:T(8,128)}, f32[513,256]{1,0:T(8,128)S(1)}, u32[]{:S(2)}, u32[]{:S(2)}) %collective-permute-start.16) | collective-permute-done | bytes 525344 | tf_op jit(solution)/shard_map/ppermute | solution.py:13
  231.8 9.4 %collective-permute-start.17 = (f32[513,256]{1,0:T(8,128)S(1)}, f32[513,256]{1,0:T(8,128)S(1)}, u32[]{:S(2)}, u32[]{:S(2)}) collective-permute-start(f32[513,256]{1,0:T(8,128)S(1)} %pad_maximum_fusion.4), channel_id=1, source_target_pairs={{1,0},{2,1},{3,2},{4,3},{5,4},{6,5},{7,6},{8,7},{9,8},{10,9},{11,1... | collective-permute-start | bytes 1575944 | tf_op jit(solution)/shard_map/ppermute | solution.py:13
  241.9 1.5 collective-permute-start.18
  243.5 12.5 %collective-permute-done.17 = f32[513,256]{1,0:T(8,128)S(1)} collective-permute-done((f32[513,256]{1,0:T(8,128)S(1)}, f32[513,256]{1,0:T(8,128)S(1)}, u32[]{:S(2)}, u32[]{:S(2)}) %collective-permute-start.17) | collective-permute-done | bytes 525344 | tf_op jit(solution)/shard_map/ppermute | solution.py:13
  258.7 6.3 %all-to-all-start.4 = ((f32[4,1,256]{2,1,0:T(1,128)}), f32[4,1,256]{2,1,0:T(1,128)S(1)}, u32[]{:S(2)}, u32[]{:S(2)}) async-start(f32[4,1,256]{2,1,0:T(1,128)} %reshape.172), calls=%async_computation.4 | async-start | bytes 8192 | tf_op jit(solution)/shard_map/all_to_all | solution.py:213
  269.2 1.6 copy.48
  270.8 4.2 %all-to-all-start.5 = ((f32[4,256,256]{2,0,1:T(4,128)}), f32[4,256,256]{2,0,1:T(4,128)S(1)}, u32[]{:S(2)}, u32[]{:S(2)}) async-start(f32[4,256,256]{2,0,1:T(4,128)} %copy.48), calls=%async_computation.5 | async-start | bytes 2097152 | tf_op jit(solution)/shard_map/all_to_all | solution.py:213
  276.3 12.6 %all-to-all-done.5 = f32[4,256,256]{2,0,1:T(4,128)S(1)} async-done(((f32[4,256,256]{2,0,1:T(4,128)}), f32[4,256,256]{2,0,1:T(4,128)S(1)}, u32[]{:S(2)}, u32[]{:S(2)}) %all-to-all-start.5) | async-done | bytes 1048608 | tf_op jit(solution)/shard_map/all_to_all | solution.py:213
  288.9 1.2 copy.49
  (197 shorter events, 39.3 us)
Async XLA Ops:
  0.6 1.2 copy-start
  12.6 3.7 %copy-start.16 = (f32[256,256]{1,0:T(8,128)S(1)}, f32[256,256]{1,0:T(8,128)}, u32[]{:S(2)}) copy-start(f32[256,256]{1,0:T(8,128)} %param.10) | copy-start | bytes 786436
  12.6 16.6 %all-to-all-start = ((f32[16,64,256]{2,1,0:T(8,128)}), f32[16,64,256]{2,1,0:T(8,128)S(1)}, u32[]{:S(2)}, u32[]{:S(2)}) async-start(f32[16,64,256]{2,1,0:T(8,128)} %param.18), calls=%async_computation | async-start | bytes 2097152 | tf_op jit(solution)/shard_map/all_to_all | solution.py:210
  16.3 0.7 copy-start.19
  16.3 1.0 copy-start.17
  17.3 0.7 copy-start.20
  18.2 43.6 %copy-start.5 = (f32[256,256]{0,1:T(8,128)}, f32[256,256]{0,1:T(8,128)S(1)}, u32[]{:S(2)}) copy-start(f32[256,256]{0,1:T(8,128)S(1)} %bitcast_multiply_fusion.1) | copy-start | bytes 786436
  29.3 15.3 %all-to-all-start.2 = ((f32[16,64,256]{2,1,0:T(8,128)}), f32[16,64,256]{2,1,0:T(8,128)S(1)}, u32[]{:S(2)}, u32[]{:S(2)}) async-start(f32[16,64,256]{2,1,0:T(8,128)} %fusion), calls=%async_computation.2 | async-start | bytes 2097152 | tf_op jit(solution)/shard_map/all_to_all | solution.py:210
  32.8 0.7 copy-start.21
  44.6 14.9 %all-to-all-start.1 = ((f32[16,64,256]{2,1,0:T(8,128)}), f32[16,64,256]{2,1,0:T(8,128)}, u32[]{:S(2)}, u32[]{:S(2)}) async-start(f32[16,64,256]{2,1,0:T(8,128)} %param.19), calls=%async_computation.1 | async-start | bytes 2097152 | tf_op jit(solution)/shard_map/all_to_all | solution.py:210
  50.1 6.0 %copy-start.9 = (f32[4,4,64,256]{3,2,0,1:T(8,128)S(1)}, f32[4,4,64,256]{3,2,0,1:T(8,128)}, u32[]{:S(2)}) copy-start(f32[4,4,64,256]{3,2,0,1:T(8,128)} %copy.37) | copy-start | bytes 3145732
  50.9 1.8 copy-start.10
  50.9 0.7 copy-start.18
  52.6 19.1 %collective-permute-start.3 = (f32[257,256]{1,0:T(8,128)}, f32[257,256]{1,0:T(8,128)}, u32[]{:S(2)}, u32[]{:S(2)}) collective-permute-start(f32[257,256]{1,0:T(8,128)} %pad_maximum_fusion.8), channel_id=1, source_target_pairs={{0,1},{1,2},{2,3},{3,4},{4,5},{5,6},{6,7},{7,8},{8,9},{9,10},{10,1... | collective-permute-start | bytes 789512 | tf_op jit(solution)/shard_map/ppermute | solution.py:13
  60.8 1.1 copy-start.14
  65.1 1.4 copy-start.1
  65.8 1.0 copy-start.7
  67.2 4.5 %copy-start.11 = (f32[256,256]{1,0:T(8,128)S(1)}, f32[256,256]{1,0:T(8,128)}, u32[]{:S(2)}) copy-start(f32[256,256]{1,0:T(8,128)} %copy-done.10) | copy-start | bytes 786436
  74.1 11.3 %collective-permute-start.4 = (f32[257,256]{1,0:T(8,128)S(1)}, f32[257,256]{1,0:T(8,128)S(1)}, u32[]{:S(2)}, u32[]{:S(2)}) collective-permute-start(f32[257,256]{1,0:T(8,128)S(1)} %pad_maximum_fusion.9), channel_id=1, source_target_pairs={{0,2},{1,3},{2,4},{3,5},{4,6},{5,7},{6,8},{7,9},{8,10},{9,11},{10,... | collective-permute-start | bytes 789512 | tf_op jit(solution)/shard_map/ppermute | solution.py:13
  76.5 20.3 %collective-permute-start = (f32[512,256]{1,0:T(8,128)S(1)}, f32[512,256]{1,0:T(8,128)S(1)}, u32[]{:S(2)}, u32[]{:S(2)}) collective-permute-start(f32[512,256]{1,0:T(8,128)S(1)} %pad_maximum_fusion.5), channel_id=1, source_target_pairs={{1,0},{2,1},{3,2},{4,3},{5,4},{6,5},{7,6},{8,7},{9,8},{10,9},{11,1... | collective-permute-start | bytes 1572872 | tf_op jit(solution)/shard_map/ppermute | solution.py:13
  86.2 14.0 %collective-permute-start.5 = (f32[257,256]{1,0:T(8,128)S(1)}, f32[257,256]{1,0:T(8,128)S(1)}, u32[]{:S(2)}, u32[]{:S(2)}) collective-permute-start(f32[257,256]{1,0:T(8,128)S(1)} %pad_maximum_fusion.10), channel_id=1, source_target_pairs={{0,4},{1,5},{2,6},{3,7},{4,8},{5,9},{6,10},{7,11},{8,12},{9,13},{1... | collective-permute-start | bytes 789512 | tf_op jit(solution)/shard_map/ppermute | solution.py:13
  101.0 10.3 %collective-permute-start.6 = (f32[257,256]{1,0:T(8,128)S(1)}, f32[257,256]{1,0:T(8,128)S(1)}, u32[]{:S(2)}, u32[]{:S(2)}) collective-permute-start(f32[257,256]{1,0:T(8,128)S(1)} %pad_maximum_fusion.11), channel_id=1, source_target_pairs={{0,8},{1,9},{2,10},{3,11},{4,12},{5,13},{6,14},{7,15},{8,16},{9,17... | collective-permute-start | bytes 789512 | tf_op jit(solution)/shard_map/ppermute | solution.py:13
  103.3 23.4 %copy-start.3 = (f32[256,256]{1,0:T(8,128)}, f32[256,256]{1,0:T(8,128)S(1)}, u32[]{:S(2)}) copy-start(f32[256,256]{1,0:T(8,128)S(1)} %convolution_select_fusion.11) | copy-start | bytes 786436
  103.3 15.8 %collective-permute-start.1 = (f32[512,256]{1,0:T(8,128)S(1)}, f32[512,256]{1,0:T(8,128)S(1)}, u32[]{:S(2)}, u32[]{:S(2)}) collective-permute-start(f32[512,256]{1,0:T(8,128)S(1)} %pad_maximum_fusion.6), channel_id=1, source_target_pairs={{2,0},{3,1},{4,2},{5,3},{6,4},{7,5},{8,6},{9,7},{10,8},{11,9},{12,... | collective-permute-start | bytes 1572872 | tf_op jit(solution)/shard_map/ppermute | solution.py:13
  112.0 10.8 %collective-permute-start.7 = (f32[257,256]{1,0:T(8,128)S(1)}, f32[257,256]{1,0:T(8,128)S(1)}, u32[]{:S(2)}, u32[]{:S(2)}) collective-permute-start(f32[257,256]{1,0:T(8,128)S(1)} %pad_maximum_fusion.12), channel_id=1, source_target_pairs={{0,16},{1,17},{2,18},{3,19},{4,20},{5,21},{6,22},{7,23},{8,24},{9,... | collective-permute-start | bytes 789512 | tf_op jit(solution)/shard_map/ppermute | solution.py:13
  123.6 8.4 %collective-permute-start.8 = (f32[257,256]{1,0:T(8,128)S(1)}, f32[257,256]{1,0:T(8,128)S(1)}, u32[]{:S(2)}, u32[]{:S(2)}) collective-permute-start(f32[257,256]{1,0:T(8,128)S(1)} %pad_maximum_fusion.13), channel_id=1, source_target_pairs={{0,32},{1,33},{2,34},{3,35},{4,36},{5,37},{6,38},{7,39},{8,40},{9,... | collective-permute-start | bytes 789512 | tf_op jit(solution)/shard_map/ppermute | solution.py:13
  127.1 10.8 %copy-start.12 = (f32[256,256]{1,0:T(8,128)}, f32[256,256]{1,0:T(8,128)S(1)}, u32[]{:S(2)}) copy-start(f32[256,256]{1,0:T(8,128)S(1)} %fusion.7) | copy-start | bytes 786436
  132.3 3.3 %collective-permute-start.9 = (f32[256]{0:T(256)S(1)}, f32[256]{0:T(256)S(1)}, u32[]{:S(2)}, u32[]{:S(2)}) collective-permute-start(f32[256]{0:T(256)S(1)} %add_select_fusion.8), channel_id=1, source_target_pairs={{0,64},{1,65},{2,66},{3,67},{4,68},{5,69},{6,70},{7,71},{8,72},{9,... | collective-permute-start | bytes 3080 | tf_op jit(solution)/shard_map/ppermute | solution.py:13
  135.9 7.8 %collective-permute-start.10 = (f32[256]{0:T(256)S(1)}, f32[256]{0:T(256)S(1)}, u32[]{:S(2)}, u32[]{:S(2)}) collective-permute-start(f32[256]{0:T(256)S(1)} %add_select_fusion.7), channel_id=1, source_target_pairs={{0,1},{1,2},{2,3},{3,4},{4,5},{5,6},{6,7},{7,8},{8,9},{9,10},{10,1... | collective-permute-start | bytes 3080 | tf_op jit(solution)/shard_map/ppermute | solution.py:13
  138.7 19.5 %collective-permute-start.2 = (f32[512,256]{1,0:T(8,128)}, f32[512,256]{1,0:T(8,128)}, u32[]{:S(2)}, u32[]{:S(2)}) collective-permute-start(f32[512,256]{1,0:T(8,128)} %pad_maximum_fusion.7), channel_id=1, source_target_pairs={{4,0},{5,1},{6,2},{7,3},{8,4},{9,5},{10,6},{11,7},{12,8},{13,9},{1... | collective-permute-start | bytes 1572872 | tf_op jit(solution)/shard_map/ppermute | solution.py:13
  144.3 1.0 copy-start.6
  146.5 1.1 copy-start.8
  147.9 11.7 %collective-permute-start.11 = (f32[256]{0:T(256)S(1)}, f32[256]{0:T(256)S(1)}, u32[]{:S(2)}, u32[]{:S(2)}) collective-permute-start(f32[256]{0:T(256)S(1)} %bitcast.384), channel_id=1, source_target_pairs={{1,0},{2,1},{3,2},{4,3},{5,4},{6,5},{7,6},{8,7},{9,8},{10,9},{11,1... | collective-permute-start | bytes 3080 | tf_op jit(solution)/shard_map/ppermute | solution.py:13
  159.6 2.4 copy-start.13
  159.9 6.0 %copy-start.4 = (f32[256,256]{1,0:T(8,128)S(1)}, f32[256,256]{1,0:T(8,128)}, u32[]{:S(2)}) copy-start(f32[256,256]{1,0:T(8,128)} %copy-done.3) | copy-start | bytes 786436
  159.9 5.9 %collective-permute-start.12 = (f32[256]{0:T(256)S(1)}, f32[256]{0:T(256)S(1)}, u32[]{:S(2)}, u32[]{:S(2)}) collective-permute-start(f32[256]{0:T(256)S(1)} %add_select_fusion.6), channel_id=1, source_target_pairs={{2,0},{3,1},{4,2},{5,3},{6,4},{7,5},{8,6},{9,7},{10,8},{11,9},{12,... | collective-permute-start | bytes 3080 | tf_op jit(solution)/shard_map/ppermute | solution.py:13
  166.2 7.9 %collective-permute-start.13 = (f32[256]{0:T(256)S(1)}, f32[256]{0:T(256)S(1)}, u32[]{:S(2)}, u32[]{:S(2)}) collective-permute-start(f32[256]{0:T(256)S(1)} %add_select_fusion.5), channel_id=1, source_target_pairs={{4,0},{5,1},{6,2},{7,3},{8,4},{9,5},{10,6},{11,7},{12,8},{13,9},{1... | collective-permute-start | bytes 3080 | tf_op jit(solution)/shard_map/ppermute | solution.py:13
  175.2 14.9 %collective-permute-start.14 = (f32[513,256]{1,0:T(8,128)}, f32[513,256]{1,0:T(8,128)S(1)}, u32[]{:S(2)}, u32[]{:S(2)}) collective-permute-start(f32[513,256]{1,0:T(8,128)} %pad_maximum_fusion.1), channel_id=1, source_target_pairs={{8,0},{9,1},{10,2},{11,3},{12,4},{13,5},{14,6},{15,7},{16,8},{17,9... | collective-permute-start | bytes 1575944 | tf_op jit(solution)/shard_map/ppermute | solution.py:13
  190.1 0.8 copy-start.15
  193.9 16.4 %collective-permute-start.15 = (f32[513,256]{1,0:T(8,128)}, f32[513,256]{1,0:T(8,128)}, u32[]{:S(2)}, u32[]{:S(2)}) collective-permute-start(f32[513,256]{1,0:T(8,128)} %pad_maximum_fusion.2), channel_id=1, source_target_pairs={{16,0},{17,1},{18,2},{19,3},{20,4},{21,5},{22,6},{23,7},{24,8},{25... | collective-permute-start | bytes 1575944 | tf_op jit(solution)/shard_map/ppermute | solution.py:13
  215.3 14.9 %collective-permute-start.16 = (f32[513,256]{1,0:T(8,128)}, f32[513,256]{1,0:T(8,128)S(1)}, u32[]{:S(2)}, u32[]{:S(2)}) collective-permute-start(f32[513,256]{1,0:T(8,128)} %pad_maximum_fusion.3), channel_id=1, source_target_pairs={{32,0},{33,1},{34,2},{35,3},{36,4},{37,5},{38,6},{39,7},{40,8},{41... | collective-permute-start | bytes 1575944 | tf_op jit(solution)/shard_map/ppermute | solution.py:13
  231.8 24.2 %collective-permute-start.17 = (f32[513,256]{1,0:T(8,128)S(1)}, f32[513,256]{1,0:T(8,128)S(1)}, u32[]{:S(2)}, u32[]{:S(2)}) collective-permute-start(f32[513,256]{1,0:T(8,128)S(1)} %pad_maximum_fusion.4), channel_id=1, source_target_pairs={{1,0},{2,1},{3,2},{4,3},{5,4},{6,5},{7,6},{8,7},{9,8},{10,9},{11,1... | collective-permute-start | bytes 1575944 | tf_op jit(solution)/shard_map/ppermute | solution.py:13
  241.9 14.1 %collective-permute-start.18 = (f32[257,256]{1,0:T(8,128)}, f32[257,256]{1,0:T(8,128)S(1)}, u32[]{:S(2)}, u32[]{:S(2)}) collective-permute-start(f32[257,256]{1,0:T(8,128)} %pad_maximum_fusion.14), channel_id=1, source_target_pairs={{65,0},{66,1},{67,2},{68,3},{69,4},{70,5},{71,6},{72,7},{73,8},{74... | collective-permute-start | bytes 789512 | tf_op jit(solution)/shard_map/ppermute | solution.py:13
  258.7 12.1 %all-to-all-start.4 = ((f32[4,1,256]{2,1,0:T(1,128)}), f32[4,1,256]{2,1,0:T(1,128)S(1)}, u32[]{:S(2)}, u32[]{:S(2)}) async-start(f32[4,1,256]{2,1,0:T(1,128)} %reshape.172), calls=%async_computation.4 | async-start | bytes 8192 | tf_op jit(solution)/shard_map/all_to_all | solution.py:213
  265.0 1.2 copy-start.2
  270.8 18.1 %all-to-all-start.5 = ((f32[4,256,256]{2,0,1:T(4,128)}), f32[4,256,256]{2,0,1:T(4,128)S(1)}, u32[]{:S(2)}, u32[]{:S(2)}) async-start(f32[4,256,256]{2,0,1:T(4,128)} %copy.48), calls=%async_computation.5 | async-start | bytes 2097152 | tf_op jit(solution)/shard_map/all_to_all | solution.py:213

commit v7 on v4

--- a/solution.py
+++ b/solution.py
@@ -183,14 +183,19 @@
     def rows_of_steps(whole):
         return lax.all_to_all(whole, "blk", 1, 0, tiled=True)
 
+    gain_whole = steps_whole(smooth_gains)
+    cov_whole = steps_whole(filt_cov)
+    map_rows, shift_rows, gain_whole, cov_whole = lax.optimization_barrier(
+        (map_rows, shift_rows, gain_whole, cov_whole)
+    )
     means_out, cov_out = window_work(
         trans_map,
         process_noise,
         initial_expectation,
         steps_whole(map_rows),
         steps_whole(shift_rows),
-        steps_whole(smooth_gains),
-        steps_whole(filt_cov),
+        gain_whole,
+        cov_whole,
         lax.axis_index(CHUNKS),
         lax.axis_size(CHUNKS),
     )

time: 285 us -> 288 us (1.011)
  starting transfers between devices: 99.3 us -> 112 us
  blocking collectives: 8.97 us -> 0 us
  waiting for transfers between devices: 109 us -> 106 us
    all_to_all x1 -> x0, blocking collectives: 8.97 us -> none  [steps_whole(): return lax.all_to_all(rows, 'blk', 0, 1, tiled=True)]
    ppermute x24, starting transfers between devices: 81.1 us -> 87.4 us  [from_behind(): return lax.ppermute(block, axis, route)]
    ppermute x24, waiting for transfers between devices: 79.7 us -> 74.4 us  [from_behind(): return lax.ppermute(block, axis, route)]
    all_to_all x3 -> x4, starting transfers between devices: 11.4 us -> 16.1 us  [steps_whole(): return lax.all_to_all(rows, 'blk', 0, 1, tiled=True)]
    unnamed x52 -> x60, local copies, waits for them, and re-layouts: 6.72 us -> 8.01 us
    all_to_all x3 -> x4, waiting for transfers between devices: 17.4 us -> 17.7 us  [steps_whole(): return lax.all_to_all(rows, 'blk', 0, 1, tiled=True)]
  transfers between devices with their start and end apart: 29 -> 30, of which waited for: 22 -> 20; matrix products, arithmetic and copies ran while one was open for 14% -> 18% of each run, Pallas kernels for 0% -> 0%
where the time goes in v7:
time: 288 us; the launch traced here: 285 us
  starting transfers between devices  112 us (39%)
  waiting for transfers between devices  106 us (37%)
  matrix products  43.6 us (15%)
  local copies, waits for them, and re-layouts  16.2 us (6%)
  other arithmetic  5.38 us (2%)
    ppermute x24, starting transfers between devices, from_behind(): return lax.ppermute(block, axis, route)  87.4 us
    ppermute x24, waiting for transfers between devices, from_behind(): return lax.ppermute(block, axis, route)  74.4 us
    dot_general x48, matrix products, matmul(): return jnp.matmul(left, right, precision=highest)  33.4 us
    all_to_all x4, waiting for transfers between devices, steps_whole(): return lax.all_to_all(rows, 'blk', 0, 1, tiled=True)  17.7 us
    all_to_all x4, starting transfers between devices, steps_whole(): return lax.all_to_all(rows, 'blk', 0, 1, tiled=True)  16.1 us
    all_to_all x2, waiting for transfers between devices, rows_of_steps(): return lax.all_to_all(whole, 'blk', 1, 0, tiled=True)  14 us
    unnamed x60, local copies, waits for them, and re-layouts  8.01 us
    dot_general x27, matrix products, matvec(): return jnp.einsum('...ij,...j->...i', left, right, precision=highest)  8 us
  transfers between devices with their start and end apart: 30, of which 20 were waited for; matrix products, arithmetic and copies ran while one was open for 18% of the time, Pallas kernels for 0%

profile of v7, /device:TPU:15, one launch (start us, length us, event | category | flops | bytes accessed | tf_op | source)
XLA Modules:
  0.0 285.4 jit_solution(17837069179447510806)
XLA Ops:
  0.7 5.2 %all-to-all-start = ((f32[16,64,256]{2,1,0:T(8,128)}), f32[16,64,256]{2,1,0:T(8,128)S(1)}, u32[]{:S(2)}, u32[]{:S(2)}) async-start(f32[16,64,256]{2,1,0:T(8,128)} %param.18), calls=%async_computation | async-start | bytes 2097152 | tf_op jit(solution)/shard_map/all_to_all | solution.py:181
  7.9 1.3 convolution_bitcast_fusion.3
  9.2 10.8 %all-to-all-done = f32[16,64,256]{2,1,0:T(8,128)S(1)} async-done(((f32[16,64,256]{2,1,0:T(8,128)}), f32[16,64,256]{2,1,0:T(8,128)S(1)}, u32[]{:S(2)}, u32[]{:S(2)}) %all-to-all-start) | async-done | bytes 1048608 | tf_op jit(solution)/shard_map/all_to_all | solution.py:181
  20.0 3.5 %all-to-all-start.1 = ((f32[16,64,256]{2,1,0:T(8,128)}), f32[16,64,256]{2,1,0:T(8,128)S(1)}, u32[]{:S(2)}, u32[]{:S(2)}) async-start(f32[16,64,256]{2,1,0:T(8,128)} %param.19), calls=%async_computation.1 | async-start | bytes 2097152 | tf_op jit(solution)/shard_map/all_to_all | solution.py:181
  26.8 2.0 fusion
  28.8 1.1 copy.42
  29.9 6.9 %all-to-all-done.1 = f32[16,64,256]{2,1,0:T(8,128)S(1)} async-done(((f32[16,64,256]{2,1,0:T(8,128)}), f32[16,64,256]{2,1,0:T(8,128)S(1)}, u32[]{:S(2)}, u32[]{:S(2)}) %all-to-all-start.1) | async-done | bytes 1048608 | tf_op jit(solution)/shard_map/all_to_all | solution.py:181
  37.8 1.3 copy.43
  39.8 3.2 %all-to-all-start.3 = ((f32[4,1,256]{2,1,0:T(1,128)}), f32[4,1,256]{2,1,0:T(1,128)S(1)}, u32[]{:S(2)}, u32[]{:S(2)}) async-start(f32[4,1,256]{2,1,0:T(1,128)} %reshape.170), calls=%async_computation.3 | async-start | bytes 8192 | tf_op jit(solution)/shard_map/all_to_all | solution.py:181
  43.0 1.0 convolution_bitcast_fusion
  46.2 1.1 fusion.91
  47.3 1.2 convolution_subtract_fusion
  49.2 1.5 convolution_add_fusion.1
  50.7 1.5 fusion.15
  52.1 4.2 %all-to-all-start.2 = ((f32[16,64,256]{2,1,0:T(8,128)}), f32[16,64,256]{2,1,0:T(8,128)S(1)}, u32[]{:S(2)}, u32[]{:S(2)}) async-start(f32[16,64,256]{2,1,0:T(8,128)} %fusion), calls=%async_computation.2 | async-start | bytes 2097152 | tf_op jit(solution)/shard_map/all_to_all | solution.py:181
  56.3 1.5 fusion.50
  57.8 1.4 fusion.10
  60.7 8.3 %collective-permute-start = (f32[512,256]{1,0:T(8,128)}, f32[512,256]{1,0:T(8,128)}, u32[]{:S(2)}, u32[]{:S(2)}) collective-permute-start(f32[512,256]{1,0:T(8,128)} %pad_maximum_fusion.1), channel_id=1, source_target_pairs={{1,0},{2,1},{3,2},{4,3},{5,4},{6,5},{7,6},{8,7},{9,8},{10,9},{11,1... | collective-permute-start | bytes 1572872 | tf_op jit(solution)/shard_map/ppermute | solution.py:13
  73.9 2.1 collective-permute-start.6
  75.9 6.8 %collective-permute-done = f32[512,256]{1,0:T(8,128)} collective-permute-done((f32[512,256]{1,0:T(8,128)}, f32[512,256]{1,0:T(8,128)}, u32[]{:S(2)}, u32[]{:S(2)}) %collective-permute-start) | collective-permute-done | bytes 524320 | tf_op jit(solution)/shard_map/ppermute | solution.py:13
  82.8 1.3 fusion.47
  84.5 3.2 %collective-permute-done.6 = f32[257,256]{1,0:T(8,128)S(1)} collective-permute-done((f32[257,256]{1,0:T(8,128)S(1)}, f32[257,256]{1,0:T(8,128)S(1)}, u32[]{:S(2)}, u32[]{:S(2)}) %collective-permute-start.6) | collective-permute-done | bytes 263200 | tf_op jit(solution)/shard_map/ppermute | solution.py:13
  88.5 1.9 collective-permute-start.7
  90.4 1.3 convolution_select_fusion.11
  91.8 5.1 %collective-permute-start.1 = (f32[512,256]{1,0:T(8,128)S(1)}, f32[512,256]{1,0:T(8,128)S(1)}, u32[]{:S(2)}, u32[]{:S(2)}) collective-permute-start(f32[512,256]{1,0:T(8,128)S(1)} %pad_maximum_fusion.2), channel_id=1, source_target_pairs={{2,0},{3,1},{4,2},{5,3},{6,4},{7,5},{8,6},{9,7},{10,8},{11,9},{12,... | collective-permute-start | bytes 1572872 | tf_op jit(solution)/shard_map/ppermute | solution.py:13
  96.9 2.7 collective-permute-done.7
  100.4 4.2 %collective-permute-start.8 = (f32[257,256]{1,0:T(8,128)S(1)}, f32[257,256]{1,0:T(8,128)S(1)}, u32[]{:S(2)}, u32[]{:S(2)}) collective-permute-start(f32[257,256]{1,0:T(8,128)S(1)} %pad_maximum_fusion.9), channel_id=1, source_target_pairs={{0,4},{1,5},{2,6},{3,7},{4,8},{5,9},{6,10},{7,11},{8,12},{9,13},{1... | collective-permute-start | bytes 789512 | tf_op jit(solution)/shard_map/ppermute | solution.py:13
  104.6 5.3 %collective-permute-done.1 = f32[512,256]{1,0:T(8,128)S(1)} collective-permute-done((f32[512,256]{1,0:T(8,128)S(1)}, f32[512,256]{1,0:T(8,128)S(1)}, u32[]{:S(2)}, u32[]{:S(2)}) %collective-permute-start.1) | collective-permute-done | bytes 524320 | tf_op jit(solution)/shard_map/ppermute | solution.py:13
  111.5 4.9 %collective-permute-start.9 = (f32[257,256]{1,0:T(8,128)S(1)}, f32[257,256]{1,0:T(8,128)S(1)}, u32[]{:S(2)}, u32[]{:S(2)}) collective-permute-start(f32[257,256]{1,0:T(8,128)S(1)} %pad_maximum_fusion.10), channel_id=1, source_target_pairs={{0,8},{1,9},{2,10},{3,11},{4,12},{5,13},{6,14},{7,15},{8,16},{9,17... | collective-permute-start | bytes 789512 | tf_op jit(solution)/shard_map/ppermute | solution.py:13
  116.9 5.2 %collective-permute-start.2 = (f32[512,256]{1,0:T(8,128)S(1)}, f32[512,256]{1,0:T(8,128)S(1)}, u32[]{:S(2)}, u32[]{:S(2)}) collective-permute-start(f32[512,256]{1,0:T(8,128)S(1)} %pad_maximum_fusion.3), channel_id=1, source_target_pairs={{4,0},{5,1},{6,2},{7,3},{8,4},{9,5},{10,6},{11,7},{12,8},{13,9},{1... | collective-permute-start | bytes 1572872 | tf_op jit(solution)/shard_map/ppermute | solution.py:13
  122.8 1.9 collective-permute-start.10
  124.8 10.4 %collective-permute-done.2 = f32[512,256]{1,0:T(8,128)S(1)} collective-permute-done((f32[512,256]{1,0:T(8,128)S(1)}, f32[512,256]{1,0:T(8,128)S(1)}, u32[]{:S(2)}, u32[]{:S(2)}) %collective-permute-start.2) | collective-permute-done | bytes 524320 | tf_op jit(solution)/shard_map/ppermute | solution.py:13
  136.4 2.9 %collective-permute-start.11 = (f32[257,256]{1,0:T(8,128)S(1)}, f32[257,256]{1,0:T(8,128)S(1)}, u32[]{:S(2)}, u32[]{:S(2)}) collective-permute-start(f32[257,256]{1,0:T(8,128)S(1)} %pad_maximum_fusion.12), channel_id=1, source_target_pairs={{0,32},{1,33},{2,34},{3,35},{4,36},{5,37},{6,38},{7,39},{8,40},{9,... | collective-permute-start | bytes 789512 | tf_op jit(solution)/shard_map/ppermute | solution.py:13
  140.1 6.5 %collective-permute-done.11 = f32[257,256]{1,0:T(8,128)S(1)} collective-permute-done((f32[257,256]{1,0:T(8,128)S(1)}, f32[257,256]{1,0:T(8,128)S(1)}, u32[]{:S(2)}, u32[]{:S(2)}) %collective-permute-start.11) | collective-permute-done | bytes 263200 | tf_op jit(solution)/shard_map/ppermute | solution.py:13
  146.9 2.3 collective-permute-start.12
  150.2 2.1 collective-permute-start.13
  153.2 2.1 collective-permute-start.3
  160.5 3.7 %collective-permute-start.14 = (f32[256]{0:T(256)S(1)}, f32[256]{0:T(256)S(1)}, u32[]{:S(2)}, u32[]{:S(2)}) collective-permute-start(f32[256]{0:T(256)S(1)} %bitcast.369), channel_id=1, source_target_pairs={{1,0},{2,1},{3,2},{4,3},{5,4},{6,5},{7,6},{8,7},{9,8},{10,9},{11,1... | collective-permute-start | bytes 3080 | tf_op jit(solution)/shard_map/ppermute | solution.py:13
  164.3 4.7 %collective-permute-done.3 = f32[512,256]{1,0:T(8,128)} collective-permute-done((f32[512,256]{1,0:T(8,128)}, f32[512,256]{1,0:T(8,128)}, u32[]{:S(2)}, u32[]{:S(2)}) %collective-permute-start.3) | collective-permute-done | bytes 524320 | tf_op jit(solution)/shard_map/ppermute | solution.py:13
  168.9 1.3 fusion.38
  170.6 5.7 %collective-permute-start.15 = (f32[256]{0:T(256)S(1)}, f32[256]{0:T(256)S(1)}, u32[]{:S(2)}, u32[]{:S(2)}) collective-permute-start(f32[256]{0:T(256)S(1)} %add_select_fusion.6), channel_id=1, source_target_pairs={{2,0},{3,1},{4,2},{5,3},{6,4},{7,5},{8,6},{9,7},{10,8},{11,9},{12,... | collective-permute-start | bytes 3080 | tf_op jit(solution)/shard_map/ppermute | solution.py:13
  177.4 5.6 %collective-permute-start.16 = (f32[256]{0:T(256)S(1)}, f32[256]{0:T(256)S(1)}, u32[]{:S(2)}, u32[]{:S(2)}) collective-permute-start(f32[256]{0:T(256)S(1)} %add_select_fusion.5), channel_id=1, source_target_pairs={{4,0},{5,1},{6,2},{7,3},{8,4},{9,5},{10,6},{11,7},{12,8},{13,9},{1... | collective-permute-start | bytes 3080 | tf_op jit(solution)/shard_map/ppermute | solution.py:13
  183.0 1.3 convolution_select_fusion.8
  184.3 1.6 collective-permute-done.16
  186.2 1.9 collective-permute-start.17
  189.0 2.1 collective-permute-start.4
  191.1 1.6 collective-permute-done.17
  193.0 5.0 %collective-permute-start.18 = (f32[256]{0:T(256)S(1)}, f32[256]{0:T(256)S(1)}, u32[]{:S(2)}, u32[]{:S(2)}) collective-permute-start(f32[256]{0:T(256)S(1)} %add_select_fusion.3), channel_id=1, source_target_pairs={{16,0},{17,1},{18,2},{19,3},{20,4},{21,5},{22,6},{23,7},{24,8},{25... | collective-permute-start | bytes 3080 | tf_op jit(solution)/shard_map/ppermute | solution.py:13
  198.0 8.1 %collective-permute-done.18 = f32[256]{0:T(256)S(1)} collective-permute-done((f32[256]{0:T(256)S(1)}, f32[256]{0:T(256)S(1)}, u32[]{:S(2)}, u32[]{:S(2)}) %collective-permute-start.18) | collective-permute-done | bytes 1056 | tf_op jit(solution)/shard_map/ppermute | solution.py:13
  206.5 4.4 %collective-permute-start.19 = (f32[256]{0:T(256)S(1)}, f32[256]{0:T(256)S(1)}, u32[]{:S(2)}, u32[]{:S(2)}) collective-permute-start(f32[256]{0:T(256)S(1)} %add_select_fusion.2), channel_id=1, source_target_pairs={{32,0},{33,1},{34,2},{35,3},{36,4},{37,5},{38,6},{39,7},{40,8},{41... | collective-permute-start | bytes 3080 | tf_op jit(solution)/shard_map/ppermute | solution.py:13
  212.1 1.9 collective-permute-start.5
  214.4 1.3 collective-permute-start.20
  215.7 11.6 %collective-permute-done.5 = f32[512,256]{1,0:T(8,128)S(1)} collective-permute-done((f32[512,256]{1,0:T(8,128)S(1)}, f32[512,256]{1,0:T(8,128)S(1)}, u32[]{:S(2)}, u32[]{:S(2)}) %collective-permute-start.5) | collective-permute-done | bytes 524320 | tf_op jit(solution)/shard_map/ppermute | solution.py:13
  228.8 7.6 %collective-permute-start.21 = (f32[256]{0:T(256)S(1)}, f32[256]{0:T(256)S(1)}, u32[]{:S(2)}, u32[]{:S(2)}) collective-permute-start(f32[256]{0:T(256)S(1)} %add_select_fusion), channel_id=1, source_target_pairs={{1,0},{2,1},{3,2},{4,3},{5,4},{6,5},{7,6},{8,7},{9,8},{10,9},{11,1... | collective-permute-start | bytes 3080 | tf_op jit(solution)/shard_map/ppermute | solution.py:13
  237.2 1.3 collective-permute-start.22
  239.8 7.7 %collective-permute-done.22 = f32[256,256]{1,0:T(8,128)S(1)} collective-permute-done((f32[256,256]{1,0:T(8,128)S(1)}, f32[256,256]{1,0:T(8,128)S(1)}, u32[]{:S(2)}, u32[]{:S(2)}) %collective-permute-start.22) | collective-permute-done | bytes 262176 | tf_op jit(solution)/shard_map/ppermute | solution.py:13
  247.9 1.1 fusion.2
  249.0 3.9 %collective-permute-start.23 = (f32[256,256]{1,0:T(8,128)}, f32[256,256]{1,0:T(8,128)S(1)}, u32[]{:S(2)}, u32[]{:S(2)}) collective-permute-start(f32[256,256]{1,0:T(8,128)} %fusion.2), channel_id=1, source_target_pairs={{1,0},{2,1},{3,2},{4,3},{5,4},{6,5},{7,6},{8,7},{9,8},{10,9},{11,1... | collective-permute-start | bytes 786440 | tf_op jit(solution)/shard_map/ppermute | solution.py:13
  254.1 3.5 %all-to-all-start.4 = ((f32[4,1,256]{2,1,0:T(1,128)}), f32[4,1,256]{2,1,0:T(1,128)S(1)}, u32[]{:S(2)}, u32[]{:S(2)}) async-start(f32[4,1,256]{2,1,0:T(1,128)} %reshape.172), calls=%async_computation.4 | async-start | bytes 8192 | tf_op jit(solution)/shard_map/all_to_all | solution.py:184
  257.6 1.8 collective-permute-done.23
  262.7 1.6 copy.48
  264.4 4.5 %all-to-all-start.5 = ((f32[4,256,256]{2,0,1:T(4,128)}), f32[4,256,256]{2,0,1:T(4,128)S(1)}, u32[]{:S(2)}, u32[]{:S(2)}) async-start(f32[4,256,256]{2,0,1:T(4,128)} %copy.48), calls=%async_computation.5 | async-start | bytes 2097152 | tf_op jit(solution)/shard_map/all_to_all | solution.py:184
  270.2 14.0 %all-to-all-done.5 = f32[4,256,256]{2,0,1:T(4,128)S(1)} async-done(((f32[4,256,256]{2,0,1:T(4,128)}), f32[4,256,256]{2,0,1:T(4,128)S(1)}, u32[]{:S(2)}, u32[]{:S(2)}) %all-to-all-start.5) | async-done | bytes 1048608 | tf_op jit(solution)/shard_map/all_to_all | solution.py:184
  284.2 1.2 copy.49
  (215 shorter events, 43.6 us)
Async XLA Ops:
  0.6 25.2 %copy-start = (f32[16,64,256]{2,1,0:T(8,128)S(1)}, f32[16,64,256]{2,1,0:T(8,128)}, u32[]{:S(2)}) copy-start(f32[16,64,256]{2,1,0:T(8,128)} %param.16) | copy-start | bytes 3145732
  0.6 5.2 %copy-start.20 = (f32[256,256]{1,0:T(8,128)S(1)}, f32[256,256]{1,0:T(8,128)}, u32[]{:S(2)}) copy-start(f32[256,256]{1,0:T(8,128)} %param.12) | copy-start | bytes 786436
  0.7 19.4 %all-to-all-start = ((f32[16,64,256]{2,1,0:T(8,128)}), f32[16,64,256]{2,1,0:T(8,128)S(1)}, u32[]{:S(2)}, u32[]{:S(2)}) async-start(f32[16,64,256]{2,1,0:T(8,128)} %param.18), calls=%async_computation | async-start | bytes 2097152 | tf_op jit(solution)/shard_map/all_to_all | solution.py:181
  5.8 0.7 copy-start.24
  5.8 1.0 copy-start.21
  6.8 0.7 copy-start.25
  7.8 36.7 %copy-start.7 = (f32[256,256]{0,1:T(8,128)}, f32[256,256]{0,1:T(8,128)S(1)}, u32[]{:S(2)}) copy-start(f32[256,256]{0,1:T(8,128)S(1)} %get-tuple-element.25) | copy-start | bytes 786436
  20.0 16.8 %all-to-all-start.1 = ((f32[16,64,256]{2,1,0:T(8,128)}), f32[16,64,256]{2,1,0:T(8,128)S(1)}, u32[]{:S(2)}, u32[]{:S(2)}) async-start(f32[16,64,256]{2,1,0:T(8,128)} %param.19), calls=%async_computation.1 | async-start | bytes 2097152 | tf_op jit(solution)/shard_map/all_to_all | solution.py:181
  24.3 0.7 copy-start.26
  25.0 0.8 copy-start.22
  25.8 1.0 copy-start.15
  25.8 1.0 copy-start.19
  36.8 1.0 copy-start.12
  39.8 12.4 %all-to-all-start.3 = ((f32[4,1,256]{2,1,0:T(1,128)}), f32[4,1,256]{2,1,0:T(1,128)S(1)}, u32[]{:S(2)}, u32[]{:S(2)}) async-start(f32[4,1,256]{2,1,0:T(1,128)} %reshape.170), calls=%async_computation.3 | async-start | bytes 8192 | tf_op jit(solution)/shard_map/all_to_all | solution.py:181
  43.0 1.2 copy-start.11
  44.2 0.9 copy-start.16
  48.5 2.2 copy-start.1
  52.1 18.6 %all-to-all-start.2 = ((f32[16,64,256]{2,1,0:T(8,128)}), f32[16,64,256]{2,1,0:T(8,128)S(1)}, u32[]{:S(2)}, u32[]{:S(2)}) async-start(f32[16,64,256]{2,1,0:T(8,128)} %fusion), calls=%async_computation.2 | async-start | bytes 2097152 | tf_op jit(solution)/shard_map/all_to_all | solution.py:181
  56.3 1.5 copy-start.9
  59.2 0.7 copy-start.13
  60.7 22.1 %collective-permute-start = (f32[512,256]{1,0:T(8,128)}, f32[512,256]{1,0:T(8,128)}, u32[]{:S(2)}, u32[]{:S(2)}) collective-permute-start(f32[512,256]{1,0:T(8,128)} %pad_maximum_fusion.1), channel_id=1, source_target_pairs={{1,0},{2,1},{3,2},{4,3},{5,4},{6,5},{7,6},{8,7},{9,8},{10,9},{11,1... | collective-permute-start | bytes 1572872 | tf_op jit(solution)/shard_map/ppermute | solution.py:13
  72.8 0.7 copy-start.23
  73.9 10.2 %copy-start.14 = (f32[256,256]{1,0:T(8,128)S(1)}, f32[256,256]{1,0:T(8,128)}, u32[]{:S(2)}) copy-start(f32[256,256]{1,0:T(8,128)} %copy-done.13) | copy-start | bytes 786436
  73.9 13.8 %collective-permute-start.6 = (f32[257,256]{1,0:T(8,128)S(1)}, f32[257,256]{1,0:T(8,128)S(1)}, u32[]{:S(2)}, u32[]{:S(2)}) collective-permute-start(f32[257,256]{1,0:T(8,128)S(1)} %pad_maximum_fusion.7), channel_id=1, source_target_pairs={{0,1},{1,2},{2,3},{3,4},{4,5},{5,6},{6,7},{7,8},{8,9},{9,10},{10,1... | collective-permute-start | bytes 789512 | tf_op jit(solution)/shard_map/ppermute | solution.py:13
  88.5 11.2 %collective-permute-start.7 = (f32[257,256]{1,0:T(8,128)S(1)}, f32[257,256]{1,0:T(8,128)S(1)}, u32[]{:S(2)}, u32[]{:S(2)}) collective-permute-start(f32[257,256]{1,0:T(8,128)S(1)} %pad_maximum_fusion.8), channel_id=1, source_target_pairs={{0,2},{1,3},{2,4},{3,5},{4,6},{5,7},{6,8},{7,9},{8,10},{9,11},{10,... | collective-permute-start | bytes 789512 | tf_op jit(solution)/shard_map/ppermute | solution.py:13
  91.7 24.7 %copy-start.3 = (f32[256,256]{1,0:T(8,128)}, f32[256,256]{1,0:T(8,128)S(1)}, u32[]{:S(2)}) copy-start(f32[256,256]{1,0:T(8,128)S(1)} %convolution_select_fusion.11) | copy-start | bytes 786436
  91.8 18.2 %collective-permute-start.1 = (f32[512,256]{1,0:T(8,128)S(1)}, f32[512,256]{1,0:T(8,128)S(1)}, u32[]{:S(2)}, u32[]{:S(2)}) collective-permute-start(f32[512,256]{1,0:T(8,128)S(1)} %pad_maximum_fusion.2), channel_id=1, source_target_pairs={{2,0},{3,1},{4,2},{5,3},{6,4},{7,5},{8,6},{9,7},{10,8},{11,9},{12,... | collective-permute-start | bytes 1572872 | tf_op jit(solution)/shard_map/ppermute | solution.py:13
  100.4 10.4 %collective-permute-start.8 = (f32[257,256]{1,0:T(8,128)S(1)}, f32[257,256]{1,0:T(8,128)S(1)}, u32[]{:S(2)}, u32[]{:S(2)}) collective-permute-start(f32[257,256]{1,0:T(8,128)S(1)} %pad_maximum_fusion.9), channel_id=1, source_target_pairs={{0,4},{1,5},{2,6},{3,7},{4,8},{5,9},{6,10},{7,11},{8,12},{9,13},{1... | collective-permute-start | bytes 789512 | tf_op jit(solution)/shard_map/ppermute | solution.py:13
  111.5 10.5 %collective-permute-start.9 = (f32[257,256]{1,0:T(8,128)S(1)}, f32[257,256]{1,0:T(8,128)S(1)}, u32[]{:S(2)}, u32[]{:S(2)}) collective-permute-start(f32[257,256]{1,0:T(8,128)S(1)} %pad_maximum_fusion.10), channel_id=1, source_target_pairs={{0,8},{1,9},{2,10},{3,11},{4,12},{5,13},{6,14},{7,15},{8,16},{9,17... | collective-permute-start | bytes 789512 | tf_op jit(solution)/shard_map/ppermute | solution.py:13
  116.8 22.9 %copy-start.5 = (f32[256,256]{1,0:T(8,128)}, f32[256,256]{1,0:T(8,128)S(1)}, u32[]{:S(2)}) copy-start(f32[256,256]{1,0:T(8,128)S(1)} %convolution_select_fusion.10) | copy-start | bytes 786436
  116.9 18.4 %collective-permute-start.2 = (f32[512,256]{1,0:T(8,128)S(1)}, f32[512,256]{1,0:T(8,128)S(1)}, u32[]{:S(2)}, u32[]{:S(2)}) collective-permute-start(f32[512,256]{1,0:T(8,128)S(1)} %pad_maximum_fusion.3), channel_id=1, source_target_pairs={{4,0},{5,1},{6,2},{7,3},{8,4},{9,5},{10,6},{11,7},{12,8},{13,9},{1... | collective-permute-start | bytes 1572872 | tf_op jit(solution)/shard_map/ppermute | solution.py:13
  122.8 12.8 %collective-permute-start.10 = (f32[257,256]{1,0:T(8,128)S(1)}, f32[257,256]{1,0:T(8,128)S(1)}, u32[]{:S(2)}, u32[]{:S(2)}) collective-permute-start(f32[257,256]{1,0:T(8,128)S(1)} %pad_maximum_fusion.11), channel_id=1, source_target_pairs={{0,16},{1,17},{2,18},{3,19},{4,20},{5,21},{6,22},{7,23},{8,24},{9,... | collective-permute-start | bytes 789512 | tf_op jit(solution)/shard_map/ppermute | solution.py:13
  136.4 10.2 %collective-permute-start.11 = (f32[257,256]{1,0:T(8,128)S(1)}, f32[257,256]{1,0:T(8,128)S(1)}, u32[]{:S(2)}, u32[]{:S(2)}) collective-permute-start(f32[257,256]{1,0:T(8,128)S(1)} %pad_maximum_fusion.12), channel_id=1, source_target_pairs={{0,32},{1,33},{2,34},{3,35},{4,36},{5,37},{6,38},{7,39},{8,40},{9,... | collective-permute-start | bytes 789512 | tf_op jit(solution)/shard_map/ppermute | solution.py:13
  146.9 3.0 %collective-permute-start.12 = (f32[256]{0:T(256)S(1)}, f32[256]{0:T(256)S(1)}, u32[]{:S(2)}, u32[]{:S(2)}) collective-permute-start(f32[256]{0:T(256)S(1)} %add_select_fusion.8), channel_id=1, source_target_pairs={{0,64},{1,65},{2,66},{3,67},{4,68},{5,69},{6,70},{7,71},{8,72},{9,... | collective-permute-start | bytes 3080 | tf_op jit(solution)/shard_map/ppermute | solution.py:13
  150.2 6.1 %collective-permute-start.13 = (f32[256]{0:T(256)S(1)}, f32[256]{0:T(256)S(1)}, u32[]{:S(2)}, u32[]{:S(2)}) collective-permute-start(f32[256]{0:T(256)S(1)} %add_select_fusion.7), channel_id=1, source_target_pairs={{0,1},{1,2},{2,3},{3,4},{4,5},{5,6},{6,7},{7,8},{8,9},{9,10},{10,1... | collective-permute-start | bytes 3080 | tf_op jit(solution)/shard_map/ppermute | solution.py:13
  153.2 15.8 %collective-permute-start.3 = (f32[512,256]{1,0:T(8,128)}, f32[512,256]{1,0:T(8,128)}, u32[]{:S(2)}, u32[]{:S(2)}) collective-permute-start(f32[512,256]{1,0:T(8,128)} %pad_maximum_fusion.4), channel_id=1, source_target_pairs={{8,0},{9,1},{10,2},{11,3},{12,4},{13,5},{14,6},{15,7},{16,8},{17,9... | collective-permute-start | bytes 1572872 | tf_op jit(solution)/shard_map/ppermute | solution.py:13
  157.0 1.0 copy-start.8
  159.2 1.1 copy-start.10
  160.5 9.8 %collective-permute-start.14 = (f32[256]{0:T(256)S(1)}, f32[256]{0:T(256)S(1)}, u32[]{:S(2)}, u32[]{:S(2)}) collective-permute-start(f32[256]{0:T(256)S(1)} %bitcast.369), channel_id=1, source_target_pairs={{1,0},{2,1},{3,2},{4,3},{5,4},{6,5},{7,6},{8,7},{9,8},{10,9},{11,1... | collective-permute-start | bytes 3080 | tf_op jit(solution)/shard_map/ppermute | solution.py:13
  170.6 6.5 %copy-start.4 = (f32[256,256]{1,0:T(8,128)S(1)}, f32[256,256]{1,0:T(8,128)}, u32[]{:S(2)}) copy-start(f32[256,256]{1,0:T(8,128)} %copy-done.3) | copy-start | bytes 786436
  170.6 6.4 %collective-permute-start.15 = (f32[256]{0:T(256)S(1)}, f32[256]{0:T(256)S(1)}, u32[]{:S(2)}, u32[]{:S(2)}) collective-permute-start(f32[256]{0:T(256)S(1)} %add_select_fusion.6), channel_id=1, source_target_pairs={{2,0},{3,1},{4,2},{5,3},{6,4},{7,5},{8,6},{9,7},{10,8},{11,9},{12,... | collective-permute-start | bytes 3080 | tf_op jit(solution)/shard_map/ppermute | solution.py:13
  177.4 8.5 %copy-start.6 = (f32[256,256]{1,0:T(8,128)S(1)}, f32[256,256]{1,0:T(8,128)}, u32[]{:S(2)}) copy-start(f32[256,256]{1,0:T(8,128)} %copy-done.5) | copy-start | bytes 786436
  177.4 8.5 %collective-permute-start.16 = (f32[256]{0:T(256)S(1)}, f32[256]{0:T(256)S(1)}, u32[]{:S(2)}, u32[]{:S(2)}) collective-permute-start(f32[256]{0:T(256)S(1)} %add_select_fusion.5), channel_id=1, source_target_pairs={{4,0},{5,1},{6,2},{7,3},{8,4},{9,5},{10,6},{11,7},{12,8},{13,9},{1... | collective-permute-start | bytes 3080 | tf_op jit(solution)/shard_map/ppermute | solution.py:13
  186.2 6.4 %collective-permute-start.17 = (f32[256]{0:T(256)S(1)}, f32[256]{0:T(256)S(1)}, u32[]{:S(2)}, u32[]{:S(2)}) collective-permute-start(f32[256]{0:T(256)S(1)} %add_select_fusion.4), channel_id=1, source_target_pairs={{8,0},{9,1},{10,2},{11,3},{12,4},{13,5},{14,6},{15,7},{16,8},{17,9... | collective-permute-start | bytes 3080 | tf_op jit(solution)/shard_map/ppermute | solution.py:13
  189.0 21.8 %collective-permute-start.4 = (f32[512,256]{1,0:T(8,128)}, f32[512,256]{1,0:T(8,128)S(1)}, u32[]{:S(2)}, u32[]{:S(2)}) collective-permute-start(f32[512,256]{1,0:T(8,128)} %pad_maximum_fusion.5), channel_id=1, source_target_pairs={{16,0},{17,1},{18,2},{19,3},{20,4},{21,5},{22,6},{23,7},{24,8},{25... | collective-permute-start | bytes 1572872 | tf_op jit(solution)/shard_map/ppermute | solution.py:13
  193.0 13.1 %collective-permute-start.18 = (f32[256]{0:T(256)S(1)}, f32[256]{0:T(256)S(1)}, u32[]{:S(2)}, u32[]{:S(2)}) collective-permute-start(f32[256]{0:T(256)S(1)} %add_select_fusion.3), channel_id=1, source_target_pairs={{16,0},{17,1},{18,2},{19,3},{20,4},{21,5},{22,6},{23,7},{24,8},{25... | collective-permute-start | bytes 3080 | tf_op jit(solution)/shard_map/ppermute | solution.py:13
  206.5 7.6 %collective-permute-start.19 = (f32[256]{0:T(256)S(1)}, f32[256]{0:T(256)S(1)}, u32[]{:S(2)}, u32[]{:S(2)}) collective-permute-start(f32[256]{0:T(256)S(1)} %add_select_fusion.2), channel_id=1, source_target_pairs={{32,0},{33,1},{34,2},{35,3},{36,4},{37,5},{38,6},{39,7},{40,8},{41... | collective-permute-start | bytes 3080 | tf_op jit(solution)/shard_map/ppermute | solution.py:13
  212.1 15.2 %collective-permute-start.5 = (f32[512,256]{1,0:T(8,128)S(1)}, f32[512,256]{1,0:T(8,128)S(1)}, u32[]{:S(2)}, u32[]{:S(2)}) collective-permute-start(f32[512,256]{1,0:T(8,128)S(1)} %pad_maximum_fusion.6), channel_id=1, source_target_pairs={{32,0},{33,1},{34,2},{35,3},{36,4},{37,5},{38,6},{39,7},{40,8},{41... | collective-permute-start | bytes 1572872 | tf_op jit(solution)/shard_map/ppermute | solution.py:13
  214.4 14.0 %collective-permute-start.20 = (f32[256]{0:T(256)S(1)}, f32[256]{0:T(256)S(1)}, u32[]{:S(2)}, u32[]{:S(2)}) collective-permute-start(f32[256]{0:T(256)S(1)} %add_select_fusion.1), channel_id=1, source_target_pairs={{64,0},{65,1},{66,2},{67,3},{68,4},{69,5},{70,6},{71,7},{72,8},{73... | collective-permute-start | bytes 3080 | tf_op jit(solution)/shard_map/ppermute | solution.py:13
  228.8 9.7 %collective-permute-start.21 = (f32[256]{0:T(256)S(1)}, f32[256]{0:T(256)S(1)}, u32[]{:S(2)}, u32[]{:S(2)}) collective-permute-start(f32[256]{0:T(256)S(1)} %add_select_fusion), channel_id=1, source_target_pairs={{1,0},{2,1},{3,2},{4,3},{5,4},{6,5},{7,6},{8,7},{9,8},{10,9},{11,1... | collective-permute-start | bytes 3080 | tf_op jit(solution)/shard_map/ppermute | solution.py:13
  237.2 1.9 copy-start.17
  237.2 10.3 %collective-permute-start.22 = (f32[256,256]{1,0:T(8,128)S(1)}, f32[256,256]{1,0:T(8,128)S(1)}, u32[]{:S(2)}, u32[]{:S(2)}) collective-permute-start(f32[256,256]{1,0:T(8,128)S(1)} %fusion.3), channel_id=1, source_target_pairs={{64,0},{65,1},{66,2},{67,3},{68,4},{69,5},{70,6},{71,7},{72,8},{73... | collective-permute-start | bytes 786440 | tf_op jit(solution)/shard_map/ppermute | solution.py:13
  239.8 8.1 %copy-start.18 = (f32[256,256]{1,0:T(8,128)S(1)}, f32[256,256]{1,0:T(8,128)}, u32[]{:S(2)}) copy-start(f32[256,256]{1,0:T(8,128)} %copy-done.17) | copy-start | bytes 786436
  247.9 11.9 %copy-start.2 = (f32[4,256,256]{2,1,0:T(8,128)S(1)}, f32[4,256,256]{2,1,0:T(8,128)}, u32[]{:S(2)}) copy-start(f32[4,256,256]{2,1,0:T(8,128)} %copy-done.1) | copy-start | bytes 3145732
  249.0 10.4 %collective-permute-start.23 = (f32[256,256]{1,0:T(8,128)}, f32[256,256]{1,0:T(8,128)S(1)}, u32[]{:S(2)}, u32[]{:S(2)}) collective-permute-start(f32[256,256]{1,0:T(8,128)} %fusion.2), channel_id=1, source_target_pairs={{1,0},{2,1},{3,2},{4,3},{5,4},{6,5},{7,6},{8,7},{9,8},{10,9},{11,1... | collective-permute-start | bytes 786440 | tf_op jit(solution)/shard_map/ppermute | solution.py:13
  254.1 10.3 %all-to-all-start.4 = ((f32[4,1,256]{2,1,0:T(1,128)}), f32[4,1,256]{2,1,0:T(1,128)S(1)}, u32[]{:S(2)}, u32[]{:S(2)}) async-start(f32[4,1,256]{2,1,0:T(1,128)} %reshape.172), calls=%async_computation.4 | async-start | bytes 8192 | tf_op jit(solution)/shard_map/all_to_all | solution.py:184
  264.4 19.8 %all-to-all-start.5 = ((f32[4,256,256]{2,0,1:T(4,128)}), f32[4,256,256]{2,0,1:T(4,128)S(1)}, u32[]{:S(2)}, u32[]{:S(2)}) async-start(f32[4,256,256]{2,0,1:T(4,128)} %copy.48), calls=%async_computation.5 | async-start | bytes 2097152 | tf_op jit(solution)/shard_map/all_to_all | solution.py:184

commit v8 on v4

--- a/solution.py
+++ b/solution.py
@@ -83,11 +83,9 @@
     while distance < tm_count:
         has_right = tm_index + distance < tm_count
         round_gains.append(gain)
-        if 2 * distance >= tm_count:
-            resid_right = from_behind(resid, CHUNKS, -distance)
-        else:
-            arrived = from_behind(jnp.concatenate([gain, resid], axis=0), CHUNKS, -distance)
-            gain_right, resid_right = jnp.split(arrived, 2, axis=0)
+        resid_right = from_behind(resid, CHUNKS, -distance)
+        if 2 * distance < tm_count:
+            gain_right = from_behind(gain, CHUNKS, -distance)
         new_resid = matmul(matmul(gain, resid_right), gain.T) + resid
         resid = jnp.where(has_right, new_resid, resid)
         if 2 * distance < tm_count:

time: 285 us -> 262 us (0.919)
  waiting for transfers between devices: 109 us -> 61 us
  starting transfers between devices: 99.3 us -> 133 us
  blocking collectives: 8.97 us -> 0 us
    ppermute x24 -> x30, waiting for transfers between devices: 79.7 us -> 33 us  [from_behind(): return lax.ppermute(block, axis, route)]
    ppermute x24 -> x30, starting transfers between devices: 81.1 us -> 101 us  [from_behind(): return lax.ppermute(block, axis, route)]
    all_to_all x1 -> x0, blocking collectives: 8.97 us -> none  [steps_whole(): return lax.all_to_all(rows, 'blk', 0, 1, tiled=True)]
    all_to_all x2, starting transfers between devices: 6.76 us -> 13.7 us  [rows_of_steps(): return lax.all_to_all(whole, 'blk', 1, 0, tiled=True)]
    all_to_all x3 -> x4, starting transfers between devices: 11.4 us -> 17.8 us  [steps_whole(): return lax.all_to_all(rows, 'blk', 0, 1, tiled=True)]
    all_to_all x2, waiting for transfers between devices: 12.1 us -> 8.46 us  [rows_of_steps(): return lax.all_to_all(whole, 'blk', 1, 0, tiled=True)]
    all_to_all x3 -> x4, waiting for transfers between devices: 17.4 us -> 19.6 us  [steps_whole(): return lax.all_to_all(rows, 'blk', 0, 1, tiled=True)]
    unnamed x52 -> x46, local copies, waits for them, and re-layouts: 6.72 us -> 8.39 us
  transfers between devices with their start and end apart: 29 -> 36, of which waited for: 22 -> 16; matrix products, arithmetic and copies ran while one was open for 14% -> 20% of each run, Pallas kernels for 0% -> 0%
where the time goes in v8:
time: 262 us; the launch traced here: 260 us
  starting transfers between devices  133 us (51%)
  waiting for transfers between devices  61 us (23%)
  matrix products  44.4 us (17%)
  local copies, waits for them, and re-layouts  16.2 us (6%)
  other arithmetic  3.7 us (1%)
    ppermute x30, starting transfers between devices, from_behind(): return lax.ppermute(block, axis, route)  101 us
    ppermute x30, waiting for transfers between devices, from_behind(): return lax.ppermute(block, axis, route)  33 us
    dot_general x48, matrix products, matmul(): return jnp.matmul(left, right, precision=highest)  31.6 us
    all_to_all x4, waiting for transfers between devices, steps_whole(): return lax.all_to_all(rows, 'blk', 0, 1, tiled=True)  19.6 us
    all_to_all x4, starting transfers between devices, steps_whole(): return lax.all_to_all(rows, 'blk', 0, 1, tiled=True)  17.8 us
    all_to_all x2, starting transfers between devices, rows_of_steps(): return lax.all_to_all(whole, 'blk', 1, 0, tiled=True)  13.7 us
    dot_general x27, matrix products, matvec(): return jnp.einsum('...ij,...j->...i', left, right, precision=highest)  9.76 us
    all_to_all x2, waiting for transfers between devices, rows_of_steps(): return lax.all_to_all(whole, 'blk', 1, 0, tiled=True)  8.46 us
  transfers between devices with their start and end apart: 36, of which 16 were waited for; matrix products, arithmetic and copies ran while one was open for 20% of the time, Pallas kernels for 0%

profile of v8, /device:TPU:15, one launch (start us, length us, event | category | flops | bytes accessed | tf_op | source)
XLA Modules:
  0.0 260.2 jit_solution(11035859434600721444)
XLA Ops:
  0.6 1.2 copy-done
  1.9 1.7 fusion.56
  4.3 5.0 %all-to-all-start.2 = ((f32[4,1,256]{2,1,0:T(1,128)}), f32[4,1,256]{2,1,0:T(1,128)S(1)}, u32[]{:S(2)}, u32[]{:S(2)}) async-start(f32[4,1,256]{2,1,0:T(1,128)} %reshape.170), calls=%async_computation.2 | async-start | bytes 8192 | tf_op jit(solution)/shard_map/all_to_all | solution.py:179
  12.1 2.0 fusion
  14.1 4.2 %all-to-all-start.1 = ((f32[16,64,256]{2,1,0:T(8,128)}), f32[16,64,256]{2,1,0:T(8,128)S(1)}, u32[]{:S(2)}, u32[]{:S(2)}) async-start(f32[16,64,256]{2,1,0:T(8,128)} %fusion), calls=%async_computation.1 | async-start | bytes 2097152 | tf_op jit(solution)/shard_map/all_to_all | solution.py:179
  21.7 10.2 %all-to-all-done.1 = f32[16,64,256]{2,1,0:T(8,128)S(1)} async-done(((f32[16,64,256]{2,1,0:T(8,128)}), f32[16,64,256]{2,1,0:T(8,128)S(1)}, u32[]{:S(2)}, u32[]{:S(2)}) %all-to-all-start.1) | async-done | bytes 1048608 | tf_op jit(solution)/shard_map/all_to_all | solution.py:179
  31.9 4.3 %all-to-all-start = ((f32[16,64,256]{2,1,0:T(8,128)}), f32[16,64,256]{2,1,0:T(8,128)}, u32[]{:S(2)}, u32[]{:S(2)}) async-start(f32[16,64,256]{2,1,0:T(8,128)} %param.18), calls=%async_computation | async-start | bytes 2097152 | tf_op jit(solution)/shard_map/all_to_all | solution.py:179
  39.3 9.3 %all-to-all-done = f32[16,64,256]{2,1,0:T(8,128)} async-done(((f32[16,64,256]{2,1,0:T(8,128)}), f32[16,64,256]{2,1,0:T(8,128)}, u32[]{:S(2)}, u32[]{:S(2)}) %all-to-all-start) | async-done | bytes 1048608 | tf_op jit(solution)/shard_map/all_to_all | solution.py:179
  48.6 4.3 %all-to-all-start.4 = ((f32[16,64,256]{2,1,0:T(8,128)}), f32[16,64,256]{2,1,0:T(8,128)}, u32[]{:S(2)}, u32[]{:S(2)}) async-start(f32[16,64,256]{2,1,0:T(8,128)} %param.19), calls=%async_computation.4 | async-start | bytes 2097152 | tf_op jit(solution)/shard_map/all_to_all | solution.py:179
  53.6 1.3 copy.37
  55.0 3.3 %collective-permute-start.6 = (f32[257,256]{1,0:T(8,128)}, f32[257,256]{1,0:T(8,128)}, u32[]{:S(2)}, u32[]{:S(2)}) collective-permute-start(f32[257,256]{1,0:T(8,128)} %pad_maximum_fusion.1), channel_id=1, source_target_pairs={{0,1},{1,2},{2,3},{3,4},{4,5},{5,6},{6,7},{7,8},{8,9},{9,10},{10,1... | collective-permute-start | bytes 789512 | tf_op jit(solution)/shard_map/ppermute | solution.py:13
  61.0 7.1 %collective-permute-start = (f32[256,256]{1,0:T(8,128)}, f32[256,256]{1,0:T(8,128)}, u32[]{:S(2)}, u32[]{:S(2)}) collective-permute-start(f32[256,256]{1,0:T(8,128)} %fusion.33), channel_id=1, source_target_pairs={{1,0},{2,1},{3,2},{4,3},{5,4},{6,5},{7,6},{8,7},{9,8},{10,9},{11,1... | collective-permute-start | bytes 786440 | tf_op jit(solution)/shard_map/ppermute | solution.py:13
  68.2 1.3 copy.45
  71.5 1.1 fusion.86
  72.7 1.2 convolution_subtract_fusion
  76.4 4.8 %collective-permute-start.22 = (f32[256,256]{1,0:T(8,128)S(1)}, f32[256,256]{1,0:T(8,128)S(1)}, u32[]{:S(2)}, u32[]{:S(2)}) collective-permute-start(f32[256,256]{1,0:T(8,128)S(1)} %fusion.10), channel_id=1, source_target_pairs={{1,0},{2,1},{3,2},{4,3},{5,4},{6,5},{7,6},{8,7},{9,8},{10,9},{11,1... | collective-permute-start | bytes 786440 | tf_op jit(solution)/shard_map/ppermute | solution.py:13
  82.3 1.4 convolution_select_fusion.5
  83.7 1.9 collective-permute-start.7
  85.7 1.5 convolution_select_fusion.11
  87.2 5.1 %collective-permute-start.1 = (f32[256,256]{1,0:T(8,128)S(1)}, f32[256,256]{1,0:T(8,128)S(1)}, u32[]{:S(2)}, u32[]{:S(2)}) collective-permute-start(f32[256,256]{1,0:T(8,128)S(1)} %convolution_select_fusion.11), channel_id=1, source_target_pairs={{2,0},{3,1},{4,2},{5,3},{6,4},{7,5},{8,6},{9,7},{10,8},{11,9},{12,... | collective-permute-start | bytes 786440 | tf_op jit(solution)/shard_map/ppermute | solution.py:13
  92.3 1.3 fusion.87
  93.7 2.2 collective-permute-done.7
  96.7 6.5 %collective-permute-start.8 = (f32[257,256]{1,0:T(8,128)S(1)}, f32[257,256]{1,0:T(8,128)S(1)}, u32[]{:S(2)}, u32[]{:S(2)}) collective-permute-start(f32[257,256]{1,0:T(8,128)S(1)} %pad_maximum_fusion.3), channel_id=1, source_target_pairs={{0,4},{1,5},{2,6},{3,7},{4,8},{5,9},{6,10},{7,11},{8,12},{9,13},{1... | collective-permute-start | bytes 789512 | tf_op jit(solution)/shard_map/ppermute | solution.py:13
  103.1 1.4 fusion.8
  104.5 1.9 collective-permute-start.23
  106.8 1.9 collective-permute-start.2
  109.5 2.6 collective-permute-start.9
  113.9 4.5 %collective-permute-start.24 = (f32[256,256]{1,0:T(8,128)S(1)}, f32[256,256]{1,0:T(8,128)S(1)}, u32[]{:S(2)}, u32[]{:S(2)}) collective-permute-start(f32[256,256]{1,0:T(8,128)S(1)} %fusion.7), channel_id=1, source_target_pairs={{4,0},{5,1},{6,2},{7,3},{8,4},{9,5},{10,6},{11,7},{12,8},{13,9},{1... | collective-permute-start | bytes 786440 | tf_op jit(solution)/shard_map/ppermute | solution.py:13
  119.2 2.5 collective-permute-start.10
  122.1 3.2 %collective-permute-start.3 = (f32[256,256]{1,0:T(8,128)S(1)}, f32[256,256]{1,0:T(8,128)S(1)}, u32[]{:S(2)}, u32[]{:S(2)}) collective-permute-start(f32[256,256]{1,0:T(8,128)S(1)} %convolution_select_fusion.9), channel_id=1, source_target_pairs={{8,0},{9,1},{10,2},{11,3},{12,4},{13,5},{14,6},{15,7},{16,8},{17,9... | collective-permute-start | bytes 786440 | tf_op jit(solution)/shard_map/ppermute | solution.py:13
  125.7 3.9 %collective-permute-done.10 = f32[257,256]{1,0:T(8,128)S(1)} collective-permute-done((f32[257,256]{1,0:T(8,128)S(1)}, f32[257,256]{1,0:T(8,128)S(1)}, u32[]{:S(2)}, u32[]{:S(2)}) %collective-permute-start.10) | collective-permute-done | bytes 263200 | tf_op jit(solution)/shard_map/ppermute | solution.py:13
  130.4 2.9 %collective-permute-start.11 = (f32[257,256]{1,0:T(8,128)S(1)}, f32[257,256]{1,0:T(8,128)S(1)}, u32[]{:S(2)}, u32[]{:S(2)}) collective-permute-start(f32[257,256]{1,0:T(8,128)S(1)} %pad_maximum_fusion.6), channel_id=1, source_target_pairs={{0,32},{1,33},{2,34},{3,35},{4,36},{5,37},{6,38},{7,39},{8,40},{9,... | collective-permute-start | bytes 789512 | tf_op jit(solution)/shard_map/ppermute | solution.py:13
  133.7 1.9 collective-permute-start.25
  137.1 1.9 collective-permute-start.4
  139.4 2.6 collective-permute-start.12
  143.0 6.5 %collective-permute-start.13 = (f32[256]{0:T(256)S(1)}, f32[256]{0:T(256)S(1)}, u32[]{:S(2)}, u32[]{:S(2)}) collective-permute-start(f32[256]{0:T(256)S(1)} %add_select_fusion.7), channel_id=1, source_target_pairs={{0,1},{1,2},{2,3},{3,4},{4,5},{5,6},{6,7},{7,8},{8,9},{9,10},{10,1... | collective-permute-start | bytes 3080 | tf_op jit(solution)/shard_map/ppermute | solution.py:13
  149.5 1.1 fusion.90
  150.6 6.5 %collective-permute-done.13 = f32[256]{0:T(256)S(1)} collective-permute-done((f32[256]{0:T(256)S(1)}, f32[256]{0:T(256)S(1)}, u32[]{:S(2)}, u32[]{:S(2)}) %collective-permute-start.13) | collective-permute-done | bytes 1056 | tf_op jit(solution)/shard_map/ppermute | solution.py:13
  161.1 4.3 %collective-permute-start.14 = (f32[256]{0:T(256)S(1)}, f32[256]{0:T(256)S(1)}, u32[]{:S(2)}, u32[]{:S(2)}) collective-permute-start(f32[256]{0:T(256)S(1)} %bitcast.380), channel_id=1, source_target_pairs={{1,0},{2,1},{3,2},{4,3},{5,4},{6,5},{7,6},{8,7},{9,8},{10,9},{11,1... | collective-permute-start | bytes 3080 | tf_op jit(solution)/shard_map/ppermute | solution.py:13
  165.8 2.0 collective-permute-start.26
  167.9 1.2 fusion.79
  169.2 4.5 %collective-permute-start.15 = (f32[256]{0:T(256)S(1)}, f32[256]{0:T(256)S(1)}, u32[]{:S(2)}, u32[]{:S(2)}) collective-permute-start(f32[256]{0:T(256)S(1)} %add_select_fusion.6), channel_id=1, source_target_pairs={{2,0},{3,1},{4,2},{5,3},{6,4},{7,5},{8,6},{9,7},{10,8},{11,9},{12,... | collective-permute-start | bytes 3080 | tf_op jit(solution)/shard_map/ppermute | solution.py:13
  173.6 1.3 convolution_select_fusion.7
  175.0 3.0 %collective-permute-start.5 = (f32[256,256]{1,0:T(8,128)S(1)}, f32[256,256]{1,0:T(8,128)S(1)}, u32[]{:S(2)}, u32[]{:S(2)}) collective-permute-start(f32[256,256]{1,0:T(8,128)S(1)} %convolution_select_fusion.7), channel_id=1, source_target_pairs={{32,0},{33,1},{34,2},{35,3},{36,4},{37,5},{38,6},{39,7},{40,8},{41... | collective-permute-start | bytes 786440 | tf_op jit(solution)/shard_map/ppermute | solution.py:13
  178.3 1.9 collective-permute-start.16
  180.6 4.7 %collective-permute-done.16 = f32[256]{0:T(256)S(1)} collective-permute-done((f32[256]{0:T(256)S(1)}, f32[256]{0:T(256)S(1)}, u32[]{:S(2)}, u32[]{:S(2)}) %collective-permute-start.16) | collective-permute-done | bytes 1056 | tf_op jit(solution)/shard_map/ppermute | solution.py:13
  185.6 2.3 collective-permute-start.17
  188.4 1.9 collective-permute-start.27
  190.3 1.8 collective-permute-done.17
  192.4 1.9 collective-permute-start.18
  194.3 3.2 %collective-permute-done.27 = f32[256,256]{1,0:T(8,128)S(1)} collective-permute-done((f32[256,256]{1,0:T(8,128)S(1)}, f32[256,256]{1,0:T(8,128)S(1)}, u32[]{:S(2)}, u32[]{:S(2)}) %collective-permute-start.27) | collective-permute-done | bytes 262176 | tf_op jit(solution)/shard_map/ppermute | solution.py:13
  197.9 1.2 collective-permute-done.18
  199.4 1.9 collective-permute-start.19
  201.8 1.3 collective-permute-start.28
  204.3 1.3 collective-permute-start.20
  206.1 5.6 %collective-permute-done.20 = f32[256]{0:T(256)S(1)} collective-permute-done((f32[256]{0:T(256)S(1)}, f32[256]{0:T(256)S(1)}, u32[]{:S(2)}, u32[]{:S(2)}) %collective-permute-start.20) | collective-permute-done | bytes 1056 | tf_op jit(solution)/shard_map/ppermute | solution.py:13
  212.0 8.2 %collective-permute-start.21 = (f32[256]{0:T(256)S(1)}, f32[256]{0:T(256)S(1)}, u32[]{:S(2)}, u32[]{:S(2)}) collective-permute-start(f32[256]{0:T(256)S(1)} %add_select_fusion), channel_id=1, source_target_pairs={{1,0},{2,1},{3,2},{4,3},{5,4},{6,5},{7,6},{8,7},{9,8},{10,9},{11,1... | collective-permute-start | bytes 3080 | tf_op jit(solution)/shard_map/ppermute | solution.py:13
  222.9 1.1 fusion.2
  224.0 5.4 %collective-permute-start.29 = (f32[256,256]{1,0:T(8,128)}, f32[256,256]{1,0:T(8,128)S(1)}, u32[]{:S(2)}, u32[]{:S(2)}) collective-permute-start(f32[256,256]{1,0:T(8,128)} %fusion.2), channel_id=1, source_target_pairs={{1,0},{2,1},{3,2},{4,3},{5,4},{6,5},{7,6},{8,7},{9,8},{10,9},{11,1... | collective-permute-start | bytes 786440 | tf_op jit(solution)/shard_map/ppermute | solution.py:13
  230.5 4.6 %all-to-all-start.3 = ((f32[4,1,256]{2,1,0:T(1,128)}), f32[4,1,256]{2,1,0:T(1,128)S(1)}, u32[]{:S(2)}, u32[]{:S(2)}) async-start(f32[4,1,256]{2,1,0:T(1,128)} %reshape.172), calls=%async_computation.3 | async-start | bytes 8192 | tf_op jit(solution)/shard_map/all_to_all | solution.py:182
  238.4 1.6 copy.48
  240.1 9.1 %all-to-all-start.5 = ((f32[4,256,256]{2,0,1:T(4,128)}), f32[4,256,256]{2,0,1:T(4,128)S(1)}, u32[]{:S(2)}, u32[]{:S(2)}) async-start(f32[4,256,256]{2,0,1:T(4,128)} %copy.48), calls=%async_computation.5 | async-start | bytes 2097152 | tf_op jit(solution)/shard_map/all_to_all | solution.py:182
  250.6 8.5 %all-to-all-done.5 = f32[4,256,256]{2,0,1:T(4,128)S(1)} async-done(((f32[4,256,256]{2,0,1:T(4,128)}), f32[4,256,256]{2,0,1:T(4,128)S(1)}, u32[]{:S(2)}, u32[]{:S(2)}) %all-to-all-start.5) | async-done | bytes 1048608 | tf_op jit(solution)/shard_map/all_to_all | solution.py:182
  259.0 1.2 copy.49
  (208 shorter events, 45.2 us)
Async XLA Ops:
  0.6 1.2 copy-start
  1.9 7.5 %copy-start.14 = (f32[256,256]{1,0:T(8,128)S(1)}, f32[256,256]{1,0:T(8,128)}, u32[]{:S(2)}) copy-start(f32[256,256]{1,0:T(8,128)} %param.10) | copy-start | bytes 786436
  4.3 9.8 %all-to-all-start.2 = ((f32[4,1,256]{2,1,0:T(1,128)}), f32[4,1,256]{2,1,0:T(1,128)S(1)}, u32[]{:S(2)}, u32[]{:S(2)}) async-start(f32[4,1,256]{2,1,0:T(1,128)} %reshape.170), calls=%async_computation.2 | async-start | bytes 8192 | tf_op jit(solution)/shard_map/all_to_all | solution.py:179
  9.3 0.7 copy-start.17
  9.3 1.0 copy-start.15
  10.3 0.7 copy-start.18
  14.1 17.9 %all-to-all-start.1 = ((f32[16,64,256]{2,1,0:T(8,128)}), f32[16,64,256]{2,1,0:T(8,128)S(1)}, u32[]{:S(2)}, u32[]{:S(2)}) async-start(f32[16,64,256]{2,1,0:T(8,128)} %fusion), calls=%async_computation.1 | async-start | bytes 2097152 | tf_op jit(solution)/shard_map/all_to_all | solution.py:179
  18.3 0.7 copy-start.19
  31.9 16.7 %all-to-all-start = ((f32[16,64,256]{2,1,0:T(8,128)}), f32[16,64,256]{2,1,0:T(8,128)}, u32[]{:S(2)}, u32[]{:S(2)}) async-start(f32[16,64,256]{2,1,0:T(8,128)} %param.18), calls=%async_computation | async-start | bytes 2097152 | tf_op jit(solution)/shard_map/all_to_all | solution.py:179
  37.9 15.0 %copy-start.6 = (f32[256,256]{1,0:T(8,128)}, f32[256,256]{1,0:T(8,128)S(1)}, u32[]{:S(2)}) copy-start(f32[256,256]{1,0:T(8,128)S(1)} %get-tuple-element.14) | copy-start | bytes 786436
  37.9 0.7 copy-start.16
  48.6 19.5 %all-to-all-start.4 = ((f32[16,64,256]{2,1,0:T(8,128)}), f32[16,64,256]{2,1,0:T(8,128)}, u32[]{:S(2)}, u32[]{:S(2)}) async-start(f32[16,64,256]{2,1,0:T(8,128)} %param.19), calls=%async_computation.4 | async-start | bytes 2097152 | tf_op jit(solution)/shard_map/all_to_all | solution.py:179
  55.0 26.4 %collective-permute-start.6 = (f32[257,256]{1,0:T(8,128)}, f32[257,256]{1,0:T(8,128)}, u32[]{:S(2)}, u32[]{:S(2)}) collective-permute-start(f32[257,256]{1,0:T(8,128)} %pad_maximum_fusion.1), channel_id=1, source_target_pairs={{0,1},{1,2},{2,3},{3,4},{4,5},{5,6},{6,7},{7,8},{8,9},{9,10},{10,1... | collective-permute-start | bytes 789512 | tf_op jit(solution)/shard_map/ppermute | solution.py:13
  59.1 0.8 copy-start.3
  61.0 24.6 %collective-permute-start = (f32[256,256]{1,0:T(8,128)}, f32[256,256]{1,0:T(8,128)}, u32[]{:S(2)}, u32[]{:S(2)}) collective-permute-start(f32[256,256]{1,0:T(8,128)} %fusion.33), channel_id=1, source_target_pairs={{1,0},{2,1},{3,2},{4,3},{5,4},{6,5},{7,6},{8,7},{9,8},{10,9},{11,1... | collective-permute-start | bytes 786440 | tf_op jit(solution)/shard_map/ppermute | solution.py:13
  69.5 1.1 copy-start.8
  73.9 1.4 copy-start.1
  74.5 1.0 copy-start.4
  76.4 5.0 %copy-start.7 = (f32[256,256]{1,0:T(8,128)S(1)}, f32[256,256]{1,0:T(8,128)}, u32[]{:S(2)}) copy-start(f32[256,256]{1,0:T(8,128)} %copy-done.6) | copy-start | bytes 786436
  76.4 15.9 %collective-permute-start.22 = (f32[256,256]{1,0:T(8,128)S(1)}, f32[256,256]{1,0:T(8,128)S(1)}, u32[]{:S(2)}, u32[]{:S(2)}) collective-permute-start(f32[256,256]{1,0:T(8,128)S(1)} %fusion.10), channel_id=1, source_target_pairs={{1,0},{2,1},{3,2},{4,3},{5,4},{6,5},{7,6},{8,7},{9,8},{10,9},{11,1... | collective-permute-start | bytes 786440 | tf_op jit(solution)/shard_map/ppermute | solution.py:13
  83.7 12.2 %collective-permute-start.7 = (f32[257,256]{1,0:T(8,128)S(1)}, f32[257,256]{1,0:T(8,128)S(1)}, u32[]{:S(2)}, u32[]{:S(2)}) collective-permute-start(f32[257,256]{1,0:T(8,128)S(1)} %pad_maximum_fusion.2), channel_id=1, source_target_pairs={{0,2},{1,3},{2,4},{3,5},{4,6},{5,7},{6,8},{7,9},{8,10},{9,11},{10,... | collective-permute-start | bytes 789512 | tf_op jit(solution)/shard_map/ppermute | solution.py:13
  87.2 19.3 %collective-permute-start.1 = (f32[256,256]{1,0:T(8,128)S(1)}, f32[256,256]{1,0:T(8,128)S(1)}, u32[]{:S(2)}, u32[]{:S(2)}) collective-permute-start(f32[256,256]{1,0:T(8,128)S(1)} %convolution_select_fusion.11), channel_id=1, source_target_pairs={{2,0},{3,1},{4,2},{5,3},{6,4},{7,5},{8,6},{9,7},{10,8},{11,9},{12,... | collective-permute-start | bytes 786440 | tf_op jit(solution)/shard_map/ppermute | solution.py:13
  96.7 12.1 %collective-permute-start.8 = (f32[257,256]{1,0:T(8,128)S(1)}, f32[257,256]{1,0:T(8,128)S(1)}, u32[]{:S(2)}, u32[]{:S(2)}) collective-permute-start(f32[257,256]{1,0:T(8,128)S(1)} %pad_maximum_fusion.3), channel_id=1, source_target_pairs={{0,4},{1,5},{2,6},{3,7},{4,8},{5,9},{6,10},{7,11},{8,12},{9,13},{1... | collective-permute-start | bytes 789512 | tf_op jit(solution)/shard_map/ppermute | solution.py:13
  104.5 8.6 %collective-permute-start.23 = (f32[256,256]{1,0:T(8,128)S(1)}, f32[256,256]{1,0:T(8,128)S(1)}, u32[]{:S(2)}, u32[]{:S(2)}) collective-permute-start(f32[256,256]{1,0:T(8,128)S(1)} %fusion.8), channel_id=1, source_target_pairs={{2,0},{3,1},{4,2},{5,3},{6,4},{7,5},{8,6},{9,7},{10,8},{11,9},{12,... | collective-permute-start | bytes 786440 | tf_op jit(solution)/shard_map/ppermute | solution.py:13
  106.8 14.9 %collective-permute-start.2 = (f32[256,256]{1,0:T(8,128)S(1)}, f32[256,256]{1,0:T(8,128)S(1)}, u32[]{:S(2)}, u32[]{:S(2)}) collective-permute-start(f32[256,256]{1,0:T(8,128)S(1)} %convolution_select_fusion.10), channel_id=1, source_target_pairs={{4,0},{5,1},{6,2},{7,3},{8,4},{9,5},{10,6},{11,7},{12,8},{13,9},{1... | collective-permute-start | bytes 786440 | tf_op jit(solution)/shard_map/ppermute | solution.py:13
  109.5 8.9 %collective-permute-start.9 = (f32[257,256]{1,0:T(8,128)S(1)}, f32[257,256]{1,0:T(8,128)S(1)}, u32[]{:S(2)}, u32[]{:S(2)}) collective-permute-start(f32[257,256]{1,0:T(8,128)S(1)} %pad_maximum_fusion.4), channel_id=1, source_target_pairs={{0,8},{1,9},{2,10},{3,11},{4,12},{5,13},{6,14},{7,15},{8,16},{9,17... | collective-permute-start | bytes 789512 | tf_op jit(solution)/shard_map/ppermute | solution.py:13
  113.9 11.4 %collective-permute-start.24 = (f32[256,256]{1,0:T(8,128)S(1)}, f32[256,256]{1,0:T(8,128)S(1)}, u32[]{:S(2)}, u32[]{:S(2)}) collective-permute-start(f32[256,256]{1,0:T(8,128)S(1)} %fusion.7), channel_id=1, source_target_pairs={{4,0},{5,1},{6,2},{7,3},{8,4},{9,5},{10,6},{11,7},{12,8},{13,9},{1... | collective-permute-start | bytes 786440 | tf_op jit(solution)/shard_map/ppermute | solution.py:13
  119.2 10.4 %collective-permute-start.10 = (f32[257,256]{1,0:T(8,128)S(1)}, f32[257,256]{1,0:T(8,128)S(1)}, u32[]{:S(2)}, u32[]{:S(2)}) collective-permute-start(f32[257,256]{1,0:T(8,128)S(1)} %pad_maximum_fusion.5), channel_id=1, source_target_pairs={{0,16},{1,17},{2,18},{3,19},{4,20},{5,21},{6,22},{7,23},{8,24},{9,... | collective-permute-start | bytes 789512 | tf_op jit(solution)/shard_map/ppermute | solution.py:13
  122.1 14.6 %collective-permute-start.3 = (f32[256,256]{1,0:T(8,128)S(1)}, f32[256,256]{1,0:T(8,128)S(1)}, u32[]{:S(2)}, u32[]{:S(2)}) collective-permute-start(f32[256,256]{1,0:T(8,128)S(1)} %convolution_select_fusion.9), channel_id=1, source_target_pairs={{8,0},{9,1},{10,2},{11,3},{12,4},{13,5},{14,6},{15,7},{16,8},{17,9... | collective-permute-start | bytes 786440 | tf_op jit(solution)/shard_map/ppermute | solution.py:13
  130.4 8.7 %collective-permute-start.11 = (f32[257,256]{1,0:T(8,128)S(1)}, f32[257,256]{1,0:T(8,128)S(1)}, u32[]{:S(2)}, u32[]{:S(2)}) collective-permute-start(f32[257,256]{1,0:T(8,128)S(1)} %pad_maximum_fusion.6), channel_id=1, source_target_pairs={{0,32},{1,33},{2,34},{3,35},{4,36},{5,37},{6,38},{7,39},{8,40},{9,... | collective-permute-start | bytes 789512 | tf_op jit(solution)/shard_map/ppermute | solution.py:13
  133.7 3.4 %copy-start.10 = (f32[256,256]{1,0:T(8,128)}, f32[256,256]{1,0:T(8,128)S(1)}, u32[]{:S(2)}) copy-start(f32[256,256]{1,0:T(8,128)S(1)} %fusion.6) | copy-start | bytes 786436
  133.7 15.8 %collective-permute-start.25 = (f32[256,256]{1,0:T(8,128)S(1)}, f32[256,256]{1,0:T(8,128)S(1)}, u32[]{:S(2)}, u32[]{:S(2)}) collective-permute-start(f32[256,256]{1,0:T(8,128)S(1)} %fusion.6), channel_id=1, source_target_pairs={{8,0},{9,1},{10,2},{11,3},{12,4},{13,5},{14,6},{15,7},{16,8},{17,9... | collective-permute-start | bytes 786440 | tf_op jit(solution)/shard_map/ppermute | solution.py:13
  137.1 36.5 %collective-permute-start.4 = (f32[256,256]{1,0:T(8,128)S(1)}, f32[256,256]{1,0:T(8,128)}, u32[]{:S(2)}, u32[]{:S(2)}) collective-permute-start(f32[256,256]{1,0:T(8,128)S(1)} %convolution_select_fusion.8), channel_id=1, source_target_pairs={{16,0},{17,1},{18,2},{19,3},{20,4},{21,5},{22,6},{23,7},{24,8},{25... | collective-permute-start | bytes 786440 | tf_op jit(solution)/shard_map/ppermute | solution.py:13
  139.4 3.3 %collective-permute-start.12 = (f32[256]{0:T(256)S(1)}, f32[256]{0:T(256)S(1)}, u32[]{:S(2)}, u32[]{:S(2)}) collective-permute-start(f32[256]{0:T(256)S(1)} %add_select_fusion.8), channel_id=1, source_target_pairs={{0,64},{1,65},{2,66},{3,67},{4,68},{5,69},{6,70},{7,71},{8,72},{9,... | collective-permute-start | bytes 3080 | tf_op jit(solution)/shard_map/ppermute | solution.py:13
  143.0 14.2 %collective-permute-start.13 = (f32[256]{0:T(256)S(1)}, f32[256]{0:T(256)S(1)}, u32[]{:S(2)}, u32[]{:S(2)}) collective-permute-start(f32[256]{0:T(256)S(1)} %add_select_fusion.7), channel_id=1, source_target_pairs={{0,1},{1,2},{2,3},{3,4},{4,5},{5,6},{6,7},{7,8},{8,9},{9,10},{10,1... | collective-permute-start | bytes 3080 | tf_op jit(solution)/shard_map/ppermute | solution.py:13
  158.7 6.7 %copy-start.11 = (f32[256,256]{1,0:T(8,128)S(1)}, f32[256,256]{1,0:T(8,128)}, u32[]{:S(2)}) copy-start(f32[256,256]{1,0:T(8,128)} %copy-done.10) | copy-start | bytes 786436
  159.8 1.0 copy-start.5
  160.4 5.1 %copy-start.9 = (f32[256,256]{1,0:T(8,128)S(1)}, f32[256,256]{1,0:T(8,128)}, u32[]{:S(2)}) copy-start(f32[256,256]{1,0:T(8,128)} %fusion.90) | copy-start | bytes 786436
  161.1 6.8 %collective-permute-start.14 = (f32[256]{0:T(256)S(1)}, f32[256]{0:T(256)S(1)}, u32[]{:S(2)}, u32[]{:S(2)}) collective-permute-start(f32[256]{0:T(256)S(1)} %bitcast.380), channel_id=1, source_target_pairs={{1,0},{2,1},{3,2},{4,3},{5,4},{6,5},{7,6},{8,7},{9,8},{10,9},{11,1... | collective-permute-start | bytes 3080 | tf_op jit(solution)/shard_map/ppermute | solution.py:13
  165.8 14.4 %collective-permute-start.26 = (f32[256,256]{1,0:T(8,128)S(1)}, f32[256,256]{1,0:T(8,128)S(1)}, u32[]{:S(2)}, u32[]{:S(2)}) collective-permute-start(f32[256,256]{1,0:T(8,128)S(1)} %fusion.5), channel_id=1, source_target_pairs={{16,0},{17,1},{18,2},{19,3},{20,4},{21,5},{22,6},{23,7},{24,8},{25... | collective-permute-start | bytes 786440 | tf_op jit(solution)/shard_map/ppermute | solution.py:13
  169.2 8.8 %collective-permute-start.15 = (f32[256]{0:T(256)S(1)}, f32[256]{0:T(256)S(1)}, u32[]{:S(2)}, u32[]{:S(2)}) collective-permute-start(f32[256]{0:T(256)S(1)} %add_select_fusion.6), channel_id=1, source_target_pairs={{2,0},{3,1},{4,2},{5,3},{6,4},{7,5},{8,6},{9,7},{10,8},{11,9},{12,... | collective-permute-start | bytes 3080 | tf_op jit(solution)/shard_map/ppermute | solution.py:13
  175.0 30.7 %collective-permute-start.5 = (f32[256,256]{1,0:T(8,128)S(1)}, f32[256,256]{1,0:T(8,128)S(1)}, u32[]{:S(2)}, u32[]{:S(2)}) collective-permute-start(f32[256,256]{1,0:T(8,128)S(1)} %convolution_select_fusion.7), channel_id=1, source_target_pairs={{32,0},{33,1},{34,2},{35,3},{36,4},{37,5},{38,6},{39,7},{40,8},{41... | collective-permute-start | bytes 786440 | tf_op jit(solution)/shard_map/ppermute | solution.py:13
  178.3 7.0 %collective-permute-start.16 = (f32[256]{0:T(256)S(1)}, f32[256]{0:T(256)S(1)}, u32[]{:S(2)}, u32[]{:S(2)}) collective-permute-start(f32[256]{0:T(256)S(1)} %add_select_fusion.5), channel_id=1, source_target_pairs={{4,0},{5,1},{6,2},{7,3},{8,4},{9,5},{10,6},{11,7},{12,8},{13,9},{1... | collective-permute-start | bytes 3080 | tf_op jit(solution)/shard_map/ppermute | solution.py:13
  185.6 6.4 %collective-permute-start.17 = (f32[256]{0:T(256)S(1)}, f32[256]{0:T(256)S(1)}, u32[]{:S(2)}, u32[]{:S(2)}) collective-permute-start(f32[256]{0:T(256)S(1)} %add_select_fusion.4), channel_id=1, source_target_pairs={{8,0},{9,1},{10,2},{11,3},{12,4},{13,5},{14,6},{15,7},{16,8},{17,9... | collective-permute-start | bytes 3080 | tf_op jit(solution)/shard_map/ppermute | solution.py:13
  188.4 9.1 %collective-permute-start.27 = (f32[256,256]{1,0:T(8,128)S(1)}, f32[256,256]{1,0:T(8,128)S(1)}, u32[]{:S(2)}, u32[]{:S(2)}) collective-permute-start(f32[256,256]{1,0:T(8,128)S(1)} %fusion.4), channel_id=1, source_target_pairs={{32,0},{33,1},{34,2},{35,3},{36,4},{37,5},{38,6},{39,7},{40,8},{41... | collective-permute-start | bytes 786440 | tf_op jit(solution)/shard_map/ppermute | solution.py:13
  192.4 6.7 %collective-permute-start.18 = (f32[256]{0:T(256)S(1)}, f32[256]{0:T(256)S(1)}, u32[]{:S(2)}, u32[]{:S(2)}) collective-permute-start(f32[256]{0:T(256)S(1)} %add_select_fusion.3), channel_id=1, source_target_pairs={{16,0},{17,1},{18,2},{19,3},{20,4},{21,5},{22,6},{23,7},{24,8},{25... | collective-permute-start | bytes 3080 | tf_op jit(solution)/shard_map/ppermute | solution.py:13
  199.4 4.6 %collective-permute-start.19 = (f32[256]{0:T(256)S(1)}, f32[256]{0:T(256)S(1)}, u32[]{:S(2)}, u32[]{:S(2)}) collective-permute-start(f32[256]{0:T(256)S(1)} %add_select_fusion.2), channel_id=1, source_target_pairs={{32,0},{33,1},{34,2},{35,3},{36,4},{37,5},{38,6},{39,7},{40,8},{41... | collective-permute-start | bytes 3080 | tf_op jit(solution)/shard_map/ppermute | solution.py:13
  201.8 4.3 %copy-start.12 = (f32[256,256]{1,0:T(8,128)}, f32[256,256]{1,0:T(8,128)S(1)}, u32[]{:S(2)}) copy-start(f32[256,256]{1,0:T(8,128)S(1)} %fusion.3) | copy-start | bytes 786436
  201.8 20.1 %collective-permute-start.28 = (f32[256,256]{1,0:T(8,128)S(1)}, f32[256,256]{1,0:T(8,128)S(1)}, u32[]{:S(2)}, u32[]{:S(2)}) collective-permute-start(f32[256,256]{1,0:T(8,128)S(1)} %fusion.3), channel_id=1, source_target_pairs={{64,0},{65,1},{66,2},{67,3},{68,4},{69,5},{70,6},{71,7},{72,8},{73... | collective-permute-start | bytes 786440 | tf_op jit(solution)/shard_map/ppermute | solution.py:13
  204.3 7.3 %collective-permute-start.20 = (f32[256]{0:T(256)S(1)}, f32[256]{0:T(256)S(1)}, u32[]{:S(2)}, u32[]{:S(2)}) collective-permute-start(f32[256]{0:T(256)S(1)} %add_select_fusion.1), channel_id=1, source_target_pairs={{64,0},{65,1},{66,2},{67,3},{68,4},{69,5},{70,6},{71,7},{72,8},{73... | collective-permute-start | bytes 3080 | tf_op jit(solution)/shard_map/ppermute | solution.py:13
  212.0 8.7 %collective-permute-start.21 = (f32[256]{0:T(256)S(1)}, f32[256]{0:T(256)S(1)}, u32[]{:S(2)}, u32[]{:S(2)}) collective-permute-start(f32[256]{0:T(256)S(1)} %add_select_fusion), channel_id=1, source_target_pairs={{1,0},{2,1},{3,2},{4,3},{5,4},{6,5},{7,6},{8,7},{9,8},{10,9},{11,1... | collective-permute-start | bytes 3080 | tf_op jit(solution)/shard_map/ppermute | solution.py:13
  221.9 1.0 copy-start.13
  222.9 12.6 %copy-start.2 = (f32[4,256,256]{2,1,0:T(8,128)S(1)}, f32[4,256,256]{2,1,0:T(8,128)}, u32[]{:S(2)}) copy-start(f32[4,256,256]{2,1,0:T(8,128)} %copy-done.1) | copy-start | bytes 3145732
  224.0 11.1 %collective-permute-start.29 = (f32[256,256]{1,0:T(8,128)}, f32[256,256]{1,0:T(8,128)S(1)}, u32[]{:S(2)}, u32[]{:S(2)}) collective-permute-start(f32[256,256]{1,0:T(8,128)} %fusion.2), channel_id=1, source_target_pairs={{1,0},{2,1},{3,2},{4,3},{5,4},{6,5},{7,6},{8,7},{9,8},{10,9},{11,1... | collective-permute-start | bytes 786440 | tf_op jit(solution)/shard_map/ppermute | solution.py:13
  230.5 9.6 %all-to-all-start.3 = ((f32[4,1,256]{2,1,0:T(1,128)}), f32[4,1,256]{2,1,0:T(1,128)S(1)}, u32[]{:S(2)}, u32[]{:S(2)}) async-start(f32[4,1,256]{2,1,0:T(1,128)} %reshape.172), calls=%async_computation.3 | async-start | bytes 8192 | tf_op jit(solution)/shard_map/all_to_all | solution.py:182
  240.1 18.9 %all-to-all-start.5 = ((f32[4,256,256]{2,0,1:T(4,128)}), f32[4,256,256]{2,0,1:T(4,128)S(1)}, u32[]{:S(2)}, u32[]{:S(2)}) async-start(f32[4,256,256]{2,0,1:T(4,128)} %copy.48), calls=%async_computation.5 | async-start | bytes 2097152 | tf_op jit(solution)/shard_map/all_to_all | solution.py:182

commit v9 on v5

--- a/solution.py
+++ b/solution.py
@@ -83,16 +83,15 @@
     while 2 * distance < tm_count:
         has_right = tm_index + distance < tm_count
         round_gains.append(gain)
-        arrived = from_behind(jnp.concatenate([gain, resid], axis=0), CHUNKS, -distance)
-        gain_right, resid_right = jnp.split(arrived, 2, axis=0)
+        resid_right = from_behind(resid, CHUNKS, -distance)
+        gain_right = from_behind(gain, CHUNKS, -distance)
         new_resid = matmul(matmul(gain, resid_right), gain.T) + resid
         resid = jnp.where(has_right, new_resid, resid)
         gain = jnp.where(has_right, matmul(gain, gain_right), gain)
         distance *= 2
     round_gains.append(gain)
-    gain_next, resid_next = jnp.split(
-        from_behind(jnp.concatenate([gain, resid], axis=0), CHUNKS, -1), 2, axis=0
-    )
+    gain_next = from_behind(gain, CHUNKS, -1)
+    resid_next = from_behind(resid, CHUNKS, -1)
     resid_far = from_behind(resid, CHUNKS, -(distance + 1))
     has_far = tm_index + distance + 1 < tm_count
     cov_after = jnp.where(

time: 287 us -> 261 us (0.909)
  waiting for transfers between devices: 110 us -> 69.4 us
  starting transfers between devices: 98.2 us -> 122 us
  blocking collectives: 8.97 us -> 0 us
  matrix products: 40.3 us -> 44.6 us
    ppermute x24 -> x31, waiting for transfers between devices: 81.1 us -> 36.7 us  [from_behind(): return lax.ppermute(block, axis, route)]
    ppermute x24 -> x31, starting transfers between devices: 80 us -> 96.5 us  [from_behind(): return lax.ppermute(block, axis, route)]
    all_to_all x1 -> x0, blocking collectives: 8.97 us -> none  [steps_whole(): return lax.all_to_all(rows, 'blk', 0, 1, tiled=True)]
    all_to_all x3 -> x4, starting transfers between devices: 11.4 us -> 17.8 us  [steps_whole(): return lax.all_to_all(rows, 'blk', 0, 1, tiled=True)]
    dot_general x48, matrix products: 28.8 us -> 31.9 us  [matmul(): return jnp.matmul(left, right, precision=highest)]
    all_to_all x3 -> x4, waiting for transfers between devices: 17.4 us -> 19.7 us  [steps_whole(): return lax.all_to_all(rows, 'blk', 0, 1, tiled=True)]
    unnamed x52 -> x40, local copies, waits for them, and re-layouts: 8.15 us -> 8.18 us
  transfers between devices with their start and end apart: 29 -> 37, of which waited for: 22 -> 15; matrix products, arithmetic and copies ran while one was open for 15% -> 21% of each run, Pallas kernels for 0% -> 0%
where the time goes in v9:
time: 261 us; the launch traced here: 258 us
  starting transfers between devices  122 us (47%)
  waiting for transfers between devices  69.4 us (27%)
  matrix products  44.6 us (17%)
  local copies, waits for them, and re-layouts  16 us (6%)
  other arithmetic  3.57 us (1%)
    ppermute x31, starting transfers between devices, from_behind(): return lax.ppermute(block, axis, route)  96.5 us
    ppermute x31, waiting for transfers between devices, from_behind(): return lax.ppermute(block, axis, route)  36.7 us
    dot_general x48, matrix products, matmul(): return jnp.matmul(left, right, precision=highest)  31.9 us
    all_to_all x4, waiting for transfers between devices, steps_whole(): return lax.all_to_all(rows, 'blk', 0, 1, tiled=True)  19.7 us
    all_to_all x4, starting transfers between devices, steps_whole(): return lax.all_to_all(rows, 'blk', 0, 1, tiled=True)  17.8 us
    all_to_all x2, waiting for transfers between devices, rows_of_steps(): return lax.all_to_all(whole, 'blk', 1, 0, tiled=True)  13 us
    dot_general x27, matrix products, matvec(): return jnp.einsum('...ij,...j->...i', left, right, precision=highest)  9.72 us
    unnamed x40, local copies, waits for them, and re-layouts  8.18 us
  transfers between devices with their start and end apart: 37, of which 15 were waited for; matrix products, arithmetic and copies ran while one was open for 21% of the time, Pallas kernels for 0%

profile of v9, /device:TPU:15, one launch (start us, length us, event | category | flops | bytes accessed | tf_op | source)
XLA Modules:
  0.0 257.8 jit_solution(7360492732490625932)
XLA Ops:
  0.6 1.2 copy-done
  1.9 1.7 fusion.54
  4.3 5.0 %all-to-all-start.2 = ((f32[4,1,256]{2,1,0:T(1,128)}), f32[4,1,256]{2,1,0:T(1,128)S(1)}, u32[]{:S(2)}, u32[]{:S(2)}) async-start(f32[4,1,256]{2,1,0:T(1,128)} %reshape.170), calls=%async_computation.2 | async-start | bytes 8192 | tf_op jit(solution)/shard_map/all_to_all | solution.py:184
  12.1 2.0 fusion
  14.1 4.2 %all-to-all-start.1 = ((f32[16,64,256]{2,1,0:T(8,128)}), f32[16,64,256]{2,1,0:T(8,128)S(1)}, u32[]{:S(2)}, u32[]{:S(2)}) async-start(f32[16,64,256]{2,1,0:T(8,128)} %fusion), calls=%async_computation.1 | async-start | bytes 2097152 | tf_op jit(solution)/shard_map/all_to_all | solution.py:184
  21.5 10.4 %all-to-all-done.1 = f32[16,64,256]{2,1,0:T(8,128)S(1)} async-done(((f32[16,64,256]{2,1,0:T(8,128)}), f32[16,64,256]{2,1,0:T(8,128)S(1)}, u32[]{:S(2)}, u32[]{:S(2)}) %all-to-all-start.1) | async-done | bytes 1048608 | tf_op jit(solution)/shard_map/all_to_all | solution.py:184
  31.9 4.3 %all-to-all-start = ((f32[16,64,256]{2,1,0:T(8,128)}), f32[16,64,256]{2,1,0:T(8,128)}, u32[]{:S(2)}, u32[]{:S(2)}) async-start(f32[16,64,256]{2,1,0:T(8,128)} %param.18), calls=%async_computation | async-start | bytes 2097152 | tf_op jit(solution)/shard_map/all_to_all | solution.py:184
  39.3 9.3 %all-to-all-done = f32[16,64,256]{2,1,0:T(8,128)} async-done(((f32[16,64,256]{2,1,0:T(8,128)}), f32[16,64,256]{2,1,0:T(8,128)}, u32[]{:S(2)}, u32[]{:S(2)}) %all-to-all-start) | async-done | bytes 1048608 | tf_op jit(solution)/shard_map/all_to_all | solution.py:184
  48.6 4.3 %all-to-all-start.4 = ((f32[16,64,256]{2,1,0:T(8,128)}), f32[16,64,256]{2,1,0:T(8,128)}, u32[]{:S(2)}, u32[]{:S(2)}) async-start(f32[16,64,256]{2,1,0:T(8,128)} %param.19), calls=%async_computation.4 | async-start | bytes 2097152 | tf_op jit(solution)/shard_map/all_to_all | solution.py:184
  53.7 1.3 copy.37
  55.0 3.3 %collective-permute-start.6 = (f32[257,256]{1,0:T(8,128)}, f32[257,256]{1,0:T(8,128)}, u32[]{:S(2)}, u32[]{:S(2)}) collective-permute-start(f32[257,256]{1,0:T(8,128)} %pad_maximum_fusion.1), channel_id=1, source_target_pairs={{0,1},{1,2},{2,3},{3,4},{4,5},{5,6},{6,7},{7,8},{8,9},{9,10},{10,1... | collective-permute-start | bytes 789512 | tf_op jit(solution)/shard_map/ppermute | solution.py:13
  61.0 7.1 %collective-permute-start = (f32[256,256]{1,0:T(8,128)}, f32[256,256]{1,0:T(8,128)}, u32[]{:S(2)}, u32[]{:S(2)}) collective-permute-start(f32[256,256]{1,0:T(8,128)} %fusion.34), channel_id=1, source_target_pairs={{1,0},{2,1},{3,2},{4,3},{5,4},{6,5},{7,6},{8,7},{9,8},{10,9},{11,1... | collective-permute-start | bytes 786440 | tf_op jit(solution)/shard_map/ppermute | solution.py:13
  68.2 1.3 copy.45
  72.7 1.2 convolution_subtract_fusion
  76.4 4.9 %collective-permute-start.23 = (f32[256,256]{1,0:T(8,128)S(1)}, f32[256,256]{1,0:T(8,128)S(1)}, u32[]{:S(2)}, u32[]{:S(2)}) collective-permute-start(f32[256,256]{1,0:T(8,128)S(1)} %fusion.11), channel_id=1, source_target_pairs={{1,0},{2,1},{3,2},{4,3},{5,4},{6,5},{7,6},{8,7},{9,8},{10,9},{11,1... | collective-permute-start | bytes 786440 | tf_op jit(solution)/shard_map/ppermute | solution.py:13
  82.3 1.4 convolution_select_fusion.5
  83.8 1.9 collective-permute-start.7
  85.7 1.5 convolution_select_fusion.11
  87.2 5.1 %collective-permute-start.1 = (f32[256,256]{1,0:T(8,128)S(1)}, f32[256,256]{1,0:T(8,128)S(1)}, u32[]{:S(2)}, u32[]{:S(2)}) collective-permute-start(f32[256,256]{1,0:T(8,128)S(1)} %convolution_select_fusion.11), channel_id=1, source_target_pairs={{2,0},{3,1},{4,2},{5,3},{6,4},{7,5},{8,6},{9,7},{10,8},{11,9},{12,... | collective-permute-start | bytes 786440 | tf_op jit(solution)/shard_map/ppermute | solution.py:13
  92.4 1.3 fusion.84
  93.7 2.2 collective-permute-done.7
  96.7 6.4 %collective-permute-start.8 = (f32[257,256]{1,0:T(8,128)S(1)}, f32[257,256]{1,0:T(8,128)S(1)}, u32[]{:S(2)}, u32[]{:S(2)}) collective-permute-start(f32[257,256]{1,0:T(8,128)S(1)} %pad_maximum_fusion.3), channel_id=1, source_target_pairs={{0,4},{1,5},{2,6},{3,7},{4,8},{5,9},{6,10},{7,11},{8,12},{9,13},{1... | collective-permute-start | bytes 789512 | tf_op jit(solution)/shard_map/ppermute | solution.py:13
  103.2 1.4 fusion.8
  104.5 1.9 collective-permute-start.24
  106.9 1.9 collective-permute-start.2
  109.6 2.6 collective-permute-start.9
  114.0 4.5 %collective-permute-start.25 = (f32[256,256]{1,0:T(8,128)S(1)}, f32[256,256]{1,0:T(8,128)S(1)}, u32[]{:S(2)}, u32[]{:S(2)}) collective-permute-start(f32[256,256]{1,0:T(8,128)S(1)} %fusion.7), channel_id=1, source_target_pairs={{4,0},{5,1},{6,2},{7,3},{8,4},{9,5},{10,6},{11,7},{12,8},{13,9},{1... | collective-permute-start | bytes 786440 | tf_op jit(solution)/shard_map/ppermute | solution.py:13
  119.2 2.6 collective-permute-start.10
  122.2 3.1 %collective-permute-start.3 = (f32[256,256]{1,0:T(8,128)S(1)}, f32[256,256]{1,0:T(8,128)S(1)}, u32[]{:S(2)}, u32[]{:S(2)}) collective-permute-start(f32[256,256]{1,0:T(8,128)S(1)} %convolution_select_fusion.9), channel_id=1, source_target_pairs={{8,0},{9,1},{10,2},{11,3},{12,4},{13,5},{14,6},{15,7},{16,8},{17,9... | collective-permute-start | bytes 786440 | tf_op jit(solution)/shard_map/ppermute | solution.py:13
  125.7 3.9 %collective-permute-done.10 = f32[257,256]{1,0:T(8,128)S(1)} collective-permute-done((f32[257,256]{1,0:T(8,128)S(1)}, f32[257,256]{1,0:T(8,128)S(1)}, u32[]{:S(2)}, u32[]{:S(2)}) %collective-permute-start.10) | collective-permute-done | bytes 263200 | tf_op jit(solution)/shard_map/ppermute | solution.py:13
  130.4 2.9 %collective-permute-start.11 = (f32[257,256]{1,0:T(8,128)S(1)}, f32[257,256]{1,0:T(8,128)S(1)}, u32[]{:S(2)}, u32[]{:S(2)}) collective-permute-start(f32[257,256]{1,0:T(8,128)S(1)} %pad_maximum_fusion.6), channel_id=1, source_target_pairs={{0,32},{1,33},{2,34},{3,35},{4,36},{5,37},{6,38},{7,39},{8,40},{9,... | collective-permute-start | bytes 789512 | tf_op jit(solution)/shard_map/ppermute | solution.py:13
  133.7 1.9 collective-permute-start.26
  137.1 1.9 collective-permute-start.4
  139.4 2.6 collective-permute-start.12
  143.0 6.5 %collective-permute-start.13 = (f32[256]{0:T(256)S(1)}, f32[256]{0:T(256)S(1)}, u32[]{:S(2)}, u32[]{:S(2)}) collective-permute-start(f32[256]{0:T(256)S(1)} %add_select_fusion.7), channel_id=1, source_target_pairs={{0,1},{1,2},{2,3},{3,4},{4,5},{5,6},{6,7},{7,8},{8,9},{9,10},{10,1... | collective-permute-start | bytes 3080 | tf_op jit(solution)/shard_map/ppermute | solution.py:13
  150.7 6.5 %collective-permute-done.13 = f32[256]{0:T(256)S(1)} collective-permute-done((f32[256]{0:T(256)S(1)}, f32[256]{0:T(256)S(1)}, u32[]{:S(2)}, u32[]{:S(2)}) %collective-permute-start.13) | collective-permute-done | bytes 1056 | tf_op jit(solution)/shard_map/ppermute | solution.py:13
  161.1 4.3 %collective-permute-start.14 = (f32[256]{0:T(256)S(1)}, f32[256]{0:T(256)S(1)}, u32[]{:S(2)}, u32[]{:S(2)}) collective-permute-start(f32[256]{0:T(256)S(1)} %bitcast.381), channel_id=1, source_target_pairs={{1,0},{2,1},{3,2},{4,3},{5,4},{6,5},{7,6},{8,7},{9,8},{10,9},{11,1... | collective-permute-start | bytes 3080 | tf_op jit(solution)/shard_map/ppermute | solution.py:13
  165.4 1.4 fusion.5
  166.8 2.0 collective-permute-start.27
  168.8 1.2 fusion.76
  170.1 4.5 %collective-permute-start.15 = (f32[256]{0:T(256)S(1)}, f32[256]{0:T(256)S(1)}, u32[]{:S(2)}, u32[]{:S(2)}) collective-permute-start(f32[256]{0:T(256)S(1)} %add_select_fusion.6), channel_id=1, source_target_pairs={{2,0},{3,1},{4,2},{5,3},{6,4},{7,5},{8,6},{9,7},{10,8},{11,9},{12,... | collective-permute-start | bytes 3080 | tf_op jit(solution)/shard_map/ppermute | solution.py:13
  174.6 1.3 convolution_select_fusion.7
  176.0 3.0 %collective-permute-start.5 = (f32[256,256]{1,0:T(8,128)S(1)}, f32[256,256]{1,0:T(8,128)S(1)}, u32[]{:S(2)}, u32[]{:S(2)}) collective-permute-start(f32[256,256]{1,0:T(8,128)S(1)} %convolution_select_fusion.7), channel_id=1, source_target_pairs={{32,0},{33,1},{34,2},{35,3},{36,4},{37,5},{38,6},{39,7},{40,8},{41... | collective-permute-start | bytes 786440 | tf_op jit(solution)/shard_map/ppermute | solution.py:13
  179.3 1.9 collective-permute-start.16
  181.6 4.7 %collective-permute-done.16 = f32[256]{0:T(256)S(1)} collective-permute-done((f32[256]{0:T(256)S(1)}, f32[256]{0:T(256)S(1)}, u32[]{:S(2)}, u32[]{:S(2)}) %collective-permute-start.16) | collective-permute-done | bytes 1056 | tf_op jit(solution)/shard_map/ppermute | solution.py:13
  186.6 2.3 collective-permute-start.17
  189.3 1.9 collective-permute-start.28
  191.3 1.8 collective-permute-done.17
  193.4 1.9 collective-permute-start.18
  195.3 3.2 %collective-permute-done.28 = f32[256,256]{1,0:T(8,128)S(1)} collective-permute-done((f32[256,256]{1,0:T(8,128)S(1)}, f32[256,256]{1,0:T(8,128)S(1)}, u32[]{:S(2)}, u32[]{:S(2)}) %collective-permute-start.28) | collective-permute-done | bytes 262176 | tf_op jit(solution)/shard_map/ppermute | solution.py:13
  198.8 1.2 collective-permute-done.18
  200.4 1.9 collective-permute-start.19
  202.8 5.1 %collective-permute-start.30 = (f32[256,256]{1,0:T(8,128)S(1)}, f32[256,256]{1,0:T(8,128)S(1)}, u32[]{:S(2)}, u32[]{:S(2)}) collective-permute-start(f32[256,256]{1,0:T(8,128)S(1)} %fusion.3), channel_id=1, source_target_pairs={{1,0},{2,1},{3,2},{4,3},{5,4},{6,5},{7,6},{8,7},{9,8},{10,9},{11,1... | collective-permute-start | bytes 786440 | tf_op jit(solution)/shard_map/ppermute | solution.py:13
  207.9 1.3 collective-permute-start.29
  209.5 1.3 collective-permute-start.20
  211.2 1.9 collective-permute-start.22
  213.1 6.3 %collective-permute-done.20 = f32[256]{0:T(256)S(1)} collective-permute-done((f32[256]{0:T(256)S(1)}, f32[256]{0:T(256)S(1)}, u32[]{:S(2)}, u32[]{:S(2)}) %collective-permute-start.20) | collective-permute-done | bytes 1056 | tf_op jit(solution)/shard_map/ppermute | solution.py:13
  219.8 1.9 collective-permute-start.21
  221.7 4.4 %collective-permute-done.21 = f32[256]{0:T(256)S(1)} collective-permute-done((f32[256]{0:T(256)S(1)}, f32[256]{0:T(256)S(1)}, u32[]{:S(2)}, u32[]{:S(2)}) %collective-permute-start.21) | collective-permute-done | bytes 1056 | tf_op jit(solution)/shard_map/ppermute | solution.py:13
  228.5 3.5 %all-to-all-start.3 = ((f32[4,1,256]{2,1,0:T(1,128)}), f32[4,1,256]{2,1,0:T(1,128)S(1)}, u32[]{:S(2)}, u32[]{:S(2)}) async-start(f32[4,1,256]{2,1,0:T(1,128)} %reshape.172), calls=%async_computation.3 | async-start | bytes 8192 | tf_op jit(solution)/shard_map/all_to_all | solution.py:187
  236.6 1.6 copy.48
  238.2 4.1 %all-to-all-start.5 = ((f32[4,256,256]{2,0,1:T(4,128)}), f32[4,256,256]{2,0,1:T(4,128)S(1)}, u32[]{:S(2)}, u32[]{:S(2)}) async-start(f32[4,256,256]{2,0,1:T(4,128)} %copy.48), calls=%async_computation.5 | async-start | bytes 2097152 | tf_op jit(solution)/shard_map/all_to_all | solution.py:187
  243.6 13.0 %all-to-all-done.5 = f32[4,256,256]{2,0,1:T(4,128)S(1)} async-done(((f32[4,256,256]{2,0,1:T(4,128)}), f32[4,256,256]{2,0,1:T(4,128)S(1)}, u32[]{:S(2)}, u32[]{:S(2)}) %all-to-all-start.5) | async-done | bytes 1048608 | tf_op jit(solution)/shard_map/all_to_all | solution.py:187
  256.6 1.2 copy.49
  (204 shorter events, 45.7 us)
Async XLA Ops:
  0.6 1.2 copy-start
  1.9 7.5 %copy-start.11 = (f32[256,256]{1,0:T(8,128)S(1)}, f32[256,256]{1,0:T(8,128)}, u32[]{:S(2)}) copy-start(f32[256,256]{1,0:T(8,128)} %param.10) | copy-start | bytes 786436
  4.3 9.8 %all-to-all-start.2 = ((f32[4,1,256]{2,1,0:T(1,128)}), f32[4,1,256]{2,1,0:T(1,128)S(1)}, u32[]{:S(2)}, u32[]{:S(2)}) async-start(f32[4,1,256]{2,1,0:T(1,128)} %reshape.170), calls=%async_computation.2 | async-start | bytes 8192 | tf_op jit(solution)/shard_map/all_to_all | solution.py:184
  9.3 0.7 copy-start.14
  9.3 1.0 copy-start.12
  10.3 0.7 copy-start.15
  14.1 17.9 %all-to-all-start.1 = ((f32[16,64,256]{2,1,0:T(8,128)}), f32[16,64,256]{2,1,0:T(8,128)S(1)}, u32[]{:S(2)}, u32[]{:S(2)}) async-start(f32[16,64,256]{2,1,0:T(8,128)} %fusion), calls=%async_computation.1 | async-start | bytes 2097152 | tf_op jit(solution)/shard_map/all_to_all | solution.py:184
  18.3 0.7 copy-start.16
  31.9 16.7 %all-to-all-start = ((f32[16,64,256]{2,1,0:T(8,128)}), f32[16,64,256]{2,1,0:T(8,128)}, u32[]{:S(2)}, u32[]{:S(2)}) async-start(f32[16,64,256]{2,1,0:T(8,128)} %param.18), calls=%async_computation | async-start | bytes 2097152 | tf_op jit(solution)/shard_map/all_to_all | solution.py:184
  37.9 15.0 %copy-start.6 = (f32[256,256]{1,0:T(8,128)}, f32[256,256]{1,0:T(8,128)S(1)}, u32[]{:S(2)}) copy-start(f32[256,256]{1,0:T(8,128)S(1)} %get-tuple-element.14) | copy-start | bytes 786436
  37.9 0.7 copy-start.13
  48.6 19.5 %all-to-all-start.4 = ((f32[16,64,256]{2,1,0:T(8,128)}), f32[16,64,256]{2,1,0:T(8,128)}, u32[]{:S(2)}, u32[]{:S(2)}) async-start(f32[16,64,256]{2,1,0:T(8,128)} %param.19), calls=%async_computation.4 | async-start | bytes 2097152 | tf_op jit(solution)/shard_map/all_to_all | solution.py:184
  55.0 26.4 %collective-permute-start.6 = (f32[257,256]{1,0:T(8,128)}, f32[257,256]{1,0:T(8,128)}, u32[]{:S(2)}, u32[]{:S(2)}) collective-permute-start(f32[257,256]{1,0:T(8,128)} %pad_maximum_fusion.1), channel_id=1, source_target_pairs={{0,1},{1,2},{2,3},{3,4},{4,5},{5,6},{6,7},{7,8},{8,9},{9,10},{10,1... | collective-permute-start | bytes 789512 | tf_op jit(solution)/shard_map/ppermute | solution.py:13
  59.1 0.8 copy-start.3
  61.0 24.7 %collective-permute-start = (f32[256,256]{1,0:T(8,128)}, f32[256,256]{1,0:T(8,128)}, u32[]{:S(2)}, u32[]{:S(2)}) collective-permute-start(f32[256,256]{1,0:T(8,128)} %fusion.34), channel_id=1, source_target_pairs={{1,0},{2,1},{3,2},{4,3},{5,4},{6,5},{7,6},{8,7},{9,8},{10,9},{11,1... | collective-permute-start | bytes 786440 | tf_op jit(solution)/shard_map/ppermute | solution.py:13
  69.5 1.1 copy-start.8
  73.9 1.4 copy-start.1
  74.5 1.0 copy-start.4
  76.4 5.0 %copy-start.7 = (f32[256,256]{1,0:T(8,128)S(1)}, f32[256,256]{1,0:T(8,128)}, u32[]{:S(2)}) copy-start(f32[256,256]{1,0:T(8,128)} %copy-done.6) | copy-start | bytes 786436
  76.4 16.0 %collective-permute-start.23 = (f32[256,256]{1,0:T(8,128)S(1)}, f32[256,256]{1,0:T(8,128)S(1)}, u32[]{:S(2)}, u32[]{:S(2)}) collective-permute-start(f32[256,256]{1,0:T(8,128)S(1)} %fusion.11), channel_id=1, source_target_pairs={{1,0},{2,1},{3,2},{4,3},{5,4},{6,5},{7,6},{8,7},{9,8},{10,9},{11,1... | collective-permute-start | bytes 786440 | tf_op jit(solution)/shard_map/ppermute | solution.py:13
  83.8 12.2 %collective-permute-start.7 = (f32[257,256]{1,0:T(8,128)S(1)}, f32[257,256]{1,0:T(8,128)S(1)}, u32[]{:S(2)}, u32[]{:S(2)}) collective-permute-start(f32[257,256]{1,0:T(8,128)S(1)} %pad_maximum_fusion.2), channel_id=1, source_target_pairs={{0,2},{1,3},{2,4},{3,5},{4,6},{5,7},{6,8},{7,9},{8,10},{9,11},{10,... | collective-permute-start | bytes 789512 | tf_op jit(solution)/shard_map/ppermute | solution.py:13
  87.2 19.2 %collective-permute-start.1 = (f32[256,256]{1,0:T(8,128)S(1)}, f32[256,256]{1,0:T(8,128)S(1)}, u32[]{:S(2)}, u32[]{:S(2)}) collective-permute-start(f32[256,256]{1,0:T(8,128)S(1)} %convolution_select_fusion.11), channel_id=1, source_target_pairs={{2,0},{3,1},{4,2},{5,3},{6,4},{7,5},{8,6},{9,7},{10,8},{11,9},{12,... | collective-permute-start | bytes 786440 | tf_op jit(solution)/shard_map/ppermute | solution.py:13
  96.7 12.1 %collective-permute-start.8 = (f32[257,256]{1,0:T(8,128)S(1)}, f32[257,256]{1,0:T(8,128)S(1)}, u32[]{:S(2)}, u32[]{:S(2)}) collective-permute-start(f32[257,256]{1,0:T(8,128)S(1)} %pad_maximum_fusion.3), channel_id=1, source_target_pairs={{0,4},{1,5},{2,6},{3,7},{4,8},{5,9},{6,10},{7,11},{8,12},{9,13},{1... | collective-permute-start | bytes 789512 | tf_op jit(solution)/shard_map/ppermute | solution.py:13
  104.5 8.6 %collective-permute-start.24 = (f32[256,256]{1,0:T(8,128)S(1)}, f32[256,256]{1,0:T(8,128)S(1)}, u32[]{:S(2)}, u32[]{:S(2)}) collective-permute-start(f32[256,256]{1,0:T(8,128)S(1)} %fusion.8), channel_id=1, source_target_pairs={{2,0},{3,1},{4,2},{5,3},{6,4},{7,5},{8,6},{9,7},{10,8},{11,9},{12,... | collective-permute-start | bytes 786440 | tf_op jit(solution)/shard_map/ppermute | solution.py:13
  106.9 14.9 %collective-permute-start.2 = (f32[256,256]{1,0:T(8,128)S(1)}, f32[256,256]{1,0:T(8,128)S(1)}, u32[]{:S(2)}, u32[]{:S(2)}) collective-permute-start(f32[256,256]{1,0:T(8,128)S(1)} %convolution_select_fusion.10), channel_id=1, source_target_pairs={{4,0},{5,1},{6,2},{7,3},{8,4},{9,5},{10,6},{11,7},{12,8},{13,9},{1... | collective-permute-start | bytes 786440 | tf_op jit(solution)/shard_map/ppermute | solution.py:13
  109.6 8.9 %collective-permute-start.9 = (f32[257,256]{1,0:T(8,128)S(1)}, f32[257,256]{1,0:T(8,128)S(1)}, u32[]{:S(2)}, u32[]{:S(2)}) collective-permute-start(f32[257,256]{1,0:T(8,128)S(1)} %pad_maximum_fusion.4), channel_id=1, source_target_pairs={{0,8},{1,9},{2,10},{3,11},{4,12},{5,13},{6,14},{7,15},{8,16},{9,17... | collective-permute-start | bytes 789512 | tf_op jit(solution)/shard_map/ppermute | solution.py:13
  114.0 11.4 %collective-permute-start.25 = (f32[256,256]{1,0:T(8,128)S(1)}, f32[256,256]{1,0:T(8,128)S(1)}, u32[]{:S(2)}, u32[]{:S(2)}) collective-permute-start(f32[256,256]{1,0:T(8,128)S(1)} %fusion.7), channel_id=1, source_target_pairs={{4,0},{5,1},{6,2},{7,3},{8,4},{9,5},{10,6},{11,7},{12,8},{13,9},{1... | collective-permute-start | bytes 786440 | tf_op jit(solution)/shard_map/ppermute | solution.py:13
  119.2 10.4 %collective-permute-start.10 = (f32[257,256]{1,0:T(8,128)S(1)}, f32[257,256]{1,0:T(8,128)S(1)}, u32[]{:S(2)}, u32[]{:S(2)}) collective-permute-start(f32[257,256]{1,0:T(8,128)S(1)} %pad_maximum_fusion.5), channel_id=1, source_target_pairs={{0,16},{1,17},{2,18},{3,19},{4,20},{5,21},{6,22},{7,23},{8,24},{9,... | collective-permute-start | bytes 789512 | tf_op jit(solution)/shard_map/ppermute | solution.py:13
  122.2 14.6 %collective-permute-start.3 = (f32[256,256]{1,0:T(8,128)S(1)}, f32[256,256]{1,0:T(8,128)S(1)}, u32[]{:S(2)}, u32[]{:S(2)}) collective-permute-start(f32[256,256]{1,0:T(8,128)S(1)} %convolution_select_fusion.9), channel_id=1, source_target_pairs={{8,0},{9,1},{10,2},{11,3},{12,4},{13,5},{14,6},{15,7},{16,8},{17,9... | collective-permute-start | bytes 786440 | tf_op jit(solution)/shard_map/ppermute | solution.py:13
  130.4 8.7 %collective-permute-start.11 = (f32[257,256]{1,0:T(8,128)S(1)}, f32[257,256]{1,0:T(8,128)S(1)}, u32[]{:S(2)}, u32[]{:S(2)}) collective-permute-start(f32[257,256]{1,0:T(8,128)S(1)} %pad_maximum_fusion.6), channel_id=1, source_target_pairs={{0,32},{1,33},{2,34},{3,35},{4,36},{5,37},{6,38},{7,39},{8,40},{9,... | collective-permute-start | bytes 789512 | tf_op jit(solution)/shard_map/ppermute | solution.py:13
  133.7 3.4 %copy-start.10 = (f32[256,256]{1,0:T(8,128)}, f32[256,256]{1,0:T(8,128)S(1)}, u32[]{:S(2)}) copy-start(f32[256,256]{1,0:T(8,128)S(1)} %fusion.6) | copy-start | bytes 786436
  133.7 15.9 %collective-permute-start.26 = (f32[256,256]{1,0:T(8,128)S(1)}, f32[256,256]{1,0:T(8,128)S(1)}, u32[]{:S(2)}, u32[]{:S(2)}) collective-permute-start(f32[256,256]{1,0:T(8,128)S(1)} %fusion.6), channel_id=1, source_target_pairs={{8,0},{9,1},{10,2},{11,3},{12,4},{13,5},{14,6},{15,7},{16,8},{17,9... | collective-permute-start | bytes 786440 | tf_op jit(solution)/shard_map/ppermute | solution.py:13
  137.1 37.5 %collective-permute-start.4 = (f32[256,256]{1,0:T(8,128)S(1)}, f32[256,256]{1,0:T(8,128)}, u32[]{:S(2)}, u32[]{:S(2)}) collective-permute-start(f32[256,256]{1,0:T(8,128)S(1)} %convolution_select_fusion.8), channel_id=1, source_target_pairs={{16,0},{17,1},{18,2},{19,3},{20,4},{21,5},{22,6},{23,7},{24,8},{25... | collective-permute-start | bytes 786440 | tf_op jit(solution)/shard_map/ppermute | solution.py:13
  139.4 3.3 %collective-permute-start.12 = (f32[256]{0:T(256)S(1)}, f32[256]{0:T(256)S(1)}, u32[]{:S(2)}, u32[]{:S(2)}) collective-permute-start(f32[256]{0:T(256)S(1)} %add_select_fusion.8), channel_id=1, source_target_pairs={{0,64},{1,65},{2,66},{3,67},{4,68},{5,69},{6,70},{7,71},{8,72},{9,... | collective-permute-start | bytes 3080 | tf_op jit(solution)/shard_map/ppermute | solution.py:13
  143.0 14.2 %collective-permute-start.13 = (f32[256]{0:T(256)S(1)}, f32[256]{0:T(256)S(1)}, u32[]{:S(2)}, u32[]{:S(2)}) collective-permute-start(f32[256]{0:T(256)S(1)} %add_select_fusion.7), channel_id=1, source_target_pairs={{0,1},{1,2},{2,3},{3,4},{4,5},{5,6},{6,7},{7,8},{8,9},{9,10},{10,1... | collective-permute-start | bytes 3080 | tf_op jit(solution)/shard_map/ppermute | solution.py:13
  159.8 1.0 copy-start.5
  160.4 5.0 %copy-start.9 = (f32[256,256]{1,0:T(8,128)S(1)}, f32[256,256]{1,0:T(8,128)}, u32[]{:S(2)}) copy-start(f32[256,256]{1,0:T(8,128)} %fusion.87) | copy-start | bytes 786436
  161.1 7.7 %collective-permute-start.14 = (f32[256]{0:T(256)S(1)}, f32[256]{0:T(256)S(1)}, u32[]{:S(2)}, u32[]{:S(2)}) collective-permute-start(f32[256]{0:T(256)S(1)} %bitcast.381), channel_id=1, source_target_pairs={{1,0},{2,1},{3,2},{4,3},{5,4},{6,5},{7,6},{8,7},{9,8},{10,9},{11,1... | collective-permute-start | bytes 3080 | tf_op jit(solution)/shard_map/ppermute | solution.py:13
  166.8 14.4 %collective-permute-start.27 = (f32[256,256]{1,0:T(8,128)S(1)}, f32[256,256]{1,0:T(8,128)S(1)}, u32[]{:S(2)}, u32[]{:S(2)}) collective-permute-start(f32[256,256]{1,0:T(8,128)S(1)} %fusion.5), channel_id=1, source_target_pairs={{16,0},{17,1},{18,2},{19,3},{20,4},{21,5},{22,6},{23,7},{24,8},{25... | collective-permute-start | bytes 786440 | tf_op jit(solution)/shard_map/ppermute | solution.py:13
  170.1 8.8 %collective-permute-start.15 = (f32[256]{0:T(256)S(1)}, f32[256]{0:T(256)S(1)}, u32[]{:S(2)}, u32[]{:S(2)}) collective-permute-start(f32[256]{0:T(256)S(1)} %add_select_fusion.6), channel_id=1, source_target_pairs={{2,0},{3,1},{4,2},{5,3},{6,4},{7,5},{8,6},{9,7},{10,8},{11,9},{12,... | collective-permute-start | bytes 3080 | tf_op jit(solution)/shard_map/ppermute | solution.py:13
  176.0 34.8 %collective-permute-start.5 = (f32[256,256]{1,0:T(8,128)S(1)}, f32[256,256]{1,0:T(8,128)S(1)}, u32[]{:S(2)}, u32[]{:S(2)}) collective-permute-start(f32[256,256]{1,0:T(8,128)S(1)} %convolution_select_fusion.7), channel_id=1, source_target_pairs={{32,0},{33,1},{34,2},{35,3},{36,4},{37,5},{38,6},{39,7},{40,8},{41... | collective-permute-start | bytes 786440 | tf_op jit(solution)/shard_map/ppermute | solution.py:13
  179.3 7.0 %collective-permute-start.16 = (f32[256]{0:T(256)S(1)}, f32[256]{0:T(256)S(1)}, u32[]{:S(2)}, u32[]{:S(2)}) collective-permute-start(f32[256]{0:T(256)S(1)} %add_select_fusion.5), channel_id=1, source_target_pairs={{4,0},{5,1},{6,2},{7,3},{8,4},{9,5},{10,6},{11,7},{12,8},{13,9},{1... | collective-permute-start | bytes 3080 | tf_op jit(solution)/shard_map/ppermute | solution.py:13
  186.6 6.4 %collective-permute-start.17 = (f32[256]{0:T(256)S(1)}, f32[256]{0:T(256)S(1)}, u32[]{:S(2)}, u32[]{:S(2)}) collective-permute-start(f32[256]{0:T(256)S(1)} %add_select_fusion.4), channel_id=1, source_target_pairs={{8,0},{9,1},{10,2},{11,3},{12,4},{13,5},{14,6},{15,7},{16,8},{17,9... | collective-permute-start | bytes 3080 | tf_op jit(solution)/shard_map/ppermute | solution.py:13
  189.3 9.1 %collective-permute-start.28 = (f32[256,256]{1,0:T(8,128)S(1)}, f32[256,256]{1,0:T(8,128)S(1)}, u32[]{:S(2)}, u32[]{:S(2)}) collective-permute-start(f32[256,256]{1,0:T(8,128)S(1)} %fusion.4), channel_id=1, source_target_pairs={{32,0},{33,1},{34,2},{35,3},{36,4},{37,5},{38,6},{39,7},{40,8},{41... | collective-permute-start | bytes 786440 | tf_op jit(solution)/shard_map/ppermute | solution.py:13
  193.4 6.7 %collective-permute-start.18 = (f32[256]{0:T(256)S(1)}, f32[256]{0:T(256)S(1)}, u32[]{:S(2)}, u32[]{:S(2)}) collective-permute-start(f32[256]{0:T(256)S(1)} %add_select_fusion.3), channel_id=1, source_target_pairs={{16,0},{17,1},{18,2},{19,3},{20,4},{21,5},{22,6},{23,7},{24,8},{25... | collective-permute-start | bytes 3080 | tf_op jit(solution)/shard_map/ppermute | solution.py:13
  200.4 8.8 %collective-permute-start.19 = (f32[256]{0:T(256)S(1)}, f32[256]{0:T(256)S(1)}, u32[]{:S(2)}, u32[]{:S(2)}) collective-permute-start(f32[256]{0:T(256)S(1)} %add_select_fusion.2), channel_id=1, source_target_pairs={{32,0},{33,1},{34,2},{35,3},{36,4},{37,5},{38,6},{39,7},{40,8},{41... | collective-permute-start | bytes 3080 | tf_op jit(solution)/shard_map/ppermute | solution.py:13
  202.8 29.7 %collective-permute-start.30 = (f32[256,256]{1,0:T(8,128)S(1)}, f32[256,256]{1,0:T(8,128)S(1)}, u32[]{:S(2)}, u32[]{:S(2)}) collective-permute-start(f32[256,256]{1,0:T(8,128)S(1)} %fusion.3), channel_id=1, source_target_pairs={{1,0},{2,1},{3,2},{4,3},{5,4},{6,5},{7,6},{8,7},{9,8},{10,9},{11,1... | collective-permute-start | bytes 786440 | tf_op jit(solution)/shard_map/ppermute | solution.py:13
  207.9 24.1 %collective-permute-start.29 = (f32[256,256]{1,0:T(8,128)S(1)}, f32[256,256]{1,0:T(8,128)S(1)}, u32[]{:S(2)}, u32[]{:S(2)}) collective-permute-start(f32[256,256]{1,0:T(8,128)S(1)} %fusion.3), channel_id=1, source_target_pairs={{65,0},{66,1},{67,2},{68,3},{69,4},{70,5},{71,6},{72,7},{73,8},{74... | collective-permute-start | bytes 786440 | tf_op jit(solution)/shard_map/ppermute | solution.py:13
  209.5 9.9 %collective-permute-start.20 = (f32[256]{0:T(256)S(1)}, f32[256]{0:T(256)S(1)}, u32[]{:S(2)}, u32[]{:S(2)}) collective-permute-start(f32[256]{0:T(256)S(1)} %add_select_fusion.1), channel_id=1, source_target_pairs={{64,0},{65,1},{66,2},{67,3},{68,4},{69,5},{70,6},{71,7},{72,8},{73... | collective-permute-start | bytes 3080 | tf_op jit(solution)/shard_map/ppermute | solution.py:13
  211.2 20.8 %collective-permute-start.22 = (f32[256,256]{1,0:T(8,128)S(1)}, f32[256,256]{1,0:T(8,128)S(1)}, u32[]{:S(2)}, u32[]{:S(2)}) collective-permute-start(f32[256,256]{1,0:T(8,128)S(1)} %convolution_select_fusion.6), channel_id=1, source_target_pairs={{1,0},{2,1},{3,2},{4,3},{5,4},{6,5},{7,6},{8,7},{9,8},{10,9},{11,1... | collective-permute-start | bytes 786440 | tf_op jit(solution)/shard_map/ppermute | solution.py:13
  219.8 6.3 %collective-permute-start.21 = (f32[256]{0:T(256)S(1)}, f32[256]{0:T(256)S(1)}, u32[]{:S(2)}, u32[]{:S(2)}) collective-permute-start(f32[256]{0:T(256)S(1)} %add_select_fusion), channel_id=1, source_target_pairs={{1,0},{2,1},{3,2},{4,3},{5,4},{6,5},{7,6},{8,7},{9,8},{10,9},{11,1... | collective-permute-start | bytes 3080 | tf_op jit(solution)/shard_map/ppermute | solution.py:13
  228.5 9.7 %all-to-all-start.3 = ((f32[4,1,256]{2,1,0:T(1,128)}), f32[4,1,256]{2,1,0:T(1,128)S(1)}, u32[]{:S(2)}, u32[]{:S(2)}) async-start(f32[4,1,256]{2,1,0:T(1,128)} %reshape.172), calls=%async_computation.3 | async-start | bytes 8192 | tf_op jit(solution)/shard_map/all_to_all | solution.py:187
  232.4 1.2 copy-start.2
  238.2 18.4 %all-to-all-start.5 = ((f32[4,256,256]{2,0,1:T(4,128)}), f32[4,256,256]{2,0,1:T(4,128)S(1)}, u32[]{:S(2)}, u32[]{:S(2)}) async-start(f32[4,256,256]{2,0,1:T(4,128)} %copy.48), calls=%async_computation.5 | async-start | bytes 2097152 | tf_op jit(solution)/shard_map/all_to_all | solution.py:187

commit v10 on v9

--- a/solution.py
+++ b/solution.py
@@ -186,12 +186,17 @@
     def rows_of_steps(whole):
         return lax.all_to_all(whole, "blk", 1, 0, tiled=True)
 
+    map_whole = steps_whole(map_rows)
+    shift_whole = steps_whole(shift_rows)
+    map_whole, shift_whole, smooth_gains, filt_cov = lax.optimization_barrier(
+        (map_whole, shift_whole, smooth_gains, filt_cov)
+    )
     means_out, cov_out = window_work(
         trans_map,
         process_noise,
         initial_expectation,
-        steps_whole(map_rows),
-        steps_whole(shift_rows),
+        map_whole,
+        shift_whole,
         steps_whole(smooth_gains),
         steps_whole(filt_cov),
         lax.axis_index(CHUNKS),

time: 261 us -> 270 us (1.034)
  starting transfers between devices: 122 us -> 125 us
    all_to_all x4, waiting for transfers between devices: 19.7 us -> 28.3 us  [steps_whole(): return lax.all_to_all(rows, 'blk', 0, 1, tiled=True)]
    ppermute x31, waiting for transfers between devices: 36.7 us -> 30.7 us  [from_behind(): return lax.ppermute(block, axis, route)]
    unnamed x40 -> x52, local copies, waits for them, and re-layouts: 8.18 us -> 7.94 us
  transfers between devices with their start and end apart: 37 -> 37, of which waited for: 15 -> 14; matrix products, arithmetic and copies ran while one was open for 21% -> 20% of each run, Pallas kernels for 0% -> 0%
where the time goes in v10:
time: 270 us; the launch traced here: 266 us
  starting transfers between devices  125 us (46%)
  waiting for transfers between devices  71.7 us (27%)
  matrix products  46.6 us (17%)
  local copies, waits for them, and re-layouts  15.1 us (6%)
  other arithmetic  5.14 us (2%)
    ppermute x31, starting transfers between devices, from_behind(): return lax.ppermute(block, axis, route)  97 us
    dot_general x48, matrix products, matmul(): return jnp.matmul(left, right, precision=highest)  32 us
    ppermute x31, waiting for transfers between devices, from_behind(): return lax.ppermute(block, axis, route)  30.7 us
    all_to_all x4, waiting for transfers between devices, steps_whole(): return lax.all_to_all(rows, 'blk', 0, 1, tiled=True)  28.3 us
    all_to_all x4, starting transfers between devices, steps_whole(): return lax.all_to_all(rows, 'blk', 0, 1, tiled=True)  20.4 us
    all_to_all x2, waiting for transfers between devices, rows_of_steps(): return lax.all_to_all(whole, 'blk', 1, 0, tiled=True)  12.7 us
    dot_general x27, matrix products, matvec(): return jnp.einsum('...ij,...j->...i', left, right, precision=highest)  11.6 us
    unnamed x52, local copies, waits for them, and re-layouts  7.94 us
  transfers between devices with their start and end apart: 37, of which 14 were waited for; matrix products, arithmetic and copies ran while one was open for 20% of the time, Pallas kernels for 0%

profile of v10, /device:TPU:15, one launch (start us, length us, event | category | flops | bytes accessed | tf_op | source)
XLA Modules:
  0.0 266.1 jit_solution(16131279043461866537)
XLA Ops:
  0.6 1.2 copy-done
  1.9 1.7 fusion.66
  4.3 5.0 %all-to-all-start.1 = ((f32[4,1,256]{2,1,0:T(1,128)}), f32[4,1,256]{2,1,0:T(1,128)S(1)}, u32[]{:S(2)}, u32[]{:S(2)}) async-start(f32[4,1,256]{2,1,0:T(1,128)} %reshape.132), calls=%async_computation.1 | async-start | bytes 8192 | tf_op jit(solution)/shard_map/all_to_all | solution.py:184
  12.9 2.0 fusion
  14.9 4.2 %all-to-all-start = ((f32[16,64,256]{2,1,0:T(8,128)}), f32[16,64,256]{2,1,0:T(8,128)S(1)}, u32[]{:S(2)}, u32[]{:S(2)}) async-start(f32[16,64,256]{2,1,0:T(8,128)} %fusion), calls=%async_computation | async-start | bytes 2097152 | tf_op jit(solution)/shard_map/all_to_all | solution.py:184
  20.4 12.3 %all-to-all-done = f32[16,64,256]{2,1,0:T(8,128)S(1)} async-done(((f32[16,64,256]{2,1,0:T(8,128)}), f32[16,64,256]{2,1,0:T(8,128)S(1)}, u32[]{:S(2)}, u32[]{:S(2)}) %all-to-all-start) | async-done | bytes 1048608 | tf_op jit(solution)/shard_map/all_to_all | solution.py:184
  36.6 2.2 collective-permute-start.6
  40.3 6.9 %all-to-all-start.2 = ((f32[16,64,256]{2,1,0:T(8,128)}), f32[16,64,256]{2,1,0:T(8,128)S(1)}, u32[]{:S(2)}, u32[]{:S(2)}) async-start(f32[16,64,256]{2,1,0:T(8,128)} %param.18), calls=%async_computation.2 | async-start | bytes 2097152 | tf_op jit(solution)/shard_map/all_to_all | solution.py:184
  47.2 1.9 collective-permute-done.6
  49.1 1.2 fusion.77
  50.4 1.3 convolution_select_fusion.5
  52.5 3.1 %collective-permute-start.7 = (f32[257,256]{1,0:T(8,128)}, f32[257,256]{1,0:T(8,128)}, u32[]{:S(2)}, u32[]{:S(2)}) collective-permute-start(f32[257,256]{1,0:T(8,128)} %pad_maximum_fusion.2), channel_id=1, source_target_pairs={{0,2},{1,3},{2,4},{3,5},{4,6},{5,7},{6,8},{7,9},{8,10},{9,11},{10,... | collective-permute-start | bytes 789512 | tf_op jit(solution)/shard_map/ppermute | solution.py:13
  55.7 9.8 %all-to-all-done.2 = f32[16,64,256]{2,1,0:T(8,128)S(1)} async-done(((f32[16,64,256]{2,1,0:T(8,128)}), f32[16,64,256]{2,1,0:T(8,128)S(1)}, u32[]{:S(2)}, u32[]{:S(2)}) %all-to-all-start.2) | async-done | bytes 1048608 | tf_op jit(solution)/shard_map/all_to_all | solution.py:184
  65.5 4.3 %all-to-all-start.4 = ((f32[16,64,256]{2,1,0:T(8,128)}), f32[16,64,256]{2,1,0:T(8,128)}, u32[]{:S(2)}, u32[]{:S(2)}) async-start(f32[16,64,256]{2,1,0:T(8,128)} %param.19), calls=%async_computation.4 | async-start | bytes 2097152 | tf_op jit(solution)/shard_map/all_to_all | solution.py:184
  69.7 1.3 fusion.76
  71.1 1.3 convolution_select_fusion.4
  73.3 3.8 %collective-permute-start.8 = (f32[257,256]{1,0:T(8,128)}, f32[257,256]{1,0:T(8,128)}, u32[]{:S(2)}, u32[]{:S(2)}) collective-permute-start(f32[257,256]{1,0:T(8,128)} %pad_maximum_fusion.3), channel_id=1, source_target_pairs={{0,4},{1,5},{2,6},{3,7},{4,8},{5,9},{6,10},{7,11},{8,12},{9,13},{1... | collective-permute-start | bytes 789512 | tf_op jit(solution)/shard_map/ppermute | solution.py:13
  78.2 6.1 %all-to-all-done.4 = f32[16,64,256]{2,1,0:T(8,128)} async-done(((f32[16,64,256]{2,1,0:T(8,128)}), f32[16,64,256]{2,1,0:T(8,128)}, u32[]{:S(2)}, u32[]{:S(2)}) %all-to-all-start.4) | async-done | bytes 1048608 | tf_op jit(solution)/shard_map/all_to_all | solution.py:184
  84.3 1.3 copy.45
  93.5 4.2 %collective-permute-start.23 = (f32[256,256]{1,0:T(8,128)S(1)}, f32[256,256]{1,0:T(8,128)S(1)}, u32[]{:S(2)}, u32[]{:S(2)}) collective-permute-start(f32[256,256]{1,0:T(8,128)S(1)} %fusion.11), channel_id=1, source_target_pairs={{1,0},{2,1},{3,2},{4,3},{5,4},{6,5},{7,6},{8,7},{9,8},{10,9},{11,1... | collective-permute-start | bytes 786440 | tf_op jit(solution)/shard_map/ppermute | solution.py:13
  98.8 1.3 convolution_select_fusion.3
  100.1 3.1 %collective-permute-start.9 = (f32[257,256]{1,0:T(8,128)S(1)}, f32[257,256]{1,0:T(8,128)S(1)}, u32[]{:S(2)}, u32[]{:S(2)}) collective-permute-start(f32[257,256]{1,0:T(8,128)S(1)} %pad_maximum_fusion.4), channel_id=1, source_target_pairs={{0,8},{1,9},{2,10},{3,11},{4,12},{5,13},{6,14},{7,15},{8,16},{9,17... | collective-permute-start | bytes 789512 | tf_op jit(solution)/shard_map/ppermute | solution.py:13
  103.7 2.2 collective-permute-start
  106.3 4.0 %collective-permute-done.9 = f32[257,256]{1,0:T(8,128)S(1)} collective-permute-done((f32[257,256]{1,0:T(8,128)S(1)}, f32[257,256]{1,0:T(8,128)S(1)}, u32[]{:S(2)}, u32[]{:S(2)}) %collective-permute-start.9) | collective-permute-done | bytes 263200 | tf_op jit(solution)/shard_map/ppermute | solution.py:13
  111.0 4.2 %collective-permute-start.10 = (f32[257,256]{1,0:T(8,128)S(1)}, f32[257,256]{1,0:T(8,128)S(1)}, u32[]{:S(2)}, u32[]{:S(2)}) collective-permute-start(f32[257,256]{1,0:T(8,128)S(1)} %pad_maximum_fusion.5), channel_id=1, source_target_pairs={{0,16},{1,17},{2,18},{3,19},{4,20},{5,21},{6,22},{7,23},{8,24},{9,... | collective-permute-start | bytes 789512 | tf_op jit(solution)/shard_map/ppermute | solution.py:13
  115.7 2.2 collective-permute-start.24
  118.4 5.4 %collective-permute-start.1 = (f32[256,256]{1,0:T(8,128)S(1)}, f32[256,256]{1,0:T(8,128)S(1)}, u32[]{:S(2)}, u32[]{:S(2)}) collective-permute-start(f32[256,256]{1,0:T(8,128)S(1)} %convolution_select_fusion.11), channel_id=1, source_target_pairs={{2,0},{3,1},{4,2},{5,3},{6,4},{7,5},{8,6},{9,7},{10,8},{11,9},{12,... | collective-permute-start | bytes 786440 | tf_op jit(solution)/shard_map/ppermute | solution.py:13
  124.6 3.1 %collective-permute-start.11 = (f32[257,256]{1,0:T(8,128)S(1)}, f32[257,256]{1,0:T(8,128)S(1)}, u32[]{:S(2)}, u32[]{:S(2)}) collective-permute-start(f32[257,256]{1,0:T(8,128)S(1)} %pad_maximum_fusion.6), channel_id=1, source_target_pairs={{0,32},{1,33},{2,34},{3,35},{4,36},{5,37},{6,38},{7,39},{8,40},{9,... | collective-permute-start | bytes 789512 | tf_op jit(solution)/shard_map/ppermute | solution.py:13
  129.2 3.2 %collective-permute-start.25 = (f32[256,256]{1,0:T(8,128)}, f32[256,256]{1,0:T(8,128)}, u32[]{:S(2)}, u32[]{:S(2)}) collective-permute-start(f32[256,256]{1,0:T(8,128)} %fusion.7), channel_id=1, source_target_pairs={{4,0},{5,1},{6,2},{7,3},{8,4},{9,5},{10,6},{11,7},{12,8},{13,9},{1... | collective-permute-start | bytes 786440 | tf_op jit(solution)/shard_map/ppermute | solution.py:13
  132.4 2.4 collective-permute-done.11
  135.2 2.4 collective-permute-start.12
  138.7 1.9 collective-permute-start.13
  141.7 3.4 %collective-permute-start.2 = (f32[256,256]{1,0:T(8,128)}, f32[256,256]{1,0:T(8,128)}, u32[]{:S(2)}, u32[]{:S(2)}) collective-permute-start(f32[256,256]{1,0:T(8,128)} %convolution_select_fusion.10), channel_id=1, source_target_pairs={{4,0},{5,1},{6,2},{7,3},{8,4},{9,5},{10,6},{11,7},{12,8},{13,9},{1... | collective-permute-start | bytes 786440 | tf_op jit(solution)/shard_map/ppermute | solution.py:13
  149.1 6.1 %collective-permute-start.14 = (f32[256]{0:T(256)S(1)}, f32[256]{0:T(256)S(1)}, u32[]{:S(2)}, u32[]{:S(2)}) collective-permute-start(f32[256]{0:T(256)S(1)} %bitcast.388), channel_id=1, source_target_pairs={{1,0},{2,1},{3,2},{4,3},{5,4},{6,5},{7,6},{8,7},{9,8},{10,9},{11,1... | collective-permute-start | bytes 3080 | tf_op jit(solution)/shard_map/ppermute | solution.py:13
  155.2 1.4 fusion.94
  157.0 3.6 %collective-permute-start.15 = (f32[256]{0:T(256)S(1)}, f32[256]{0:T(256)S(1)}, u32[]{:S(2)}, u32[]{:S(2)}) collective-permute-start(f32[256]{0:T(256)S(1)} %add_select_fusion.6), channel_id=1, source_target_pairs={{2,0},{3,1},{4,2},{5,3},{6,4},{7,5},{8,6},{9,7},{10,8},{11,9},{12,... | collective-permute-start | bytes 3080 | tf_op jit(solution)/shard_map/ppermute | solution.py:13
  160.6 1.4 fusion.6
  162.1 3.7 %collective-permute-start.26 = (f32[256,256]{1,0:T(8,128)S(1)}, f32[256,256]{1,0:T(8,128)S(1)}, u32[]{:S(2)}, u32[]{:S(2)}) collective-permute-start(f32[256,256]{1,0:T(8,128)S(1)} %fusion.6), channel_id=1, source_target_pairs={{8,0},{9,1},{10,2},{11,3},{12,4},{13,5},{14,6},{15,7},{16,8},{17,9... | collective-permute-start | bytes 786440 | tf_op jit(solution)/shard_map/ppermute | solution.py:13
  166.1 1.9 collective-permute-start.16
  168.0 1.5 convolution_select_fusion.9
  169.5 2.1 collective-permute-start.3
  171.6 3.8 %collective-permute-done.16 = f32[256]{0:T(256)S(1)} collective-permute-done((f32[256]{0:T(256)S(1)}, f32[256]{0:T(256)S(1)}, u32[]{:S(2)}, u32[]{:S(2)}) %collective-permute-start.16) | collective-permute-done | bytes 1056 | tf_op jit(solution)/shard_map/ppermute | solution.py:13
  175.4 1.2 fusion.86
  176.7 1.9 collective-permute-start.17
  178.6 4.5 %collective-permute-done.17 = f32[256]{0:T(256)S(1)} collective-permute-done((f32[256]{0:T(256)S(1)}, f32[256]{0:T(256)S(1)}, u32[]{:S(2)}, u32[]{:S(2)}) %collective-permute-start.17) | collective-permute-done | bytes 1056 | tf_op jit(solution)/shard_map/ppermute | solution.py:13
  183.4 1.9 collective-permute-start.18
  186.2 4.6 %collective-permute-start.27 = (f32[256,256]{1,0:T(8,128)S(1)}, f32[256,256]{1,0:T(8,128)S(1)}, u32[]{:S(2)}, u32[]{:S(2)}) collective-permute-start(f32[256,256]{1,0:T(8,128)S(1)} %fusion.5), channel_id=1, source_target_pairs={{16,0},{17,1},{18,2},{19,3},{20,4},{21,5},{22,6},{23,7},{24,8},{25... | collective-permute-start | bytes 786440 | tf_op jit(solution)/shard_map/ppermute | solution.py:13
  191.1 1.9 collective-permute-start.4
  193.4 1.9 collective-permute-start.19
  195.3 2.3 collective-permute-done.27
  198.4 2.9 %collective-permute-start.28 = (f32[256,256]{1,0:T(8,128)S(1)}, f32[256,256]{1,0:T(8,128)S(1)}, u32[]{:S(2)}, u32[]{:S(2)}) collective-permute-start(f32[256,256]{1,0:T(8,128)S(1)} %fusion.4), channel_id=1, source_target_pairs={{32,0},{33,1},{34,2},{35,3},{36,4},{37,5},{38,6},{39,7},{40,8},{41... | collective-permute-start | bytes 786440 | tf_op jit(solution)/shard_map/ppermute | solution.py:13
  201.3 2.5 collective-permute-done.4
  204.2 2.3 collective-permute-start.5
  206.9 1.3 collective-permute-start.20
  208.2 6.4 %collective-permute-done.5 = f32[256,256]{1,0:T(8,128)S(1)} collective-permute-done((f32[256,256]{1,0:T(8,128)S(1)}, f32[256,256]{1,0:T(8,128)S(1)}, u32[]{:S(2)}, u32[]{:S(2)}) %collective-permute-start.5) | collective-permute-done | bytes 262176 | tf_op jit(solution)/shard_map/ppermute | solution.py:13
  214.9 10.5 %collective-permute-start.22 = (f32[256,256]{1,0:T(8,128)S(1)}, f32[256,256]{1,0:T(8,128)S(1)}, u32[]{:S(2)}, u32[]{:S(2)}) collective-permute-start(f32[256,256]{1,0:T(8,128)S(1)} %convolution_select_fusion.6), channel_id=1, source_target_pairs={{1,0},{2,1},{3,2},{4,3},{5,4},{6,5},{7,6},{8,7},{9,8},{10,9},{11,1... | collective-permute-start | bytes 786440 | tf_op jit(solution)/shard_map/ppermute | solution.py:13
  225.8 1.9 collective-permute-start.21
  228.5 1.3 collective-permute-start.29
  229.8 2.4 collective-permute-start.30
  234.7 4.2 %all-to-all-start.3 = ((f32[4,1,256]{2,1,0:T(1,128)}), f32[4,1,256]{2,1,0:T(1,128)S(1)}, u32[]{:S(2)}, u32[]{:S(2)}) async-start(f32[4,1,256]{2,1,0:T(1,128)} %reshape.134), calls=%async_computation.3 | async-start | bytes 8192 | tf_op jit(solution)/shard_map/all_to_all | solution.py:187
  239.3 2.7 %collective-permute-done.30 = f32[256,256]{1,0:T(8,128)S(1)} collective-permute-done((f32[256,256]{1,0:T(8,128)S(1)}, f32[256,256]{1,0:T(8,128)S(1)}, u32[]{:S(2)}, u32[]{:S(2)}) %collective-permute-start.30) | collective-permute-done | bytes 262176 | tf_op jit(solution)/shard_map/ppermute | solution.py:13
  245.7 1.6 copy.48
  247.4 3.5 %all-to-all-start.5 = ((f32[4,256,256]{2,0,1:T(4,128)}), f32[4,256,256]{2,0,1:T(4,128)S(1)}, u32[]{:S(2)}, u32[]{:S(2)}) async-start(f32[4,256,256]{2,0,1:T(4,128)} %copy.48), calls=%async_computation.5 | async-start | bytes 2097152 | tf_op jit(solution)/shard_map/all_to_all | solution.py:187
  252.2 12.7 %all-to-all-done.5 = f32[4,256,256]{2,0,1:T(4,128)S(1)} async-done(((f32[4,256,256]{2,0,1:T(4,128)}), f32[4,256,256]{2,0,1:T(4,128)S(1)}, u32[]{:S(2)}, u32[]{:S(2)}) %all-to-all-start.5) | async-done | bytes 1048608 | tf_op jit(solution)/shard_map/all_to_all | solution.py:187
  (210 shorter events, 47.3 us)
Async XLA Ops:
  0.6 1.2 copy-start
  1.9 7.5 %copy-start.17 = (f32[256,256]{1,0:T(8,128)S(1)}, f32[256,256]{1,0:T(8,128)}, u32[]{:S(2)}) copy-start(f32[256,256]{1,0:T(8,128)} %param.10) | copy-start | bytes 786436
  4.3 10.6 %all-to-all-start.1 = ((f32[4,1,256]{2,1,0:T(1,128)}), f32[4,1,256]{2,1,0:T(1,128)S(1)}, u32[]{:S(2)}, u32[]{:S(2)}) async-start(f32[4,1,256]{2,1,0:T(1,128)} %reshape.132), calls=%async_computation.1 | async-start | bytes 8192 | tf_op jit(solution)/shard_map/all_to_all | solution.py:184
  9.3 1.0 copy-start.18
  10.3 0.7 copy-start.20
  11.1 0.7 copy-start.21
  14.9 17.8 %all-to-all-start = ((f32[16,64,256]{2,1,0:T(8,128)}), f32[16,64,256]{2,1,0:T(8,128)S(1)}, u32[]{:S(2)}, u32[]{:S(2)}) async-start(f32[16,64,256]{2,1,0:T(8,128)} %fusion), calls=%async_computation | async-start | bytes 2097152 | tf_op jit(solution)/shard_map/all_to_all | solution.py:184
  34.8 1.8 copy-start.14
  34.8 0.7 copy-start.19
  36.6 12.5 %collective-permute-start.6 = (f32[257,256]{1,0:T(8,128)}, f32[257,256]{1,0:T(8,128)}, u32[]{:S(2)}, u32[]{:S(2)}) collective-permute-start(f32[257,256]{1,0:T(8,128)} %pad_maximum_fusion.1), channel_id=1, source_target_pairs={{0,1},{1,2},{2,3},{3,4},{4,5},{5,6},{6,7},{7,8},{8,9},{9,10},{10,1... | collective-permute-start | bytes 789512 | tf_op jit(solution)/shard_map/ppermute | solution.py:13
  38.8 0.7 copy-start.22
  40.3 25.2 %all-to-all-start.2 = ((f32[16,64,256]{2,1,0:T(8,128)}), f32[16,64,256]{2,1,0:T(8,128)S(1)}, u32[]{:S(2)}, u32[]{:S(2)}) async-start(f32[16,64,256]{2,1,0:T(8,128)} %param.18), calls=%async_computation.2 | async-start | bytes 2097152 | tf_op jit(solution)/shard_map/all_to_all | solution.py:184
  47.2 3.1 %copy-start.15 = (f32[256,256]{1,0:T(8,128)S(1)}, f32[256,256]{1,0:T(8,128)}, u32[]{:S(2)}) copy-start(f32[256,256]{1,0:T(8,128)} %copy-done.14) | copy-start | bytes 786436
  51.7 0.8 copy-start.10
  52.5 17.2 %collective-permute-start.7 = (f32[257,256]{1,0:T(8,128)}, f32[257,256]{1,0:T(8,128)}, u32[]{:S(2)}, u32[]{:S(2)}) collective-permute-start(f32[257,256]{1,0:T(8,128)} %pad_maximum_fusion.2), channel_id=1, source_target_pairs={{0,2},{1,3},{2,4},{3,5},{4,6},{5,7},{6,8},{7,9},{8,10},{9,11},{10,... | collective-permute-start | bytes 789512 | tf_op jit(solution)/shard_map/ppermute | solution.py:13
  65.5 18.9 %all-to-all-start.4 = ((f32[16,64,256]{2,1,0:T(8,128)}), f32[16,64,256]{2,1,0:T(8,128)}, u32[]{:S(2)}, u32[]{:S(2)}) async-start(f32[16,64,256]{2,1,0:T(8,128)} %param.19), calls=%async_computation.4 | async-start | bytes 2097152 | tf_op jit(solution)/shard_map/all_to_all | solution.py:184
  69.7 1.4 copy-start.11
  72.4 0.8 copy-start.12
  73.3 24.4 %collective-permute-start.8 = (f32[257,256]{1,0:T(8,128)}, f32[257,256]{1,0:T(8,128)}, u32[]{:S(2)}, u32[]{:S(2)}) collective-permute-start(f32[257,256]{1,0:T(8,128)} %pad_maximum_fusion.3), channel_id=1, source_target_pairs={{0,4},{1,5},{2,6},{3,7},{4,8},{5,9},{6,10},{7,11},{8,12},{9,13},{1... | collective-permute-start | bytes 789512 | tf_op jit(solution)/shard_map/ppermute | solution.py:13
  85.6 1.2 copy-start.9
  87.0 1.0 copy-start.16
  88.0 15.3 %copy-start.7 = (f32[2,256,256]{2,1,0:T(8,128)}, f32[2,256,256]{2,1,0:T(8,128)S(1)}, u32[]{:S(2)}) copy-start(f32[2,256,256]{2,1,0:T(8,128)S(1)} %fusion.16) | copy-start | bytes 1572868
  91.3 1.4 copy-start.1
  93.0 4.7 %copy-start.13 = (f32[256,256]{1,0:T(8,128)S(1)}, f32[256,256]{1,0:T(8,128)}, u32[]{:S(2)}) copy-start(f32[256,256]{1,0:T(8,128)} %copy-done.12) | copy-start | bytes 786436
  93.5 12.4 %collective-permute-start.23 = (f32[256,256]{1,0:T(8,128)S(1)}, f32[256,256]{1,0:T(8,128)S(1)}, u32[]{:S(2)}, u32[]{:S(2)}) collective-permute-start(f32[256,256]{1,0:T(8,128)S(1)} %fusion.11), channel_id=1, source_target_pairs={{1,0},{2,1},{3,2},{4,3},{5,4},{6,5},{7,6},{8,7},{9,8},{10,9},{11,1... | collective-permute-start | bytes 786440 | tf_op jit(solution)/shard_map/ppermute | solution.py:13
  100.1 10.2 %collective-permute-start.9 = (f32[257,256]{1,0:T(8,128)S(1)}, f32[257,256]{1,0:T(8,128)S(1)}, u32[]{:S(2)}, u32[]{:S(2)}) collective-permute-start(f32[257,256]{1,0:T(8,128)S(1)} %pad_maximum_fusion.4), channel_id=1, source_target_pairs={{0,8},{1,9},{2,10},{3,11},{4,12},{5,13},{6,14},{7,15},{8,16},{9,17... | collective-permute-start | bytes 789512 | tf_op jit(solution)/shard_map/ppermute | solution.py:13
  103.6 14.3 %copy-start.3 = (f32[256,256]{1,0:T(8,128)}, f32[256,256]{1,0:T(8,128)S(1)}, u32[]{:S(2)}) copy-start(f32[256,256]{1,0:T(8,128)S(1)} %fusion.34) | copy-start | bytes 786436
  103.7 14.3 %collective-permute-start = (f32[256,256]{1,0:T(8,128)S(1)}, f32[256,256]{1,0:T(8,128)S(1)}, u32[]{:S(2)}, u32[]{:S(2)}) collective-permute-start(f32[256,256]{1,0:T(8,128)S(1)} %fusion.34), channel_id=1, source_target_pairs={{1,0},{2,1},{3,2},{4,3},{5,4},{6,5},{7,6},{8,7},{9,8},{10,9},{11,1... | collective-permute-start | bytes 786440 | tf_op jit(solution)/shard_map/ppermute | solution.py:13
  111.0 12.8 %collective-permute-start.10 = (f32[257,256]{1,0:T(8,128)S(1)}, f32[257,256]{1,0:T(8,128)S(1)}, u32[]{:S(2)}, u32[]{:S(2)}) collective-permute-start(f32[257,256]{1,0:T(8,128)S(1)} %pad_maximum_fusion.5), channel_id=1, source_target_pairs={{0,16},{1,17},{2,18},{3,19},{4,20},{5,21},{6,22},{7,23},{8,24},{9,... | collective-permute-start | bytes 789512 | tf_op jit(solution)/shard_map/ppermute | solution.py:13
  115.7 12.0 %collective-permute-start.24 = (f32[256,256]{1,0:T(8,128)S(1)}, f32[256,256]{1,0:T(8,128)S(1)}, u32[]{:S(2)}, u32[]{:S(2)}) collective-permute-start(f32[256,256]{1,0:T(8,128)S(1)} %fusion.8), channel_id=1, source_target_pairs={{2,0},{3,1},{4,2},{5,3},{6,4},{7,5},{8,6},{9,7},{10,8},{11,9},{12,... | collective-permute-start | bytes 786440 | tf_op jit(solution)/shard_map/ppermute | solution.py:13
  118.4 22.3 %copy-start.5 = (f32[256,256]{1,0:T(8,128)}, f32[256,256]{1,0:T(8,128)S(1)}, u32[]{:S(2)}) copy-start(f32[256,256]{1,0:T(8,128)S(1)} %convolution_select_fusion.11) | copy-start | bytes 786436
  118.4 22.2 %collective-permute-start.1 = (f32[256,256]{1,0:T(8,128)S(1)}, f32[256,256]{1,0:T(8,128)S(1)}, u32[]{:S(2)}, u32[]{:S(2)}) collective-permute-start(f32[256,256]{1,0:T(8,128)S(1)} %convolution_select_fusion.11), channel_id=1, source_target_pairs={{2,0},{3,1},{4,2},{5,3},{6,4},{7,5},{8,6},{9,7},{10,8},{11,9},{12,... | collective-permute-start | bytes 786440 | tf_op jit(solution)/shard_map/ppermute | solution.py:13
  124.6 10.3 %collective-permute-start.11 = (f32[257,256]{1,0:T(8,128)S(1)}, f32[257,256]{1,0:T(8,128)S(1)}, u32[]{:S(2)}, u32[]{:S(2)}) collective-permute-start(f32[257,256]{1,0:T(8,128)S(1)} %pad_maximum_fusion.6), channel_id=1, source_target_pairs={{0,32},{1,33},{2,34},{3,35},{4,36},{5,37},{6,38},{7,39},{8,40},{9,... | collective-permute-start | bytes 789512 | tf_op jit(solution)/shard_map/ppermute | solution.py:13
  129.2 26.0 %collective-permute-start.25 = (f32[256,256]{1,0:T(8,128)}, f32[256,256]{1,0:T(8,128)}, u32[]{:S(2)}, u32[]{:S(2)}) collective-permute-start(f32[256,256]{1,0:T(8,128)} %fusion.7), channel_id=1, source_target_pairs={{4,0},{5,1},{6,2},{7,3},{8,4},{9,5},{10,6},{11,7},{12,8},{13,9},{1... | collective-permute-start | bytes 786440 | tf_op jit(solution)/shard_map/ppermute | solution.py:13
  135.2 3.2 %collective-permute-start.12 = (f32[256]{0:T(256)S(1)}, f32[256]{0:T(256)S(1)}, u32[]{:S(2)}, u32[]{:S(2)}) collective-permute-start(f32[256]{0:T(256)S(1)} %add_select_fusion.8), channel_id=1, source_target_pairs={{0,64},{1,65},{2,66},{3,67},{4,68},{5,69},{6,70},{7,71},{8,72},{9,... | collective-permute-start | bytes 3080 | tf_op jit(solution)/shard_map/ppermute | solution.py:13
  138.7 6.5 %collective-permute-start.13 = (f32[256]{0:T(256)S(1)}, f32[256]{0:T(256)S(1)}, u32[]{:S(2)}, u32[]{:S(2)}) collective-permute-start(f32[256]{0:T(256)S(1)} %add_select_fusion.7), channel_id=1, source_target_pairs={{0,1},{1,2},{2,3},{3,4},{4,5},{5,6},{6,7},{7,8},{8,9},{9,10},{10,1... | collective-permute-start | bytes 3080 | tf_op jit(solution)/shard_map/ppermute | solution.py:13
  141.7 26.3 %collective-permute-start.2 = (f32[256,256]{1,0:T(8,128)}, f32[256,256]{1,0:T(8,128)}, u32[]{:S(2)}, u32[]{:S(2)}) collective-permute-start(f32[256,256]{1,0:T(8,128)} %convolution_select_fusion.10), channel_id=1, source_target_pairs={{4,0},{5,1},{6,2},{7,3},{8,4},{9,5},{10,6},{11,7},{12,8},{13,9},{1... | collective-permute-start | bytes 786440 | tf_op jit(solution)/shard_map/ppermute | solution.py:13
  147.8 1.1 copy-start.8
  149.1 7.5 %copy-start.4 = (f32[256,256]{1,0:T(8,128)S(1)}, f32[256,256]{1,0:T(8,128)}, u32[]{:S(2)}) copy-start(f32[256,256]{1,0:T(8,128)} %copy-done.3) | copy-start | bytes 786436
  149.1 7.5 %collective-permute-start.14 = (f32[256]{0:T(256)S(1)}, f32[256]{0:T(256)S(1)}, u32[]{:S(2)}, u32[]{:S(2)}) collective-permute-start(f32[256]{0:T(256)S(1)} %bitcast.388), channel_id=1, source_target_pairs={{1,0},{2,1},{3,2},{4,3},{5,4},{6,5},{7,6},{8,7},{9,8},{10,9},{11,1... | collective-permute-start | bytes 3080 | tf_op jit(solution)/shard_map/ppermute | solution.py:13
  157.0 8.8 %copy-start.6 = (f32[256,256]{1,0:T(8,128)S(1)}, f32[256,256]{1,0:T(8,128)}, u32[]{:S(2)}) copy-start(f32[256,256]{1,0:T(8,128)} %copy-done.5) | copy-start | bytes 786436
  157.0 8.7 %collective-permute-start.15 = (f32[256]{0:T(256)S(1)}, f32[256]{0:T(256)S(1)}, u32[]{:S(2)}, u32[]{:S(2)}) collective-permute-start(f32[256]{0:T(256)S(1)} %add_select_fusion.6), channel_id=1, source_target_pairs={{2,0},{3,1},{4,2},{5,3},{6,4},{7,5},{8,6},{9,7},{10,8},{11,9},{12,... | collective-permute-start | bytes 3080 | tf_op jit(solution)/shard_map/ppermute | solution.py:13
  162.1 23.3 %collective-permute-start.26 = (f32[256,256]{1,0:T(8,128)S(1)}, f32[256,256]{1,0:T(8,128)S(1)}, u32[]{:S(2)}, u32[]{:S(2)}) collective-permute-start(f32[256,256]{1,0:T(8,128)S(1)} %fusion.6), channel_id=1, source_target_pairs={{8,0},{9,1},{10,2},{11,3},{12,4},{13,5},{14,6},{15,7},{16,8},{17,9... | collective-permute-start | bytes 786440 | tf_op jit(solution)/shard_map/ppermute | solution.py:13
  166.1 9.3 %collective-permute-start.16 = (f32[256]{0:T(256)S(1)}, f32[256]{0:T(256)S(1)}, u32[]{:S(2)}, u32[]{:S(2)}) collective-permute-start(f32[256]{0:T(256)S(1)} %add_select_fusion.5), channel_id=1, source_target_pairs={{4,0},{5,1},{6,2},{7,3},{8,4},{9,5},{10,6},{11,7},{12,8},{13,9},{1... | collective-permute-start | bytes 3080 | tf_op jit(solution)/shard_map/ppermute | solution.py:13
  169.5 21.2 %collective-permute-start.3 = (f32[256,256]{1,0:T(8,128)S(1)}, f32[256,256]{1,0:T(8,128)S(1)}, u32[]{:S(2)}, u32[]{:S(2)}) collective-permute-start(f32[256,256]{1,0:T(8,128)S(1)} %convolution_select_fusion.9), channel_id=1, source_target_pairs={{8,0},{9,1},{10,2},{11,3},{12,4},{13,5},{14,6},{15,7},{16,8},{17,9... | collective-permute-start | bytes 786440 | tf_op jit(solution)/shard_map/ppermute | solution.py:13
  176.7 6.4 %collective-permute-start.17 = (f32[256]{0:T(256)S(1)}, f32[256]{0:T(256)S(1)}, u32[]{:S(2)}, u32[]{:S(2)}) collective-permute-start(f32[256]{0:T(256)S(1)} %add_select_fusion.4), channel_id=1, source_target_pairs={{8,0},{9,1},{10,2},{11,3},{12,4},{13,5},{14,6},{15,7},{16,8},{17,9... | collective-permute-start | bytes 3080 | tf_op jit(solution)/shard_map/ppermute | solution.py:13
  183.4 9.7 %collective-permute-start.18 = (f32[256]{0:T(256)S(1)}, f32[256]{0:T(256)S(1)}, u32[]{:S(2)}, u32[]{:S(2)}) collective-permute-start(f32[256]{0:T(256)S(1)} %add_select_fusion.3), channel_id=1, source_target_pairs={{16,0},{17,1},{18,2},{19,3},{20,4},{21,5},{22,6},{23,7},{24,8},{25... | collective-permute-start | bytes 3080 | tf_op jit(solution)/shard_map/ppermute | solution.py:13
  186.2 11.4 %collective-permute-start.27 = (f32[256,256]{1,0:T(8,128)S(1)}, f32[256,256]{1,0:T(8,128)S(1)}, u32[]{:S(2)}, u32[]{:S(2)}) collective-permute-start(f32[256,256]{1,0:T(8,128)S(1)} %fusion.5), channel_id=1, source_target_pairs={{16,0},{17,1},{18,2},{19,3},{20,4},{21,5},{22,6},{23,7},{24,8},{25... | collective-permute-start | bytes 786440 | tf_op jit(solution)/shard_map/ppermute | solution.py:13
  191.1 12.7 %collective-permute-start.4 = (f32[256,256]{1,0:T(8,128)S(1)}, f32[256,256]{1,0:T(8,128)S(1)}, u32[]{:S(2)}, u32[]{:S(2)}) collective-permute-start(f32[256,256]{1,0:T(8,128)S(1)} %convolution_select_fusion.8), channel_id=1, source_target_pairs={{16,0},{17,1},{18,2},{19,3},{20,4},{21,5},{22,6},{23,7},{24,8},{25... | collective-permute-start | bytes 786440 | tf_op jit(solution)/shard_map/ppermute | solution.py:13
  193.4 13.1 %collective-permute-start.19 = (f32[256]{0:T(256)S(1)}, f32[256]{0:T(256)S(1)}, u32[]{:S(2)}, u32[]{:S(2)}) collective-permute-start(f32[256]{0:T(256)S(1)} %add_select_fusion.2), channel_id=1, source_target_pairs={{32,0},{33,1},{34,2},{35,3},{36,4},{37,5},{38,6},{39,7},{40,8},{41... | collective-permute-start | bytes 3080 | tf_op jit(solution)/shard_map/ppermute | solution.py:13
  198.4 29.3 %collective-permute-start.28 = (f32[256,256]{1,0:T(8,128)S(1)}, f32[256,256]{1,0:T(8,128)S(1)}, u32[]{:S(2)}, u32[]{:S(2)}) collective-permute-start(f32[256,256]{1,0:T(8,128)S(1)} %fusion.4), channel_id=1, source_target_pairs={{32,0},{33,1},{34,2},{35,3},{36,4},{37,5},{38,6},{39,7},{40,8},{41... | collective-permute-start | bytes 786440 | tf_op jit(solution)/shard_map/ppermute | solution.py:13
  204.2 10.3 %collective-permute-start.5 = (f32[256,256]{1,0:T(8,128)S(1)}, f32[256,256]{1,0:T(8,128)S(1)}, u32[]{:S(2)}, u32[]{:S(2)}) collective-permute-start(f32[256,256]{1,0:T(8,128)S(1)} %convolution_select_fusion.7), channel_id=1, source_target_pairs={{32,0},{33,1},{34,2},{35,3},{36,4},{37,5},{38,6},{39,7},{40,8},{41... | collective-permute-start | bytes 786440 | tf_op jit(solution)/shard_map/ppermute | solution.py:13
  206.9 18.6 %collective-permute-start.20 = (f32[256]{0:T(256)S(1)}, f32[256]{0:T(256)S(1)}, u32[]{:S(2)}, u32[]{:S(2)}) collective-permute-start(f32[256]{0:T(256)S(1)} %add_select_fusion.1), channel_id=1, source_target_pairs={{64,0},{65,1},{66,2},{67,3},{68,4},{69,5},{70,6},{71,7},{72,8},{73... | collective-permute-start | bytes 3080 | tf_op jit(solution)/shard_map/ppermute | solution.py:13
  214.9 24.0 %collective-permute-start.22 = (f32[256,256]{1,0:T(8,128)S(1)}, f32[256,256]{1,0:T(8,128)S(1)}, u32[]{:S(2)}, u32[]{:S(2)}) collective-permute-start(f32[256,256]{1,0:T(8,128)S(1)} %convolution_select_fusion.6), channel_id=1, source_target_pairs={{1,0},{2,1},{3,2},{4,3},{5,4},{6,5},{7,6},{8,7},{9,8},{10,9},{11,1... | collective-permute-start | bytes 786440 | tf_op jit(solution)/shard_map/ppermute | solution.py:13
  225.8 6.5 %collective-permute-start.21 = (f32[256]{0:T(256)S(1)}, f32[256]{0:T(256)S(1)}, u32[]{:S(2)}, u32[]{:S(2)}) collective-permute-start(f32[256]{0:T(256)S(1)} %add_select_fusion), channel_id=1, source_target_pairs={{1,0},{2,1},{3,2},{4,3},{5,4},{6,5},{7,6},{8,7},{9,8},{10,9},{11,1... | collective-permute-start | bytes 3080 | tf_op jit(solution)/shard_map/ppermute | solution.py:13
  228.5 10.4 %collective-permute-start.29 = (f32[256,256]{1,0:T(8,128)S(1)}, f32[256,256]{1,0:T(8,128)S(1)}, u32[]{:S(2)}, u32[]{:S(2)}) collective-permute-start(f32[256,256]{1,0:T(8,128)S(1)} %fusion.3), channel_id=1, source_target_pairs={{65,0},{66,1},{67,2},{68,3},{69,4},{70,5},{71,6},{72,7},{73,8},{74... | collective-permute-start | bytes 786440 | tf_op jit(solution)/shard_map/ppermute | solution.py:13
  229.8 12.2 %collective-permute-start.30 = (f32[256,256]{1,0:T(8,128)S(1)}, f32[256,256]{1,0:T(8,128)S(1)}, u32[]{:S(2)}, u32[]{:S(2)}) collective-permute-start(f32[256,256]{1,0:T(8,128)S(1)} %fusion.3), channel_id=1, source_target_pairs={{1,0},{2,1},{3,2},{4,3},{5,4},{6,5},{7,6},{8,7},{9,8},{10,9},{11,1... | collective-permute-start | bytes 786440 | tf_op jit(solution)/shard_map/ppermute | solution.py:13
  234.7 12.7 %all-to-all-start.3 = ((f32[4,1,256]{2,1,0:T(1,128)}), f32[4,1,256]{2,1,0:T(1,128)S(1)}, u32[]{:S(2)}, u32[]{:S(2)}) async-start(f32[4,1,256]{2,1,0:T(1,128)} %reshape.134), calls=%async_computation.3 | async-start | bytes 8192 | tf_op jit(solution)/shard_map/all_to_all | solution.py:187
  239.3 3.5 %copy-start.2 = (f32[4,256,256]{2,1,0:T(8,128)S(1)}, f32[4,256,256]{2,1,0:T(8,128)}, u32[]{:S(2)}) copy-start(f32[4,256,256]{2,1,0:T(8,128)} %copy-done.1) | copy-start | bytes 3145732
  247.4 17.5 %all-to-all-start.5 = ((f32[4,256,256]{2,0,1:T(4,128)}), f32[4,256,256]{2,0,1:T(4,128)S(1)}, u32[]{:S(2)}, u32[]{:S(2)}) async-start(f32[4,256,256]{2,0,1:T(4,128)} %copy.48), calls=%async_computation.5 | async-start | bytes 2097152 | tf_op jit(solution)/shard_map/all_to_all | solution.py:187

commit v11 on v9

--- a/solution.py
+++ b/solution.py
@@ -90,6 +90,10 @@
         gain = jnp.where(has_right, matmul(gain, gain_right), gain)
         distance *= 2
     round_gains.append(gain)
+    return gain, resid, distance, round_gains
+
+
+def cov_finish(gain, resid, distance, tm_index, tm_count):
     gain_next = from_behind(gain, CHUNKS, -1)
     resid_next = from_behind(resid, CHUNKS, -1)
     resid_far = from_behind(resid, CHUNKS, -(distance + 1))
@@ -97,7 +101,7 @@
     cov_after = jnp.where(
         has_far, matmul(matmul(gain_next, resid_far), gain_next.T) + resid_next, resid_next
     )
-    return jnp.where(tm_index == tm_count - 1, jnp.float32(0.0), cov_after), round_gains
+    return jnp.where(tm_index == tm_count - 1, jnp.float32(0.0), cov_after)
 
 
 def offset_scan(window_offset, round_gains, tm_index, tm_count):
@@ -131,7 +135,7 @@
     gain_trans = jnp.swapaxes(gain_full, 1, 2)
     residual_cov = cov_full - matmul(matmul(gain_full, predicted), gain_trans)
     window_gain, window_resid, gain_levels = smooth_tree(gain_full, residual_cov)
-    cov_after, round_gains = cov_scan(window_gain, window_resid, tm_index, tm_count)
+    scan_gain, scan_resid, distance, round_gains = cov_scan(window_gain, window_resid, tm_index, tm_count)
 
     window_map, window_shift = filter_tree(transition_operators, step_shifts)
     mean_in = filter_scan(window_map, window_shift, initial_expectation, tm_index, tm_count)
@@ -145,6 +149,8 @@
     moved_means = jnp.einsum("ij,tj->ti", trans_map, filt_means, precision=highest)
     offsets = filt_means - jnp.einsum("tij,tj->ti", gain_full, moved_means, precision=highest)
     mean_after = offset_scan(offset_tree(gain_levels, offsets), round_gains, tm_index, tm_count)
+    scan_gain, scan_resid, mean_after = lax.optimization_barrier((scan_gain, scan_resid, mean_after))
+    cov_after = cov_finish(scan_gain, scan_resid, distance, tm_index, tm_count)
 
     cov_steps = [None] * step_count
     mean_steps = [None] * step_count

time: 261 us -> 272 us (1.042)
  starting transfers between devices: 122 us -> 128 us
    ppermute x31, starting transfers between devices: 96.5 us -> 102 us  [from_behind(): return lax.ppermute(block, axis, route)]
    ppermute x31, waiting for transfers between devices: 36.7 us -> 39.5 us  [from_behind(): return lax.ppermute(block, axis, route)]
  transfers between devices with their start and end apart: 37 -> 37, of which waited for: 15 -> 18; matrix products, arithmetic and copies ran while one was open for 21% -> 20% of each run, Pallas kernels for 0% -> 0%
where the time goes in v11:
time: 272 us; the launch traced here: 267 us
  starting transfers between devices  128 us (47%)
  waiting for transfers between devices  72 us (26%)
  matrix products  44.6 us (16%)
  local copies, waits for them, and re-layouts  16.8 us (6%)
  other arithmetic  3.55 us (1%)
    ppermute x31, starting transfers between devices, from_behind(): return lax.ppermute(block, axis, route)  102 us
    ppermute x31, waiting for transfers between devices, from_behind(): return lax.ppermute(block, axis, route)  39.5 us
    dot_general x48, matrix products, matmul(): return jnp.matmul(left, right, precision=highest)  31.9 us
    all_to_all x4, waiting for transfers between devices, steps_whole(): return lax.all_to_all(rows, 'blk', 0, 1, tiled=True)  19.7 us
    all_to_all x4, starting transfers between devices, steps_whole(): return lax.all_to_all(rows, 'blk', 0, 1, tiled=True)  17.8 us
    all_to_all x2, waiting for transfers between devices, rows_of_steps(): return lax.all_to_all(whole, 'blk', 1, 0, tiled=True)  12.8 us
    dot_general x27, matrix products, matvec(): return jnp.einsum('...ij,...j->...i', left, right, precision=highest)  9.72 us
    unnamed x40, local copies, waits for them, and re-layouts  8.89 us
  transfers between devices with their start and end apart: 37, of which 18 were waited for; matrix products, arithmetic and copies ran while one was open for 20% of the time, Pallas kernels for 0%

profile of v11, /device:TPU:15, one launch (start us, length us, event | category | flops | bytes accessed | tf_op | source)
XLA Modules:
  0.0 267.0 jit_solution(10333957521197334669)
XLA Ops:
  0.6 1.2 copy-done
  1.9 1.7 fusion.54
  4.3 5.0 %all-to-all-start.3 = ((f32[4,1,256]{2,1,0:T(1,128)}), f32[4,1,256]{2,1,0:T(1,128)S(1)}, u32[]{:S(2)}, u32[]{:S(2)}) async-start(f32[4,1,256]{2,1,0:T(1,128)} %reshape.170), calls=%async_computation.3 | async-start | bytes 8192 | tf_op jit(solution)/shard_map/all_to_all | solution.py:190
  12.8 2.0 fusion
  14.8 4.2 %all-to-all-start.2 = ((f32[16,64,256]{2,1,0:T(8,128)}), f32[16,64,256]{2,1,0:T(8,128)S(1)}, u32[]{:S(2)}, u32[]{:S(2)}) async-start(f32[16,64,256]{2,1,0:T(8,128)} %fusion), calls=%async_computation.2 | async-start | bytes 2097152 | tf_op jit(solution)/shard_map/all_to_all | solution.py:190
  22.3 10.4 %all-to-all-done.2 = f32[16,64,256]{2,1,0:T(8,128)S(1)} async-done(((f32[16,64,256]{2,1,0:T(8,128)}), f32[16,64,256]{2,1,0:T(8,128)S(1)}, u32[]{:S(2)}, u32[]{:S(2)}) %all-to-all-start.2) | async-done | bytes 1048608 | tf_op jit(solution)/shard_map/all_to_all | solution.py:190
  32.6 4.3 %all-to-all-start = ((f32[16,64,256]{2,1,0:T(8,128)}), f32[16,64,256]{2,1,0:T(8,128)}, u32[]{:S(2)}, u32[]{:S(2)}) async-start(f32[16,64,256]{2,1,0:T(8,128)} %param.18), calls=%async_computation | async-start | bytes 2097152 | tf_op jit(solution)/shard_map/all_to_all | solution.py:190
  40.0 9.3 %all-to-all-done = f32[16,64,256]{2,1,0:T(8,128)} async-done(((f32[16,64,256]{2,1,0:T(8,128)}), f32[16,64,256]{2,1,0:T(8,128)}, u32[]{:S(2)}, u32[]{:S(2)}) %all-to-all-start) | async-done | bytes 1048608 | tf_op jit(solution)/shard_map/all_to_all | solution.py:190
  49.4 4.3 %all-to-all-start.1 = ((f32[16,64,256]{2,1,0:T(8,128)}), f32[16,64,256]{2,1,0:T(8,128)}, u32[]{:S(2)}, u32[]{:S(2)}) async-start(f32[16,64,256]{2,1,0:T(8,128)} %param.19), calls=%async_computation.1 | async-start | bytes 2097152 | tf_op jit(solution)/shard_map/all_to_all | solution.py:190
  54.4 3.3 %collective-permute-start.12 = (f32[257,256]{1,0:T(8,128)}, f32[257,256]{1,0:T(8,128)}, u32[]{:S(2)}, u32[]{:S(2)}) collective-permute-start(f32[257,256]{1,0:T(8,128)} %pad_maximum_fusion.1), channel_id=1, source_target_pairs={{0,1},{1,2},{2,3},{3,4},{4,5},{5,6},{6,7},{7,8},{8,9},{9,10},{10,1... | collective-permute-start | bytes 789512 | tf_op jit(solution)/shard_map/ppermute | solution.py:13
  57.7 1.3 copy.37
  61.7 7.1 %collective-permute-start = (f32[256,256]{1,0:T(8,128)}, f32[256,256]{1,0:T(8,128)}, u32[]{:S(2)}, u32[]{:S(2)}) collective-permute-start(f32[256,256]{1,0:T(8,128)} %fusion.34), channel_id=1, source_target_pairs={{1,0},{2,1},{3,2},{4,3},{5,4},{6,5},{7,6},{8,7},{9,8},{10,9},{11,1... | collective-permute-start | bytes 786440 | tf_op jit(solution)/shard_map/ppermute | solution.py:13
  68.9 1.3 copy.38
  77.1 4.9 %collective-permute-start.6 = (f32[256,256]{1,0:T(8,128)S(1)}, f32[256,256]{1,0:T(8,128)S(1)}, u32[]{:S(2)}, u32[]{:S(2)}) collective-permute-start(f32[256,256]{1,0:T(8,128)S(1)} %fusion.11), channel_id=1, source_target_pairs={{1,0},{2,1},{3,2},{4,3},{5,4},{6,5},{7,6},{8,7},{9,8},{10,9},{11,1... | collective-permute-start | bytes 786440 | tf_op jit(solution)/shard_map/ppermute | solution.py:13
  83.1 1.4 convolution_select_fusion.5
  84.5 1.9 collective-permute-start.13
  86.5 1.5 convolution_select_fusion.11
  88.0 5.1 %collective-permute-start.1 = (f32[256,256]{1,0:T(8,128)S(1)}, f32[256,256]{1,0:T(8,128)S(1)}, u32[]{:S(2)}, u32[]{:S(2)}) collective-permute-start(f32[256,256]{1,0:T(8,128)S(1)} %convolution_select_fusion.11), channel_id=1, source_target_pairs={{2,0},{3,1},{4,2},{5,3},{6,4},{7,5},{8,6},{9,7},{10,8},{11,9},{12,... | collective-permute-start | bytes 786440 | tf_op jit(solution)/shard_map/ppermute | solution.py:13
  93.1 1.3 fusion.71
  94.5 2.8 %collective-permute-done.13 = f32[257,256]{1,0:T(8,128)S(1)} collective-permute-done((f32[257,256]{1,0:T(8,128)S(1)}, f32[257,256]{1,0:T(8,128)S(1)}, u32[]{:S(2)}, u32[]{:S(2)}) %collective-permute-start.13) | collective-permute-done | bytes 263200 | tf_op jit(solution)/shard_map/ppermute | solution.py:13
  98.0 4.8 %collective-permute-start.14 = (f32[257,256]{1,0:T(8,128)S(1)}, f32[257,256]{1,0:T(8,128)S(1)}, u32[]{:S(2)}, u32[]{:S(2)}) collective-permute-start(f32[257,256]{1,0:T(8,128)S(1)} %pad_maximum_fusion.3), channel_id=1, source_target_pairs={{0,4},{1,5},{2,6},{3,7},{4,8},{5,9},{6,10},{7,11},{8,12},{9,13},{1... | collective-permute-start | bytes 789512 | tf_op jit(solution)/shard_map/ppermute | solution.py:13
  102.8 1.4 fusion.8
  104.2 1.9 collective-permute-start.7
  106.5 1.9 collective-permute-start.2
  109.2 3.4 %collective-permute-start.15 = (f32[257,256]{1,0:T(8,128)S(1)}, f32[257,256]{1,0:T(8,128)S(1)}, u32[]{:S(2)}, u32[]{:S(2)}) collective-permute-start(f32[257,256]{1,0:T(8,128)S(1)} %pad_maximum_fusion.4), channel_id=1, source_target_pairs={{0,8},{1,9},{2,10},{3,11},{4,12},{5,13},{6,14},{7,15},{8,16},{9,17... | collective-permute-start | bytes 789512 | tf_op jit(solution)/shard_map/ppermute | solution.py:13
  114.5 3.6 %collective-permute-start.8 = (f32[256,256]{1,0:T(8,128)S(1)}, f32[256,256]{1,0:T(8,128)S(1)}, u32[]{:S(2)}, u32[]{:S(2)}) collective-permute-start(f32[256,256]{1,0:T(8,128)S(1)} %fusion.7), channel_id=1, source_target_pairs={{4,0},{5,1},{6,2},{7,3},{8,4},{9,5},{10,6},{11,7},{12,8},{13,9},{1... | collective-permute-start | bytes 786440 | tf_op jit(solution)/shard_map/ppermute | solution.py:13
  119.3 3.2 %collective-permute-start.16 = (f32[257,256]{1,0:T(8,128)S(1)}, f32[257,256]{1,0:T(8,128)S(1)}, u32[]{:S(2)}, u32[]{:S(2)}) collective-permute-start(f32[257,256]{1,0:T(8,128)S(1)} %pad_maximum_fusion.5), channel_id=1, source_target_pairs={{0,16},{1,17},{2,18},{3,19},{4,20},{5,21},{6,22},{7,23},{8,24},{9,... | collective-permute-start | bytes 789512 | tf_op jit(solution)/shard_map/ppermute | solution.py:13
  122.9 2.8 %collective-permute-start.3 = (f32[256,256]{1,0:T(8,128)S(1)}, f32[256,256]{1,0:T(8,128)S(1)}, u32[]{:S(2)}, u32[]{:S(2)}) collective-permute-start(f32[256,256]{1,0:T(8,128)S(1)} %convolution_select_fusion.9), channel_id=1, source_target_pairs={{8,0},{9,1},{10,2},{11,3},{12,4},{13,5},{14,6},{15,7},{16,8},{17,9... | collective-permute-start | bytes 786440 | tf_op jit(solution)/shard_map/ppermute | solution.py:13
  126.2 4.1 %collective-permute-done.16 = f32[257,256]{1,0:T(8,128)S(1)} collective-permute-done((f32[257,256]{1,0:T(8,128)S(1)}, f32[257,256]{1,0:T(8,128)S(1)}, u32[]{:S(2)}, u32[]{:S(2)}) %collective-permute-start.16) | collective-permute-done | bytes 263200 | tf_op jit(solution)/shard_map/ppermute | solution.py:13
  131.0 3.6 %collective-permute-start.17 = (f32[257,256]{1,0:T(8,128)S(1)}, f32[257,256]{1,0:T(8,128)S(1)}, u32[]{:S(2)}, u32[]{:S(2)}) collective-permute-start(f32[257,256]{1,0:T(8,128)S(1)} %pad_maximum_fusion.6), channel_id=1, source_target_pairs={{0,32},{1,33},{2,34},{3,35},{4,36},{5,37},{6,38},{7,39},{8,40},{9,... | collective-permute-start | bytes 789512 | tf_op jit(solution)/shard_map/ppermute | solution.py:13
  135.1 1.9 collective-permute-start.9
  138.4 1.9 collective-permute-start.4
  140.6 1.9 collective-permute-start.18
  143.6 7.6 %collective-permute-start.19 = (f32[256]{0:T(256)S(1)}, f32[256]{0:T(256)S(1)}, u32[]{:S(2)}, u32[]{:S(2)}) collective-permute-start(f32[256]{0:T(256)S(1)} %add_select_fusion.7), channel_id=1, source_target_pairs={{0,1},{1,2},{2,3},{3,4},{4,5},{5,6},{6,7},{7,8},{8,9},{9,10},{10,1... | collective-permute-start | bytes 3080 | tf_op jit(solution)/shard_map/ppermute | solution.py:13
  152.3 4.5 %collective-permute-done.19 = f32[256]{0:T(256)S(1)} collective-permute-done((f32[256]{0:T(256)S(1)}, f32[256]{0:T(256)S(1)}, u32[]{:S(2)}, u32[]{:S(2)}) %collective-permute-start.19) | collective-permute-done | bytes 1056 | tf_op jit(solution)/shard_map/ppermute | solution.py:13
  160.8 4.4 %collective-permute-start.20 = (f32[256]{0:T(256)S(1)}, f32[256]{0:T(256)S(1)}, u32[]{:S(2)}, u32[]{:S(2)}) collective-permute-start(f32[256]{0:T(256)S(1)} %bitcast.381), channel_id=1, source_target_pairs={{1,0},{2,1},{3,2},{4,3},{5,4},{6,5},{7,6},{8,7},{9,8},{10,9},{11,1... | collective-permute-start | bytes 3080 | tf_op jit(solution)/shard_map/ppermute | solution.py:13
  165.1 1.4 fusion.5
  166.5 2.5 collective-permute-start.10
  169.1 1.2 fusion.83
  170.4 5.0 %collective-permute-start.21 = (f32[256]{0:T(256)S(1)}, f32[256]{0:T(256)S(1)}, u32[]{:S(2)}, u32[]{:S(2)}) collective-permute-start(f32[256]{0:T(256)S(1)} %add_select_fusion.6), channel_id=1, source_target_pairs={{2,0},{3,1},{4,2},{5,3},{6,4},{7,5},{8,6},{9,7},{10,8},{11,9},{12,... | collective-permute-start | bytes 3080 | tf_op jit(solution)/shard_map/ppermute | solution.py:13
  175.4 1.3 convolution_select_fusion.7
  176.7 3.4 %collective-permute-start.5 = (f32[256,256]{1,0:T(8,128)S(1)}, f32[256,256]{1,0:T(8,128)S(1)}, u32[]{:S(2)}, u32[]{:S(2)}) collective-permute-start(f32[256,256]{1,0:T(8,128)S(1)} %convolution_select_fusion.7), channel_id=1, source_target_pairs={{32,0},{33,1},{34,2},{35,3},{36,4},{37,5},{38,6},{39,7},{40,8},{41... | collective-permute-start | bytes 786440 | tf_op jit(solution)/shard_map/ppermute | solution.py:13
  180.5 1.9 collective-permute-start.22
  182.8 4.7 %collective-permute-done.22 = f32[256]{0:T(256)S(1)} collective-permute-done((f32[256]{0:T(256)S(1)}, f32[256]{0:T(256)S(1)}, u32[]{:S(2)}, u32[]{:S(2)}) %collective-permute-start.22) | collective-permute-done | bytes 1056 | tf_op jit(solution)/shard_map/ppermute | solution.py:13
  187.8 1.9 collective-permute-start.23
  190.2 1.9 collective-permute-start.11
  192.1 2.2 collective-permute-done.23
  194.6 1.9 collective-permute-start.24
  196.5 2.7 collective-permute-done.11
  199.6 1.7 collective-permute-done.24
  201.6 1.9 collective-permute-start.25
  204.0 2.2 collective-permute-done.25
  206.5 1.3 collective-permute-start.26
  208.2 4.1 %collective-permute-done.26 = f32[256]{0:T(256)S(1)} collective-permute-done((f32[256]{0:T(256)S(1)}, f32[256]{0:T(256)S(1)}, u32[]{:S(2)}, u32[]{:S(2)}) %collective-permute-start.26) | collective-permute-done | bytes 1056 | tf_op jit(solution)/shard_map/ppermute | solution.py:13
  212.7 6.5 %collective-permute-start.27 = (f32[256]{0:T(256)S(1)}, f32[256]{0:T(256)S(1)}, u32[]{:S(2)}, u32[]{:S(2)}) collective-permute-start(f32[256]{0:T(256)S(1)} %add_select_fusion), channel_id=1, source_target_pairs={{1,0},{2,1},{3,2},{4,3},{5,4},{6,5},{7,6},{8,7},{9,8},{10,9},{11,1... | collective-permute-start | bytes 3080 | tf_op jit(solution)/shard_map/ppermute | solution.py:13
  219.8 1.3 collective-permute-start.29
  221.1 5.4 %collective-permute-start.30 = (f32[256,256]{1,0:T(8,128)S(1)}, f32[256,256]{1,0:T(8,128)S(1)}, u32[]{:S(2)}, u32[]{:S(2)}) collective-permute-start(f32[256,256]{1,0:T(8,128)S(1)} %fusion.3), channel_id=1, source_target_pairs={{1,0},{2,1},{3,2},{4,3},{5,4},{6,5},{7,6},{8,7},{9,8},{10,9},{11,1... | collective-permute-start | bytes 786440 | tf_op jit(solution)/shard_map/ppermute | solution.py:13
  226.5 1.9 collective-permute-start.28
  230.8 3.5 %all-to-all-start.4 = ((f32[4,1,256]{2,1,0:T(1,128)}), f32[4,1,256]{2,1,0:T(1,128)S(1)}, u32[]{:S(2)}, u32[]{:S(2)}) async-start(f32[4,1,256]{2,1,0:T(1,128)} %reshape.172), calls=%async_computation.4 | async-start | bytes 8192 | tf_op jit(solution)/shard_map/all_to_all | solution.py:193
  234.4 7.0 %collective-permute-done.28 = f32[256,256]{1,0:T(8,128)S(1)} collective-permute-done((f32[256,256]{1,0:T(8,128)S(1)}, f32[256,256]{1,0:T(8,128)S(1)}, u32[]{:S(2)}, u32[]{:S(2)}) %collective-permute-start.28) | collective-permute-done | bytes 262176 | tf_op jit(solution)/shard_map/ppermute | solution.py:13
  245.9 1.6 copy.48
  247.5 4.2 %all-to-all-start.5 = ((f32[4,256,256]{2,0,1:T(4,128)}), f32[4,256,256]{2,0,1:T(4,128)S(1)}, u32[]{:S(2)}, u32[]{:S(2)}) async-start(f32[4,256,256]{2,0,1:T(4,128)} %copy.48), calls=%async_computation.5 | async-start | bytes 2097152 | tf_op jit(solution)/shard_map/all_to_all | solution.py:193
  253.0 12.8 %all-to-all-done.5 = f32[4,256,256]{2,0,1:T(4,128)S(1)} async-done(((f32[4,256,256]{2,0,1:T(4,128)}), f32[4,256,256]{2,0,1:T(4,128)S(1)}, u32[]{:S(2)}, u32[]{:S(2)}) %all-to-all-start.5) | async-done | bytes 1048608 | tf_op jit(solution)/shard_map/all_to_all | solution.py:193
  265.8 1.2 copy.49
  (204 shorter events, 48.7 us)
Async XLA Ops:
  0.6 1.2 copy-start
  1.9 7.5 %copy-start.11 = (f32[256,256]{1,0:T(8,128)S(1)}, f32[256,256]{1,0:T(8,128)}, u32[]{:S(2)}) copy-start(f32[256,256]{1,0:T(8,128)} %param.10) | copy-start | bytes 786436
  4.3 10.5 %all-to-all-start.3 = ((f32[4,1,256]{2,1,0:T(1,128)}), f32[4,1,256]{2,1,0:T(1,128)S(1)}, u32[]{:S(2)}, u32[]{:S(2)}) async-start(f32[4,1,256]{2,1,0:T(1,128)} %reshape.170), calls=%async_computation.3 | async-start | bytes 8192 | tf_op jit(solution)/shard_map/all_to_all | solution.py:190
  9.3 0.7 copy-start.14
  10.3 1.0 copy-start.12
  11.2 0.7 copy-start.15
  14.8 17.9 %all-to-all-start.2 = ((f32[16,64,256]{2,1,0:T(8,128)}), f32[16,64,256]{2,1,0:T(8,128)S(1)}, u32[]{:S(2)}, u32[]{:S(2)}) async-start(f32[16,64,256]{2,1,0:T(8,128)} %fusion), calls=%async_computation.2 | async-start | bytes 2097152 | tf_op jit(solution)/shard_map/all_to_all | solution.py:190
  19.0 0.7 copy-start.16
  32.6 16.7 %all-to-all-start = ((f32[16,64,256]{2,1,0:T(8,128)}), f32[16,64,256]{2,1,0:T(8,128)}, u32[]{:S(2)}, u32[]{:S(2)}) async-start(f32[16,64,256]{2,1,0:T(8,128)} %param.18), calls=%async_computation | async-start | bytes 2097152 | tf_op jit(solution)/shard_map/all_to_all | solution.py:190
  38.6 15.0 %copy-start.6 = (f32[256,256]{1,0:T(8,128)}, f32[256,256]{1,0:T(8,128)S(1)}, u32[]{:S(2)}) copy-start(f32[256,256]{1,0:T(8,128)S(1)} %get-tuple-element.20) | copy-start | bytes 786436
  38.6 0.7 copy-start.13
  49.4 19.5 %all-to-all-start.1 = ((f32[16,64,256]{2,1,0:T(8,128)}), f32[16,64,256]{2,1,0:T(8,128)}, u32[]{:S(2)}, u32[]{:S(2)}) async-start(f32[16,64,256]{2,1,0:T(8,128)} %param.19), calls=%async_computation.1 | async-start | bytes 2097152 | tf_op jit(solution)/shard_map/all_to_all | solution.py:190
  54.4 27.7 %collective-permute-start.12 = (f32[257,256]{1,0:T(8,128)}, f32[257,256]{1,0:T(8,128)}, u32[]{:S(2)}, u32[]{:S(2)}) collective-permute-start(f32[257,256]{1,0:T(8,128)} %pad_maximum_fusion.1), channel_id=1, source_target_pairs={{0,1},{1,2},{2,3},{3,4},{4,5},{5,6},{6,7},{7,8},{8,9},{9,10},{10,1... | collective-permute-start | bytes 789512 | tf_op jit(solution)/shard_map/ppermute | solution.py:13
  59.8 0.8 copy-start.3
  61.7 24.7 %collective-permute-start = (f32[256,256]{1,0:T(8,128)}, f32[256,256]{1,0:T(8,128)}, u32[]{:S(2)}, u32[]{:S(2)}) collective-permute-start(f32[256,256]{1,0:T(8,128)} %fusion.34), channel_id=1, source_target_pairs={{1,0},{2,1},{3,2},{4,3},{5,4},{6,5},{7,6},{8,7},{9,8},{10,9},{11,1... | collective-permute-start | bytes 786440 | tf_op jit(solution)/shard_map/ppermute | solution.py:13
  70.2 1.1 copy-start.8
  74.6 1.4 copy-start.1
  75.2 1.0 copy-start.4
  77.1 5.0 %copy-start.7 = (f32[256,256]{1,0:T(8,128)S(1)}, f32[256,256]{1,0:T(8,128)}, u32[]{:S(2)}) copy-start(f32[256,256]{1,0:T(8,128)} %copy-done.6) | copy-start | bytes 786436
  77.1 16.0 %collective-permute-start.6 = (f32[256,256]{1,0:T(8,128)S(1)}, f32[256,256]{1,0:T(8,128)S(1)}, u32[]{:S(2)}, u32[]{:S(2)}) collective-permute-start(f32[256,256]{1,0:T(8,128)S(1)} %fusion.11), channel_id=1, source_target_pairs={{1,0},{2,1},{3,2},{4,3},{5,4},{6,5},{7,6},{8,7},{9,8},{10,9},{11,1... | collective-permute-start | bytes 786440 | tf_op jit(solution)/shard_map/ppermute | solution.py:13
  84.5 12.7 %collective-permute-start.13 = (f32[257,256]{1,0:T(8,128)S(1)}, f32[257,256]{1,0:T(8,128)S(1)}, u32[]{:S(2)}, u32[]{:S(2)}) collective-permute-start(f32[257,256]{1,0:T(8,128)S(1)} %pad_maximum_fusion.2), channel_id=1, source_target_pairs={{0,2},{1,3},{2,4},{3,5},{4,6},{5,7},{6,8},{7,9},{8,10},{9,11},{10,... | collective-permute-start | bytes 789512 | tf_op jit(solution)/shard_map/ppermute | solution.py:13
  88.0 18.1 %collective-permute-start.1 = (f32[256,256]{1,0:T(8,128)S(1)}, f32[256,256]{1,0:T(8,128)S(1)}, u32[]{:S(2)}, u32[]{:S(2)}) collective-permute-start(f32[256,256]{1,0:T(8,128)S(1)} %convolution_select_fusion.11), channel_id=1, source_target_pairs={{2,0},{3,1},{4,2},{5,3},{6,4},{7,5},{8,6},{9,7},{10,8},{11,9},{12,... | collective-permute-start | bytes 786440 | tf_op jit(solution)/shard_map/ppermute | solution.py:13
  98.0 10.4 %collective-permute-start.14 = (f32[257,256]{1,0:T(8,128)S(1)}, f32[257,256]{1,0:T(8,128)S(1)}, u32[]{:S(2)}, u32[]{:S(2)}) collective-permute-start(f32[257,256]{1,0:T(8,128)S(1)} %pad_maximum_fusion.3), channel_id=1, source_target_pairs={{0,4},{1,5},{2,6},{3,7},{4,8},{5,9},{6,10},{7,11},{8,12},{9,13},{1... | collective-permute-start | bytes 789512 | tf_op jit(solution)/shard_map/ppermute | solution.py:13
  104.2 9.5 %collective-permute-start.7 = (f32[256,256]{1,0:T(8,128)S(1)}, f32[256,256]{1,0:T(8,128)S(1)}, u32[]{:S(2)}, u32[]{:S(2)}) collective-permute-start(f32[256,256]{1,0:T(8,128)S(1)} %fusion.8), channel_id=1, source_target_pairs={{2,0},{3,1},{4,2},{5,3},{6,4},{7,5},{8,6},{9,7},{10,8},{11,9},{12,... | collective-permute-start | bytes 786440 | tf_op jit(solution)/shard_map/ppermute | solution.py:13
  106.5 16.1 %collective-permute-start.2 = (f32[256,256]{1,0:T(8,128)S(1)}, f32[256,256]{1,0:T(8,128)S(1)}, u32[]{:S(2)}, u32[]{:S(2)}) collective-permute-start(f32[256,256]{1,0:T(8,128)S(1)} %convolution_select_fusion.10), channel_id=1, source_target_pairs={{4,0},{5,1},{6,2},{7,3},{8,4},{9,5},{10,6},{11,7},{12,8},{13,9},{1... | collective-permute-start | bytes 786440 | tf_op jit(solution)/shard_map/ppermute | solution.py:13
  109.2 9.4 %collective-permute-start.15 = (f32[257,256]{1,0:T(8,128)S(1)}, f32[257,256]{1,0:T(8,128)S(1)}, u32[]{:S(2)}, u32[]{:S(2)}) collective-permute-start(f32[257,256]{1,0:T(8,128)S(1)} %pad_maximum_fusion.4), channel_id=1, source_target_pairs={{0,8},{1,9},{2,10},{3,11},{4,12},{5,13},{6,14},{7,15},{8,16},{9,17... | collective-permute-start | bytes 789512 | tf_op jit(solution)/shard_map/ppermute | solution.py:13
  114.5 11.3 %collective-permute-start.8 = (f32[256,256]{1,0:T(8,128)S(1)}, f32[256,256]{1,0:T(8,128)S(1)}, u32[]{:S(2)}, u32[]{:S(2)}) collective-permute-start(f32[256,256]{1,0:T(8,128)S(1)} %fusion.7), channel_id=1, source_target_pairs={{4,0},{5,1},{6,2},{7,3},{8,4},{9,5},{10,6},{11,7},{12,8},{13,9},{1... | collective-permute-start | bytes 786440 | tf_op jit(solution)/shard_map/ppermute | solution.py:13
  119.3 10.9 %collective-permute-start.16 = (f32[257,256]{1,0:T(8,128)S(1)}, f32[257,256]{1,0:T(8,128)S(1)}, u32[]{:S(2)}, u32[]{:S(2)}) collective-permute-start(f32[257,256]{1,0:T(8,128)S(1)} %pad_maximum_fusion.5), channel_id=1, source_target_pairs={{0,16},{1,17},{2,18},{3,19},{4,20},{5,21},{6,22},{7,23},{8,24},{9,... | collective-permute-start | bytes 789512 | tf_op jit(solution)/shard_map/ppermute | solution.py:13
  122.9 15.0 %collective-permute-start.3 = (f32[256,256]{1,0:T(8,128)S(1)}, f32[256,256]{1,0:T(8,128)S(1)}, u32[]{:S(2)}, u32[]{:S(2)}) collective-permute-start(f32[256,256]{1,0:T(8,128)S(1)} %convolution_select_fusion.9), channel_id=1, source_target_pairs={{8,0},{9,1},{10,2},{11,3},{12,4},{13,5},{14,6},{15,7},{16,8},{17,9... | collective-permute-start | bytes 786440 | tf_op jit(solution)/shard_map/ppermute | solution.py:13
  131.0 9.3 %collective-permute-start.17 = (f32[257,256]{1,0:T(8,128)S(1)}, f32[257,256]{1,0:T(8,128)S(1)}, u32[]{:S(2)}, u32[]{:S(2)}) collective-permute-start(f32[257,256]{1,0:T(8,128)S(1)} %pad_maximum_fusion.6), channel_id=1, source_target_pairs={{0,32},{1,33},{2,34},{3,35},{4,36},{5,37},{6,38},{7,39},{8,40},{9,... | collective-permute-start | bytes 789512 | tf_op jit(solution)/shard_map/ppermute | solution.py:13
  135.1 3.3 %copy-start.10 = (f32[256,256]{1,0:T(8,128)}, f32[256,256]{1,0:T(8,128)S(1)}, u32[]{:S(2)}) copy-start(f32[256,256]{1,0:T(8,128)S(1)} %fusion.6) | copy-start | bytes 786436
  135.1 16.1 %collective-permute-start.9 = (f32[256,256]{1,0:T(8,128)S(1)}, f32[256,256]{1,0:T(8,128)S(1)}, u32[]{:S(2)}, u32[]{:S(2)}) collective-permute-start(f32[256,256]{1,0:T(8,128)S(1)} %fusion.6), channel_id=1, source_target_pairs={{8,0},{9,1},{10,2},{11,3},{12,4},{13,5},{14,6},{15,7},{16,8},{17,9... | collective-permute-start | bytes 786440 | tf_op jit(solution)/shard_map/ppermute | solution.py:13
  138.4 37.0 %collective-permute-start.4 = (f32[256,256]{1,0:T(8,128)S(1)}, f32[256,256]{1,0:T(8,128)}, u32[]{:S(2)}, u32[]{:S(2)}) collective-permute-start(f32[256,256]{1,0:T(8,128)S(1)} %convolution_select_fusion.8), channel_id=1, source_target_pairs={{16,0},{17,1},{18,2},{19,3},{20,4},{21,5},{22,6},{23,7},{24,8},{25... | collective-permute-start | bytes 786440 | tf_op jit(solution)/shard_map/ppermute | solution.py:13
  140.6 2.6 collective-permute-start.18
  143.6 13.2 %collective-permute-start.19 = (f32[256]{0:T(256)S(1)}, f32[256]{0:T(256)S(1)}, u32[]{:S(2)}, u32[]{:S(2)}) collective-permute-start(f32[256]{0:T(256)S(1)} %add_select_fusion.7), channel_id=1, source_target_pairs={{0,1},{1,2},{2,3},{3,4},{4,5},{5,6},{6,7},{7,8},{8,9},{9,10},{10,1... | collective-permute-start | bytes 3080 | tf_op jit(solution)/shard_map/ppermute | solution.py:13
  159.5 1.0 copy-start.5
  160.0 5.1 %copy-start.9 = (f32[256,256]{1,0:T(8,128)S(1)}, f32[256,256]{1,0:T(8,128)}, u32[]{:S(2)}) copy-start(f32[256,256]{1,0:T(8,128)} %fusion.74) | copy-start | bytes 786436
  160.8 8.3 %collective-permute-start.20 = (f32[256]{0:T(256)S(1)}, f32[256]{0:T(256)S(1)}, u32[]{:S(2)}, u32[]{:S(2)}) collective-permute-start(f32[256]{0:T(256)S(1)} %bitcast.381), channel_id=1, source_target_pairs={{1,0},{2,1},{3,2},{4,3},{5,4},{6,5},{7,6},{8,7},{9,8},{10,9},{11,1... | collective-permute-start | bytes 3080 | tf_op jit(solution)/shard_map/ppermute | solution.py:13
  166.5 15.9 %collective-permute-start.10 = (f32[256,256]{1,0:T(8,128)S(1)}, f32[256,256]{1,0:T(8,128)S(1)}, u32[]{:S(2)}, u32[]{:S(2)}) collective-permute-start(f32[256,256]{1,0:T(8,128)S(1)} %fusion.5), channel_id=1, source_target_pairs={{16,0},{17,1},{18,2},{19,3},{20,4},{21,5},{22,6},{23,7},{24,8},{25... | collective-permute-start | bytes 786440 | tf_op jit(solution)/shard_map/ppermute | solution.py:13
  170.4 9.8 %collective-permute-start.21 = (f32[256]{0:T(256)S(1)}, f32[256]{0:T(256)S(1)}, u32[]{:S(2)}, u32[]{:S(2)}) collective-permute-start(f32[256]{0:T(256)S(1)} %add_select_fusion.6), channel_id=1, source_target_pairs={{2,0},{3,1},{4,2},{5,3},{6,4},{7,5},{8,6},{9,7},{10,8},{11,9},{12,... | collective-permute-start | bytes 3080 | tf_op jit(solution)/shard_map/ppermute | solution.py:13
  176.7 31.1 %collective-permute-start.5 = (f32[256,256]{1,0:T(8,128)S(1)}, f32[256,256]{1,0:T(8,128)S(1)}, u32[]{:S(2)}, u32[]{:S(2)}) collective-permute-start(f32[256,256]{1,0:T(8,128)S(1)} %convolution_select_fusion.7), channel_id=1, source_target_pairs={{32,0},{33,1},{34,2},{35,3},{36,4},{37,5},{38,6},{39,7},{40,8},{41... | collective-permute-start | bytes 786440 | tf_op jit(solution)/shard_map/ppermute | solution.py:13
  180.5 7.0 %collective-permute-start.22 = (f32[256]{0:T(256)S(1)}, f32[256]{0:T(256)S(1)}, u32[]{:S(2)}, u32[]{:S(2)}) collective-permute-start(f32[256]{0:T(256)S(1)} %add_select_fusion.5), channel_id=1, source_target_pairs={{4,0},{5,1},{6,2},{7,3},{8,4},{9,5},{10,6},{11,7},{12,8},{13,9},{1... | collective-permute-start | bytes 3080 | tf_op jit(solution)/shard_map/ppermute | solution.py:13
  187.8 6.4 %collective-permute-start.23 = (f32[256]{0:T(256)S(1)}, f32[256]{0:T(256)S(1)}, u32[]{:S(2)}, u32[]{:S(2)}) collective-permute-start(f32[256]{0:T(256)S(1)} %add_select_fusion.4), channel_id=1, source_target_pairs={{8,0},{9,1},{10,2},{11,3},{12,4},{13,5},{14,6},{15,7},{16,8},{17,9... | collective-permute-start | bytes 3080 | tf_op jit(solution)/shard_map/ppermute | solution.py:13
  190.2 9.0 %collective-permute-start.11 = (f32[256,256]{1,0:T(8,128)S(1)}, f32[256,256]{1,0:T(8,128)S(1)}, u32[]{:S(2)}, u32[]{:S(2)}) collective-permute-start(f32[256,256]{1,0:T(8,128)S(1)} %fusion.4), channel_id=1, source_target_pairs={{32,0},{33,1},{34,2},{35,3},{36,4},{37,5},{38,6},{39,7},{40,8},{41... | collective-permute-start | bytes 786440 | tf_op jit(solution)/shard_map/ppermute | solution.py:13
  194.6 6.7 %collective-permute-start.24 = (f32[256]{0:T(256)S(1)}, f32[256]{0:T(256)S(1)}, u32[]{:S(2)}, u32[]{:S(2)}) collective-permute-start(f32[256]{0:T(256)S(1)} %add_select_fusion.3), channel_id=1, source_target_pairs={{16,0},{17,1},{18,2},{19,3},{20,4},{21,5},{22,6},{23,7},{24,8},{25... | collective-permute-start | bytes 3080 | tf_op jit(solution)/shard_map/ppermute | solution.py:13
  201.6 4.6 %collective-permute-start.25 = (f32[256]{0:T(256)S(1)}, f32[256]{0:T(256)S(1)}, u32[]{:S(2)}, u32[]{:S(2)}) collective-permute-start(f32[256]{0:T(256)S(1)} %add_select_fusion.2), channel_id=1, source_target_pairs={{32,0},{33,1},{34,2},{35,3},{36,4},{37,5},{38,6},{39,7},{40,8},{41... | collective-permute-start | bytes 3080 | tf_op jit(solution)/shard_map/ppermute | solution.py:13
  206.5 5.8 %collective-permute-start.26 = (f32[256]{0:T(256)S(1)}, f32[256]{0:T(256)S(1)}, u32[]{:S(2)}, u32[]{:S(2)}) collective-permute-start(f32[256]{0:T(256)S(1)} %add_select_fusion.1), channel_id=1, source_target_pairs={{64,0},{65,1},{66,2},{67,3},{68,4},{69,5},{70,6},{71,7},{72,8},{73... | collective-permute-start | bytes 3080 | tf_op jit(solution)/shard_map/ppermute | solution.py:13
  212.7 7.2 %collective-permute-start.27 = (f32[256]{0:T(256)S(1)}, f32[256]{0:T(256)S(1)}, u32[]{:S(2)}, u32[]{:S(2)}) collective-permute-start(f32[256]{0:T(256)S(1)} %add_select_fusion), channel_id=1, source_target_pairs={{1,0},{2,1},{3,2},{4,3},{5,4},{6,5},{7,6},{8,7},{9,8},{10,9},{11,1... | collective-permute-start | bytes 3080 | tf_op jit(solution)/shard_map/ppermute | solution.py:13
  219.8 21.5 %collective-permute-start.29 = (f32[256,256]{1,0:T(8,128)S(1)}, f32[256,256]{1,0:T(8,128)S(1)}, u32[]{:S(2)}, u32[]{:S(2)}) collective-permute-start(f32[256,256]{1,0:T(8,128)S(1)} %fusion.3), channel_id=1, source_target_pairs={{65,0},{66,1},{67,2},{68,3},{69,4},{70,5},{71,6},{72,7},{73,8},{74... | collective-permute-start | bytes 786440 | tf_op jit(solution)/shard_map/ppermute | solution.py:13
  221.1 20.6 %collective-permute-start.30 = (f32[256,256]{1,0:T(8,128)S(1)}, f32[256,256]{1,0:T(8,128)S(1)}, u32[]{:S(2)}, u32[]{:S(2)}) collective-permute-start(f32[256,256]{1,0:T(8,128)S(1)} %fusion.3), channel_id=1, source_target_pairs={{1,0},{2,1},{3,2},{4,3},{5,4},{6,5},{7,6},{8,7},{9,8},{10,9},{11,1... | collective-permute-start | bytes 786440 | tf_op jit(solution)/shard_map/ppermute | solution.py:13
  226.5 14.8 %collective-permute-start.28 = (f32[256,256]{1,0:T(8,128)S(1)}, f32[256,256]{1,0:T(8,128)S(1)}, u32[]{:S(2)}, u32[]{:S(2)}) collective-permute-start(f32[256,256]{1,0:T(8,128)S(1)} %convolution_select_fusion.6), channel_id=1, source_target_pairs={{1,0},{2,1},{3,2},{4,3},{5,4},{6,5},{7,6},{8,7},{9,8},{10,9},{11,1... | collective-permute-start | bytes 786440 | tf_op jit(solution)/shard_map/ppermute | solution.py:13
  230.8 16.7 %all-to-all-start.4 = ((f32[4,1,256]{2,1,0:T(1,128)}), f32[4,1,256]{2,1,0:T(1,128)S(1)}, u32[]{:S(2)}, u32[]{:S(2)}) async-start(f32[4,1,256]{2,1,0:T(1,128)} %reshape.172), calls=%async_computation.4 | async-start | bytes 8192 | tf_op jit(solution)/shard_map/all_to_all | solution.py:193
  241.7 1.2 copy-start.2
  247.5 18.3 %all-to-all-start.5 = ((f32[4,256,256]{2,0,1:T(4,128)}), f32[4,256,256]{2,0,1:T(4,128)S(1)}, u32[]{:S(2)}, u32[]{:S(2)}) async-start(f32[4,256,256]{2,0,1:T(4,128)} %copy.48), calls=%async_computation.5 | async-start | bytes 2097152 | tf_op jit(solution)/shard_map/all_to_all | solution.py:193
